TPU v7x, 32 devices: a whole 2x2x4 slice. The times are simulated.
32 devices in a mesh: band: 8 (over z, x), slab: 4 (over y, core).
Axes of the slice: x: 2, y: 2, z: 4, core: 2. Of those that a mesh axis runs over, the one named last changes fastest.
Arguments:
- orbitals: float32 [32, 48, 2304], P('band', 'slab'), may hold values from -6 to 6
- partners: int32 [8, 2], replicated, may hold values from 0 to 7, as said below
- counts: int32 [8, 2], replicated, may hold values from 1 to 4
Outputs:
- forces: float32 [32, 48, 2304], P('band', 'slab')
- energy: float32 [], replicated
Inputs may be any that keep to these rules, and one draw needn't show every extreme that they name: `partners`: row g names two different band groups, neither of them g.
All inputs are finite; a program needn't handle non-finite values.
Results may differ from a plain program's by a relative error of at most 0.0001.
Values sent between devices are 32-bit elements; how exact they have to be, the bound alone decides.
No kernel may reach another device: no remote copies, remote signals or barrier semaphores. Data moves between devices by JAX's collectives and lax.ppermute only.
A program may use at most 64 MiB of HBM per device.

v0:
```python
import functools
import math

import jax
import jax.numpy as jnp
from jax import lax
from jax.experimental import pallas as pl
from jax.experimental.pallas import tpu as pltpu
from jax.sharding import PartitionSpec as P


NX = 48
NY = 48
NZ = 48
NZP = 96


slater_coeff = -((3.0 / math.pi) ** (1.0 / 3.0))
exchange_mix = 0.25
screening = 0.25
row_row = (((1,), (1,)), ((), ()))


def split(value):
    high = value.astype(jnp.bfloat16)
    low = (value - high.astype(jnp.float32)).astype(jnp.bfloat16)
    return high, low


def cas(rows, cols, length):
    phase_angle = 2.0 * math.pi / length * (rows * cols % length).astype(jnp.float32)
    return jnp.cos(phase_angle) + jnp.sin(phase_angle)


def split_table(matrix):
    high = lax.reduce_precision(matrix, 8, 7)
    return high.astype(jnp.bfloat16), (matrix - high).astype(jnp.bfloat16)


def wide(matrix):
    high, low = split_table(matrix)
    return jnp.concatenate([high, high, low], axis=1)


def tall(matrix):
    high, low = split_table(matrix)
    return jnp.concatenate([high, low], axis=0)


def wavenumber_sq(length):
    position = jnp.arange(length, dtype=jnp.int32)
    signed = jnp.where(position > length // 2, position - length, position).astype(jnp.float32)
    wave_number = 2.0 * math.pi / length * signed
    return wave_number * wave_number


def transform_tables(held_x):
    x_waves = jnp.arange(NX, dtype=jnp.int32)
    y_cells = jnp.arange(NY, dtype=jnp.int32)
    z_cells = jnp.arange(NZ, dtype=jnp.int32)
    z_waves = jnp.arange(NZP, dtype=jnp.int32)
    total = (
        wavenumber_sq(NZP)[:, None, None]
        + wavenumber_sq(NX)[None, :, None]
        + wavenumber_sq(NY)[None, None, :]
    )
    kernel_table = 4.0 * math.pi / (NX * NY * NZP) / (total + screening * screening)
    y_matrix = cas(y_cells[:, None], y_cells[None, :], NY)
    return (
        wide(cas(x_waves[:, None], held_x[None, :], NX)),
        wide(y_matrix),
        tall(cas(z_waves[:, None], z_cells[None, :], NZP)),
        kernel_table.reshape(NZP, NX * NY),
        wide(cas(z_cells[:, None], z_waves[None, :], NZP)),
        tall(y_matrix),
        wide(cas(held_x[:, None], x_waves[None, :], NX)),
    )


def apply_left(matrix, value):
    high, low = split(value)
    stacked = jnp.concatenate([high, low, high], axis=0)
    return jnp.dot(matrix, stacked, preferred_element_type=jnp.float32)


def apply_rows(matrix, high, low):
    half = matrix.shape[0] // 2
    both = lax.dot_general(matrix, high, row_row, preferred_element_type=jnp.float32)
    rest = lax.dot_general(matrix[:half], low, row_row, preferred_element_type=jnp.float32)
    return both[:half] + both[half:] + rest


def cut_into(refs, value, part_index):
    planes = NX // len(refs)
    part = refs[0].shape[1]
    fold = NY * NZ // part
    first = part_index * planes * fold
    for r, ref in enumerate(refs):
        for f in range(fold):
            ref[first + f * planes : first + (f + 1) * planes, :] = value[
                r * planes : (r + 1) * planes, f * part : (f + 1) * part
            ]


def store_force(force_refs, value):
    if len(force_refs) == 1:
        force_refs[0][...] = value
    else:
        cut_into(force_refs, value, 0)


def pair_kernel(
    slot, weights, own_ref, other_ref, x_fwd, y_fwd, z_fwd, table, z_inv, y_inv, x_inv,
    force_in, energy_in, *refs,
):
    *refs, lines, high_rows, low_rows, field = refs
    if len(refs) == 2:
        energy_out, *force_refs = refs
    else:
        squares_in, energy_out, *force_refs = refs
        cut_into(force_refs, squares_in[...], 1)
    total_weight = weights[slot, 0]
    request_weight = weights[slot, 1]

    @pl.when(total_weight == 0.0)
    def _():
        store_force(force_refs, force_in[...])
        energy_out[...] = energy_in[...]

    @pl.when(total_weight != 0.0)
    def _():
        other = other_ref[...]
        density = own_ref[...] * other
        spectrum = apply_left(x_fwd[...], density)
        for y in range(NY):
            lines[y * NX : (y + 1) * NX, :] = spectrum[:, y * NZ : (y + 1) * NZ]
        for q in range(NX):
            plane = apply_left(y_fwd[...], lines[pl.ds(q, NY, stride=NX), :])
            high, low = split(plane)
            high_rows[q * NY : (q + 1) * NY, :] = high
            low_rows[q * NY : (q + 1) * NY, :] = low
        spectrum = apply_rows(z_fwd[...], high_rows[...], low_rows[...])
        weighted = spectrum * table[...]
        products = jnp.sum(spectrum * weighted, axis=0, keepdims=True)
        folded = products[:, :128]
        for start in range(128, NX * NY, 128):
            folded = folded + products[:, start : start + 128]
        energy_out[...] = energy_in[...] + request_weight * folded
        spectrum = apply_left(z_inv[...], weighted)
        for q in range(NX):
            high, low = split(spectrum[:, q * NY : (q + 1) * NY])
            high_rows[q * NZ : (q + 1) * NZ, :] = high
            low_rows[q * NZ : (q + 1) * NZ, :] = low
        spectrum = apply_rows(y_inv[...], high_rows[...], low_rows[...])
        for q in range(NX):
            lines[q * NY : (q + 1) * NY, :] = spectrum[:, q * NZ : (q + 1) * NZ]
        for y in range(NY):
            field[:, y * NZ : (y + 1) * NZ] = apply_left(
                x_inv[...], lines[pl.ds(y, NX, stride=NY), :]
            )
        store_force(
            force_refs, force_in[...] - (exchange_mix * total_weight) * (field[...] * other)
        )


def pair_step(slot, weights, own, other, tables, force, energy, pieces=1, squares=None):
    if pieces == 1:
        piece = force.shape
        extra = ()
    else:
        planes = NX // pieces
        fold = fold_of(planes, NY * NZ)
        piece = (2 * planes * fold, NY * NZ // fold)
        extra = (squares,)
    outs = [jax.ShapeDtypeStruct(energy.shape, jnp.float32)]
    outs += [jax.ShapeDtypeStruct(piece, jnp.float32)] * pieces
    return pl.pallas_call(
        functools.partial(pair_kernel, slot),
        out_shape=outs,
        in_specs=with_scalar(4 + len(tables) + len(extra)),
        out_specs=in_vmem(1 + pieces),
        scratch_shapes=[
            pltpu.VMEM((NX * NY, NZ), jnp.float32),
            pltpu.VMEM((NX * NY, NZ), jnp.bfloat16),
            pltpu.VMEM((NX * NY, NZ), jnp.bfloat16),
            pltpu.VMEM((NX, NY * NZ), jnp.float32),
        ],
        compiler_params=pltpu.CompilerParams(vmem_limit_bytes=32 << 20),
        cost_estimate=pl.CostEstimate(flops=3 << 30, transcendentals=0, bytes_accessed=3 << 20),
        name="pair_step",
    )(weights, own, other, *tables, force, energy, *extra)


def fold_of(planes, cells):
    return 2 if (2 * planes) % 8 == 0 and cells % 256 == 0 else 1


def in_vmem(count):
    return [pl.BlockSpec(memory_space=pltpu.VMEM)] * count


def with_scalar(count):
    return [pl.BlockSpec(memory_space=pltpu.SMEM)] + in_vmem(count)


def pick(place, choices):
    chosen = choices[0]
    for index in range(1, len(choices)):
        chosen = jnp.where(place == index, choices[index], chosen)
    return chosen


def prepare_kernel(fold, place, orbitals, *out_refs):
    planes, slabs, cells = orbitals.shape
    part = cells // fold
    for f in range(fold):
        rows = slice(f * planes, (f + 1) * planes)
        blocks = [orbitals[:, j, f * part : (f + 1) * part] for j in range(slabs)]
        for r in range(slabs):
            out_refs[r][rows, :] = pick(place[0] ^ r, blocks)


def prepare(place, orbitals):
    planes, slabs, cells = orbitals.shape
    fold = fold_of(planes, cells)
    piece = jax.ShapeDtypeStruct((planes * fold, cells // fold), jnp.float32)
    return pl.pallas_call(
        functools.partial(prepare_kernel, fold),
        out_shape=[piece] * slabs,
        in_specs=with_scalar(1),
        out_specs=in_vmem(slabs),
        compiler_params=pltpu.CompilerParams(vmem_limit_bytes=8 << 20),
        name="prepare",
    )(place, orbitals)


def assemble_kernel(fold, *refs):
    out_ref = refs[-1]
    planes = refs[0].shape[0] // fold
    part = refs[0].shape[1]
    for r, ref in enumerate(refs[:-1]):
        for f in range(fold):
            out_ref[r * planes : (r + 1) * planes, f * part : (f + 1) * part] = ref[
                f * planes : (f + 1) * planes, :
            ]


def assemble(pieces):
    _, part = pieces[0].shape
    fold = NY * NZ // part
    return pl.pallas_call(
        functools.partial(assemble_kernel, fold),
        out_shape=jax.ShapeDtypeStruct((NX, NY * NZ), jnp.float32),
        in_specs=in_vmem(len(pieces)),
        out_specs=in_vmem(1)[0],
        compiler_params=pltpu.CompilerParams(vmem_limit_bytes=8 << 20),
        name="assemble",
    )(*pieces)


def finish_kernel(fold, place, orbitals, local_pot, *refs):
    out_ref = refs[-1]
    planes, slabs, cells = orbitals.shape
    part = cells // fold
    for f in range(fold):
        rows = slice(f * planes, (f + 1) * planes)
        cols = slice(f * part, (f + 1) * part)
        pieces = [ref[rows, :] for ref in refs[:-1]]
        local = local_pot[rows, :]
        for j in range(slabs):
            out_ref[:, j, cols] = local * orbitals[:, j, cols] + pick(place[0] ^ j, pieces)


def finish(place, orbitals, local_pot, pieces):
    planes, _, cells = orbitals.shape
    return pl.pallas_call(
        functools.partial(finish_kernel, fold_of(planes, cells)),
        out_shape=jax.ShapeDtypeStruct(orbitals.shape, jnp.float32),
        in_specs=with_scalar(2 + len(pieces)),
        out_specs=in_vmem(1)[0],
        compiler_params=pltpu.CompilerParams(vmem_limit_bytes=8 << 20),
        name="finish",
    )(place, orbitals, local_pot, *pieces)


def swap(value, axis, reach):
    size = lax.axis_size(axis)
    return lax.ppermute(value, axis, [(i, i ^ reach) for i in range(size)])


def share(value, devices):
    sent = jnp.broadcast_to(value[None], (devices,) + value.shape)
    return lax.all_to_all(sent, ("band", "slab"), 0, 0)


def gather_line(own, band_index, bands):
    place = band_index // 2
    inner = (place == 1) | (place == 2)
    half = own.shape[0] // 2

    def along(value, pairs):
        moves = [(2 * a + side, 2 * b + side) for a, b in pairs for side in (0, 1)]
        return lax.ppermute(value, "band", moves)

    def across_sides(value, places):
        moves = [(i, i ^ 1) for i in range(bands) if i // 2 in places]
        return lax.ppermute(value, "band", moves)

    outer_pairs = [(1, 0), (2, 3)]
    inner_pairs = [(1, 2), (2, 1)]
    places = (0, 1, 2, 3)
    near = along(own, [(0, 1), (1, 0), (2, 3), (3, 2)])
    side_own = across_sides(own, places)
    middle = along(own, inner_pairs)

    outward = along(middle, outer_pairs)
    side_near = across_sides(near, places)
    across = along(near, inner_pairs)

    outer = along(across, outer_pairs)
    second = jnp.where(inner, middle, outward)
    side_late = across_sides(jnp.where(inner, across, outward), places)
    side_middle = along(side_own, inner_pairs)
    third = jnp.where(inner, across, outer)

    side_head = across_sides(outer[:half], (0, 3))
    side_tail = along(side_late[half:], outer_pairs)
    side_last = jnp.where(inner, side_middle, jnp.concatenate([side_head, side_tail], axis=0))

    side = band_index % 2
    near_group = band_index ^ 2
    second_group = jnp.where(place < 2, 2, 1) * 2 + side
    third_group = jnp.where(place < 2, 3, 0) * 2 + side
    late_group = jnp.where(inner, third_group, second_group) ^ 1
    last_group = jnp.where(inner, second_group, third_group) ^ 1
    blocks = [
        (near, near_group),
        (side_own, band_index ^ 1),
        (side_near, near_group ^ 1),
        (second, second_group),
        (third, third_group),
        (side_late, late_group),
        (side_last, last_group),
    ]
    return blocks


def gather_doubling(own, band_index, bands):
    held = [(own, band_index)]
    reach = 1
    while reach < bands:
        held = held + [(swap(block, "band", reach), group ^ reach) for block, group in held]
        reach *= 2
    return held[1:]


def on_line(bands):
    return bands // 2 == 4


def body(orbitals, partners, counts):
    bands = lax.axis_size("band")
    slabs = lax.axis_size("slab")
    band_index = lax.axis_index("band")
    slab_index = lax.axis_index("slab")
    orb_group, planes, _ = orbitals.shape
    total_orbs = orb_group * bands
    assert orb_group == slabs

    place = slab_index.astype(jnp.int32).reshape(1)
    by_plane = jnp.transpose(orbitals, (1, 0, 2))
    sends = prepare(place, by_plane)
    own = assemble([sends[0]] + [swap(sends[r], "slab", r) for r in range(1, slabs)])

    gather = gather_line if on_line(bands) else gather_doubling
    others = gather(own, band_index, bands)

    row = jnp.arange(NX, dtype=jnp.int32)
    held_x = (slab_index ^ (row // planes)) * planes + row % planes
    tables = transform_tables(held_x)

    groups = jnp.stack([group for _, group in others]).astype(jnp.int32)
    active = (slab_index < counts).astype(jnp.float32)
    mine = jnp.arange(bands, dtype=jnp.int32)[:, None] == band_index
    my_partners = jnp.sum(jnp.where(mine, partners, 0), axis=0)
    my_active = jnp.sum(jnp.where(mine, active, 0.0), axis=0)
    requested = jnp.sum(
        jnp.where(groups[:, None] == my_partners[None, :], my_active[None, :], 0.0), axis=1
    )
    wanted_by = jnp.sum(jnp.where(partners == band_index, active, 0.0), axis=1)
    chosen = groups[:, None] == jnp.arange(bands, dtype=jnp.int32)[None, :]
    returned = jnp.sum(jnp.where(chosen, wanted_by[None, :], 0.0), axis=1)
    weights = jnp.stack([requested + returned, requested], axis=1)

    force = jnp.zeros((NX, NY * NZ), jnp.float32)
    energy = jnp.zeros((1, 128), jnp.float32)
    squares = own * own
    for other, _ in others:
        squares = squares + other * other
    for slot, (other, _) in enumerate(others):
        if slot < len(others) - 1:
            energy, force = pair_step(slot, weights, own, other, tables, force, energy)
        else:
            energy, *outgoing = pair_step(
                slot, weights, own, other, tables, force, energy, slabs, squares
            )

    arrived = [outgoing[0]] + [swap(outgoing[r], "slab", r) for r in range(1, slabs)]
    shared = share(energy, bands * slabs)
    rows = arrived[0].shape[0] // 2
    density = 2.0 / total_orbs * sum(piece[rows:] for piece in arrived)
    local_pot = slater_coeff * jnp.cbrt(density)
    forces = finish(place, by_plane, local_pot, arrived)
    energy_total = jnp.sum(shared)
    return (
        jnp.transpose(forces, (1, 0, 2)),
        -energy_total / (2.0 * total_orbs * NX * NY * NZ),
    )


def solution(mesh):
    placed = (P("band", "slab", None), P(), P())
    return jax.shard_map(
        body, mesh=mesh, in_specs=placed, out_specs=(P("band", "slab", None), P()), check_vma=False
    )
```

profile of v0, /device:TPU:0, one launch (start us, length us, event | category | flops | bytes accessed | tf_op | source)
XLA Modules:
  0.0 86.4 jit_solution(4786347463022302298)
XLA Ops:
  0.6 1.0 %copy-done = f32[4,12,2304]{2,0,1:T(4,128)S(1)} copy-done((f32[4,12,2304]{2,0,1:T(4,128)S(1)}, f32[4,12,2304]{2,0,1:T(4,128)}, u32[]{:S(2)}) %copy-start) | copy-done | bytes 442392
  2.4 2.6 %collective-permute-start.1 = (f32[24,1152]{1,0:T(8,128)S(1)}, f32[24,1152]{1,0:T(8,128)S(1)}, u32[]{:S(2)}, u32[]{:S(2)}) collective-permute-start(f32[24,1152]{1,0:T(8,128)S(1)} %get-tuple-element.25), channel_id=1, source_target_pairs={{0,2},{1,3},{2,0},{3,1},{4,6},{5,7},{6,4},{7,5},{8,10},{9,11},{10,... | collective-permute-start | bytes 331784 | tf_op jit(solution)/shard_map/ppermute | solution.py:288
  5.4 0.8 select_reduce_fusion.2
  6.2 0.8 fusion.33
  8.9 1.8 %collective-permute-done.2.refs_3_ = f32[24,1152]{1,0:T(8,128)S(1)} collective-permute-done((f32[24,1152]{1,0:T(8,128)S(1)}, f32[24,1152]{1,0:T(8,128)S(1)}, u32[]{:S(2)}, u32[]{:S(2)}) %collective-permute-start.2) | collective-permute-done | bytes 110624 | tf_op jit(solution)/shard_map/ppermute | solution.py:288
  10.8 1.6 %collective-permute-start.5 = (f32[48,2304]{1,0:T(8,128)S(1)}, f32[48,2304]{1,0:T(8,128)S(1)}, u32[]{:S(2)}, u32[]{:S(2)}) collective-permute-start(f32[48,2304]{1,0:T(8,128)S(1)} %assemble.1.own_ref), channel_id=1, source_target_pairs={{0,8},{4,12},{8,0},{12,4},{16,24},{20,28},{24,16},{28,20},{1,9},{5... | collective-permute-start | bytes 1327112 | tf_op jit(solution)/shard_map/ppermute | solution.py:303
  12.4 0.7 collective-permute-start.9
  13.5 1.6 %collective-permute-start.3 = (f32[48,2304]{1,0:T(8,128)S(1)}, f32[48,2304]{1,0:T(8,128)S(1)}, u32[]{:S(2)}, u32[]{:S(2)}) collective-permute-start(f32[48,2304]{1,0:T(8,128)S(1)} %assemble.1.own_ref), channel_id=1, source_target_pairs={{0,4},{4,0},{8,12},{12,8},{16,20},{20,16},{24,28},{28,24},{1,5},{5... | collective-permute-start | bytes 1327112 | tf_op jit(solution)/shard_map/ppermute | solution.py:307
  15.0 8.1 %collective-permute-done.5.other_ref = f32[48,2304]{1,0:T(8,128)S(1)} collective-permute-done((f32[48,2304]{1,0:T(8,128)S(1)}, f32[48,2304]{1,0:T(8,128)S(1)}, u32[]{:S(2)}, u32[]{:S(2)}) %collective-permute-start.5) | collective-permute-done | bytes 442400 | tf_op jit(solution)/shard_map/ppermute | solution.py:303
  23.1 0.7 collective-permute-start.6
  23.8 1.3 %collective-permute-start.10 = (f32[48,2304]{1,0:T(8,128)S(1)}, f32[48,2304]{1,0:T(8,128)S(1)}, u32[]{:S(2)}, u32[]{:S(2)}) collective-permute-start(f32[48,2304]{1,0:T(8,128)S(1)} %collective-permute-done.9), channel_id=1, source_target_pairs={{8,0},{12,4},{16,24},{20,28},{9,1},{13,5},{17,25},{21,29},{10,2},{... | collective-permute-start | bytes 1327112 | tf_op jit(solution)/shard_map/ppermute | solution.py:303
  25.2 1.7 %collective-permute-start.13 = (f32[48,2304]{1,0:T(8,128)S(1)}, f32[48,2304]{1,0:T(8,128)S(1)}, u32[]{:S(2)}, u32[]{:S(2)}) collective-permute-start(f32[48,2304]{1,0:T(8,128)S(1)} %collective-permute-done.5.other_ref), channel_id=1, source_target_pairs={{0,4},{4,0},{8,12},{12,8},{16,20},{20,16},{24,28},{28,24},{1,5},{5... | collective-permute-start | bytes 1327112 | tf_op jit(solution)/shard_map/ppermute | solution.py:307
  26.9 0.7 collective-permute-start.4
  27.6 11.5 %collective-permute-done.10 = f32[48,2304]{1,0:T(8,128)S(1)} collective-permute-done((f32[48,2304]{1,0:T(8,128)S(1)}, f32[48,2304]{1,0:T(8,128)S(1)}, u32[]{:S(2)}, u32[]{:S(2)}) %collective-permute-start.10) | collective-permute-done | bytes 442400 | tf_op jit(solution)/shard_map/ppermute | solution.py:303
  39.2 1.6 %collective-permute-start.11 = (f32[48,2304]{1,0:T(8,128)S(1)}, f32[48,2304]{1,0:T(8,128)S(1)}, u32[]{:S(2)}, u32[]{:S(2)}) collective-permute-start(f32[48,2304]{1,0:T(8,128)S(1)} %broadcast_select_fusion.2), channel_id=1, source_target_pairs={{0,4},{4,0},{8,12},{12,8},{16,20},{20,16},{24,28},{28,24},{1,5},{5... | collective-permute-start | bytes 1327112 | tf_op jit(solution)/shard_map/ppermute | solution.py:307
  40.8 1.3 %collective-permute-start.7 = (f32[48,2304]{1,0:T(8,128)S(1)}, f32[48,2304]{1,0:T(8,128)S(1)}, u32[]{:S(2)}, u32[]{:S(2)}) collective-permute-start(f32[48,2304]{1,0:T(8,128)S(1)} %collective-permute-done.6), channel_id=1, source_target_pairs={{8,0},{12,4},{16,24},{20,28},{9,1},{13,5},{17,25},{21,29},{10,2},{... | collective-permute-start | bytes 1327112 | tf_op jit(solution)/shard_map/ppermute | solution.py:303
  42.1 4.0 %pair_step.7 = (f32[1,128]{1,0:T(1,128)S(1)}, f32[48,2304]{1,0:T(8,128)S(1)}) custom-call(f32[7,2]{1,0:T(8,128)S(1)} %copy.45.weights, f32[48,2304]{1,0:T(8,128)S(1)} %assemble.1.own_ref, f32[48,2304]{1,0:T(8,128)S(1)} %collective-permute-done.5.other_ref, bf16[48,144]{1,0:T(8,128)(2,1)S(1)} %get-tuple-element.56.x_fwd, ...), custom_call_target="tpu_custom_call" | custom-call | flops 3221225472 | bytes 3145728 | tf_op jit(solution)/shard_map/pair_step/pallas_call | solution.py:177
  46.1 0.6 pair_step.8
  46.8 3.3 %collective-permute-done.11.other_ref = f32[48,2304]{1,0:T(8,128)S(1)} collective-permute-done((f32[48,2304]{1,0:T(8,128)S(1)}, f32[48,2304]{1,0:T(8,128)S(1)}, u32[]{:S(2)}, u32[]{:S(2)}) %collective-permute-start.11) | collective-permute-done | bytes 442400 | tf_op jit(solution)/shard_map/ppermute | solution.py:307
  50.0 1.3 %collective-permute-start.12 = (f32[24,2304]{1,0:T(8,128)S(1)}, f32[24,2304]{1,0:T(8,128)S(1)}, u32[]{:S(2)}, u32[]{:S(2)}) collective-permute-start(f32[24,2304]{1,0:T(8,128)S(1)} %slice.25), channel_id=1, source_target_pairs={{8,0},{12,4},{16,24},{20,28},{9,1},{13,5},{17,25},{21,29},{10,2},{... | collective-permute-start | bytes 663560 | tf_op jit(solution)/shard_map/ppermute | solution.py:303
  51.3 1.9 %collective-permute-done.7 = f32[48,2304]{1,0:T(8,128)S(1)} collective-permute-done((f32[48,2304]{1,0:T(8,128)S(1)}, f32[48,2304]{1,0:T(8,128)S(1)}, u32[]{:S(2)}, u32[]{:S(2)}) %collective-permute-start.7) | collective-permute-done | bytes 442400 | tf_op jit(solution)/shard_map/ppermute | solution.py:303
  53.3 2.3 %collective-permute-start.8 = (f32[24,2304]{1,0:T(8,128)S(1)}, f32[24,2304]{1,0:T(8,128)S(1)}, u32[]{:S(2)}, u32[]{:S(2)}) collective-permute-start(f32[24,2304]{1,0:T(8,128)S(1)} %slice.24), channel_id=1, source_target_pairs={{0,4},{4,0},{24,28},{28,24},{1,5},{5,1},{25,29},{29,25},{2,6},{6,2... | collective-permute-start | bytes 663560 | tf_op jit(solution)/shard_map/ppermute | solution.py:307
  55.6 0.8 pair_step.9
  56.4 1.5 %collective-permute-done.12 = f32[24,2304]{1,0:T(8,128)S(1)} collective-permute-done((f32[24,2304]{1,0:T(8,128)S(1)}, f32[24,2304]{1,0:T(8,128)S(1)}, u32[]{:S(2)}, u32[]{:S(2)}) %collective-permute-start.12) | collective-permute-done | bytes 221216 | tf_op jit(solution)/shard_map/ppermute | solution.py:303
  57.9 3.2 %collective-permute-done.8 = f32[24,2304]{1,0:T(8,128)S(1)} collective-permute-done((f32[24,2304]{1,0:T(8,128)S(1)}, f32[24,2304]{1,0:T(8,128)S(1)}, u32[]{:S(2)}, u32[]{:S(2)}) %collective-permute-start.8) | collective-permute-done | bytes 221216 | tf_op jit(solution)/shard_map/ppermute | solution.py:307
  61.4 4.0 %pair_step.10 = (f32[1,128]{1,0:T(1,128)S(1)}, f32[48,2304]{1,0:T(8,128)S(1)}) custom-call(f32[7,2]{1,0:T(8,128)S(1)} %copy.45.weights, f32[48,2304]{1,0:T(8,128)S(1)} %assemble.1.own_ref, f32[48,2304]{1,0:T(8,128)S(1)} %get-tuple-element.47.other_ref, bf16[48,144]{1,0:T(8,128)(2,1)S(1)} %get-tuple-element.56.x_fwd, ...), custom_call_target="tpu_custom_call" | custom-call | flops 3221225472 | bytes 3145728 | tf_op jit(solution)/shard_map/pair_step/pallas_call | solution.py:177
  65.4 0.6 pair_step.11
  66.1 0.6 pair_step.12
  66.7 0.7 pair_step.13
  67.5 2.2 %collective-permute-start.15 = (f32[48,1152]{1,0:T(8,128)S(1)}, f32[48,1152]{1,0:T(8,128)S(1)}, u32[]{:S(2)}, u32[]{:S(2)}) collective-permute-start(f32[48,1152]{1,0:T(8,128)S(1)} %get-tuple-element.41), channel_id=1, source_target_pairs={{0,2},{1,3},{2,0},{3,1},{4,6},{5,7},{6,4},{7,5},{8,10},{9,11},{10,... | collective-permute-start | bytes 663560 | tf_op jit(solution)/shard_map/ppermute | solution.py:288
  69.8 12.9 %all_to_all.5 = f32[32,1,128]{2,1,0:T(1,128)S(1)} all-to-all(f32[32,1,128]{2,1,0:T(1,128)S(1)} %broadcast_in_dim.92), channel_id=1, replica_groups=mesh['band'=8,'slab'=4] {'band','slab'}, dimensions={0} | all-to-all | bytes 32768 | tf_op jit(solution)/shard_map/all_to_all | solution.py:293
  84.1 1.1 %finish.1 = f32[12,4,2304]{2,1,0:T(4,128)} custom-call(s32[1]{0:T(128)} %bitcast.place, f32[12,4,2304]{2,1,0:T(4,128)S(1)} %bitcast.18, f32[24,1152]{1,0:T(8,128)S(1)} %fusion.2.local_pot, f32[48,1152]{1,0:T(8,128)S(1)} %get-tuple-element.39.refs_0_, f32[48,1152]{1,0:T(8,128)S(1)} %collective-permute-done.14.refs_1_, ...), custom_call_target="tpu_custom_call" | custom-call | tf_op jit(solution)/shard_map/finish/pallas_call | solution.py:276
  (55 shorter events, 4.9 us)
Async XLA Ops:
  0.6 1.0 %copy-start = (f32[4,12,2304]{2,0,1:T(4,128)S(1)}, f32[4,12,2304]{2,0,1:T(4,128)}, u32[]{:S(2)}) copy-start(f32[4,12,2304]{2,0,1:T(4,128)} %param.3) | copy-start | bytes 1327108
  1.9 6.7 %collective-permute-start = (f32[24,1152]{1,0:T(8,128)S(1)}, f32[24,1152]{1,0:T(8,128)S(1)}, u32[]{:S(2)}, u32[]{:S(2)}) collective-permute-start(f32[24,1152]{1,0:T(8,128)S(1)} %get-tuple-element.24), channel_id=1, source_target_pairs={{0,1},{1,0},{2,3},{3,2},{4,5},{5,4},{6,7},{7,6},{8,9},{9,8},{10,11... | collective-permute-start | bytes 331784 | tf_op jit(solution)/shard_map/ppermute | solution.py:288
  2.4 6.5 %collective-permute-start.1 = (f32[24,1152]{1,0:T(8,128)S(1)}, f32[24,1152]{1,0:T(8,128)S(1)}, u32[]{:S(2)}, u32[]{:S(2)}) collective-permute-start(f32[24,1152]{1,0:T(8,128)S(1)} %get-tuple-element.25), channel_id=1, source_target_pairs={{0,2},{1,3},{2,0},{3,1},{4,6},{5,7},{6,4},{7,5},{8,10},{9,11},{10,... | collective-permute-start | bytes 331784 | tf_op jit(solution)/shard_map/ppermute | solution.py:288
  5.0 5.8 %collective-permute-start.2 = (f32[24,1152]{1,0:T(8,128)S(1)}, f32[24,1152]{1,0:T(8,128)S(1)}, u32[]{:S(2)}, u32[]{:S(2)}) collective-permute-start(f32[24,1152]{1,0:T(8,128)S(1)} %get-tuple-element.26), channel_id=1, source_target_pairs={{0,3},{1,2},{2,1},{3,0},{4,7},{5,6},{6,5},{7,4},{8,11},{9,10},{10,... | collective-permute-start | bytes 331784 | tf_op jit(solution)/shard_map/ppermute | solution.py:288
  10.8 12.3 %collective-permute-start.5 = (f32[48,2304]{1,0:T(8,128)S(1)}, f32[48,2304]{1,0:T(8,128)S(1)}, u32[]{:S(2)}, u32[]{:S(2)}) collective-permute-start(f32[48,2304]{1,0:T(8,128)S(1)} %assemble.1.own_ref), channel_id=1, source_target_pairs={{0,8},{4,12},{8,0},{12,4},{16,24},{20,28},{24,16},{28,20},{1,9},{5... | collective-permute-start | bytes 1327112 | tf_op jit(solution)/shard_map/ppermute | solution.py:303
  12.4 11.4 %collective-permute-start.9 = (f32[48,2304]{1,0:T(8,128)S(1)}, f32[48,2304]{1,0:T(8,128)S(1)}, u32[]{:S(2)}, u32[]{:S(2)}) collective-permute-start(f32[48,2304]{1,0:T(8,128)S(1)} %assemble.1.own_ref), channel_id=1, source_target_pairs={{8,16},{12,20},{16,8},{20,12},{9,17},{13,21},{17,9},{21,13},{10,18... | collective-permute-start | bytes 1327112 | tf_op jit(solution)/shard_map/ppermute | solution.py:303
  13.5 13.5 %collective-permute-start.3 = (f32[48,2304]{1,0:T(8,128)S(1)}, f32[48,2304]{1,0:T(8,128)S(1)}, u32[]{:S(2)}, u32[]{:S(2)}) collective-permute-start(f32[48,2304]{1,0:T(8,128)S(1)} %assemble.1.own_ref), channel_id=1, source_target_pairs={{0,4},{4,0},{8,12},{12,8},{16,20},{20,16},{24,28},{28,24},{1,5},{5... | collective-permute-start | bytes 1327112 | tf_op jit(solution)/shard_map/ppermute | solution.py:307
  23.1 4.5 %collective-permute-start.6 = (f32[48,2304]{1,0:T(8,128)S(1)}, f32[48,2304]{1,0:T(8,128)S(1)}, u32[]{:S(2)}, u32[]{:S(2)}) collective-permute-start(f32[48,2304]{1,0:T(8,128)S(1)} %collective-permute-done.5.other_ref), channel_id=1, source_target_pairs={{8,16},{12,20},{16,8},{20,12},{9,17},{13,21},{17,9},{21,13},{10,18... | collective-permute-start | bytes 1327112 | tf_op jit(solution)/shard_map/ppermute | solution.py:303
  23.8 15.4 %collective-permute-start.10 = (f32[48,2304]{1,0:T(8,128)S(1)}, f32[48,2304]{1,0:T(8,128)S(1)}, u32[]{:S(2)}, u32[]{:S(2)}) collective-permute-start(f32[48,2304]{1,0:T(8,128)S(1)} %collective-permute-done.9), channel_id=1, source_target_pairs={{8,0},{12,4},{16,24},{20,28},{9,1},{13,5},{17,25},{21,29},{10,2},{... | collective-permute-start | bytes 1327112 | tf_op jit(solution)/shard_map/ppermute | solution.py:303
  25.2 30.4 %collective-permute-start.13 = (f32[48,2304]{1,0:T(8,128)S(1)}, f32[48,2304]{1,0:T(8,128)S(1)}, u32[]{:S(2)}, u32[]{:S(2)}) collective-permute-start(f32[48,2304]{1,0:T(8,128)S(1)} %collective-permute-done.5.other_ref), channel_id=1, source_target_pairs={{0,4},{4,0},{8,12},{12,8},{16,20},{20,16},{24,28},{28,24},{1,5},{5... | collective-permute-start | bytes 1327112 | tf_op jit(solution)/shard_map/ppermute | solution.py:307
  26.9 29.5 %collective-permute-start.4 = (f32[48,2304]{1,0:T(8,128)S(1)}, f32[48,2304]{1,0:T(8,128)S(1)}, u32[]{:S(2)}, u32[]{:S(2)}) collective-permute-start(f32[48,2304]{1,0:T(8,128)S(1)} %collective-permute-done.3.other_ref), channel_id=1, source_target_pairs={{8,16},{12,20},{16,8},{20,12},{9,17},{13,21},{17,9},{21,13},{10,18... | collective-permute-start | bytes 1327112 | tf_op jit(solution)/shard_map/ppermute | solution.py:303
  39.2 10.8 %collective-permute-start.11 = (f32[48,2304]{1,0:T(8,128)S(1)}, f32[48,2304]{1,0:T(8,128)S(1)}, u32[]{:S(2)}, u32[]{:S(2)}) collective-permute-start(f32[48,2304]{1,0:T(8,128)S(1)} %broadcast_select_fusion.2), channel_id=1, source_target_pairs={{0,4},{4,0},{8,12},{12,8},{16,20},{20,16},{24,28},{28,24},{1,5},{5... | collective-permute-start | bytes 1327112 | tf_op jit(solution)/shard_map/ppermute | solution.py:307
  40.8 12.5 %collective-permute-start.7 = (f32[48,2304]{1,0:T(8,128)S(1)}, f32[48,2304]{1,0:T(8,128)S(1)}, u32[]{:S(2)}, u32[]{:S(2)}) collective-permute-start(f32[48,2304]{1,0:T(8,128)S(1)} %collective-permute-done.6), channel_id=1, source_target_pairs={{8,0},{12,4},{16,24},{20,28},{9,1},{13,5},{17,25},{21,29},{10,2},{... | collective-permute-start | bytes 1327112 | tf_op jit(solution)/shard_map/ppermute | solution.py:303
  50.0 7.9 %collective-permute-start.12 = (f32[24,2304]{1,0:T(8,128)S(1)}, f32[24,2304]{1,0:T(8,128)S(1)}, u32[]{:S(2)}, u32[]{:S(2)}) collective-permute-start(f32[24,2304]{1,0:T(8,128)S(1)} %slice.25), channel_id=1, source_target_pairs={{8,0},{12,4},{16,24},{20,28},{9,1},{13,5},{17,25},{21,29},{10,2},{... | collective-permute-start | bytes 663560 | tf_op jit(solution)/shard_map/ppermute | solution.py:303
  53.3 7.8 %collective-permute-start.8 = (f32[24,2304]{1,0:T(8,128)S(1)}, f32[24,2304]{1,0:T(8,128)S(1)}, u32[]{:S(2)}, u32[]{:S(2)}) collective-permute-start(f32[24,2304]{1,0:T(8,128)S(1)} %slice.24), channel_id=1, source_target_pairs={{0,4},{4,0},{24,28},{28,24},{1,5},{5,1},{25,29},{29,25},{2,6},{6,2... | collective-permute-start | bytes 663560 | tf_op jit(solution)/shard_map/ppermute | solution.py:307
  66.7 17.4 %copy-start.1 = (f32[4,12,2304]{2,0,1:T(4,128)S(1)}, f32[4,12,2304]{2,0,1:T(4,128)}, u32[]{:S(2)}) copy-start(f32[4,12,2304]{2,0,1:T(4,128)} %param.3) | copy-start | bytes 1327108
  67.4 16.6 %collective-permute-start.16 = (f32[48,1152]{1,0:T(8,128)S(1)}, f32[48,1152]{1,0:T(8,128)S(1)}, u32[]{:S(2)}, u32[]{:S(2)}) collective-permute-start(f32[48,1152]{1,0:T(8,128)S(1)} %get-tuple-element.42), channel_id=1, source_target_pairs={{0,3},{1,2},{2,1},{3,0},{4,7},{5,6},{6,5},{7,4},{8,11},{9,10},{10,... | collective-permute-start | bytes 663560 | tf_op jit(solution)/shard_map/ppermute | solution.py:288
  67.5 16.5 %collective-permute-start.15 = (f32[48,1152]{1,0:T(8,128)S(1)}, f32[48,1152]{1,0:T(8,128)S(1)}, u32[]{:S(2)}, u32[]{:S(2)}) collective-permute-start(f32[48,1152]{1,0:T(8,128)S(1)} %get-tuple-element.41), channel_id=1, source_target_pairs={{0,2},{1,3},{2,0},{3,1},{4,6},{5,7},{6,4},{7,5},{8,10},{9,11},{10,... | collective-permute-start | bytes 663560 | tf_op jit(solution)/shard_map/ppermute | solution.py:288
  69.7 14.3 %collective-permute-start.14 = (f32[48,1152]{1,0:T(8,128)S(1)}, f32[48,1152]{1,0:T(8,128)S(1)}, u32[]{:S(2)}, u32[]{:S(2)}) collective-permute-start(f32[48,1152]{1,0:T(8,128)S(1)} %get-tuple-element.40), channel_id=1, source_target_pairs={{0,1},{1,0},{2,3},{3,2},{4,5},{5,4},{6,7},{7,6},{8,9},{9,8},{10,11... | collective-permute-start | bytes 663560 | tf_op jit(solution)/shard_map/ppermute | solution.py:288
where the time goes:
time: 86.7 us; the launch traced here: 86.4 us
  waiting for transfers between devices  31.6 us (36%)
  starting transfers between devices  20.1 us (23%)
  blocking collectives  12.9 us (15%)
  Pallas kernels  12.7 us (15%)
  other arithmetic  4.31 us (5%)
  between operations  2.77 us (3%)
  local copies, waits for them, and re-layouts  1.87 us (2%)
    ppermute x7, waiting for transfers between devices, along(): return lax.ppermute(value, 'band', moves)  23 us
    all_to_all x1, blocking collectives, share(): return lax.all_to_all(sent, ('band', 'slab'), 0, 0)  12.9 us
    pallas_call x7, Pallas kernels, pair_step(): pl.pallas_call(functools.partial(pair_kernel, slot), out_shape=outs, in_s...  11.4 us
    ppermute x7, starting transfers between devices, along(): return lax.ppermute(value, 'band', moves)  7.48 us
    ppermute x4, starting transfers between devices, across_sides(): return lax.ppermute(value, 'band', moves)  7.13 us
    ppermute x4, waiting for transfers between devices, across_sides(): return lax.ppermute(value, 'band', moves)  6.44 us
    ppermute x6, starting transfers between devices, swap(): return lax.ppermute(value, axis, [(i, i ^ reach) for i in range(size)])  5.53 us
    ppermute x6, waiting for transfers between devices, swap(): return lax.ppermute(value, axis, [(i, i ^ reach) for i in range(size)])  2.18 us
  transfers between devices with their start and end apart: 17, of which 8 were waited for; matrix products, arithmetic and copies ran while one was open for 5% of the time, Pallas kernels for 6%

commit v1 on v0

--- a/solution.py
+++ b/solution.py
@@ -124,8 +124,9 @@
 
     @pl.when(total_weight == 0.0)
     def _():
-        store_force(force_refs, force_in[...])
         energy_out[...] = energy_in[...]
+        if len(force_refs) > 1:
+            store_force(force_refs, force_in[...])
 
     @pl.when(total_weight != 0.0)
     def _():
@@ -185,6 +186,7 @@
             pltpu.VMEM((NX * NY, NZ), jnp.bfloat16),
             pltpu.VMEM((NX, NY * NZ), jnp.float32),
         ],
+        input_output_aliases={3 + len(tables): 1} if pieces == 1 else {},
         compiler_params=pltpu.CompilerParams(vmem_limit_bytes=32 << 20),
         cost_estimate=pl.CostEstimate(flops=3 << 30, transcendentals=0, bytes_accessed=3 << 20),
         name="pair_step",
@@ -309,19 +311,22 @@
     outer_pairs = [(1, 0), (2, 3)]
     inner_pairs = [(1, 2), (2, 1)]
     places = (0, 1, 2, 3)
+    middle = along(own, inner_pairs)
     near = along(own, [(0, 1), (1, 0), (2, 3), (3, 2)])
     side_own = across_sides(own, places)
-    middle = along(own, inner_pairs)
-
+
+    across = along(near, inner_pairs)
     outward = along(middle, outer_pairs)
     side_near = across_sides(near, places)
-    across = along(near, inner_pairs)
-
+
+    second = jnp.where(inner, middle, outward)
+    second, outward = lax.optimization_barrier((second, outward))
+    late = jnp.where(inner, across, outward)
     outer = along(across, outer_pairs)
-    second = jnp.where(inner, middle, outward)
-    side_late = across_sides(jnp.where(inner, across, outward), places)
+    side_late = across_sides(late, places)
     side_middle = along(side_own, inner_pairs)
-    third = jnp.where(inner, across, outer)
+    late, outer = lax.optimization_barrier((late, outer))
+    third = lax.optimization_barrier(jnp.where(inner, across, outer))
 
     side_head = across_sides(outer[:half], (0, 3))
     side_tail = along(side_late[half:], outer_pairs)

time: 86.7 us -> 82.8 us (0.955)
  waiting for transfers between devices: 31.6 us -> 27.6 us
    ppermute x4, waiting for transfers between devices: 6.44 us -> 1.31 us  [across_sides(): return lax.ppermute(value, 'band', moves)]
    ppermute x7, waiting for transfers between devices: 23 us -> 24.5 us  [along(): return lax.ppermute(value, 'band', moves)]
  transfers between devices with their start and end apart: 17 -> 17, of which waited for: 8 -> 6; matrix products, arithmetic and copies ran while one was open for 5% -> 6% of each run, Pallas kernels for 6% -> 13%
where the time goes in v1:
time: 82.8 us; the launch traced here: 82.5 us
  waiting for transfers between devices  27.6 us (33%)
  starting transfers between devices  19.9 us (24%)
  blocking collectives  13.5 us (16%)
  Pallas kernels  12.6 us (15%)
  other arithmetic  4.29 us (5%)
  between operations  2.81 us (3%)
  local copies, waits for them, and re-layouts  1.87 us (2%)
    ppermute x7, waiting for transfers between devices, along(): return lax.ppermute(value, 'band', moves)  24.5 us
    all_to_all x1, blocking collectives, share(): return lax.all_to_all(sent, ('band', 'slab'), 0, 0)  13.5 us
    pallas_call x7, Pallas kernels, pair_step(): pl.pallas_call(functools.partial(pair_kernel, slot), out_shape=outs, in_s...  11.2 us
    ppermute x7, starting transfers between devices, along(): return lax.ppermute(value, 'band', moves)  7.48 us
    ppermute x4, starting transfers between devices, across_sides(): return lax.ppermute(value, 'band', moves)  7.28 us
    ppermute x6, starting transfers between devices, swap(): return lax.ppermute(value, axis, [(i, i ^ reach) for i in range(size)])  5.1 us
    ppermute x6, waiting for transfers between devices, swap(): return lax.ppermute(value, axis, [(i, i ^ reach) for i in range(size)])  1.79 us
  transfers between devices with their start and end apart: 17, of which 6 were waited for; matrix products, arithmetic and copies ran while one was open for 6% of the time, Pallas kernels for 13%

profile of v1, /device:TPU:0, one launch (start us, length us, event | category | flops | bytes accessed | tf_op | source)
XLA Modules:
  0.0 82.5 jit_solution(6984258545479561115)
XLA Ops:
  0.6 1.0 %copy-done = f32[4,12,2304]{2,0,1:T(4,128)S(1)} copy-done((f32[4,12,2304]{2,0,1:T(4,128)S(1)}, f32[4,12,2304]{2,0,1:T(4,128)}, u32[]{:S(2)}) %copy-start) | copy-done | bytes 442392
  2.4 2.6 %collective-permute-start.1 = (f32[24,1152]{1,0:T(8,128)S(1)}, f32[24,1152]{1,0:T(8,128)S(1)}, u32[]{:S(2)}, u32[]{:S(2)}) collective-permute-start(f32[24,1152]{1,0:T(8,128)S(1)} %get-tuple-element.28), channel_id=1, source_target_pairs={{0,2},{1,3},{2,0},{3,1},{4,6},{5,7},{6,4},{7,5},{8,10},{9,11},{10,... | collective-permute-start | bytes 331784 | tf_op jit(solution)/shard_map/ppermute | solution.py:290
  5.4 0.8 select_reduce_fusion.2
  6.2 0.8 fusion.33
  9.0 1.8 %collective-permute-done.2.refs_3_ = f32[24,1152]{1,0:T(8,128)S(1)} collective-permute-done((f32[24,1152]{1,0:T(8,128)S(1)}, f32[24,1152]{1,0:T(8,128)S(1)}, u32[]{:S(2)}, u32[]{:S(2)}) %collective-permute-start.2) | collective-permute-done | bytes 110624 | tf_op jit(solution)/shard_map/ppermute | solution.py:290
  10.8 1.6 %collective-permute-start.5 = (f32[48,2304]{1,0:T(8,128)S(1)}, f32[48,2304]{1,0:T(8,128)S(1)}, u32[]{:S(2)}, u32[]{:S(2)}) collective-permute-start(f32[48,2304]{1,0:T(8,128)S(1)} %assemble.1.own_ref), channel_id=1, source_target_pairs={{0,8},{4,12},{8,0},{12,4},{16,24},{20,28},{24,16},{28,20},{1,9},{5... | collective-permute-start | bytes 1327112 | tf_op jit(solution)/shard_map/ppermute | solution.py:305
  12.4 0.7 collective-permute-start.7
  13.1 1.6 %collective-permute-start.3 = (f32[48,2304]{1,0:T(8,128)S(1)}, f32[48,2304]{1,0:T(8,128)S(1)}, u32[]{:S(2)}, u32[]{:S(2)}) collective-permute-start(f32[48,2304]{1,0:T(8,128)S(1)} %assemble.1.own_ref), channel_id=1, source_target_pairs={{0,4},{4,0},{8,12},{12,8},{16,20},{20,16},{24,28},{28,24},{1,5},{5... | collective-permute-start | bytes 1327112 | tf_op jit(solution)/shard_map/ppermute | solution.py:309
  14.8 8.3 %collective-permute-done.5.other_ref = f32[48,2304]{1,0:T(8,128)S(1)} collective-permute-done((f32[48,2304]{1,0:T(8,128)S(1)}, f32[48,2304]{1,0:T(8,128)S(1)}, u32[]{:S(2)}, u32[]{:S(2)}) %collective-permute-start.5) | collective-permute-done | bytes 442400 | tf_op jit(solution)/shard_map/ppermute | solution.py:305
  23.1 0.7 collective-permute-start.6
  23.8 1.7 %collective-permute-start.13 = (f32[48,2304]{1,0:T(8,128)S(1)}, f32[48,2304]{1,0:T(8,128)S(1)}, u32[]{:S(2)}, u32[]{:S(2)}) collective-permute-start(f32[48,2304]{1,0:T(8,128)S(1)} %collective-permute-done.5.other_ref), channel_id=1, source_target_pairs={{0,4},{4,0},{8,12},{12,8},{16,20},{20,16},{24,28},{28,24},{1,5},{5... | collective-permute-start | bytes 1327112 | tf_op jit(solution)/shard_map/ppermute | solution.py:309
  25.5 1.3 %collective-permute-start.8 = (f32[48,2304]{1,0:T(8,128)S(1)}, f32[48,2304]{1,0:T(8,128)S(1)}, u32[]{:S(2)}, u32[]{:S(2)}) collective-permute-start(f32[48,2304]{1,0:T(8,128)S(1)} %collective-permute-done.7), channel_id=1, source_target_pairs={{8,0},{12,4},{16,24},{20,28},{9,1},{13,5},{17,25},{21,29},{10,2},{... | collective-permute-start | bytes 1327112 | tf_op jit(solution)/shard_map/ppermute | solution.py:305
  26.8 0.7 collective-permute-start.4
  27.6 4.0 %pair_step.7 = (f32[1,128]{1,0:T(1,128)S(1)}, f32[48,2304]{1,0:T(8,128)S(1)}) custom-call(f32[7,2]{1,0:T(8,128)S(1)} %copy.51.weights, f32[48,2304]{1,0:T(8,128)S(1)} %assemble.1.own_ref, f32[48,2304]{1,0:T(8,128)S(1)} %collective-permute-done.5.other_ref, bf16[48,144]{1,0:T(8,128)(2,1)S(1)} %get-tuple-element.60.x_fwd, ...), custom_call_target="tpu_custom_call", output_to_operand_aliasing={{1}: (10, {})} | custom-call | flops 3221225472 | bytes 3145728 | tf_op jit(solution)/shard_map/pair_step/pallas_call | solution.py:178
  31.5 0.6 pair_step.8
  32.1 8.3 %collective-permute-done.8 = f32[48,2304]{1,0:T(8,128)S(1)} collective-permute-done((f32[48,2304]{1,0:T(8,128)S(1)}, f32[48,2304]{1,0:T(8,128)S(1)}, u32[]{:S(2)}, u32[]{:S(2)}) %collective-permute-start.8) | collective-permute-done | bytes 442400 | tf_op jit(solution)/shard_map/ppermute | solution.py:305
  40.5 0.6 collective-permute-start.11
  41.1 1.3 %collective-permute-start.9 = (f32[48,2304]{1,0:T(8,128)S(1)}, f32[48,2304]{1,0:T(8,128)S(1)}, u32[]{:S(2)}, u32[]{:S(2)}) collective-permute-start(f32[48,2304]{1,0:T(8,128)S(1)} %collective-permute-done.6), channel_id=1, source_target_pairs={{8,0},{12,4},{16,24},{20,28},{9,1},{13,5},{17,25},{21,29},{10,2},{... | collective-permute-start | bytes 1327112 | tf_op jit(solution)/shard_map/ppermute | solution.py:305
  42.4 0.6 pair_step.9
  43.1 4.1 %pair_step.10 = (f32[1,128]{1,0:T(1,128)S(1)}, f32[48,2304]{1,0:T(8,128)S(1)}) custom-call(f32[7,2]{1,0:T(8,128)S(1)} %copy.51.weights, f32[48,2304]{1,0:T(8,128)S(1)} %assemble.1.own_ref, f32[48,2304]{1,0:T(8,128)S(1)} %broadcast_select_fusion.2.other_ref, bf16[48,144]{1,0:T(8,128)(2,1)S(1)} %get-tuple-element.60.x_fwd, ...), custom_call_target="tpu_custom_call", output_to_operand_aliasing={{1}: (10, {})} | custom-call | flops 3221225472 | bytes 3145728 | tf_op jit(solution)/shard_map/pair_step/pallas_call | solution.py:178
  47.2 6.0 %collective-permute-done.9 = f32[48,2304]{1,0:T(8,128)S(1)} collective-permute-done((f32[48,2304]{1,0:T(8,128)S(1)}, f32[48,2304]{1,0:T(8,128)S(1)}, u32[]{:S(2)}, u32[]{:S(2)}) %collective-permute-start.9) | collective-permute-done | bytes 442400 | tf_op jit(solution)/shard_map/ppermute | solution.py:305
  53.3 1.3 %collective-permute-start.12 = (f32[24,2304]{1,0:T(8,128)S(1)}, f32[24,2304]{1,0:T(8,128)S(1)}, u32[]{:S(2)}, u32[]{:S(2)}) collective-permute-start(f32[24,2304]{1,0:T(8,128)S(1)} %slice.24), channel_id=1, source_target_pairs={{8,0},{12,4},{16,24},{20,28},{9,1},{13,5},{17,25},{21,29},{10,2},{... | collective-permute-start | bytes 663560 | tf_op jit(solution)/shard_map/ppermute | solution.py:305
  54.6 3.4 %collective-permute-start.10 = (f32[24,2304]{1,0:T(8,128)S(1)}, f32[24,2304]{1,0:T(8,128)S(1)}, u32[]{:S(2)}, u32[]{:S(2)}) collective-permute-start(f32[24,2304]{1,0:T(8,128)S(1)} %slice.18), channel_id=1, source_target_pairs={{0,4},{4,0},{24,28},{28,24},{1,5},{5,1},{25,29},{29,25},{2,6},{6,2... | collective-permute-start | bytes 663560 | tf_op jit(solution)/shard_map/ppermute | solution.py:309
  58.0 0.6 pair_step.11
  58.6 0.6 pair_step.12
  59.2 1.9 %collective-permute-done.12 = f32[24,2304]{1,0:T(8,128)S(1)} collective-permute-done((f32[24,2304]{1,0:T(8,128)S(1)}, f32[24,2304]{1,0:T(8,128)S(1)}, u32[]{:S(2)}, u32[]{:S(2)}) %collective-permute-start.12) | collective-permute-done | bytes 221216 | tf_op jit(solution)/shard_map/ppermute | solution.py:305
  61.1 1.3 %collective-permute-done.10 = f32[24,2304]{1,0:T(8,128)S(1)} collective-permute-done((f32[24,2304]{1,0:T(8,128)S(1)}, f32[24,2304]{1,0:T(8,128)S(1)}, u32[]{:S(2)}, u32[]{:S(2)}) %collective-permute-start.10) | collective-permute-done | bytes 221216 | tf_op jit(solution)/shard_map/ppermute | solution.py:309
  62.7 0.7 pair_step.13
  63.5 1.6 %collective-permute-start.15 = (f32[48,1152]{1,0:T(8,128)S(1)}, f32[48,1152]{1,0:T(8,128)S(1)}, u32[]{:S(2)}, u32[]{:S(2)}) collective-permute-start(f32[48,1152]{1,0:T(8,128)S(1)} %get-tuple-element.47), channel_id=1, source_target_pairs={{0,2},{1,3},{2,0},{3,1},{4,6},{5,7},{6,4},{7,5},{8,10},{9,11},{10,... | collective-permute-start | bytes 663560 | tf_op jit(solution)/shard_map/ppermute | solution.py:290
  65.3 13.5 %all_to_all.5 = f32[32,1,128]{2,1,0:T(1,128)S(1)} all-to-all(f32[32,1,128]{2,1,0:T(1,128)S(1)} %broadcast_in_dim.92), channel_id=1, replica_groups=mesh['band'=8,'slab'=4] {'band','slab'}, dimensions={0} | all-to-all | bytes 32768 | tf_op jit(solution)/shard_map/all_to_all | solution.py:295
  78.8 0.6 reduce_sum.65
  80.3 1.1 %finish.1 = f32[12,4,2304]{2,1,0:T(4,128)} custom-call(s32[1]{0:T(128)} %bitcast.place, f32[12,4,2304]{2,1,0:T(4,128)S(1)} %bitcast.18, f32[24,1152]{1,0:T(8,128)S(1)} %fusion.2.local_pot, f32[48,1152]{1,0:T(8,128)S(1)} %get-tuple-element.45.refs_0_, f32[48,1152]{1,0:T(8,128)S(1)} %collective-permute-done.14.refs_1_, ...), custom_call_target="tpu_custom_call" | custom-call | tf_op jit(solution)/shard_map/finish/pallas_call | solution.py:278
  (57 shorter events, 4.2 us)
Async XLA Ops:
  0.6 1.0 %copy-start = (f32[4,12,2304]{2,0,1:T(4,128)S(1)}, f32[4,12,2304]{2,0,1:T(4,128)}, u32[]{:S(2)}) copy-start(f32[4,12,2304]{2,0,1:T(4,128)} %param.3) | copy-start | bytes 1327108
  1.9 7.1 %collective-permute-start = (f32[24,1152]{1,0:T(8,128)S(1)}, f32[24,1152]{1,0:T(8,128)S(1)}, u32[]{:S(2)}, u32[]{:S(2)}) collective-permute-start(f32[24,1152]{1,0:T(8,128)S(1)} %get-tuple-element.27), channel_id=1, source_target_pairs={{0,1},{1,0},{2,3},{3,2},{4,5},{5,4},{6,7},{7,6},{8,9},{9,8},{10,11... | collective-permute-start | bytes 331784 | tf_op jit(solution)/shard_map/ppermute | solution.py:290
  2.4 6.6 %collective-permute-start.1 = (f32[24,1152]{1,0:T(8,128)S(1)}, f32[24,1152]{1,0:T(8,128)S(1)}, u32[]{:S(2)}, u32[]{:S(2)}) collective-permute-start(f32[24,1152]{1,0:T(8,128)S(1)} %get-tuple-element.28), channel_id=1, source_target_pairs={{0,2},{1,3},{2,0},{3,1},{4,6},{5,7},{6,4},{7,5},{8,10},{9,11},{10,... | collective-permute-start | bytes 331784 | tf_op jit(solution)/shard_map/ppermute | solution.py:290
  5.0 5.8 %collective-permute-start.2 = (f32[24,1152]{1,0:T(8,128)S(1)}, f32[24,1152]{1,0:T(8,128)S(1)}, u32[]{:S(2)}, u32[]{:S(2)}) collective-permute-start(f32[24,1152]{1,0:T(8,128)S(1)} %get-tuple-element.29), channel_id=1, source_target_pairs={{0,3},{1,2},{2,1},{3,0},{4,7},{5,6},{6,5},{7,4},{8,11},{9,10},{10,... | collective-permute-start | bytes 331784 | tf_op jit(solution)/shard_map/ppermute | solution.py:290
  10.8 12.3 %collective-permute-start.5 = (f32[48,2304]{1,0:T(8,128)S(1)}, f32[48,2304]{1,0:T(8,128)S(1)}, u32[]{:S(2)}, u32[]{:S(2)}) collective-permute-start(f32[48,2304]{1,0:T(8,128)S(1)} %assemble.1.own_ref), channel_id=1, source_target_pairs={{0,8},{4,12},{8,0},{12,4},{16,24},{20,28},{24,16},{28,20},{1,9},{5... | collective-permute-start | bytes 1327112 | tf_op jit(solution)/shard_map/ppermute | solution.py:305
  12.4 13.1 %collective-permute-start.7 = (f32[48,2304]{1,0:T(8,128)S(1)}, f32[48,2304]{1,0:T(8,128)S(1)}, u32[]{:S(2)}, u32[]{:S(2)}) collective-permute-start(f32[48,2304]{1,0:T(8,128)S(1)} %assemble.1.own_ref), channel_id=1, source_target_pairs={{8,16},{12,20},{16,8},{20,12},{9,17},{13,21},{17,9},{21,13},{10,18... | collective-permute-start | bytes 1327112 | tf_op jit(solution)/shard_map/ppermute | solution.py:305
  13.1 13.7 %collective-permute-start.3 = (f32[48,2304]{1,0:T(8,128)S(1)}, f32[48,2304]{1,0:T(8,128)S(1)}, u32[]{:S(2)}, u32[]{:S(2)}) collective-permute-start(f32[48,2304]{1,0:T(8,128)S(1)} %assemble.1.own_ref), channel_id=1, source_target_pairs={{0,4},{4,0},{8,12},{12,8},{16,20},{20,16},{24,28},{28,24},{1,5},{5... | collective-permute-start | bytes 1327112 | tf_op jit(solution)/shard_map/ppermute | solution.py:309
  23.1 17.4 %collective-permute-start.6 = (f32[48,2304]{1,0:T(8,128)S(1)}, f32[48,2304]{1,0:T(8,128)S(1)}, u32[]{:S(2)}, u32[]{:S(2)}) collective-permute-start(f32[48,2304]{1,0:T(8,128)S(1)} %collective-permute-done.5.other_ref), channel_id=1, source_target_pairs={{8,16},{12,20},{16,8},{20,12},{9,17},{13,21},{17,9},{21,13},{10,18... | collective-permute-start | bytes 1327112 | tf_op jit(solution)/shard_map/ppermute | solution.py:305
  23.8 18.6 %collective-permute-start.13 = (f32[48,2304]{1,0:T(8,128)S(1)}, f32[48,2304]{1,0:T(8,128)S(1)}, u32[]{:S(2)}, u32[]{:S(2)}) collective-permute-start(f32[48,2304]{1,0:T(8,128)S(1)} %collective-permute-done.5.other_ref), channel_id=1, source_target_pairs={{0,4},{4,0},{8,12},{12,8},{16,20},{20,16},{24,28},{28,24},{1,5},{5... | collective-permute-start | bytes 1327112 | tf_op jit(solution)/shard_map/ppermute | solution.py:309
  25.5 14.9 %collective-permute-start.8 = (f32[48,2304]{1,0:T(8,128)S(1)}, f32[48,2304]{1,0:T(8,128)S(1)}, u32[]{:S(2)}, u32[]{:S(2)}) collective-permute-start(f32[48,2304]{1,0:T(8,128)S(1)} %collective-permute-done.7), channel_id=1, source_target_pairs={{8,0},{12,4},{16,24},{20,28},{9,1},{13,5},{17,25},{21,29},{10,2},{... | collective-permute-start | bytes 1327112 | tf_op jit(solution)/shard_map/ppermute | solution.py:305
  26.8 32.4 %collective-permute-start.4 = (f32[48,2304]{1,0:T(8,128)S(1)}, f32[48,2304]{1,0:T(8,128)S(1)}, u32[]{:S(2)}, u32[]{:S(2)}) collective-permute-start(f32[48,2304]{1,0:T(8,128)S(1)} %collective-permute-done.3.other_ref), channel_id=1, source_target_pairs={{8,16},{12,20},{16,8},{20,12},{9,17},{13,21},{17,9},{21,13},{10,18... | collective-permute-start | bytes 1327112 | tf_op jit(solution)/shard_map/ppermute | solution.py:305
  40.5 12.7 %collective-permute-start.11 = (f32[48,2304]{1,0:T(8,128)S(1)}, f32[48,2304]{1,0:T(8,128)S(1)}, u32[]{:S(2)}, u32[]{:S(2)}) collective-permute-start(f32[48,2304]{1,0:T(8,128)S(1)} %broadcast_select_fusion.1), channel_id=1, source_target_pairs={{0,4},{4,0},{8,12},{12,8},{16,20},{20,16},{24,28},{28,24},{1,5},{5... | collective-permute-start | bytes 1327112 | tf_op jit(solution)/shard_map/ppermute | solution.py:309
  41.1 12.0 %collective-permute-start.9 = (f32[48,2304]{1,0:T(8,128)S(1)}, f32[48,2304]{1,0:T(8,128)S(1)}, u32[]{:S(2)}, u32[]{:S(2)}) collective-permute-start(f32[48,2304]{1,0:T(8,128)S(1)} %collective-permute-done.6), channel_id=1, source_target_pairs={{8,0},{12,4},{16,24},{20,28},{9,1},{13,5},{17,25},{21,29},{10,2},{... | collective-permute-start | bytes 1327112 | tf_op jit(solution)/shard_map/ppermute | solution.py:305
  53.3 7.8 %collective-permute-start.12 = (f32[24,2304]{1,0:T(8,128)S(1)}, f32[24,2304]{1,0:T(8,128)S(1)}, u32[]{:S(2)}, u32[]{:S(2)}) collective-permute-start(f32[24,2304]{1,0:T(8,128)S(1)} %slice.24), channel_id=1, source_target_pairs={{8,0},{12,4},{16,24},{20,28},{9,1},{13,5},{17,25},{21,29},{10,2},{... | collective-permute-start | bytes 663560 | tf_op jit(solution)/shard_map/ppermute | solution.py:305
  54.6 7.8 %collective-permute-start.10 = (f32[24,2304]{1,0:T(8,128)S(1)}, f32[24,2304]{1,0:T(8,128)S(1)}, u32[]{:S(2)}, u32[]{:S(2)}) collective-permute-start(f32[24,2304]{1,0:T(8,128)S(1)} %slice.18), channel_id=1, source_target_pairs={{0,4},{4,0},{24,28},{28,24},{1,5},{5,1},{25,29},{29,25},{2,6},{6,2... | collective-permute-start | bytes 663560 | tf_op jit(solution)/shard_map/ppermute | solution.py:309
  62.7 17.6 %copy-start.1 = (f32[4,12,2304]{2,0,1:T(4,128)S(1)}, f32[4,12,2304]{2,0,1:T(4,128)}, u32[]{:S(2)}) copy-start(f32[4,12,2304]{2,0,1:T(4,128)} %param.3) | copy-start | bytes 1327108
  63.4 16.7 %collective-permute-start.16 = (f32[48,1152]{1,0:T(8,128)S(1)}, f32[48,1152]{1,0:T(8,128)S(1)}, u32[]{:S(2)}, u32[]{:S(2)}) collective-permute-start(f32[48,1152]{1,0:T(8,128)S(1)} %get-tuple-element.48), channel_id=1, source_target_pairs={{0,3},{1,2},{2,1},{3,0},{4,7},{5,6},{6,5},{7,4},{8,11},{9,10},{10,... | collective-permute-start | bytes 663560 | tf_op jit(solution)/shard_map/ppermute | solution.py:290
  63.5 16.6 %collective-permute-start.15 = (f32[48,1152]{1,0:T(8,128)S(1)}, f32[48,1152]{1,0:T(8,128)S(1)}, u32[]{:S(2)}, u32[]{:S(2)}) collective-permute-start(f32[48,1152]{1,0:T(8,128)S(1)} %get-tuple-element.47), channel_id=1, source_target_pairs={{0,2},{1,3},{2,0},{3,1},{4,6},{5,7},{6,4},{7,5},{8,10},{9,11},{10,... | collective-permute-start | bytes 663560 | tf_op jit(solution)/shard_map/ppermute | solution.py:290
  65.1 15.0 %collective-permute-start.14 = (f32[48,1152]{1,0:T(8,128)S(1)}, f32[48,1152]{1,0:T(8,128)S(1)}, u32[]{:S(2)}, u32[]{:S(2)}) collective-permute-start(f32[48,1152]{1,0:T(8,128)S(1)} %get-tuple-element.46), channel_id=1, source_target_pairs={{0,1},{1,0},{2,3},{3,2},{4,5},{5,4},{6,7},{7,6},{8,9},{9,8},{10,11... | collective-permute-start | bytes 663560 | tf_op jit(solution)/shard_map/ppermute | solution.py:290

commit v2 on v1

--- a/solution.py
+++ b/solution.py
@@ -119,8 +119,8 @@
     else:
         squares_in, energy_out, *force_refs = refs
         cut_into(force_refs, squares_in[...], 1)
-    total_weight = weights[slot, 0]
-    request_weight = weights[slot, 1]
+    total_weight = jnp.max(weights[2 * slot : 2 * slot + 1, :])
+    request_weight = weights[2 * slot + 1 : 2 * slot + 2, :]
 
     @pl.when(total_weight == 0.0)
     def _():
@@ -178,7 +178,7 @@
     return pl.pallas_call(
         functools.partial(pair_kernel, slot),
         out_shape=outs,
-        in_specs=with_scalar(4 + len(tables) + len(extra)),
+        in_specs=in_vmem(5 + len(tables) + len(extra)),
         out_specs=in_vmem(1 + pieces),
         scratch_shapes=[
             pltpu.VMEM((NX * NY, NZ), jnp.float32),
@@ -395,7 +395,8 @@
     wanted_by = jnp.sum(jnp.where(partners == band_index, active, 0.0), axis=1)
     chosen = groups[:, None] == jnp.arange(bands, dtype=jnp.int32)[None, :]
     returned = jnp.sum(jnp.where(chosen, wanted_by[None, :], 0.0), axis=1)
-    weights = jnp.stack([requested + returned, requested], axis=1)
+    weights = jnp.stack([requested + returned, requested], axis=1).reshape(-1)
+    weights = jnp.broadcast_to(weights[:, None], weights.shape + (128,))
 
     force = jnp.zeros((NX, NY * NZ), jnp.float32)
     energy = jnp.zeros((1, 128), jnp.float32)

time: 82.8 us -> 82.4 us (level)
  Pallas kernels: 12.6 us -> 9.2 us
  waiting for transfers between devices: 27.6 us -> 30.3 us
    pallas_call x7, Pallas kernels: 11.2 us -> 7.86 us  [pair_step(): pl.pallas_call(functools.partial(pair_kernel, slot), out_shape=outs, in_s...]
    ppermute x7, waiting for transfers between devices: 24.5 us -> 27.3 us  [along(): return lax.ppermute(value, 'band', moves)]
  transfers between devices with their start and end apart: 17 -> 17, of which waited for: 6 -> 6; matrix products, arithmetic and copies ran while one was open for 6% -> 6% of each run, Pallas kernels for 13% -> 9%
where the time goes in v2:
time: 82.4 us; the launch traced here: 82 us
  waiting for transfers between devices  30.3 us (37%)
  starting transfers between devices  19.8 us (24%)
  blocking collectives  13.5 us (16%)
  Pallas kernels  9.2 us (11%)
  other arithmetic  4.37 us (5%)
  between operations  2.79 us (3%)
  local copies, waits for them, and re-layouts  2.02 us (2%)
    ppermute x7, waiting for transfers between devices, along(): return lax.ppermute(value, 'band', moves)  27.3 us
    all_to_all x1, blocking collectives, share(): return lax.all_to_all(sent, ('band', 'slab'), 0, 0)  13.5 us
    pallas_call x7, Pallas kernels, pair_step(): pl.pallas_call(functools.partial(pair_kernel, slot), out_shape=outs, in_s...  7.86 us
    ppermute x7, starting transfers between devices, along(): return lax.ppermute(value, 'band', moves)  7.48 us
    ppermute x4, starting transfers between devices, across_sides(): return lax.ppermute(value, 'band', moves)  7.27 us
    ppermute x6, starting transfers between devices, swap(): return lax.ppermute(value, axis, [(i, i ^ reach) for i in range(size)])  5.1 us
    ppermute x6, waiting for transfers between devices, swap(): return lax.ppermute(value, axis, [(i, i ^ reach) for i in range(size)])  1.71 us
  transfers between devices with their start and end apart: 17, of which 6 were waited for; matrix products, arithmetic and copies ran while one was open for 6% of the time, Pallas kernels for 9%

profile of v2, /device:TPU:0, one launch (start us, length us, event | category | flops | bytes accessed | tf_op | source)
XLA Modules:
  0.0 82.0 jit_solution(10458804738248982616)
XLA Ops:
  0.6 1.0 %copy-done = f32[4,12,2304]{2,0,1:T(4,128)S(1)} copy-done((f32[4,12,2304]{2,0,1:T(4,128)S(1)}, f32[4,12,2304]{2,0,1:T(4,128)}, u32[]{:S(2)}) %copy-start) | copy-done | bytes 442392
  1.9 0.6 collective-permute-start
  2.4 2.6 %collective-permute-start.1 = (f32[24,1152]{1,0:T(8,128)S(1)}, f32[24,1152]{1,0:T(8,128)S(1)}, u32[]{:S(2)}, u32[]{:S(2)}) collective-permute-start(f32[24,1152]{1,0:T(8,128)S(1)} %get-tuple-element.28), channel_id=1, source_target_pairs={{0,2},{1,3},{2,0},{3,1},{4,6},{5,7},{6,4},{7,5},{8,10},{9,11},{10,... | collective-permute-start | bytes 331784 | tf_op jit(solution)/shard_map/ppermute | solution.py:290
  5.4 0.8 select_reduce_fusion.2
  6.2 0.8 fusion.33
  7.6 0.3 reduce-precision_convert_fusion.1
  8.3 0.4 copy.21
  9.1 1.7 %collective-permute-done.2.refs_3_ = f32[24,1152]{1,0:T(8,128)S(1)} collective-permute-done((f32[24,1152]{1,0:T(8,128)S(1)}, f32[24,1152]{1,0:T(8,128)S(1)}, u32[]{:S(2)}, u32[]{:S(2)}) %collective-permute-start.2) | collective-permute-done | bytes 110624 | tf_op jit(solution)/shard_map/ppermute | solution.py:290
  10.8 1.6 %collective-permute-start.5 = (f32[48,2304]{1,0:T(8,128)S(1)}, f32[48,2304]{1,0:T(8,128)S(1)}, u32[]{:S(2)}, u32[]{:S(2)}) collective-permute-start(f32[48,2304]{1,0:T(8,128)S(1)} %assemble.1.own_ref), channel_id=1, source_target_pairs={{0,8},{4,12},{8,0},{12,4},{16,24},{20,28},{24,16},{28,20},{1,9},{5... | collective-permute-start | bytes 1327112 | tf_op jit(solution)/shard_map/ppermute | solution.py:305
  12.4 0.7 collective-permute-start.7
  13.1 1.6 %collective-permute-start.3 = (f32[48,2304]{1,0:T(8,128)S(1)}, f32[48,2304]{1,0:T(8,128)S(1)}, u32[]{:S(2)}, u32[]{:S(2)}) collective-permute-start(f32[48,2304]{1,0:T(8,128)S(1)} %assemble.1.own_ref), channel_id=1, source_target_pairs={{0,4},{4,0},{8,12},{12,8},{16,20},{20,16},{24,28},{28,24},{1,5},{5... | collective-permute-start | bytes 1327112 | tf_op jit(solution)/shard_map/ppermute | solution.py:309
  14.8 8.3 %collective-permute-done.5.other_ref = f32[48,2304]{1,0:T(8,128)S(1)} collective-permute-done((f32[48,2304]{1,0:T(8,128)S(1)}, f32[48,2304]{1,0:T(8,128)S(1)}, u32[]{:S(2)}, u32[]{:S(2)}) %collective-permute-start.5) | collective-permute-done | bytes 442400 | tf_op jit(solution)/shard_map/ppermute | solution.py:305
  23.1 0.7 collective-permute-start.6
  23.8 1.7 %collective-permute-start.13 = (f32[48,2304]{1,0:T(8,128)S(1)}, f32[48,2304]{1,0:T(8,128)S(1)}, u32[]{:S(2)}, u32[]{:S(2)}) collective-permute-start(f32[48,2304]{1,0:T(8,128)S(1)} %collective-permute-done.5.other_ref), channel_id=1, source_target_pairs={{0,4},{4,0},{8,12},{12,8},{16,20},{20,16},{24,28},{28,24},{1,5},{5... | collective-permute-start | bytes 1327112 | tf_op jit(solution)/shard_map/ppermute | solution.py:309
  25.5 1.3 %collective-permute-start.8 = (f32[48,2304]{1,0:T(8,128)S(1)}, f32[48,2304]{1,0:T(8,128)S(1)}, u32[]{:S(2)}, u32[]{:S(2)}) collective-permute-start(f32[48,2304]{1,0:T(8,128)S(1)} %collective-permute-done.7), channel_id=1, source_target_pairs={{8,0},{12,4},{16,24},{20,28},{9,1},{13,5},{17,25},{21,29},{10,2},{... | collective-permute-start | bytes 1327112 | tf_op jit(solution)/shard_map/ppermute | solution.py:305
  26.8 0.7 collective-permute-start.4
  27.6 3.5 %pair_step.7 = (f32[1,128]{1,0:T(1,128)S(1)}, f32[48,2304]{1,0:T(8,128)S(1)}) custom-call(f32[14,128]{1,0:T(8,128)S(1)} %broadcast_in_dim.97.weights, f32[48,2304]{1,0:T(8,128)S(1)} %assemble.1.own_ref, f32[48,2304]{1,0:T(8,128)S(1)} %collective-permute-done.5.other_ref, ...), custom_call_target="tpu_custom_call", output_to_operand_aliasing={{1}: (10, {})} | custom-call | flops 3221225472 | bytes 3145728 | tf_op jit(solution)/shard_map/pair_step/pallas_call | solution.py:178
  31.2 9.2 %collective-permute-done.8 = f32[48,2304]{1,0:T(8,128)S(1)} collective-permute-done((f32[48,2304]{1,0:T(8,128)S(1)}, f32[48,2304]{1,0:T(8,128)S(1)}, u32[]{:S(2)}, u32[]{:S(2)}) %collective-permute-start.8) | collective-permute-done | bytes 442400 | tf_op jit(solution)/shard_map/ppermute | solution.py:305
  40.6 0.6 collective-permute-start.11
  41.2 1.3 %collective-permute-start.9 = (f32[48,2304]{1,0:T(8,128)S(1)}, f32[48,2304]{1,0:T(8,128)S(1)}, u32[]{:S(2)}, u32[]{:S(2)}) collective-permute-start(f32[48,2304]{1,0:T(8,128)S(1)} %collective-permute-done.6), channel_id=1, source_target_pairs={{8,0},{12,4},{16,24},{20,28},{9,1},{13,5},{17,25},{21,29},{10,2},{... | collective-permute-start | bytes 1327112 | tf_op jit(solution)/shard_map/ppermute | solution.py:305
  42.6 3.7 %pair_step.10 = (f32[1,128]{1,0:T(1,128)S(1)}, f32[48,2304]{1,0:T(8,128)S(1)}) custom-call(f32[14,128]{1,0:T(8,128)S(1)} %broadcast_in_dim.97.weights, f32[48,2304]{1,0:T(8,128)S(1)} %assemble.1.own_ref, f32[48,2304]{1,0:T(8,128)S(1)} %broadcast_select_fusion.2.other_ref, ...), custom_call_target="tpu_custom_call", output_to_operand_aliasing={{1}: (10, {})} | custom-call | flops 3221225472 | bytes 3145728 | tf_op jit(solution)/shard_map/pair_step/pallas_call | solution.py:178
  46.3 6.9 %collective-permute-done.9 = f32[48,2304]{1,0:T(8,128)S(1)} collective-permute-done((f32[48,2304]{1,0:T(8,128)S(1)}, f32[48,2304]{1,0:T(8,128)S(1)}, u32[]{:S(2)}, u32[]{:S(2)}) %collective-permute-start.9) | collective-permute-done | bytes 442400 | tf_op jit(solution)/shard_map/ppermute | solution.py:305
  53.3 1.3 %collective-permute-start.12 = (f32[24,2304]{1,0:T(8,128)S(1)}, f32[24,2304]{1,0:T(8,128)S(1)}, u32[]{:S(2)}, u32[]{:S(2)}) collective-permute-start(f32[24,2304]{1,0:T(8,128)S(1)} %slice.24), channel_id=1, source_target_pairs={{8,0},{12,4},{16,24},{20,28},{9,1},{13,5},{17,25},{21,29},{10,2},{... | collective-permute-start | bytes 663560 | tf_op jit(solution)/shard_map/ppermute | solution.py:305
  54.6 3.4 %collective-permute-start.10 = (f32[24,2304]{1,0:T(8,128)S(1)}, f32[24,2304]{1,0:T(8,128)S(1)}, u32[]{:S(2)}, u32[]{:S(2)}) collective-permute-start(f32[24,2304]{1,0:T(8,128)S(1)} %slice.18), channel_id=1, source_target_pairs={{0,4},{4,0},{24,28},{28,24},{1,5},{5,1},{25,29},{29,25},{2,6},{6,2... | collective-permute-start | bytes 663560 | tf_op jit(solution)/shard_map/ppermute | solution.py:309
  58.3 2.8 %collective-permute-done.12 = f32[24,2304]{1,0:T(8,128)S(1)} collective-permute-done((f32[24,2304]{1,0:T(8,128)S(1)}, f32[24,2304]{1,0:T(8,128)S(1)}, u32[]{:S(2)}, u32[]{:S(2)}) %collective-permute-start.12) | collective-permute-done | bytes 221216 | tf_op jit(solution)/shard_map/ppermute | solution.py:305
  61.2 1.3 %collective-permute-done.10 = f32[24,2304]{1,0:T(8,128)S(1)} collective-permute-done((f32[24,2304]{1,0:T(8,128)S(1)}, f32[24,2304]{1,0:T(8,128)S(1)}, u32[]{:S(2)}, u32[]{:S(2)}) %collective-permute-start.10) | collective-permute-done | bytes 221216 | tf_op jit(solution)/shard_map/ppermute | solution.py:309
  62.5 0.3 multiply_add_fusion
  63.0 1.6 %collective-permute-start.15 = (f32[48,1152]{1,0:T(8,128)S(1)}, f32[48,1152]{1,0:T(8,128)S(1)}, u32[]{:S(2)}, u32[]{:S(2)}) collective-permute-start(f32[48,1152]{1,0:T(8,128)S(1)} %get-tuple-element.47), channel_id=1, source_target_pairs={{0,2},{1,3},{2,0},{3,1},{4,6},{5,7},{6,4},{7,5},{8,10},{9,11},{10,... | collective-permute-start | bytes 663560 | tf_op jit(solution)/shard_map/ppermute | solution.py:290
  64.6 0.3 collective-permute-start.14
  64.9 13.5 %all_to_all.5 = f32[32,1,128]{2,1,0:T(1,128)S(1)} all-to-all(f32[32,1,128]{2,1,0:T(1,128)S(1)} %broadcast_in_dim.101), channel_id=1, replica_groups=mesh['band'=8,'slab'=4] {'band','slab'}, dimensions={0} | all-to-all | bytes 32768 | tf_op jit(solution)/shard_map/all_to_all | solution.py:295
  78.4 0.6 reduce_sum.65
  79.8 1.1 %finish.1 = f32[12,4,2304]{2,1,0:T(4,128)} custom-call(s32[1]{0:T(128)} %bitcast.place, f32[12,4,2304]{2,1,0:T(4,128)S(1)} %bitcast.18, f32[24,1152]{1,0:T(8,128)S(1)} %fusion.2.local_pot, f32[48,1152]{1,0:T(8,128)S(1)} %get-tuple-element.45.refs_0_, f32[48,1152]{1,0:T(8,128)S(1)} %collective-permute-done.14.refs_1_, ...), custom_call_target="tpu_custom_call" | custom-call | tf_op jit(solution)/shard_map/finish/pallas_call | solution.py:278
  (59 shorter events, 3.4 us)
Async XLA Ops:
  0.6 1.0 %copy-start = (f32[4,12,2304]{2,0,1:T(4,128)S(1)}, f32[4,12,2304]{2,0,1:T(4,128)}, u32[]{:S(2)}) copy-start(f32[4,12,2304]{2,0,1:T(4,128)} %param.3) | copy-start | bytes 1327108
  1.9 7.2 %collective-permute-start = (f32[24,1152]{1,0:T(8,128)S(1)}, f32[24,1152]{1,0:T(8,128)S(1)}, u32[]{:S(2)}, u32[]{:S(2)}) collective-permute-start(f32[24,1152]{1,0:T(8,128)S(1)} %get-tuple-element.27), channel_id=1, source_target_pairs={{0,1},{1,0},{2,3},{3,2},{4,5},{5,4},{6,7},{7,6},{8,9},{9,8},{10,11... | collective-permute-start | bytes 331784 | tf_op jit(solution)/shard_map/ppermute | solution.py:290
  2.4 6.6 %collective-permute-start.1 = (f32[24,1152]{1,0:T(8,128)S(1)}, f32[24,1152]{1,0:T(8,128)S(1)}, u32[]{:S(2)}, u32[]{:S(2)}) collective-permute-start(f32[24,1152]{1,0:T(8,128)S(1)} %get-tuple-element.28), channel_id=1, source_target_pairs={{0,2},{1,3},{2,0},{3,1},{4,6},{5,7},{6,4},{7,5},{8,10},{9,11},{10,... | collective-permute-start | bytes 331784 | tf_op jit(solution)/shard_map/ppermute | solution.py:290
  5.0 5.8 %collective-permute-start.2 = (f32[24,1152]{1,0:T(8,128)S(1)}, f32[24,1152]{1,0:T(8,128)S(1)}, u32[]{:S(2)}, u32[]{:S(2)}) collective-permute-start(f32[24,1152]{1,0:T(8,128)S(1)} %get-tuple-element.29), channel_id=1, source_target_pairs={{0,3},{1,2},{2,1},{3,0},{4,7},{5,6},{6,5},{7,4},{8,11},{9,10},{10,... | collective-permute-start | bytes 331784 | tf_op jit(solution)/shard_map/ppermute | solution.py:290
  10.8 12.3 %collective-permute-start.5 = (f32[48,2304]{1,0:T(8,128)S(1)}, f32[48,2304]{1,0:T(8,128)S(1)}, u32[]{:S(2)}, u32[]{:S(2)}) collective-permute-start(f32[48,2304]{1,0:T(8,128)S(1)} %assemble.1.own_ref), channel_id=1, source_target_pairs={{0,8},{4,12},{8,0},{12,4},{16,24},{20,28},{24,16},{28,20},{1,9},{5... | collective-permute-start | bytes 1327112 | tf_op jit(solution)/shard_map/ppermute | solution.py:305
  12.4 13.1 %collective-permute-start.7 = (f32[48,2304]{1,0:T(8,128)S(1)}, f32[48,2304]{1,0:T(8,128)S(1)}, u32[]{:S(2)}, u32[]{:S(2)}) collective-permute-start(f32[48,2304]{1,0:T(8,128)S(1)} %assemble.1.own_ref), channel_id=1, source_target_pairs={{8,16},{12,20},{16,8},{20,12},{9,17},{13,21},{17,9},{21,13},{10,18... | collective-permute-start | bytes 1327112 | tf_op jit(solution)/shard_map/ppermute | solution.py:305
  13.1 13.7 %collective-permute-start.3 = (f32[48,2304]{1,0:T(8,128)S(1)}, f32[48,2304]{1,0:T(8,128)S(1)}, u32[]{:S(2)}, u32[]{:S(2)}) collective-permute-start(f32[48,2304]{1,0:T(8,128)S(1)} %assemble.1.own_ref), channel_id=1, source_target_pairs={{0,4},{4,0},{8,12},{12,8},{16,20},{20,16},{24,28},{28,24},{1,5},{5... | collective-permute-start | bytes 1327112 | tf_op jit(solution)/shard_map/ppermute | solution.py:309
  23.1 17.4 %collective-permute-start.6 = (f32[48,2304]{1,0:T(8,128)S(1)}, f32[48,2304]{1,0:T(8,128)S(1)}, u32[]{:S(2)}, u32[]{:S(2)}) collective-permute-start(f32[48,2304]{1,0:T(8,128)S(1)} %collective-permute-done.5.other_ref), channel_id=1, source_target_pairs={{8,16},{12,20},{16,8},{20,12},{9,17},{13,21},{17,9},{21,13},{10,18... | collective-permute-start | bytes 1327112 | tf_op jit(solution)/shard_map/ppermute | solution.py:305
  23.8 18.7 %collective-permute-start.13 = (f32[48,2304]{1,0:T(8,128)S(1)}, f32[48,2304]{1,0:T(8,128)S(1)}, u32[]{:S(2)}, u32[]{:S(2)}) collective-permute-start(f32[48,2304]{1,0:T(8,128)S(1)} %collective-permute-done.5.other_ref), channel_id=1, source_target_pairs={{0,4},{4,0},{8,12},{12,8},{16,20},{20,16},{24,28},{28,24},{1,5},{5... | collective-permute-start | bytes 1327112 | tf_op jit(solution)/shard_map/ppermute | solution.py:309
  25.5 14.9 %collective-permute-start.8 = (f32[48,2304]{1,0:T(8,128)S(1)}, f32[48,2304]{1,0:T(8,128)S(1)}, u32[]{:S(2)}, u32[]{:S(2)}) collective-permute-start(f32[48,2304]{1,0:T(8,128)S(1)} %collective-permute-done.7), channel_id=1, source_target_pairs={{8,0},{12,4},{16,24},{20,28},{9,1},{13,5},{17,25},{21,29},{10,2},{... | collective-permute-start | bytes 1327112 | tf_op jit(solution)/shard_map/ppermute | solution.py:305
  26.8 31.5 %collective-permute-start.4 = (f32[48,2304]{1,0:T(8,128)S(1)}, f32[48,2304]{1,0:T(8,128)S(1)}, u32[]{:S(2)}, u32[]{:S(2)}) collective-permute-start(f32[48,2304]{1,0:T(8,128)S(1)} %collective-permute-done.3.other_ref), channel_id=1, source_target_pairs={{8,16},{12,20},{16,8},{20,12},{9,17},{13,21},{17,9},{21,13},{10,18... | collective-permute-start | bytes 1327112 | tf_op jit(solution)/shard_map/ppermute | solution.py:305
  40.6 12.7 %collective-permute-start.11 = (f32[48,2304]{1,0:T(8,128)S(1)}, f32[48,2304]{1,0:T(8,128)S(1)}, u32[]{:S(2)}, u32[]{:S(2)}) collective-permute-start(f32[48,2304]{1,0:T(8,128)S(1)} %broadcast_select_fusion.1), channel_id=1, source_target_pairs={{0,4},{4,0},{8,12},{12,8},{16,20},{20,16},{24,28},{28,24},{1,5},{5... | collective-permute-start | bytes 1327112 | tf_op jit(solution)/shard_map/ppermute | solution.py:309
  41.2 12.0 %collective-permute-start.9 = (f32[48,2304]{1,0:T(8,128)S(1)}, f32[48,2304]{1,0:T(8,128)S(1)}, u32[]{:S(2)}, u32[]{:S(2)}) collective-permute-start(f32[48,2304]{1,0:T(8,128)S(1)} %collective-permute-done.6), channel_id=1, source_target_pairs={{8,0},{12,4},{16,24},{20,28},{9,1},{13,5},{17,25},{21,29},{10,2},{... | collective-permute-start | bytes 1327112 | tf_op jit(solution)/shard_map/ppermute | solution.py:305
  53.3 7.8 %collective-permute-start.12 = (f32[24,2304]{1,0:T(8,128)S(1)}, f32[24,2304]{1,0:T(8,128)S(1)}, u32[]{:S(2)}, u32[]{:S(2)}) collective-permute-start(f32[24,2304]{1,0:T(8,128)S(1)} %slice.24), channel_id=1, source_target_pairs={{8,0},{12,4},{16,24},{20,28},{9,1},{13,5},{17,25},{21,29},{10,2},{... | collective-permute-start | bytes 663560 | tf_op jit(solution)/shard_map/ppermute | solution.py:305
  54.6 7.8 %collective-permute-start.10 = (f32[24,2304]{1,0:T(8,128)S(1)}, f32[24,2304]{1,0:T(8,128)S(1)}, u32[]{:S(2)}, u32[]{:S(2)}) collective-permute-start(f32[24,2304]{1,0:T(8,128)S(1)} %slice.18), channel_id=1, source_target_pairs={{0,4},{4,0},{24,28},{28,24},{1,5},{5,1},{25,29},{29,25},{2,6},{6,2... | collective-permute-start | bytes 663560 | tf_op jit(solution)/shard_map/ppermute | solution.py:309
  62.7 17.1 %copy-start.1 = (f32[4,12,2304]{2,0,1:T(4,128)S(1)}, f32[4,12,2304]{2,0,1:T(4,128)}, u32[]{:S(2)}) copy-start(f32[4,12,2304]{2,0,1:T(4,128)} %param.3) | copy-start | bytes 1327108
  63.0 16.7 %collective-permute-start.16 = (f32[48,1152]{1,0:T(8,128)S(1)}, f32[48,1152]{1,0:T(8,128)S(1)}, u32[]{:S(2)}, u32[]{:S(2)}) collective-permute-start(f32[48,1152]{1,0:T(8,128)S(1)} %get-tuple-element.48), channel_id=1, source_target_pairs={{0,3},{1,2},{2,1},{3,0},{4,7},{5,6},{6,5},{7,4},{8,11},{9,10},{10,... | collective-permute-start | bytes 663560 | tf_op jit(solution)/shard_map/ppermute | solution.py:290
  63.0 16.6 %collective-permute-start.15 = (f32[48,1152]{1,0:T(8,128)S(1)}, f32[48,1152]{1,0:T(8,128)S(1)}, u32[]{:S(2)}, u32[]{:S(2)}) collective-permute-start(f32[48,1152]{1,0:T(8,128)S(1)} %get-tuple-element.47), channel_id=1, source_target_pairs={{0,2},{1,3},{2,0},{3,1},{4,6},{5,7},{6,4},{7,5},{8,10},{9,11},{10,... | collective-permute-start | bytes 663560 | tf_op jit(solution)/shard_map/ppermute | solution.py:290
  64.6 15.1 %collective-permute-start.14 = (f32[48,1152]{1,0:T(8,128)S(1)}, f32[48,1152]{1,0:T(8,128)S(1)}, u32[]{:S(2)}, u32[]{:S(2)}) collective-permute-start(f32[48,1152]{1,0:T(8,128)S(1)} %get-tuple-element.46), channel_id=1, source_target_pairs={{0,1},{1,0},{2,3},{3,2},{4,5},{5,4},{6,7},{7,6},{8,9},{9,8},{10,11... | collective-permute-start | bytes 663560 | tf_op jit(solution)/shard_map/ppermute | solution.py:290

commit v3 on v2

--- a/solution.py
+++ b/solution.py
@@ -295,72 +295,32 @@
     return lax.all_to_all(sent, ("band", "slab"), 0, 0)
 
 
-def gather_line(own, band_index, bands):
+def gather_ring(own, band_index, bands):
+    groups = [2 * p if p < bands // 2 else 2 * (bands - 1 - p) + 1 for p in range(bands)]
     place = band_index // 2
-    inner = (place == 1) | (place == 2)
+    position = jnp.where(band_index % 2 == 0, place, bands - 1 - place)
+
+    def group_at(position):
+        position = position % bands
+        return jnp.where(position < bands // 2, 2 * position, 2 * (bands - 1 - position) + 1)
+
+    def shift(value, by):
+        moves = [(groups[p], groups[(p + by) % bands]) for p in range(bands)]
+        return lax.ppermute(value, "band", moves)
+
+    ahead = behind = own
+    blocks = []
+    steps = bands // 2 - 1
+    for step in range(steps):
+        ahead = shift(ahead, 1)
+        behind = shift(behind, -1)
+        blocks.append((ahead, group_at(position - step - 1)))
+        blocks.append((behind, group_at(position + step + 1)))
     half = own.shape[0] // 2
-
-    def along(value, pairs):
-        moves = [(2 * a + side, 2 * b + side) for a, b in pairs for side in (0, 1)]
-        return lax.ppermute(value, "band", moves)
-
-    def across_sides(value, places):
-        moves = [(i, i ^ 1) for i in range(bands) if i // 2 in places]
-        return lax.ppermute(value, "band", moves)
-
-    outer_pairs = [(1, 0), (2, 3)]
-    inner_pairs = [(1, 2), (2, 1)]
-    places = (0, 1, 2, 3)
-    middle = along(own, inner_pairs)
-    near = along(own, [(0, 1), (1, 0), (2, 3), (3, 2)])
-    side_own = across_sides(own, places)
-
-    across = along(near, inner_pairs)
-    outward = along(middle, outer_pairs)
-    side_near = across_sides(near, places)
-
-    second = jnp.where(inner, middle, outward)
-    second, outward = lax.optimization_barrier((second, outward))
-    late = jnp.where(inner, across, outward)
-    outer = along(across, outer_pairs)
-    side_late = across_sides(late, places)
-    side_middle = along(side_own, inner_pairs)
-    late, outer = lax.optimization_barrier((late, outer))
-    third = lax.optimization_barrier(jnp.where(inner, across, outer))
-
-    side_head = across_sides(outer[:half], (0, 3))
-    side_tail = along(side_late[half:], outer_pairs)
-    side_last = jnp.where(inner, side_middle, jnp.concatenate([side_head, side_tail], axis=0))
-
-    side = band_index % 2
-    near_group = band_index ^ 2
-    second_group = jnp.where(place < 2, 2, 1) * 2 + side
-    third_group = jnp.where(place < 2, 3, 0) * 2 + side
-    late_group = jnp.where(inner, third_group, second_group) ^ 1
-    last_group = jnp.where(inner, second_group, third_group) ^ 1
-    blocks = [
-        (near, near_group),
-        (side_own, band_index ^ 1),
-        (side_near, near_group ^ 1),
-        (second, second_group),
-        (third, third_group),
-        (side_late, late_group),
-        (side_last, last_group),
-    ]
+    head = shift(ahead[:half], 1)
+    tail = shift(behind[half:], -1)
+    blocks.append((jnp.concatenate([head, tail], axis=0), group_at(position + steps + 1)))
     return blocks
-
-
-def gather_doubling(own, band_index, bands):
-    held = [(own, band_index)]
-    reach = 1
-    while reach < bands:
-        held = held + [(swap(block, "band", reach), group ^ reach) for block, group in held]
-        reach *= 2
-    return held[1:]
-
-
-def on_line(bands):
-    return bands // 2 == 4
 
 
 def body(orbitals, partners, counts):
@@ -377,8 +337,7 @@
     sends = prepare(place, by_plane)
     own = assemble([sends[0]] + [swap(sends[r], "slab", r) for r in range(1, slabs)])
 
-    gather = gather_line if on_line(bands) else gather_doubling
-    others = gather(own, band_index, bands)
+    others = gather_ring(own, band_index, bands)
 
     row = jnp.arange(NX, dtype=jnp.int32)
     held_x = (slab_index ^ (row // planes)) * planes + row % planes

time: 82.4 us -> 74.6 us (0.905)
  starting transfers between devices: 19.8 us -> 13.4 us
  waiting for transfers between devices: 30.3 us -> 27.8 us
  blocking collectives: 13.5 us -> 15.1 us
    ppermute x11 -> x8, starting transfers between devices: 14.8 us -> 8.26 us  [shift(): return lax.ppermute(value, 'band', moves)]
    ppermute x11 -> x8, waiting for transfers between devices: 28.6 us -> 26.1 us  [shift(): return lax.ppermute(value, 'band', moves)]
    all_to_all x1, blocking collectives: 13.5 us -> 15.1 us  [share(): return lax.all_to_all(sent, ('band', 'slab'), 0, 0)]
  transfers between devices with their start and end apart: 17 -> 14, of which waited for: 6 -> 6; matrix products, arithmetic and copies ran while one was open for 6% -> 6% of each run, Pallas kernels for 9% -> 10%
where the time goes in v3:
time: 74.6 us; the launch traced here: 74.4 us
  waiting for transfers between devices  27.8 us (37%)
  blocking collectives  15.1 us (20%)
  starting transfers between devices  13.4 us (18%)
  Pallas kernels  9.19 us (12%)
  other arithmetic  4.11 us (6%)
  between operations  2.76 us (4%)
  local copies, waits for them, and re-layouts  2.05 us (3%)
    ppermute x8, waiting for transfers between devices, shift(): return lax.ppermute(value, 'band', moves)  26.1 us
    all_to_all x1, blocking collectives, share(): return lax.all_to_all(sent, ('band', 'slab'), 0, 0)  15.1 us
    ppermute x8, starting transfers between devices, shift(): return lax.ppermute(value, 'band', moves)  8.26 us
    pallas_call x7, Pallas kernels, pair_step(): pl.pallas_call(functools.partial(pair_kernel, slot), out_shape=outs, in_s...  7.84 us
    ppermute x6, starting transfers between devices, swap(): return lax.ppermute(value, axis, [(i, i ^ reach) for i in range(size)])  5.1 us
    ppermute x6, waiting for transfers between devices, swap(): return lax.ppermute(value, axis, [(i, i ^ reach) for i in range(size)])  1.65 us
  transfers between devices with their start and end apart: 14, of which 6 were waited for; matrix products, arithmetic and copies ran while one was open for 6% of the time, Pallas kernels for 10%

profile of v3, /device:TPU:0, one launch (start us, length us, event | category | flops | bytes accessed | tf_op | source)
XLA Modules:
  0.0 74.4 jit_solution(13925446950605841507)
XLA Ops:
  0.6 1.0 %copy-done = f32[4,12,2304]{2,0,1:T(4,128)S(1)} copy-done((f32[4,12,2304]{2,0,1:T(4,128)S(1)}, f32[4,12,2304]{2,0,1:T(4,128)}, u32[]{:S(2)}) %copy-start) | copy-done | bytes 442392
  1.7 0.2 prepare.1
  1.9 0.6 collective-permute-start
  2.4 2.6 %collective-permute-start.1 = (f32[24,1152]{1,0:T(8,128)S(1)}, f32[24,1152]{1,0:T(8,128)S(1)}, u32[]{:S(2)}, u32[]{:S(2)}) collective-permute-start(f32[24,1152]{1,0:T(8,128)S(1)} %get-tuple-element.25), channel_id=1, source_target_pairs={{0,2},{1,3},{2,0},{3,1},{4,6},{5,7},{6,4},{7,5},{8,10},{9,11},{10,... | collective-permute-start | bytes 331784 | tf_op jit(solution)/shard_map/ppermute | solution.py:290
  5.4 0.8 %select_reduce_fusion.2 = s32[2]{0:T(128)S(1)} fusion(s32[8,2]{0,1:T(2,128)} %param.4, pred[8]{0:T(512)(128)(4,1)S(1)} %iota_compare_fusion.1), kind=kLoop, calls=%fused_computation.87 | loop fusion | flops 30 | bytes 80 | tf_op jit(solution)/shard_map/reduce_sum | solution.py:349
  6.2 0.8 %fusion.33 = (f32[8]{0:T(128)S(1)}, f32[2]{0:T(128)S(1)}) fusion(s32[8,2]{0,1:T(2,128)} %param.4, s32[8,2]{0,1:T(2,128)} %param.5, s32[]{:T(128)S(6)} %axis_index.25, s32[]{:T(128)} %axis_index.22, pred[8]{0:T(512)(128)(4,1)S(1)} %iota_compare_fusion.1), kind=kLoop, calls=%fused_computation.81 | loop fusion | flops 102 | bytes 184 | tf_op jit(solution)/shard_map/reduce_sum | solution.py:354
  7.6 0.3 reduce-precision_convert_fusion.1
  8.0 0.2 reduce-precision_convert_fusion
  8.3 0.4 copy.21
  9.1 1.6 %collective-permute-done.2.refs_3_ = f32[24,1152]{1,0:T(8,128)S(1)} collective-permute-done((f32[24,1152]{1,0:T(8,128)S(1)}, f32[24,1152]{1,0:T(8,128)S(1)}, u32[]{:S(2)}, u32[]{:S(2)}) %collective-permute-start.2) | collective-permute-done | bytes 110624 | tf_op jit(solution)/shard_map/ppermute | solution.py:290
  10.8 1.6 %collective-permute-start.3 = (f32[48,2304]{1,0:T(8,128)S(1)}, f32[48,2304]{1,0:T(8,128)S(1)}, u32[]{:S(2)}, u32[]{:S(2)}) collective-permute-start(f32[48,2304]{1,0:T(8,128)S(1)} %assemble.1.own_ref), channel_id=1, source_target_pairs={{0,8},{8,16},{16,24},{24,28},{28,20},{20,12},{12,4},{4,0},{1,9},{9... | collective-permute-start | bytes 1327112 | tf_op jit(solution)/shard_map/ppermute | solution.py:309
  12.4 0.5 collective-permute-start.7
  13.0 10.0 %collective-permute-done.3.other_ref = f32[48,2304]{1,0:T(8,128)S(1)} collective-permute-done((f32[48,2304]{1,0:T(8,128)S(1)}, f32[48,2304]{1,0:T(8,128)S(1)}, u32[]{:S(2)}, u32[]{:S(2)}) %collective-permute-start.3) | collective-permute-done | bytes 442400 | tf_op jit(solution)/shard_map/ppermute | solution.py:309
  23.1 1.8 %collective-permute-start.4 = (f32[48,2304]{1,0:T(8,128)S(1)}, f32[48,2304]{1,0:T(8,128)S(1)}, u32[]{:S(2)}, u32[]{:S(2)}) collective-permute-start(f32[48,2304]{1,0:T(8,128)S(1)} %collective-permute-done.3.other_ref), channel_id=1, source_target_pairs={{0,8},{8,16},{16,24},{24,28},{28,20},{20,12},{12,4},{4,0},{1,9},{9... | collective-permute-start | bytes 1327112 | tf_op jit(solution)/shard_map/ppermute | solution.py:309
  24.8 0.3 collective-permute-start.8
  25.3 3.5 %pair_step.8 = (f32[1,128]{1,0:T(1,128)S(1)}, f32[48,2304]{1,0:T(8,128)S(1)}) custom-call(f32[14,128]{1,0:T(8,128)S(1)} %broadcast_in_dim.97.weights, f32[48,2304]{1,0:T(8,128)S(1)} %assemble.1.own_ref, f32[48,2304]{1,0:T(8,128)S(1)} %collective-permute-done.7.other_ref, ...), custom_call_target="tpu_custom_call", output_to_operand_aliasing={{1}: (10, {})} | custom-call | flops 3221225472 | bytes 3145728 | tf_op jit(solution)/shard_map/pair_step/pallas_call | solution.py:178
  28.8 5.8 %collective-permute-done.4.other_ref = f32[48,2304]{1,0:T(8,128)S(1)} collective-permute-done((f32[48,2304]{1,0:T(8,128)S(1)}, f32[48,2304]{1,0:T(8,128)S(1)}, u32[]{:S(2)}, u32[]{:S(2)}) %collective-permute-start.4) | collective-permute-done | bytes 442400 | tf_op jit(solution)/shard_map/ppermute | solution.py:309
  34.6 1.8 %collective-permute-start.5 = (f32[48,2304]{1,0:T(8,128)S(1)}, f32[48,2304]{1,0:T(8,128)S(1)}, u32[]{:S(2)}, u32[]{:S(2)}) collective-permute-start(f32[48,2304]{1,0:T(8,128)S(1)} %collective-permute-done.4.other_ref), channel_id=1, source_target_pairs={{0,8},{8,16},{16,24},{24,28},{28,20},{20,12},{12,4},{4,0},{1,9},{9... | collective-permute-start | bytes 1327112 | tf_op jit(solution)/shard_map/ppermute | solution.py:309
  36.4 0.2 collective-permute-start.9
  36.7 3.7 %pair_step.10 = (f32[1,128]{1,0:T(1,128)S(1)}, f32[48,2304]{1,0:T(8,128)S(1)}) custom-call(f32[14,128]{1,0:T(8,128)S(1)} %broadcast_in_dim.97.weights, f32[48,2304]{1,0:T(8,128)S(1)} %assemble.1.own_ref, f32[48,2304]{1,0:T(8,128)S(1)} %collective-permute-done.8.other_ref, ...), custom_call_target="tpu_custom_call", output_to_operand_aliasing={{1}: (10, {})} | custom-call | flops 3221225472 | bytes 3145728 | tf_op jit(solution)/shard_map/pair_step/pallas_call | solution.py:178
  40.4 4.9 %collective-permute-done.5.other_ref = f32[48,2304]{1,0:T(8,128)S(1)} collective-permute-done((f32[48,2304]{1,0:T(8,128)S(1)}, f32[48,2304]{1,0:T(8,128)S(1)}, u32[]{:S(2)}, u32[]{:S(2)}) %collective-permute-start.5) | collective-permute-done | bytes 442400 | tf_op jit(solution)/shard_map/ppermute | solution.py:309
  45.3 1.9 %collective-permute-start.6 = (f32[24,2304]{1,0:T(8,128)S(1)}, f32[24,2304]{1,0:T(8,128)S(1)}, u32[]{:S(2)}, u32[]{:S(2)}) collective-permute-start(f32[24,2304]{1,0:T(8,128)S(1)} %slice.24), channel_id=1, source_target_pairs={{0,8},{8,16},{16,24},{24,28},{28,20},{20,12},{12,4},{4,0},{1,9},{9... | collective-permute-start | bytes 663560 | tf_op jit(solution)/shard_map/ppermute | solution.py:309
  47.2 0.2 collective-permute-start.10
  47.7 3.6 %collective-permute-done.6 = f32[24,2304]{1,0:T(8,128)S(1)} collective-permute-done((f32[24,2304]{1,0:T(8,128)S(1)}, f32[24,2304]{1,0:T(8,128)S(1)}, u32[]{:S(2)}, u32[]{:S(2)}) %collective-permute-start.6) | collective-permute-done | bytes 221216 | tf_op jit(solution)/shard_map/ppermute | solution.py:309
  51.3 1.9 %collective-permute-done.10 = f32[24,2304]{1,0:T(8,128)S(1)} collective-permute-done((f32[24,2304]{1,0:T(8,128)S(1)}, f32[24,2304]{1,0:T(8,128)S(1)}, u32[]{:S(2)}, u32[]{:S(2)}) %collective-permute-start.10) | collective-permute-done | bytes 221216 | tf_op jit(solution)/shard_map/ppermute | solution.py:309
  53.2 0.2 multiply_add_fusion.refs_0_
  53.5 0.2 pair_step.13
  53.8 1.6 %collective-permute-start.12 = (f32[48,1152]{1,0:T(8,128)S(1)}, f32[48,1152]{1,0:T(8,128)S(1)}, u32[]{:S(2)}, u32[]{:S(2)}) collective-permute-start(f32[48,1152]{1,0:T(8,128)S(1)} %get-tuple-element.41), channel_id=1, source_target_pairs={{0,2},{1,3},{2,0},{3,1},{4,6},{5,7},{6,4},{7,5},{8,10},{9,11},{10,... | collective-permute-start | bytes 663560 | tf_op jit(solution)/shard_map/ppermute | solution.py:290
  55.3 0.3 collective-permute-start.11
  55.6 15.1 %all_to_all.5 = f32[32,1,128]{2,1,0:T(1,128)S(1)} all-to-all(f32[32,1,128]{2,1,0:T(1,128)S(1)} %broadcast_in_dim.101), channel_id=1, replica_groups=mesh['band'=8,'slab'=4] {'band','slab'}, dimensions={0} | all-to-all | bytes 32768 | tf_op jit(solution)/shard_map/all_to_all | solution.py:295
  70.8 0.6 reduce_sum.65
  72.2 1.1 %finish.1 = f32[12,4,2304]{2,1,0:T(4,128)} custom-call(s32[1]{0:T(128)} %bitcast.place, f32[12,4,2304]{2,1,0:T(4,128)S(1)} %bitcast.18, f32[24,1152]{1,0:T(8,128)S(1)} %fusion.2.local_pot, f32[48,1152]{1,0:T(8,128)S(1)} %get-tuple-element.39.refs_0_, f32[48,1152]{1,0:T(8,128)S(1)} %collective-permute-done.11.refs_1_, ...), custom_call_target="tpu_custom_call" | custom-call | tf_op jit(solution)/shard_map/finish/pallas_call | solution.py:278
  (52 shorter events, 2.6 us)
Async XLA Ops:
  0.6 1.0 %copy-start = (f32[4,12,2304]{2,0,1:T(4,128)S(1)}, f32[4,12,2304]{2,0,1:T(4,128)}, u32[]{:S(2)}) copy-start(f32[4,12,2304]{2,0,1:T(4,128)} %param.3) | copy-start | bytes 1327108
  1.9 7.2 %collective-permute-start = (f32[24,1152]{1,0:T(8,128)S(1)}, f32[24,1152]{1,0:T(8,128)S(1)}, u32[]{:S(2)}, u32[]{:S(2)}) collective-permute-start(f32[24,1152]{1,0:T(8,128)S(1)} %get-tuple-element.24), channel_id=1, source_target_pairs={{0,1},{1,0},{2,3},{3,2},{4,5},{5,4},{6,7},{7,6},{8,9},{9,8},{10,11... | collective-permute-start | bytes 331784 | tf_op jit(solution)/shard_map/ppermute | solution.py:290
  2.4 6.7 %collective-permute-start.1 = (f32[24,1152]{1,0:T(8,128)S(1)}, f32[24,1152]{1,0:T(8,128)S(1)}, u32[]{:S(2)}, u32[]{:S(2)}) collective-permute-start(f32[24,1152]{1,0:T(8,128)S(1)} %get-tuple-element.25), channel_id=1, source_target_pairs={{0,2},{1,3},{2,0},{3,1},{4,6},{5,7},{6,4},{7,5},{8,10},{9,11},{10,... | collective-permute-start | bytes 331784 | tf_op jit(solution)/shard_map/ppermute | solution.py:290
  5.0 5.8 %collective-permute-start.2 = (f32[24,1152]{1,0:T(8,128)S(1)}, f32[24,1152]{1,0:T(8,128)S(1)}, u32[]{:S(2)}, u32[]{:S(2)}) collective-permute-start(f32[24,1152]{1,0:T(8,128)S(1)} %get-tuple-element.26), channel_id=1, source_target_pairs={{0,3},{1,2},{2,1},{3,0},{4,7},{5,6},{6,5},{7,4},{8,11},{9,10},{10,... | collective-permute-start | bytes 331784 | tf_op jit(solution)/shard_map/ppermute | solution.py:290
  10.8 12.2 %collective-permute-start.3 = (f32[48,2304]{1,0:T(8,128)S(1)}, f32[48,2304]{1,0:T(8,128)S(1)}, u32[]{:S(2)}, u32[]{:S(2)}) collective-permute-start(f32[48,2304]{1,0:T(8,128)S(1)} %assemble.1.own_ref), channel_id=1, source_target_pairs={{0,8},{8,16},{16,24},{24,28},{28,20},{20,12},{12,4},{4,0},{1,9},{9... | collective-permute-start | bytes 1327112 | tf_op jit(solution)/shard_map/ppermute | solution.py:309
  12.4 12.4 %collective-permute-start.7 = (f32[48,2304]{1,0:T(8,128)S(1)}, f32[48,2304]{1,0:T(8,128)S(1)}, u32[]{:S(2)}, u32[]{:S(2)}) collective-permute-start(f32[48,2304]{1,0:T(8,128)S(1)} %assemble.1.own_ref), channel_id=1, source_target_pairs={{0,4},{8,0},{16,8},{24,16},{28,24},{20,28},{12,20},{4,12},{1,5},{9... | collective-permute-start | bytes 1327112 | tf_op jit(solution)/shard_map/ppermute | solution.py:309
  23.1 11.5 %collective-permute-start.4 = (f32[48,2304]{1,0:T(8,128)S(1)}, f32[48,2304]{1,0:T(8,128)S(1)}, u32[]{:S(2)}, u32[]{:S(2)}) collective-permute-start(f32[48,2304]{1,0:T(8,128)S(1)} %collective-permute-done.3.other_ref), channel_id=1, source_target_pairs={{0,8},{8,16},{16,24},{24,28},{28,20},{20,12},{12,4},{4,0},{1,9},{9... | collective-permute-start | bytes 1327112 | tf_op jit(solution)/shard_map/ppermute | solution.py:309
  24.8 11.6 %collective-permute-start.8 = (f32[48,2304]{1,0:T(8,128)S(1)}, f32[48,2304]{1,0:T(8,128)S(1)}, u32[]{:S(2)}, u32[]{:S(2)}) collective-permute-start(f32[48,2304]{1,0:T(8,128)S(1)} %collective-permute-done.7.other_ref), channel_id=1, source_target_pairs={{0,4},{8,0},{16,8},{24,16},{28,24},{20,28},{12,20},{4,12},{1,5},{9... | collective-permute-start | bytes 1327112 | tf_op jit(solution)/shard_map/ppermute | solution.py:309
  34.6 10.7 %collective-permute-start.5 = (f32[48,2304]{1,0:T(8,128)S(1)}, f32[48,2304]{1,0:T(8,128)S(1)}, u32[]{:S(2)}, u32[]{:S(2)}) collective-permute-start(f32[48,2304]{1,0:T(8,128)S(1)} %collective-permute-done.4.other_ref), channel_id=1, source_target_pairs={{0,8},{8,16},{16,24},{24,28},{28,20},{20,12},{12,4},{4,0},{1,9},{9... | collective-permute-start | bytes 1327112 | tf_op jit(solution)/shard_map/ppermute | solution.py:309
  36.4 10.8 %collective-permute-start.9 = (f32[48,2304]{1,0:T(8,128)S(1)}, f32[48,2304]{1,0:T(8,128)S(1)}, u32[]{:S(2)}, u32[]{:S(2)}) collective-permute-start(f32[48,2304]{1,0:T(8,128)S(1)} %collective-permute-done.8.other_ref), channel_id=1, source_target_pairs={{0,4},{8,0},{16,8},{24,16},{28,24},{20,28},{12,20},{4,12},{1,5},{9... | collective-permute-start | bytes 1327112 | tf_op jit(solution)/shard_map/ppermute | solution.py:309
  45.3 6.0 %collective-permute-start.6 = (f32[24,2304]{1,0:T(8,128)S(1)}, f32[24,2304]{1,0:T(8,128)S(1)}, u32[]{:S(2)}, u32[]{:S(2)}) collective-permute-start(f32[24,2304]{1,0:T(8,128)S(1)} %slice.24), channel_id=1, source_target_pairs={{0,8},{8,16},{16,24},{24,28},{28,20},{20,12},{12,4},{4,0},{1,9},{9... | collective-permute-start | bytes 663560 | tf_op jit(solution)/shard_map/ppermute | solution.py:309
  47.2 6.0 %collective-permute-start.10 = (f32[24,2304]{1,0:T(8,128)S(1)}, f32[24,2304]{1,0:T(8,128)S(1)}, u32[]{:S(2)}, u32[]{:S(2)}) collective-permute-start(f32[24,2304]{1,0:T(8,128)S(1)} %slice.25), channel_id=1, source_target_pairs={{0,4},{8,0},{16,8},{24,16},{28,24},{20,28},{12,20},{4,12},{1,5},{9... | collective-permute-start | bytes 663560 | tf_op jit(solution)/shard_map/ppermute | solution.py:309
  53.5 18.7 %copy-start.1 = (f32[4,12,2304]{2,0,1:T(4,128)S(1)}, f32[4,12,2304]{2,0,1:T(4,128)}, u32[]{:S(2)}) copy-start(f32[4,12,2304]{2,0,1:T(4,128)} %param.3) | copy-start | bytes 1327108
  53.7 18.3 %collective-permute-start.13 = (f32[48,1152]{1,0:T(8,128)S(1)}, f32[48,1152]{1,0:T(8,128)S(1)}, u32[]{:S(2)}, u32[]{:S(2)}) collective-permute-start(f32[48,1152]{1,0:T(8,128)S(1)} %get-tuple-element.42), channel_id=1, source_target_pairs={{0,3},{1,2},{2,1},{3,0},{4,7},{5,6},{6,5},{7,4},{8,11},{9,10},{10,... | collective-permute-start | bytes 663560 | tf_op jit(solution)/shard_map/ppermute | solution.py:290
  53.8 18.3 %collective-permute-start.12 = (f32[48,1152]{1,0:T(8,128)S(1)}, f32[48,1152]{1,0:T(8,128)S(1)}, u32[]{:S(2)}, u32[]{:S(2)}) collective-permute-start(f32[48,1152]{1,0:T(8,128)S(1)} %get-tuple-element.41), channel_id=1, source_target_pairs={{0,2},{1,3},{2,0},{3,1},{4,6},{5,7},{6,4},{7,5},{8,10},{9,11},{10,... | collective-permute-start | bytes 663560 | tf_op jit(solution)/shard_map/ppermute | solution.py:290
  55.3 16.7 %collective-permute-start.11 = (f32[48,1152]{1,0:T(8,128)S(1)}, f32[48,1152]{1,0:T(8,128)S(1)}, u32[]{:S(2)}, u32[]{:S(2)}) collective-permute-start(f32[48,1152]{1,0:T(8,128)S(1)} %get-tuple-element.40), channel_id=1, source_target_pairs={{0,1},{1,0},{2,3},{3,2},{4,5},{5,4},{6,7},{7,6},{8,9},{9,8},{10,11... | collective-permute-start | bytes 663560 | tf_op jit(solution)/shard_map/ppermute | solution.py:290

commit v4 on v3

--- a/solution.py
+++ b/solution.py
@@ -47,22 +47,22 @@
     return jnp.concatenate([high, low], axis=0)
 
 
-def wavenumber_sq(length):
-    position = jnp.arange(length, dtype=jnp.int32)
+def wavenumber_sq(position):
+    length = position.shape[0]
     signed = jnp.where(position > length // 2, position - length, position).astype(jnp.float32)
     wave_number = 2.0 * math.pi / length * signed
     return wave_number * wave_number
 
 
-def transform_tables(held_x):
-    x_waves = jnp.arange(NX, dtype=jnp.int32)
-    y_cells = jnp.arange(NY, dtype=jnp.int32)
-    z_cells = jnp.arange(NZ, dtype=jnp.int32)
-    z_waves = jnp.arange(NZP, dtype=jnp.int32)
+def transform_tables(count, held_x):
+    x_waves = count[:NX]
+    y_cells = count[:NY]
+    z_cells = count[:NZ]
+    z_waves = count[:NZP]
     total = (
-        wavenumber_sq(NZP)[:, None, None]
-        + wavenumber_sq(NX)[None, :, None]
-        + wavenumber_sq(NY)[None, None, :]
+        wavenumber_sq(z_waves)[:, None, None]
+        + wavenumber_sq(x_waves)[None, :, None]
+        + wavenumber_sq(y_cells)[None, None, :]
     )
     kernel_table = 4.0 * math.pi / (NX * NY * NZP) / (total + screening * screening)
     y_matrix = cas(y_cells[:, None], y_cells[None, :], NY)
@@ -248,16 +248,50 @@
 
 
 def assemble(pieces):
-    _, part = pieces[0].shape
+    rows, part = pieces[0].shape
     fold = NY * NZ // part
     return pl.pallas_call(
         functools.partial(assemble_kernel, fold),
-        out_shape=jax.ShapeDtypeStruct((NX, NY * NZ), jnp.float32),
+        out_shape=jax.ShapeDtypeStruct((rows // fold * len(pieces), NY * NZ), jnp.float32),
         in_specs=in_vmem(len(pieces)),
         out_specs=in_vmem(1)[0],
         compiler_params=pltpu.CompilerParams(vmem_limit_bytes=8 << 20),
         name="assemble",
     )(*pieces)
+
+
+def clear_kernel(out_ref):
+    out_ref[...] = jnp.zeros_like(out_ref)
+
+
+def clear(shape):
+    return pl.pallas_call(
+        clear_kernel,
+        out_shape=jax.ShapeDtypeStruct(shape, jnp.float32),
+        out_specs=in_vmem(1)[0],
+        compiler_params=pltpu.CompilerParams(vmem_limit_bytes=8 << 20),
+        name="clear",
+    )()
+
+
+def join_kernel(*refs):
+    out_ref = refs[-1]
+    first = 0
+    for ref in refs[:-1]:
+        out_ref[first : first + ref.shape[0], :] = ref[...]
+        first += ref.shape[0]
+
+
+def join(*parts):
+    rows = sum(part.shape[0] for part in parts)
+    return pl.pallas_call(
+        join_kernel,
+        out_shape=jax.ShapeDtypeStruct((rows,) + parts[0].shape[1:], jnp.float32),
+        in_specs=in_vmem(len(parts)),
+        out_specs=in_vmem(1)[0],
+        compiler_params=pltpu.CompilerParams(vmem_limit_bytes=8 << 20),
+        name="join",
+    )(*parts)
 
 
 def finish_kernel(fold, place, orbitals, local_pot, *refs):
@@ -285,9 +319,9 @@
     )(place, orbitals, local_pot, *pieces)
 
 
-def swap(value, axis, reach):
-    size = lax.axis_size(axis)
-    return lax.ppermute(value, axis, [(i, i ^ reach) for i in range(size)])
+def slab_swap(value, reach):
+    size = lax.axis_size("slab")
+    return lax.ppermute(value, "slab", [(i, i ^ reach) for i in range(size)])
 
 
 def share(value, devices):
@@ -295,7 +329,7 @@
     return lax.all_to_all(sent, ("band", "slab"), 0, 0)
 
 
-def gather_ring(own, band_index, bands):
+def gather_ring(halves, band_index, bands):
     groups = [2 * p if p < bands // 2 else 2 * (bands - 1 - p) + 1 for p in range(bands)]
     place = band_index // 2
     position = jnp.where(band_index % 2 == 0, place, bands - 1 - place)
@@ -308,18 +342,21 @@
         moves = [(groups[p], groups[(p + by) % bands]) for p in range(bands)]
         return lax.ppermute(value, "band", moves)
 
-    ahead = behind = own
+    came = [(shift(half, 1), shift(half, -1)) for half in halves]
     blocks = []
     steps = bands // 2 - 1
     for step in range(steps):
-        ahead = shift(ahead, 1)
-        behind = shift(behind, -1)
+        if step == 0:
+            ahead, behind = (join(*pair) for pair in zip(*came))
+        else:
+            ahead = shift(ahead, 1)
+            behind = shift(behind, -1)
         blocks.append((ahead, group_at(position - step - 1)))
         blocks.append((behind, group_at(position + step + 1)))
-    half = own.shape[0] // 2
+    half = ahead.shape[0] // 2
     head = shift(ahead[:half], 1)
     tail = shift(behind[half:], -1)
-    blocks.append((jnp.concatenate([head, tail], axis=0), group_at(position + steps + 1)))
+    blocks.append((join(head, tail), group_at(position + steps + 1)))
     return blocks
 
 
@@ -335,13 +372,17 @@
     place = slab_index.astype(jnp.int32).reshape(1)
     by_plane = jnp.transpose(orbitals, (1, 0, 2))
     sends = prepare(place, by_plane)
-    own = assemble([sends[0]] + [swap(sends[r], "slab", r) for r in range(1, slabs)])
-
-    others = gather_ring(own, band_index, bands)
-
-    row = jnp.arange(NX, dtype=jnp.int32)
+    pieces = [sends[0]] + [slab_swap(sends[r], r) for r in range(1, slabs)]
+    halves = [assemble(pieces[: slabs // 2]), assemble(pieces[slabs // 2 :])]
+    own = join(*halves)
+    others = gather_ring(halves, band_index, bands)
+    force = clear((NX, NY * NZ))
+
+    count = jnp.arange(max(NX, NY, NZP), dtype=jnp.int32)
+    own, count, partners, counts = lax.optimization_barrier((own, count, partners, counts))
+    row = count[:NX]
     held_x = (slab_index ^ (row // planes)) * planes + row % planes
-    tables = transform_tables(held_x)
+    tables = transform_tables(count, held_x)
 
     groups = jnp.stack([group for _, group in others]).astype(jnp.int32)
     active = (slab_index < counts).astype(jnp.float32)
@@ -357,7 +398,6 @@
     weights = jnp.stack([requested + returned, requested], axis=1).reshape(-1)
     weights = jnp.broadcast_to(weights[:, None], weights.shape + (128,))
 
-    force = jnp.zeros((NX, NY * NZ), jnp.float32)
     energy = jnp.zeros((1, 128), jnp.float32)
     squares = own * own
     for other, _ in others:
@@ -370,7 +410,7 @@
                 slot, weights, own, other, tables, force, energy, slabs, squares
             )
 
-    arrived = [outgoing[0]] + [swap(outgoing[r], "slab", r) for r in range(1, slabs)]
+    arrived = [outgoing[0]] + [slab_swap(outgoing[r], r) for r in range(1, slabs)]
     shared = share(energy, bands * slabs)
     rows = arrived[0].shape[0] // 2
     density = 2.0 / total_orbs * sum(piece[rows:] for piece in arrived)

time: 74.6 us -> 74.9 us (level)
  waiting for transfers between devices: 27.8 us -> 25.4 us
  other arithmetic: 4.11 us -> 6.09 us
  local copies, waits for them, and re-layouts: 2.05 us -> 2.95 us
    ppermute x8 -> x10, waiting for transfers between devices: 26.1 us -> 21.8 us  [shift(): return lax.ppermute(value, 'band', moves)]
    ppermute x6, waiting for transfers between devices: 1.65 us -> 3.63 us  [slab_swap(): return lax.ppermute(value, 'slab', [(i, i ^ reach) for i in range(size)])]
    convert_element_type x4 -> x3, other arithmetic: 0.71 us -> 1.99 us  [split_table(): return (high.astype(jnp.bfloat16), (matrix - high).astype(jnp.bfloat16))]
    div x1, other arithmetic: 0.12 us -> 1.29 us  [transform_tables(): 4.0 * math.pi / (NX * NY * NZP) / (total + screening * screening)]
    add x4, local copies, waits for them, and re-layouts: 0.51 us -> 1.44 us  [transform_tables(): wavenumber_sq(z_waves)[:, None, None]]
    concatenate x3, other arithmetic: 0.27 us -> 1.05 us  [wide(): return jnp.concatenate([high, high, low], axis=1)]
    ppermute x8 -> x10, starting transfers between devices: 8.26 us -> 7.69 us  [shift(): return lax.ppermute(value, 'band', moves)]
  transfers between devices with their start and end apart: 14 -> 16, of which waited for: 6 -> 9; matrix products, arithmetic and copies ran while one was open for 6% -> 10% of each run, Pallas kernels for 10% -> 10%
where the time goes in v4:
time: 74.9 us; the launch traced here: 74.6 us
  waiting for transfers between devices  25.4 us (34%)
  blocking collectives  15.2 us (20%)
  starting transfers between devices  12.8 us (17%)
  Pallas kernels  9.35 us (12%)
  other arithmetic  6.09 us (8%)
  local copies, waits for them, and re-layouts  2.95 us (4%)
  between operations  2.83 us (4%)
    ppermute x10, waiting for transfers between devices, shift(): return lax.ppermute(value, 'band', moves)  21.8 us
    all_to_all x1, blocking collectives, share(): return lax.all_to_all(sent, ('band', 'slab'), 0, 0)  15.2 us
    pallas_call x7, Pallas kernels, pair_step(): pl.pallas_call(functools.partial(pair_kernel, slot), out_shape=outs, in_s...  7.85 us
    ppermute x10, starting transfers between devices, shift(): return lax.ppermute(value, 'band', moves)  7.69 us
    ppermute x6, starting transfers between devices, slab_swap(): return lax.ppermute(value, 'slab', [(i, i ^ reach) for i in range(size)])  5.1 us
    ppermute x6, waiting for transfers between devices, slab_swap(): return lax.ppermute(value, 'slab', [(i, i ^ reach) for i in range(size)])  3.63 us
    convert_element_type x3, other arithmetic, split_table(): return (high.astype(jnp.bfloat16), (matrix - high).astype(jnp.bfloat16))  1.99 us
  transfers between devices with their start and end apart: 16, of which 9 were waited for; matrix products, arithmetic and copies ran while one was open for 10% of the time, Pallas kernels for 10%

profile of v4, /device:TPU:0, one launch (start us, length us, event | category | flops | bytes accessed | tf_op | source)
XLA Modules:
  0.0 74.6 jit_solution(12469424393419026050)
XLA Ops:
  0.6 1.0 %copy-done = f32[4,12,2304]{2,0,1:T(4,128)S(1)} copy-done((f32[4,12,2304]{2,0,1:T(4,128)S(1)}, f32[4,12,2304]{2,0,1:T(4,128)}, u32[]{:S(2)}) %copy-start) | copy-done | bytes 442392
  1.9 0.6 collective-permute-start
  2.4 2.6 %collective-permute-start.1 = (f32[24,1152]{1,0:T(8,128)S(1)}, f32[24,1152]{1,0:T(8,128)S(1)}, u32[]{:S(2)}, u32[]{:S(2)}) collective-permute-start(f32[24,1152]{1,0:T(8,128)S(1)} %get-tuple-element.29), channel_id=1, source_target_pairs={{0,2},{1,3},{2,0},{3,1},{4,6},{5,7},{6,4},{7,5},{8,10},{9,11},{10,... | collective-permute-start | bytes 331784 | tf_op jit(solution)/shard_map/ppermute | solution.py:324
  5.3 1.9 %collective-permute-start.3 = (f32[24,2304]{1,0:T(8,128)S(1)}, f32[24,2304]{1,0:T(8,128)S(1)}, u32[]{:S(2)}, u32[]{:S(2)}) collective-permute-start(f32[24,2304]{1,0:T(8,128)S(1)} %assemble.2.refs_0_), channel_id=1, source_target_pairs={{0,8},{8,16},{16,24},{24,28},{28,20},{20,12},{12,4},{4,0},{1,9},{9... | collective-permute-start | bytes 663560 | tf_op jit(solution)/shard_map/ppermute | solution.py:343
  7.1 1.8 %collective-permute-done.1.refs_0_ = f32[24,1152]{1,0:T(8,128)S(1)} collective-permute-done((f32[24,1152]{1,0:T(8,128)S(1)}, f32[24,1152]{1,0:T(8,128)S(1)}, u32[]{:S(2)}, u32[]{:S(2)}) %collective-permute-start.1) | collective-permute-done | bytes 110624 | tf_op jit(solution)/shard_map/ppermute | solution.py:324
  8.9 1.8 %collective-permute-done.2.refs_1_ = f32[24,1152]{1,0:T(8,128)S(1)} collective-permute-done((f32[24,1152]{1,0:T(8,128)S(1)}, f32[24,1152]{1,0:T(8,128)S(1)}, u32[]{:S(2)}, u32[]{:S(2)}) %collective-permute-start.2) | collective-permute-done | bytes 110624 | tf_op jit(solution)/shard_map/ppermute | solution.py:324
  10.8 1.6 %collective-permute-start.4 = (f32[24,2304]{1,0:T(8,128)S(1)}, f32[24,2304]{1,0:T(8,128)S(1)}, u32[]{:S(2)}, u32[]{:S(2)}) collective-permute-start(f32[24,2304]{1,0:T(8,128)S(1)} %assemble.3.refs_1_), channel_id=1, source_target_pairs={{0,8},{8,16},{16,24},{24,28},{28,20},{20,12},{12,4},{4,0},{1,9},{9... | collective-permute-start | bytes 663560 | tf_op jit(solution)/shard_map/ppermute | solution.py:343
  12.4 0.5 collective-permute-start.8
  12.9 1.4 %collective-permute-start.9 = (f32[24,2304]{1,0:T(8,128)S(1)}, f32[24,2304]{1,0:T(8,128)S(1)}, u32[]{:S(2)}, u32[]{:S(2)}) collective-permute-start(f32[24,2304]{1,0:T(8,128)S(1)} %assemble.3.refs_1_), channel_id=1, source_target_pairs={{0,4},{8,0},{16,8},{24,16},{28,24},{20,28},{12,20},{4,12},{1,5},{9... | collective-permute-start | bytes 663560 | tf_op jit(solution)/shard_map/ppermute | solution.py:343
  14.5 0.8 %reduce-precision_convert_fusion.2 = (bf16[48,96]{1,0:T(8,128)(2,1)}, bf16[48,96]{1,0:T(8,128)(2,1)}) fusion(s32[96]{0:T(128)S(1)} %iota.13, s32[48]{0:T(128)S(1)} %get-tuple-element.64), kind=kLoop, calls=%fused_computation.22 | loop fusion | flops 64512 | bytes 19008 | tf_op jit(solution)/shard_map/convert_element_type | solution.py:37
  16.0 1.0 %reduce-precision_convert_fusion.1 = (bf16[48,48]{1,0:T(8,128)(2,1)}, bf16[48,48]{1,0:T(8,128)(2,1)}, bf16[48,48]{1,0:T(8,128)(2,1)}, bf16[48,48]{1,0:T(8,128)(2...) fusion(s32[48]{0:T(128)S(1)} %get-tuple-element.65, s32[48]{0:T(128)S(1)} %get-tuple-element.64), kind=kLoop, calls=%fused_computation.20 | loop fusion | flops 96768 | bytes 28032 | tf_op jit(solution)/shard_map/convert_element_type | solution.py:37
  17.5 1.3 %copy.21 = f32[96,2304]{1,0:T(8,128)} copy(f32[96,2304]{0,1:T(8,128)S(1)} %bitcast.20) | data formatting | bytes 1769472 | tf_op jit(solution)/shard_map/add | solution.py:63
  18.9 0.9 %pad_maximum_fusion.2 = (bf16[48,144]{1,0:T(8,128)(2,1)S(1)}, bf16[48,144]{1,0:T(8,128)(2,1)S(1)}) fusion(bf16[48,48]{1,0:T(8,128)(2,1)} %get-tuple-element.57, bf16[48,48]{1,0:T(8,128)(2,1)} %get-tuple-element.59, bf16[48,48]{1,0:T(8,128)(2,1)S(1)} %get-tuple-element.63, bf16[48,48]{1,0:T(8,128)(2,1)S(1)} %get-tuple-element.62), kind=kLoop, calls=%fused_computation.40 | loop fusion | flops 82944 | bytes 46080 | tf_op jit(solution)/shard_map/concatenate | solution.py:42
  19.8 1.3 %add_divide_fusion.table = f32[96,2304]{1,0:T(8,128)S(1)} fusion(f32[96,2304]{1,0:T(8,128)} %copy.21, f32[2304]{0:T(1024)S(1)} %add.248), kind=kLoop, calls=%fused_computation | loop fusion | flops 663552 | bytes 1778688 | tf_op jit(solution)/shard_map/div | solution.py:67
  21.4 0.6 collective-permute-start.5
  22.0 2.9 %collective-permute-done.9.refs_1_ = f32[24,2304]{1,0:T(8,128)S(1)} collective-permute-done((f32[24,2304]{1,0:T(8,128)S(1)}, f32[24,2304]{1,0:T(8,128)S(1)}, u32[]{:S(2)}, u32[]{:S(2)}) %collective-permute-start.9) | collective-permute-done | bytes 221216 | tf_op jit(solution)/shard_map/ppermute | solution.py:343
  24.9 0.3 collective-permute-start.10
  25.4 3.5 %pair_step.8 = (f32[1,128]{1,0:T(1,128)S(1)}, f32[48,2304]{1,0:T(8,128)S(1)}) custom-call(f32[14,128]{1,0:T(8,128)S(1)} %broadcast_in_dim.94.weights, f32[48,2304]{1,0:T(8,128)S(1)} %join.4.own_ref, f32[48,2304]{1,0:T(8,128)S(1)} %join.6.other_ref, bf16[48,144]{1,0:T(8,128)(2,1)S(1)} %get-tuple-element.66.x_fwd, ...), custom_call_target="tpu_custom_call", output_to_operand_aliasing={{1}: (10, {})} | custom-call | flops 3221225472 | bytes 3145728 | tf_op jit(solution)/shard_map/pair_step/pallas_call | solution.py:178
  28.9 4.4 %collective-permute-done.5.other_ref = f32[48,2304]{1,0:T(8,128)S(1)} collective-permute-done((f32[48,2304]{1,0:T(8,128)S(1)}, f32[48,2304]{1,0:T(8,128)S(1)}, u32[]{:S(2)}, u32[]{:S(2)}) %collective-permute-start.5) | collective-permute-done | bytes 442400 | tf_op jit(solution)/shard_map/ppermute | solution.py:343
  33.3 0.4 collective-permute-start.6
  33.7 2.8 %collective-permute-done.10.other_ref = f32[48,2304]{1,0:T(8,128)S(1)} collective-permute-done((f32[48,2304]{1,0:T(8,128)S(1)}, f32[48,2304]{1,0:T(8,128)S(1)}, u32[]{:S(2)}, u32[]{:S(2)}) %collective-permute-start.10) | collective-permute-done | bytes 442400 | tf_op jit(solution)/shard_map/ppermute | solution.py:343
  37.0 3.7 %pair_step.10 = (f32[1,128]{1,0:T(1,128)S(1)}, f32[48,2304]{1,0:T(8,128)S(1)}) custom-call(f32[14,128]{1,0:T(8,128)S(1)} %broadcast_in_dim.94.weights, f32[48,2304]{1,0:T(8,128)S(1)} %join.4.own_ref, f32[48,2304]{1,0:T(8,128)S(1)} %collective-permute-done.10.other_ref, ...), custom_call_target="tpu_custom_call", output_to_operand_aliasing={{1}: (10, {})} | custom-call | flops 3221225472 | bytes 3145728 | tf_op jit(solution)/shard_map/pair_step/pallas_call | solution.py:178
  40.6 3.7 %collective-permute-done.6.other_ref = f32[48,2304]{1,0:T(8,128)S(1)} collective-permute-done((f32[48,2304]{1,0:T(8,128)S(1)}, f32[48,2304]{1,0:T(8,128)S(1)}, u32[]{:S(2)}, u32[]{:S(2)}) %collective-permute-start.6) | collective-permute-done | bytes 442400 | tf_op jit(solution)/shard_map/ppermute | solution.py:343
  44.4 0.3 collective-permute-start.7
  44.7 2.6 %collective-permute-done.11.other_ref = f32[48,2304]{1,0:T(8,128)S(1)} collective-permute-done((f32[48,2304]{1,0:T(8,128)S(1)}, f32[48,2304]{1,0:T(8,128)S(1)}, u32[]{:S(2)}, u32[]{:S(2)}) %collective-permute-start.11) | collective-permute-done | bytes 442400 | tf_op jit(solution)/shard_map/ppermute | solution.py:343
  47.3 0.3 collective-permute-start.12
  47.9 2.4 %collective-permute-done.7.refs_0_ = f32[24,2304]{1,0:T(8,128)S(1)} collective-permute-done((f32[24,2304]{1,0:T(8,128)S(1)}, f32[24,2304]{1,0:T(8,128)S(1)}, u32[]{:S(2)}, u32[]{:S(2)}) %collective-permute-start.7) | collective-permute-done | bytes 221216 | tf_op jit(solution)/shard_map/ppermute | solution.py:343
  50.3 2.9 %collective-permute-done.12.refs_1_ = f32[24,2304]{1,0:T(8,128)S(1)} collective-permute-done((f32[24,2304]{1,0:T(8,128)S(1)}, f32[24,2304]{1,0:T(8,128)S(1)}, u32[]{:S(2)}, u32[]{:S(2)}) %collective-permute-start.12) | collective-permute-done | bytes 221216 | tf_op jit(solution)/shard_map/ppermute | solution.py:343
  53.9 1.6 %collective-permute-start.14 = (f32[48,1152]{1,0:T(8,128)S(1)}, f32[48,1152]{1,0:T(8,128)S(1)}, u32[]{:S(2)}, u32[]{:S(2)}) collective-permute-start(f32[48,1152]{1,0:T(8,128)S(1)} %get-tuple-element.49), channel_id=1, source_target_pairs={{0,2},{1,3},{2,0},{3,1},{4,6},{5,7},{6,4},{7,5},{8,10},{9,11},{10,... | collective-permute-start | bytes 663560 | tf_op jit(solution)/shard_map/ppermute | solution.py:324
  55.8 15.2 %all_to_all.5 = f32[32,1,128]{2,1,0:T(1,128)S(1)} all-to-all(f32[32,1,128]{2,1,0:T(1,128)S(1)} %broadcast_in_dim.97), channel_id=1, replica_groups=mesh['band'=8,'slab'=4] {'band','slab'}, dimensions={0} | all-to-all | bytes 32768 | tf_op jit(solution)/shard_map/all_to_all | solution.py:329
  70.9 0.6 reduce_sum.65
  72.3 1.1 %finish.1 = f32[12,4,2304]{2,1,0:T(4,128)} custom-call(s32[1]{0:T(128)} %bitcast.place, f32[12,4,2304]{2,1,0:T(4,128)S(1)} %bitcast.18, f32[24,1152]{1,0:T(8,128)S(1)} %fusion.2.local_pot, f32[48,1152]{1,0:T(8,128)S(1)} %get-tuple-element.47.refs_0_, f32[48,1152]{1,0:T(8,128)S(1)} %collective-permute-done.13.refs_1_, ...), custom_call_target="tpu_custom_call" | custom-call | tf_op jit(solution)/shard_map/finish/pallas_call | solution.py:312
  (75 shorter events, 4.0 us)
Async XLA Ops:
  0.6 1.0 %copy-start = (f32[4,12,2304]{2,0,1:T(4,128)S(1)}, f32[4,12,2304]{2,0,1:T(4,128)}, u32[]{:S(2)}) copy-start(f32[4,12,2304]{2,0,1:T(4,128)} %param.3) | copy-start | bytes 1327108
  1.9 3.4 %collective-permute-start = (f32[24,1152]{1,0:T(8,128)S(1)}, f32[24,1152]{1,0:T(8,128)S(1)}, u32[]{:S(2)}, u32[]{:S(2)}) collective-permute-start(f32[24,1152]{1,0:T(8,128)S(1)} %get-tuple-element.28), channel_id=1, source_target_pairs={{0,1},{1,0},{2,3},{3,2},{4,5},{5,4},{6,7},{7,6},{8,9},{9,8},{10,11... | collective-permute-start | bytes 331784 | tf_op jit(solution)/shard_map/ppermute | solution.py:324
  2.4 6.5 %collective-permute-start.1 = (f32[24,1152]{1,0:T(8,128)S(1)}, f32[24,1152]{1,0:T(8,128)S(1)}, u32[]{:S(2)}, u32[]{:S(2)}) collective-permute-start(f32[24,1152]{1,0:T(8,128)S(1)} %get-tuple-element.29), channel_id=1, source_target_pairs={{0,2},{1,3},{2,0},{3,1},{4,6},{5,7},{6,4},{7,5},{8,10},{9,11},{10,... | collective-permute-start | bytes 331784 | tf_op jit(solution)/shard_map/ppermute | solution.py:324
  5.0 5.8 %collective-permute-start.2 = (f32[24,1152]{1,0:T(8,128)S(1)}, f32[24,1152]{1,0:T(8,128)S(1)}, u32[]{:S(2)}, u32[]{:S(2)}) collective-permute-start(f32[24,1152]{1,0:T(8,128)S(1)} %get-tuple-element.30), channel_id=1, source_target_pairs={{0,3},{1,2},{2,1},{3,0},{4,7},{5,6},{6,5},{7,4},{8,11},{9,10},{10,... | collective-permute-start | bytes 331784 | tf_op jit(solution)/shard_map/ppermute | solution.py:324
  5.0 10.2 %copy-start.6 = (s32[8,2]{0,1:T(2,128)S(1)}, s32[8,2]{0,1:T(2,128)}, u32[]{:S(2)}) copy-start(s32[8,2]{0,1:T(2,128)} %param.4) | copy-start | bytes 196
  5.0 10.4 %copy-start.9 = (s32[8,2]{0,1:T(2,128)S(1)}, s32[8,2]{0,1:T(2,128)}, u32[]{:S(2)}) copy-start(s32[8,2]{0,1:T(2,128)} %param.5) | copy-start | bytes 196
  5.3 16.0 %collective-permute-start.3 = (f32[24,2304]{1,0:T(8,128)S(1)}, f32[24,2304]{1,0:T(8,128)S(1)}, u32[]{:S(2)}, u32[]{:S(2)}) collective-permute-start(f32[24,2304]{1,0:T(8,128)S(1)} %assemble.2.refs_0_), channel_id=1, source_target_pairs={{0,8},{8,16},{16,24},{24,28},{28,20},{20,12},{12,4},{4,0},{1,9},{9... | collective-permute-start | bytes 663560 | tf_op jit(solution)/shard_map/ppermute | solution.py:343
  10.8 10.5 %collective-permute-start.4 = (f32[24,2304]{1,0:T(8,128)S(1)}, f32[24,2304]{1,0:T(8,128)S(1)}, u32[]{:S(2)}, u32[]{:S(2)}) collective-permute-start(f32[24,2304]{1,0:T(8,128)S(1)} %assemble.3.refs_1_), channel_id=1, source_target_pairs={{0,8},{8,16},{16,24},{24,28},{28,20},{20,12},{12,4},{4,0},{1,9},{9... | collective-permute-start | bytes 663560 | tf_op jit(solution)/shard_map/ppermute | solution.py:343
  12.4 9.6 %collective-permute-start.8 = (f32[24,2304]{1,0:T(8,128)S(1)}, f32[24,2304]{1,0:T(8,128)S(1)}, u32[]{:S(2)}, u32[]{:S(2)}) collective-permute-start(f32[24,2304]{1,0:T(8,128)S(1)} %assemble.2.refs_0_), channel_id=1, source_target_pairs={{0,4},{8,0},{16,8},{24,16},{28,24},{20,28},{12,20},{4,12},{1,5},{9... | collective-permute-start | bytes 663560 | tf_op jit(solution)/shard_map/ppermute | solution.py:343
  12.9 11.9 %collective-permute-start.9 = (f32[24,2304]{1,0:T(8,128)S(1)}, f32[24,2304]{1,0:T(8,128)S(1)}, u32[]{:S(2)}, u32[]{:S(2)}) collective-permute-start(f32[24,2304]{1,0:T(8,128)S(1)} %assemble.3.refs_1_), channel_id=1, source_target_pairs={{0,4},{8,0},{16,8},{24,16},{28,24},{20,28},{12,20},{4,12},{1,5},{9... | collective-permute-start | bytes 663560 | tf_op jit(solution)/shard_map/ppermute | solution.py:343
  14.4 2.9 %copy-start.7 = (f32[48]{0:T(128)}, f32[48]{0:T(128)S(1)}, u32[]{:S(2)}) copy-start(f32[48]{0:T(128)S(1)} %fusion.40) | copy-start | bytes 580
  17.4 1.3 %copy-start.8 = (f32[48]{0:T(128)S(1)}, f32[48]{0:T(128)}, u32[]{:S(2)}) copy-start(f32[48]{0:T(128)} %copy-done.7) | copy-start | bytes 580
  18.7 2.3 %copy-start.4 = (bf16[48,96]{1,0:T(8,128)(2,1)S(1)}, bf16[48,96]{1,0:T(8,128)(2,1)}, u32[]{:S(2)}) copy-start(bf16[48,96]{1,0:T(8,128)(2,1)} %get-tuple-element.60) | copy-start | bytes 27652
  18.8 2.3 %copy-start.5 = (bf16[48,96]{1,0:T(8,128)(2,1)S(1)}, bf16[48,96]{1,0:T(8,128)(2,1)}, u32[]{:S(2)}) copy-start(bf16[48,96]{1,0:T(8,128)(2,1)} %get-tuple-element.61) | copy-start | bytes 27652
  18.8 2.4 %copy-start.2 = (bf16[48,48]{1,0:T(8,128)(2,1)S(1)}, bf16[48,48]{1,0:T(8,128)(2,1)}, u32[]{:S(2)}) copy-start(bf16[48,48]{1,0:T(8,128)(2,1)} %get-tuple-element.56) | copy-start | bytes 13828
  18.8 2.4 %copy-start.3 = (bf16[48,48]{1,0:T(8,128)(2,1)S(1)}, bf16[48,48]{1,0:T(8,128)(2,1)}, u32[]{:S(2)}) copy-start(bf16[48,48]{1,0:T(8,128)(2,1)} %get-tuple-element.58) | copy-start | bytes 13828
  21.4 11.9 %collective-permute-start.5 = (f32[48,2304]{1,0:T(8,128)S(1)}, f32[48,2304]{1,0:T(8,128)S(1)}, u32[]{:S(2)}, u32[]{:S(2)}) collective-permute-start(f32[48,2304]{1,0:T(8,128)S(1)} %join.5.other_ref), channel_id=1, source_target_pairs={{0,8},{8,16},{16,24},{24,28},{28,20},{20,12},{12,4},{4,0},{1,9},{9... | collective-permute-start | bytes 1327112 | tf_op jit(solution)/shard_map/ppermute | solution.py:343
  24.9 11.6 %collective-permute-start.10 = (f32[48,2304]{1,0:T(8,128)S(1)}, f32[48,2304]{1,0:T(8,128)S(1)}, u32[]{:S(2)}, u32[]{:S(2)}) collective-permute-start(f32[48,2304]{1,0:T(8,128)S(1)} %join.6.other_ref), channel_id=1, source_target_pairs={{0,4},{8,0},{16,8},{24,16},{28,24},{20,28},{12,20},{4,12},{1,5},{9... | collective-permute-start | bytes 1327112 | tf_op jit(solution)/shard_map/ppermute | solution.py:343
  33.3 11.0 %collective-permute-start.6 = (f32[48,2304]{1,0:T(8,128)S(1)}, f32[48,2304]{1,0:T(8,128)S(1)}, u32[]{:S(2)}, u32[]{:S(2)}) collective-permute-start(f32[48,2304]{1,0:T(8,128)S(1)} %collective-permute-done.5.other_ref), channel_id=1, source_target_pairs={{0,8},{8,16},{16,24},{24,28},{28,20},{20,12},{12,4},{4,0},{1,9},{9... | collective-permute-start | bytes 1327112 | tf_op jit(solution)/shard_map/ppermute | solution.py:343
  36.5 10.7 %collective-permute-start.11 = (f32[48,2304]{1,0:T(8,128)S(1)}, f32[48,2304]{1,0:T(8,128)S(1)}, u32[]{:S(2)}, u32[]{:S(2)}) collective-permute-start(f32[48,2304]{1,0:T(8,128)S(1)} %collective-permute-done.10.other_ref), channel_id=1, source_target_pairs={{0,4},{8,0},{16,8},{24,16},{28,24},{20,28},{12,20},{4,12},{1,5},{9... | collective-permute-start | bytes 1327112 | tf_op jit(solution)/shard_map/ppermute | solution.py:343
  44.4 6.0 %collective-permute-start.7 = (f32[24,2304]{1,0:T(8,128)S(1)}, f32[24,2304]{1,0:T(8,128)S(1)}, u32[]{:S(2)}, u32[]{:S(2)}) collective-permute-start(f32[24,2304]{1,0:T(8,128)S(1)} %slice.31), channel_id=1, source_target_pairs={{0,8},{8,16},{16,24},{24,28},{28,20},{20,12},{12,4},{4,0},{1,9},{9... | collective-permute-start | bytes 663560 | tf_op jit(solution)/shard_map/ppermute | solution.py:343
  47.3 6.0 %collective-permute-start.12 = (f32[24,2304]{1,0:T(8,128)S(1)}, f32[24,2304]{1,0:T(8,128)S(1)}, u32[]{:S(2)}, u32[]{:S(2)}) collective-permute-start(f32[24,2304]{1,0:T(8,128)S(1)} %slice.32), channel_id=1, source_target_pairs={{0,4},{8,0},{16,8},{24,16},{28,24},{20,28},{12,20},{4,12},{1,5},{9... | collective-permute-start | bytes 663560 | tf_op jit(solution)/shard_map/ppermute | solution.py:343
  53.6 18.7 %copy-start.1 = (f32[4,12,2304]{2,0,1:T(4,128)S(1)}, f32[4,12,2304]{2,0,1:T(4,128)}, u32[]{:S(2)}) copy-start(f32[4,12,2304]{2,0,1:T(4,128)} %param.3) | copy-start | bytes 1327108
  53.8 18.4 %collective-permute-start.15 = (f32[48,1152]{1,0:T(8,128)S(1)}, f32[48,1152]{1,0:T(8,128)S(1)}, u32[]{:S(2)}, u32[]{:S(2)}) collective-permute-start(f32[48,1152]{1,0:T(8,128)S(1)} %get-tuple-element.50), channel_id=1, source_target_pairs={{0,3},{1,2},{2,1},{3,0},{4,7},{5,6},{6,5},{7,4},{8,11},{9,10},{10,... | collective-permute-start | bytes 663560 | tf_op jit(solution)/shard_map/ppermute | solution.py:324
  53.9 18.3 %collective-permute-start.14 = (f32[48,1152]{1,0:T(8,128)S(1)}, f32[48,1152]{1,0:T(8,128)S(1)}, u32[]{:S(2)}, u32[]{:S(2)}) collective-permute-start(f32[48,1152]{1,0:T(8,128)S(1)} %get-tuple-element.49), channel_id=1, source_target_pairs={{0,2},{1,3},{2,0},{3,1},{4,6},{5,7},{6,4},{7,5},{8,10},{9,11},{10,... | collective-permute-start | bytes 663560 | tf_op jit(solution)/shard_map/ppermute | solution.py:324
  55.5 16.7 %collective-permute-start.13 = (f32[48,1152]{1,0:T(8,128)S(1)}, f32[48,1152]{1,0:T(8,128)S(1)}, u32[]{:S(2)}, u32[]{:S(2)}) collective-permute-start(f32[48,1152]{1,0:T(8,128)S(1)} %get-tuple-element.48), channel_id=1, source_target_pairs={{0,1},{1,0},{2,3},{3,2},{4,5},{5,4},{6,7},{7,6},{8,9},{9,8},{10,11... | collective-permute-start | bytes 663560 | tf_op jit(solution)/shard_map/ppermute | solution.py:324

commit v5 on v4

--- a/solution.py
+++ b/solution.py
@@ -3,6 +3,8 @@
 
 import jax
 import jax.numpy as jnp
+import ml_dtypes
+import numpy as np
 from jax import lax
 from jax.experimental import pallas as pl
 from jax.experimental.pallas import tpu as pltpu
@@ -28,52 +30,50 @@
 
 
 def cas(rows, cols, length):
-    phase_angle = 2.0 * math.pi / length * (rows * cols % length).astype(jnp.float32)
-    return jnp.cos(phase_angle) + jnp.sin(phase_angle)
+    phase_angle = 2.0 * math.pi / length * (np.outer(rows, cols) % length)
+    return np.cos(phase_angle) + np.sin(phase_angle)
 
 
 def split_table(matrix):
-    high = lax.reduce_precision(matrix, 8, 7)
-    return high.astype(jnp.bfloat16), (matrix - high).astype(jnp.bfloat16)
+    high = matrix.astype(ml_dtypes.bfloat16)
+    return high, (matrix - high.astype(np.float64)).astype(ml_dtypes.bfloat16)
 
 
 def wide(matrix):
     high, low = split_table(matrix)
-    return jnp.concatenate([high, high, low], axis=1)
+    return np.concatenate([high, high, low], axis=1)
 
 
 def tall(matrix):
     high, low = split_table(matrix)
-    return jnp.concatenate([high, low], axis=0)
-
-
-def wavenumber_sq(position):
-    length = position.shape[0]
-    signed = jnp.where(position > length // 2, position - length, position).astype(jnp.float32)
-    wave_number = 2.0 * math.pi / length * signed
-    return wave_number * wave_number
-
-
-def transform_tables(count, held_x):
-    x_waves = count[:NX]
-    y_cells = count[:NY]
-    z_cells = count[:NZ]
-    z_waves = count[:NZP]
+    return np.concatenate([high, low], axis=0)
+
+
+def wavenumber_sq(length):
+    return (2.0 * np.pi * np.fft.fftfreq(length)) ** 2
+
+
+def transform_tables(slab_index, slabs):
+    x_waves, y_cells, z_cells, z_waves = (np.arange(count) for count in (NX, NY, NZ, NZP))
+    planes = NX // slabs
+    held_x = [(slab ^ (x_waves // planes)) * planes + x_waves % planes for slab in range(slabs)]
     total = (
-        wavenumber_sq(z_waves)[:, None, None]
-        + wavenumber_sq(x_waves)[None, :, None]
-        + wavenumber_sq(y_cells)[None, None, :]
+        wavenumber_sq(NZP)[:, None, None]
+        + wavenumber_sq(NX)[None, :, None]
+        + wavenumber_sq(NY)[None, None, :]
     )
     kernel_table = 4.0 * math.pi / (NX * NY * NZP) / (total + screening * screening)
-    y_matrix = cas(y_cells[:, None], y_cells[None, :], NY)
+    y_matrix = cas(y_cells, y_cells, NY)
+    forward = jnp.asarray(np.stack([wide(cas(x_waves, held, NX)) for held in held_x]))
+    backward = jnp.asarray(np.stack([wide(cas(held, x_waves, NX)) for held in held_x]))
     return (
-        wide(cas(x_waves[:, None], held_x[None, :], NX)),
-        wide(y_matrix),
-        tall(cas(z_waves[:, None], z_cells[None, :], NZP)),
-        kernel_table.reshape(NZP, NX * NY),
-        wide(cas(z_cells[:, None], z_waves[None, :], NZP)),
-        tall(y_matrix),
-        wide(cas(held_x[:, None], x_waves[None, :], NX)),
+        lax.dynamic_index_in_dim(forward, slab_index, 0, keepdims=False),
+        jnp.asarray(wide(y_matrix)),
+        jnp.asarray(tall(cas(z_waves, z_cells, NZP))),
+        jnp.asarray(kernel_table.reshape(NZP, NX * NY).astype(np.float32)),
+        jnp.asarray(wide(cas(z_cells, z_waves, NZP))),
+        jnp.asarray(tall(y_matrix)),
+        lax.dynamic_index_in_dim(backward, slab_index, 0, keepdims=False),
     )
 
 
@@ -365,7 +365,7 @@
     slabs = lax.axis_size("slab")
     band_index = lax.axis_index("band")
     slab_index = lax.axis_index("slab")
-    orb_group, planes, _ = orbitals.shape
+    orb_group, _, _ = orbitals.shape
     total_orbs = orb_group * bands
     assert orb_group == slabs
 
@@ -378,11 +378,8 @@
     others = gather_ring(halves, band_index, bands)
     force = clear((NX, NY * NZ))
 
-    count = jnp.arange(max(NX, NY, NZP), dtype=jnp.int32)
-    own, count, partners, counts = lax.optimization_barrier((own, count, partners, counts))
-    row = count[:NX]
-    held_x = (slab_index ^ (row // planes)) * planes + row % planes
-    tables = transform_tables(count, held_x)
+    own, partners, counts = lax.optimization_barrier((own, partners, counts))
+    tables = transform_tables(slab_index, slabs)
 
     groups = jnp.stack([group for _, group in others]).astype(jnp.int32)
     active = (slab_index < counts).astype(jnp.float32)

time: 74.9 us -> 74.5 us (level)
  other arithmetic: 6.09 us -> 1.5 us
  starting transfers between devices: 12.8 us -> 15.6 us
  waiting for transfers between devices: 25.4 us -> 26.9 us
    ppermute x10, starting transfers between devices: 7.69 us -> 10.4 us  [shift(): return lax.ppermute(value, 'band', moves)]
    convert_element_type x4 -> x0, other arithmetic: 2.07 us -> none  [the longest x3 1.99 us: split_table(): return (high.astype(jnp.bfloat16), (matrix - high).astype(jnp.bfloat16))]
    add x4 -> x0, local copies, waits for them, and re-layouts: 1.44 us -> none  [transform_tables(): wavenumber_sq(z_waves)[:, None, None]]
    div x1 -> x0, other arithmetic: 1.29 us -> none  [transform_tables(): 4.0 * math.pi / (NX * NY * NZP) / (total + screening * screening)]
    ppermute x6, waiting for transfers between devices: 3.63 us -> 4.76 us  [slab_swap(): return lax.ppermute(value, 'slab', [(i, i ^ reach) for i in range(size)])]
    concatenate x5 -> x0, other arithmetic: 1.07 us -> none  [the longest x3 1.05 us: wide(): return jnp.concatenate([high, high, low], axis=1)]
    squeeze x0 -> x1, local copies, waits for them, and re-layouts: none -> 0.77 us  [transform_tables(): lax.dynamic_index_in_dim(backward, slab_index, 0, keepdims=False)]
    unnamed x20 -> x18, local copies, waits for them, and re-layouts: 1.05 us -> 1.61 us
  transfers between devices with their start and end apart: 16 -> 16, of which waited for: 9 -> 8; matrix products, arithmetic and copies ran while one was open for 10% -> 3% of each run, Pallas kernels for 10% -> 10%
where the time goes in v5:
time: 74.5 us; the launch traced here: 74.3 us
  waiting for transfers between devices  26.9 us (36%)
  starting transfers between devices  15.6 us (21%)
  blocking collectives  15.5 us (21%)
  Pallas kernels  9.32 us (13%)
  local copies, waits for them, and re-layouts  2.75 us (4%)
  between operations  2.74 us (4%)
  other arithmetic  1.5 us (2%)
    ppermute x10, waiting for transfers between devices, shift(): return lax.ppermute(value, 'band', moves)  22.2 us
    all_to_all x1, blocking collectives, share(): return lax.all_to_all(sent, ('band', 'slab'), 0, 0)  15.5 us
    ppermute x10, starting transfers between devices, shift(): return lax.ppermute(value, 'band', moves)  10.4 us
    pallas_call x7, Pallas kernels, pair_step(): pl.pallas_call(functools.partial(pair_kernel, slot), out_shape=outs, in_s...  7.82 us
    ppermute x6, starting transfers between devices, slab_swap(): return lax.ppermute(value, 'slab', [(i, i ^ reach) for i in range(size)])  5.12 us
    ppermute x6, waiting for transfers between devices, slab_swap(): return lax.ppermute(value, 'slab', [(i, i ^ reach) for i in range(size)])  4.76 us
    unnamed x18, local copies, waits for them, and re-layouts  1.61 us
  transfers between devices with their start and end apart: 16, of which 8 were waited for; matrix products, arithmetic and copies ran while one was open for 3% of the time, Pallas kernels for 10%

profile of v5, /device:TPU:0, one launch (start us, length us, event | category | flops | bytes accessed | tf_op | source)
XLA Modules:
  0.0 74.3 jit_solution(7848821805738715845)
XLA Ops:
  0.6 1.0 %copy-done = f32[4,12,2304]{2,0,1:T(4,128)S(1)} copy-done((f32[4,12,2304]{2,0,1:T(4,128)S(1)}, f32[4,12,2304]{2,0,1:T(4,128)}, u32[]{:S(2)}) %copy-start) | copy-done | bytes 442392
  1.7 0.2 prepare.1
  1.9 0.6 collective-permute-start
  2.4 2.6 %collective-permute-start.1 = (f32[24,1152]{1,0:T(8,128)S(1)}, f32[24,1152]{1,0:T(8,128)S(1)}, u32[]{:S(2)}, u32[]{:S(2)}) collective-permute-start(f32[24,1152]{1,0:T(8,128)S(1)} %get-tuple-element.28), channel_id=1, source_target_pairs={{0,2},{1,3},{2,0},{3,1},{4,6},{5,7},{6,4},{7,5},{8,10},{9,11},{10,... | collective-permute-start | bytes 331784 | tf_op jit(solution)/shard_map/ppermute | solution.py:324
  5.1 0.8 %dynamic-slice_bitcast_fusion = (bf16[48,144]{1,0:T(8,128)(2,1)S(1)}, bf16[48,144]{1,0:T(8,128)(2,1)S(1)}) fusion(bf16[4,48,144]{2,1,0:T(8,128)(2,1)} %constant.116.clone, s32[]{:T(128)S(6)} %select_n.110, bf16[4,48,144]{2,1,0:T(8,128)(2,1)} %constant.115.clone), kind=kLoop, calls=%fused_computation.7 | loop fusion | bytes 55300 | tf_op jit(solution)/shard_map/jit(dynamic_index_in_dim)/squeeze | solution.py:76
  6.0 2.9 %collective-permute-done.1.refs_0_ = f32[24,1152]{1,0:T(8,128)S(1)} collective-permute-done((f32[24,1152]{1,0:T(8,128)S(1)}, f32[24,1152]{1,0:T(8,128)S(1)}, u32[]{:S(2)}, u32[]{:S(2)}) %collective-permute-start.1) | collective-permute-done | bytes 110624 | tf_op jit(solution)/shard_map/ppermute | solution.py:324
  8.9 1.8 %collective-permute-done.2.refs_1_ = f32[24,1152]{1,0:T(8,128)S(1)} collective-permute-done((f32[24,1152]{1,0:T(8,128)S(1)}, f32[24,1152]{1,0:T(8,128)S(1)}, u32[]{:S(2)}, u32[]{:S(2)}) %collective-permute-start.2) | collective-permute-done | bytes 110624 | tf_op jit(solution)/shard_map/ppermute | solution.py:324
  10.8 1.5 %collective-permute-start.9 = (f32[24,2304]{1,0:T(8,128)S(1)}, f32[24,2304]{1,0:T(8,128)S(1)}, u32[]{:S(2)}, u32[]{:S(2)}) collective-permute-start(f32[24,2304]{1,0:T(8,128)S(1)} %assemble.3.refs_1_), channel_id=1, source_target_pairs={{0,4},{8,0},{16,8},{24,16},{28,24},{20,28},{12,20},{4,12},{1,5},{9... | collective-permute-start | bytes 663560 | tf_op jit(solution)/shard_map/ppermute | solution.py:343
  12.3 0.6 collective-permute-start.4
  12.9 1.5 %collective-permute-start.8 = (f32[24,2304]{1,0:T(8,128)S(1)}, f32[24,2304]{1,0:T(8,128)S(1)}, u32[]{:S(2)}, u32[]{:S(2)}) collective-permute-start(f32[24,2304]{1,0:T(8,128)S(1)} %assemble.2.refs_0_), channel_id=1, source_target_pairs={{0,4},{8,0},{16,8},{24,16},{28,24},{20,28},{12,20},{4,12},{1,5},{9... | collective-permute-start | bytes 663560 | tf_op jit(solution)/shard_map/ppermute | solution.py:343
  14.4 0.6 collective-permute-start.3
  15.2 0.6 copy-done.8
  16.3 4.3 %collective-permute-done.4.refs_1_ = f32[24,2304]{1,0:T(8,128)S(1)} collective-permute-done((f32[24,2304]{1,0:T(8,128)S(1)}, f32[24,2304]{1,0:T(8,128)S(1)}, u32[]{:S(2)}, u32[]{:S(2)}) %collective-permute-start.4) | collective-permute-done | bytes 221216 | tf_op jit(solution)/shard_map/ppermute | solution.py:343
  20.6 3.9 %collective-permute-done.3.refs_0_ = f32[24,2304]{1,0:T(8,128)S(1)} collective-permute-done((f32[24,2304]{1,0:T(8,128)S(1)}, f32[24,2304]{1,0:T(8,128)S(1)}, u32[]{:S(2)}, u32[]{:S(2)}) %collective-permute-start.3) | collective-permute-done | bytes 221216 | tf_op jit(solution)/shard_map/ppermute | solution.py:343
  24.5 0.5 collective-permute-start.5
  25.0 1.6 %collective-permute-start.10 = (f32[48,2304]{1,0:T(8,128)S(1)}, f32[48,2304]{1,0:T(8,128)S(1)}, u32[]{:S(2)}, u32[]{:S(2)}) collective-permute-start(f32[48,2304]{1,0:T(8,128)S(1)} %join.6.other_ref), channel_id=1, source_target_pairs={{0,4},{8,0},{16,8},{24,16},{28,24},{20,28},{12,20},{4,12},{1,5},{9... | collective-permute-start | bytes 1327112 | tf_op jit(solution)/shard_map/ppermute | solution.py:343
  26.9 3.5 %pair_step.8 = (f32[1,128]{1,0:T(1,128)S(1)}, f32[48,2304]{1,0:T(8,128)S(1)}) custom-call(f32[14,128]{1,0:T(8,128)S(1)} %broadcast_in_dim.81.weights, f32[48,2304]{1,0:T(8,128)S(1)} %join.4.own_ref, f32[48,2304]{1,0:T(8,128)S(1)} %join.6.other_ref, bf16[48,144]{1,0:T(8,128)(2,1)S(1)} %get-tuple-element.53.x_fwd, ...), custom_call_target="tpu_custom_call", output_to_operand_aliasing={{1}: (10, {})} | custom-call | flops 3221225472 | bytes 3145728 | tf_op jit(solution)/shard_map/pair_step/pallas_call | solution.py:178
  30.4 5.5 %collective-permute-done.5.other_ref = f32[48,2304]{1,0:T(8,128)S(1)} collective-permute-done((f32[48,2304]{1,0:T(8,128)S(1)}, f32[48,2304]{1,0:T(8,128)S(1)}, u32[]{:S(2)}, u32[]{:S(2)}) %collective-permute-start.5) | collective-permute-done | bytes 442400 | tf_op jit(solution)/shard_map/ppermute | solution.py:343
  35.9 0.3 collective-permute-start.6
  36.2 1.7 %collective-permute-start.11 = (f32[48,2304]{1,0:T(8,128)S(1)}, f32[48,2304]{1,0:T(8,128)S(1)}, u32[]{:S(2)}, u32[]{:S(2)}) collective-permute-start(f32[48,2304]{1,0:T(8,128)S(1)} %collective-permute-done.10.other_ref), channel_id=1, source_target_pairs={{0,4},{8,0},{16,8},{24,16},{28,24},{20,28},{12,20},{4,12},{1,5},{9... | collective-permute-start | bytes 1327112 | tf_op jit(solution)/shard_map/ppermute | solution.py:343
  38.0 3.6 %pair_step.10 = (f32[1,128]{1,0:T(1,128)S(1)}, f32[48,2304]{1,0:T(8,128)S(1)}) custom-call(f32[14,128]{1,0:T(8,128)S(1)} %broadcast_in_dim.81.weights, f32[48,2304]{1,0:T(8,128)S(1)} %join.4.own_ref, f32[48,2304]{1,0:T(8,128)S(1)} %collective-permute-done.10.other_ref, ...), custom_call_target="tpu_custom_call", output_to_operand_aliasing={{1}: (10, {})} | custom-call | flops 3221225472 | bytes 3145728 | tf_op jit(solution)/shard_map/pair_step/pallas_call | solution.py:178
  41.7 4.6 %collective-permute-done.6.other_ref = f32[48,2304]{1,0:T(8,128)S(1)} collective-permute-done((f32[48,2304]{1,0:T(8,128)S(1)}, f32[48,2304]{1,0:T(8,128)S(1)}, u32[]{:S(2)}, u32[]{:S(2)}) %collective-permute-start.6) | collective-permute-done | bytes 442400 | tf_op jit(solution)/shard_map/ppermute | solution.py:343
  46.3 0.3 collective-permute-start.7
  46.7 1.8 %collective-permute-start.12 = (f32[24,2304]{1,0:T(8,128)S(1)}, f32[24,2304]{1,0:T(8,128)S(1)}, u32[]{:S(2)}, u32[]{:S(2)}) collective-permute-start(f32[24,2304]{1,0:T(8,128)S(1)} %slice.25), channel_id=1, source_target_pairs={{0,4},{8,0},{16,8},{24,16},{28,24},{20,28},{12,20},{4,12},{1,5},{9... | collective-permute-start | bytes 663560 | tf_op jit(solution)/shard_map/ppermute | solution.py:343
  48.8 3.6 %collective-permute-done.7.refs_0_ = f32[24,2304]{1,0:T(8,128)S(1)} collective-permute-done((f32[24,2304]{1,0:T(8,128)S(1)}, f32[24,2304]{1,0:T(8,128)S(1)}, u32[]{:S(2)}, u32[]{:S(2)}) %collective-permute-start.7) | collective-permute-done | bytes 221216 | tf_op jit(solution)/shard_map/ppermute | solution.py:343
  52.3 0.4 collective-permute-done.12.refs_1_
  52.7 0.3 multiply_add_fusion.refs_0_
  53.0 0.2 pair_step.13
  53.3 1.8 %collective-permute-start.14 = (f32[48,1152]{1,0:T(8,128)S(1)}, f32[48,1152]{1,0:T(8,128)S(1)}, u32[]{:S(2)}, u32[]{:S(2)}) collective-permute-start(f32[48,1152]{1,0:T(8,128)S(1)} %get-tuple-element.47), channel_id=1, source_target_pairs={{0,2},{1,3},{2,0},{3,1},{4,6},{5,7},{6,4},{7,5},{8,10},{9,11},{10,... | collective-permute-start | bytes 663560 | tf_op jit(solution)/shard_map/ppermute | solution.py:324
  55.2 15.5 %all_to_all.5 = f32[32,1,128]{2,1,0:T(1,128)S(1)} all-to-all(f32[32,1,128]{2,1,0:T(1,128)S(1)} %broadcast_in_dim.84), channel_id=1, replica_groups=mesh['band'=8,'slab'=4] {'band','slab'}, dimensions={0} | all-to-all | bytes 32768 | tf_op jit(solution)/shard_map/all_to_all | solution.py:329
  70.6 0.6 reduce_sum.65
  72.0 1.1 %finish.1 = f32[12,4,2304]{2,1,0:T(4,128)} custom-call(s32[1]{0:T(128)} %bitcast.place, f32[12,4,2304]{2,1,0:T(4,128)S(1)} %bitcast.21, f32[24,1152]{1,0:T(8,128)S(1)} %fusion.2.local_pot, f32[48,1152]{1,0:T(8,128)S(1)} %get-tuple-element.45.refs_0_, f32[48,1152]{1,0:T(8,128)S(1)} %collective-permute-done.13.refs_1_, ...), custom_call_target="tpu_custom_call" | custom-call | tf_op jit(solution)/shard_map/finish/pallas_call | solution.py:312
  (54 shorter events, 1.9 us)
Async XLA Ops:
  0.6 1.0 %copy-start = (f32[4,12,2304]{2,0,1:T(4,128)S(1)}, f32[4,12,2304]{2,0,1:T(4,128)}, u32[]{:S(2)}) copy-start(f32[4,12,2304]{2,0,1:T(4,128)} %param.10) | copy-start | bytes 1327108
  1.9 11.0 %collective-permute-start = (f32[24,1152]{1,0:T(8,128)S(1)}, f32[24,1152]{1,0:T(8,128)S(1)}, u32[]{:S(2)}, u32[]{:S(2)}) collective-permute-start(f32[24,1152]{1,0:T(8,128)S(1)} %get-tuple-element.27), channel_id=1, source_target_pairs={{0,1},{1,0},{2,3},{3,2},{4,5},{5,4},{6,7},{7,6},{8,9},{9,8},{10,11... | collective-permute-start | bytes 331784 | tf_op jit(solution)/shard_map/ppermute | solution.py:324
  2.4 6.5 %collective-permute-start.1 = (f32[24,1152]{1,0:T(8,128)S(1)}, f32[24,1152]{1,0:T(8,128)S(1)}, u32[]{:S(2)}, u32[]{:S(2)}) collective-permute-start(f32[24,1152]{1,0:T(8,128)S(1)} %get-tuple-element.28), channel_id=1, source_target_pairs={{0,2},{1,3},{2,0},{3,1},{4,6},{5,7},{6,4},{7,5},{8,10},{9,11},{10,... | collective-permute-start | bytes 331784 | tf_op jit(solution)/shard_map/ppermute | solution.py:324
  5.0 5.8 %collective-permute-start.2 = (f32[24,1152]{1,0:T(8,128)S(1)}, f32[24,1152]{1,0:T(8,128)S(1)}, u32[]{:S(2)}, u32[]{:S(2)}) collective-permute-start(f32[24,1152]{1,0:T(8,128)S(1)} %get-tuple-element.29), channel_id=1, source_target_pairs={{0,3},{1,2},{2,1},{3,0},{4,7},{5,6},{6,5},{7,4},{8,11},{9,10},{10,... | collective-permute-start | bytes 331784 | tf_op jit(solution)/shard_map/ppermute | solution.py:324
  10.8 14.2 %collective-permute-start.9 = (f32[24,2304]{1,0:T(8,128)S(1)}, f32[24,2304]{1,0:T(8,128)S(1)}, u32[]{:S(2)}, u32[]{:S(2)}) collective-permute-start(f32[24,2304]{1,0:T(8,128)S(1)} %assemble.3.refs_1_), channel_id=1, source_target_pairs={{0,4},{8,0},{16,8},{24,16},{28,24},{20,28},{12,20},{4,12},{1,5},{9... | collective-permute-start | bytes 663560 | tf_op jit(solution)/shard_map/ppermute | solution.py:343
  12.3 8.3 %collective-permute-start.4 = (f32[24,2304]{1,0:T(8,128)S(1)}, f32[24,2304]{1,0:T(8,128)S(1)}, u32[]{:S(2)}, u32[]{:S(2)}) collective-permute-start(f32[24,2304]{1,0:T(8,128)S(1)} %assemble.3.refs_1_), channel_id=1, source_target_pairs={{0,8},{8,16},{16,24},{24,28},{28,20},{20,12},{12,4},{4,0},{1,9},{9... | collective-permute-start | bytes 663560 | tf_op jit(solution)/shard_map/ppermute | solution.py:343
  12.9 2.1 %copy-start.7 = (s32[8,2]{0,1:T(2,128)S(1)}, s32[8,2]{0,1:T(2,128)}, u32[]{:S(2)}) copy-start(s32[8,2]{0,1:T(2,128)} %param.11) | copy-start | bytes 196
  12.9 12.1 %collective-permute-start.8 = (f32[24,2304]{1,0:T(8,128)S(1)}, f32[24,2304]{1,0:T(8,128)S(1)}, u32[]{:S(2)}, u32[]{:S(2)}) collective-permute-start(f32[24,2304]{1,0:T(8,128)S(1)} %assemble.2.refs_0_), channel_id=1, source_target_pairs={{0,4},{8,0},{16,8},{24,16},{28,24},{20,28},{12,20},{4,12},{1,5},{9... | collective-permute-start | bytes 663560 | tf_op jit(solution)/shard_map/ppermute | solution.py:343
  14.4 10.0 %collective-permute-start.3 = (f32[24,2304]{1,0:T(8,128)S(1)}, f32[24,2304]{1,0:T(8,128)S(1)}, u32[]{:S(2)}, u32[]{:S(2)}) collective-permute-start(f32[24,2304]{1,0:T(8,128)S(1)} %assemble.2.refs_0_), channel_id=1, source_target_pairs={{0,8},{8,16},{16,24},{24,28},{28,20},{20,12},{12,4},{4,0},{1,9},{9... | collective-permute-start | bytes 663560 | tf_op jit(solution)/shard_map/ppermute | solution.py:343
  15.0 0.7 copy-start.8
  16.3 10.5 %copy-start.2 = (f32[96,2304]{1,0:T(8,128)S(1)}, f32[96,2304]{1,0:T(8,128)}, u32[]{:S(2)}) copy-start(f32[96,2304]{1,0:T(8,128)} %constant.119.clone.table) | copy-start | bytes 2654212
  24.5 2.3 %copy-start.3 = (bf16[192,48]{1,0:T(8,128)(2,1)S(1)}, bf16[192,48]{1,0:T(8,128)(2,1)}, u32[]{:S(2)}) copy-start(bf16[192,48]{1,0:T(8,128)(2,1)} %constant.118.clone.z_fwd) | copy-start | bytes 55300
  24.5 2.3 %copy-start.4 = (bf16[48,288]{1,0:T(8,128)(2,1)S(1)}, bf16[48,288]{1,0:T(8,128)(2,1)}, u32[]{:S(2)}) copy-start(bf16[48,288]{1,0:T(8,128)(2,1)} %constant.120.clone.z_inv) | copy-start | bytes 82948
  24.5 2.3 %copy-start.5 = (bf16[96,48]{1,0:T(8,128)(2,1)S(1)}, bf16[96,48]{1,0:T(8,128)(2,1)}, u32[]{:S(2)}) copy-start(bf16[96,48]{1,0:T(8,128)(2,1)} %constant.121.clone.y_inv) | copy-start | bytes 27652
  24.5 2.3 %copy-start.6 = (bf16[48,144]{1,0:T(8,128)(2,1)S(1)}, bf16[48,144]{1,0:T(8,128)(2,1)}, u32[]{:S(2)}) copy-start(bf16[48,144]{1,0:T(8,128)(2,1)} %constant.117.clone.y_fwd) | copy-start | bytes 41476
  24.5 11.4 %collective-permute-start.5 = (f32[48,2304]{1,0:T(8,128)S(1)}, f32[48,2304]{1,0:T(8,128)S(1)}, u32[]{:S(2)}, u32[]{:S(2)}) collective-permute-start(f32[48,2304]{1,0:T(8,128)S(1)} %join.5.other_ref), channel_id=1, source_target_pairs={{0,8},{8,16},{16,24},{24,28},{28,20},{20,12},{12,4},{4,0},{1,9},{9... | collective-permute-start | bytes 1327112 | tf_op jit(solution)/shard_map/ppermute | solution.py:343
  25.0 11.1 %collective-permute-start.10 = (f32[48,2304]{1,0:T(8,128)S(1)}, f32[48,2304]{1,0:T(8,128)S(1)}, u32[]{:S(2)}, u32[]{:S(2)}) collective-permute-start(f32[48,2304]{1,0:T(8,128)S(1)} %join.6.other_ref), channel_id=1, source_target_pairs={{0,4},{8,0},{16,8},{24,16},{28,24},{20,28},{12,20},{4,12},{1,5},{9... | collective-permute-start | bytes 1327112 | tf_op jit(solution)/shard_map/ppermute | solution.py:343
  35.9 10.4 %collective-permute-start.6 = (f32[48,2304]{1,0:T(8,128)S(1)}, f32[48,2304]{1,0:T(8,128)S(1)}, u32[]{:S(2)}, u32[]{:S(2)}) collective-permute-start(f32[48,2304]{1,0:T(8,128)S(1)} %collective-permute-done.5.other_ref), channel_id=1, source_target_pairs={{0,8},{8,16},{16,24},{24,28},{28,20},{20,12},{12,4},{4,0},{1,9},{9... | collective-permute-start | bytes 1327112 | tf_op jit(solution)/shard_map/ppermute | solution.py:343
  36.2 10.5 %collective-permute-start.11 = (f32[48,2304]{1,0:T(8,128)S(1)}, f32[48,2304]{1,0:T(8,128)S(1)}, u32[]{:S(2)}, u32[]{:S(2)}) collective-permute-start(f32[48,2304]{1,0:T(8,128)S(1)} %collective-permute-done.10.other_ref), channel_id=1, source_target_pairs={{0,4},{8,0},{16,8},{24,16},{28,24},{20,28},{12,20},{4,12},{1,5},{9... | collective-permute-start | bytes 1327112 | tf_op jit(solution)/shard_map/ppermute | solution.py:343
  46.3 6.0 %collective-permute-start.7 = (f32[24,2304]{1,0:T(8,128)S(1)}, f32[24,2304]{1,0:T(8,128)S(1)}, u32[]{:S(2)}, u32[]{:S(2)}) collective-permute-start(f32[24,2304]{1,0:T(8,128)S(1)} %slice.24), channel_id=1, source_target_pairs={{0,8},{8,16},{16,24},{24,28},{28,20},{20,12},{12,4},{4,0},{1,9},{9... | collective-permute-start | bytes 663560 | tf_op jit(solution)/shard_map/ppermute | solution.py:343
  46.7 6.0 %collective-permute-start.12 = (f32[24,2304]{1,0:T(8,128)S(1)}, f32[24,2304]{1,0:T(8,128)S(1)}, u32[]{:S(2)}, u32[]{:S(2)}) collective-permute-start(f32[24,2304]{1,0:T(8,128)S(1)} %slice.25), channel_id=1, source_target_pairs={{0,4},{8,0},{16,8},{24,16},{28,24},{20,28},{12,20},{4,12},{1,5},{9... | collective-permute-start | bytes 663560 | tf_op jit(solution)/shard_map/ppermute | solution.py:343
  53.2 18.8 %copy-start.1 = (f32[4,12,2304]{2,0,1:T(4,128)S(1)}, f32[4,12,2304]{2,0,1:T(4,128)}, u32[]{:S(2)}) copy-start(f32[4,12,2304]{2,0,1:T(4,128)} %param.10) | copy-start | bytes 1327108
  53.2 18.7 %collective-permute-start.13 = (f32[48,1152]{1,0:T(8,128)S(1)}, f32[48,1152]{1,0:T(8,128)S(1)}, u32[]{:S(2)}, u32[]{:S(2)}) collective-permute-start(f32[48,1152]{1,0:T(8,128)S(1)} %get-tuple-element.46), channel_id=1, source_target_pairs={{0,1},{1,0},{2,3},{3,2},{4,5},{5,4},{6,7},{7,6},{8,9},{9,8},{10,11... | collective-permute-start | bytes 663560 | tf_op jit(solution)/shard_map/ppermute | solution.py:324
  53.3 18.6 %collective-permute-start.14 = (f32[48,1152]{1,0:T(8,128)S(1)}, f32[48,1152]{1,0:T(8,128)S(1)}, u32[]{:S(2)}, u32[]{:S(2)}) collective-permute-start(f32[48,1152]{1,0:T(8,128)S(1)} %get-tuple-element.47), channel_id=1, source_target_pairs={{0,2},{1,3},{2,0},{3,1},{4,6},{5,7},{6,4},{7,5},{8,10},{9,11},{10,... | collective-permute-start | bytes 663560 | tf_op jit(solution)/shard_map/ppermute | solution.py:324
  55.1 16.8 %collective-permute-start.15 = (f32[48,1152]{1,0:T(8,128)S(1)}, f32[48,1152]{1,0:T(8,128)S(1)}, u32[]{:S(2)}, u32[]{:S(2)}) collective-permute-start(f32[48,1152]{1,0:T(8,128)S(1)} %get-tuple-element.48), channel_id=1, source_target_pairs={{0,3},{1,2},{2,1},{3,0},{4,7},{5,6},{6,5},{7,4},{8,11},{9,10},{10,... | collective-permute-start | bytes 663560 | tf_op jit(solution)/shard_map/ppermute | solution.py:324

commit v6 on v5

--- a/solution.py
+++ b/solution.py
@@ -90,14 +90,13 @@
     return both[:half] + both[half:] + rest
 
 
-def cut_into(refs, value, part_index):
+def cut_into(refs, value):
     planes = NX // len(refs)
     part = refs[0].shape[1]
     fold = NY * NZ // part
-    first = part_index * planes * fold
     for r, ref in enumerate(refs):
         for f in range(fold):
-            ref[first + f * planes : first + (f + 1) * planes, :] = value[
+            ref[f * planes : (f + 1) * planes, :] = value[
                 r * planes : (r + 1) * planes, f * part : (f + 1) * part
             ]
 
@@ -106,19 +105,14 @@
     if len(force_refs) == 1:
         force_refs[0][...] = value
     else:
-        cut_into(force_refs, value, 0)
+        cut_into(force_refs, value)
 
 
 def pair_kernel(
     slot, weights, own_ref, other_ref, x_fwd, y_fwd, z_fwd, table, z_inv, y_inv, x_inv,
     force_in, energy_in, *refs,
 ):
-    *refs, lines, high_rows, low_rows, field = refs
-    if len(refs) == 2:
-        energy_out, *force_refs = refs
-    else:
-        squares_in, energy_out, *force_refs = refs
-        cut_into(force_refs, squares_in[...], 1)
+    energy_out, *force_refs, lines, high_rows, low_rows, field = refs
     total_weight = jnp.max(weights[2 * slot : 2 * slot + 1, :])
     request_weight = weights[2 * slot + 1 : 2 * slot + 2, :]
 
@@ -164,21 +158,19 @@
         )
 
 
-def pair_step(slot, weights, own, other, tables, force, energy, pieces=1, squares=None):
-    if pieces == 1:
-        piece = force.shape
-        extra = ()
-    else:
-        planes = NX // pieces
-        fold = fold_of(planes, NY * NZ)
-        piece = (2 * planes * fold, NY * NZ // fold)
-        extra = (squares,)
+def piece_shape(planes):
+    fold = fold_of(planes, NY * NZ)
+    return (planes * fold, NY * NZ // fold)
+
+
+def pair_step(slot, weights, own, other, tables, force, energy, pieces=1):
+    piece = force.shape if pieces == 1 else piece_shape(NX // pieces)
     outs = [jax.ShapeDtypeStruct(energy.shape, jnp.float32)]
     outs += [jax.ShapeDtypeStruct(piece, jnp.float32)] * pieces
     return pl.pallas_call(
         functools.partial(pair_kernel, slot),
         out_shape=outs,
-        in_specs=in_vmem(5 + len(tables) + len(extra)),
+        in_specs=in_vmem(5 + len(tables)),
         out_specs=in_vmem(1 + pieces),
         scratch_shapes=[
             pltpu.VMEM((NX * NY, NZ), jnp.float32),
@@ -190,7 +182,7 @@
         compiler_params=pltpu.CompilerParams(vmem_limit_bytes=32 << 20),
         cost_estimate=pl.CostEstimate(flops=3 << 30, transcendentals=0, bytes_accessed=3 << 20),
         name="pair_step",
-    )(weights, own, other, *tables, force, energy, *extra)
+    )(weights, own, other, *tables, force, energy)
 
 
 def fold_of(planes, cells):
@@ -272,6 +264,46 @@
         compiler_params=pltpu.CompilerParams(vmem_limit_bytes=8 << 20),
         name="clear",
     )()
+
+
+def squares_kernel(*refs):
+    *blocks, even_ref, odd_ref = refs
+    slabs = 2 * even_ref.shape[0]
+    squares = blocks[0][...] * blocks[0][...]
+    for ref in blocks[1:]:
+        squares = squares + ref[...] * ref[...]
+    pieces = [ref.at[k] for k in range(slabs // 2) for ref in (even_ref, odd_ref)]
+    cut_into(pieces, squares)
+
+
+def squares_of(blocks, slabs):
+    stack = jax.ShapeDtypeStruct((slabs // 2,) + piece_shape(NX // slabs), jnp.float32)
+    return pl.pallas_call(
+        squares_kernel,
+        out_shape=[stack, stack],
+        in_specs=in_vmem(len(blocks)),
+        out_specs=in_vmem(2),
+        compiler_params=pltpu.CompilerParams(vmem_limit_bytes=8 << 20),
+        name="squares",
+    )(*blocks)
+
+
+def pack_kernel(k, piece, mine, theirs, out_ref):
+    rows = piece.shape[0]
+    out_ref[:rows, :] = piece[...]
+    out_ref[rows:, :] = mine[k] + theirs[k]
+
+
+def pack(k, piece, mine, theirs):
+    rows, part = piece.shape
+    return pl.pallas_call(
+        functools.partial(pack_kernel, k),
+        out_shape=jax.ShapeDtypeStruct((2 * rows, part), jnp.float32),
+        in_specs=in_vmem(3),
+        out_specs=in_vmem(1)[0],
+        compiler_params=pltpu.CompilerParams(vmem_limit_bytes=8 << 20),
+        name="pack",
+    )(piece, mine, theirs)
 
 
 def join_kernel(*refs):
@@ -396,21 +428,21 @@
     weights = jnp.broadcast_to(weights[:, None], weights.shape + (128,))
 
     energy = jnp.zeros((1, 128), jnp.float32)
-    squares = own * own
-    for other, _ in others:
-        squares = squares + other * other
+    even, odd = squares_of([own] + [other for other, _ in others], slabs)
+    from_core = slab_swap(odd, 1)
     for slot, (other, _) in enumerate(others):
         if slot < len(others) - 1:
             energy, force = pair_step(slot, weights, own, other, tables, force, energy)
         else:
-            energy, *outgoing = pair_step(
-                slot, weights, own, other, tables, force, energy, slabs, squares
-            )
-
+            energy, *outgoing = pair_step(slot, weights, own, other, tables, force, energy, slabs)
+
+    for r in range(2, slabs, 2):
+        outgoing[r] = pack(r // 2, outgoing[r], even, from_core)
     arrived = [outgoing[0]] + [slab_swap(outgoing[r], r) for r in range(1, slabs)]
     shared = share(energy, bands * slabs)
-    rows = arrived[0].shape[0] // 2
-    density = 2.0 / total_orbs * sum(piece[rows:] for piece in arrived)
+    rows = arrived[0].shape[0]
+    squares = even[0] + from_core[0] + sum(arrived[r][rows:] for r in range(2, slabs, 2))
+    density = 2.0 / total_orbs * squares
     local_pot = slater_coeff * jnp.cbrt(density)
     forces = finish(place, by_plane, local_pot, arrived)
     energy_total = jnp.sum(shared)

time: 74.5 us -> 74.1 us (level)
  blocking collectives: 15.5 us -> 0 us
  starting transfers between devices: 15.6 us -> 23.5 us
  waiting for transfers between devices: 26.9 us -> 33.3 us
    all_to_all x1 -> x0, blocking collectives: 15.5 us -> none  [share(): return lax.all_to_all(sent, ('band', 'slab'), 0, 0)]
    all_to_all x0 -> x1, starting transfers between devices: none -> 6.02 us  [share(): return lax.all_to_all(sent, ('band', 'slab'), 0, 0)]
    all_to_all x0 -> x1, waiting for transfers between devices: none -> 5.15 us  [share(): return lax.all_to_all(sent, ('band', 'slab'), 0, 0)]
    ppermute x6 -> x7, starting transfers between devices: 5.12 us -> 7.03 us  [slab_swap(): return lax.ppermute(value, 'slab', [(i, i ^ reach) for i in range(size)])]
    ppermute x6 -> x7, waiting for transfers between devices: 4.76 us -> 6.05 us  [slab_swap(): return lax.ppermute(value, 'slab', [(i, i ^ reach) for i in range(size)])]
  transfers between devices with their start and end apart: 16 -> 18, of which waited for: 8 -> 10; matrix products, arithmetic and copies ran while one was open for 3% -> 4% of each run, Pallas kernels for 10% -> 11%
where the time goes in v6:
time: 74.1 us; the launch traced here: 73.8 us
  waiting for transfers between devices  33.3 us (45%)
  starting transfers between devices  23.5 us (32%)
  Pallas kernels  9.67 us (13%)
  local copies, waits for them, and re-layouts  3.35 us (5%)
  between operations  2.74 us (4%)
  other arithmetic  1.24 us (2%)
    ppermute x10, waiting for transfers between devices, shift(): return lax.ppermute(value, 'band', moves)  22.1 us
    ppermute x10, starting transfers between devices, shift(): return lax.ppermute(value, 'band', moves)  10.4 us
    pallas_call x7, Pallas kernels, pair_step(): pl.pallas_call(functools.partial(pair_kernel, slot), out_shape=outs, in_s...  7.82 us
    ppermute x7, starting transfers between devices, slab_swap(): return lax.ppermute(value, 'slab', [(i, i ^ reach) for i in range(size)])  7.03 us
    ppermute x7, waiting for transfers between devices, slab_swap(): return lax.ppermute(value, 'slab', [(i, i ^ reach) for i in range(size)])  6.05 us
    all_to_all x1, starting transfers between devices, share(): return lax.all_to_all(sent, ('band', 'slab'), 0, 0)  6.02 us
    all_to_all x1, waiting for transfers between devices, share(): return lax.all_to_all(sent, ('band', 'slab'), 0, 0)  5.15 us
    unnamed x18, local copies, waits for them, and re-layouts  1.61 us
  transfers between devices with their start and end apart: 18, of which 10 were waited for; matrix products, arithmetic and copies ran while one was open for 4% of the time, Pallas kernels for 11%

profile of v6, /device:TPU:0, one launch (start us, length us, event | category | flops | bytes accessed | tf_op | source)
XLA Modules:
  0.0 73.8 jit_solution(6593625282306763810)
XLA Ops:
  0.6 1.0 %copy-done = f32[4,12,2304]{2,0,1:T(4,128)S(1)} copy-done((f32[4,12,2304]{2,0,1:T(4,128)S(1)}, f32[4,12,2304]{2,0,1:T(4,128)}, u32[]{:S(2)}) %copy-start) | copy-done | bytes 442392
  1.9 0.6 collective-permute-start
  2.4 2.6 %collective-permute-start.1 = (f32[24,1152]{1,0:T(8,128)S(1)}, f32[24,1152]{1,0:T(8,128)S(1)}, u32[]{:S(2)}, u32[]{:S(2)}) collective-permute-start(f32[24,1152]{1,0:T(8,128)S(1)} %get-tuple-element.30), channel_id=1, source_target_pairs={{0,2},{1,3},{2,0},{3,1},{4,6},{5,7},{6,4},{7,5},{8,10},{9,11},{10,... | collective-permute-start | bytes 331784 | tf_op jit(solution)/shard_map/ppermute | solution.py:356
  5.1 0.8 %dynamic-slice_bitcast_fusion = (bf16[48,144]{1,0:T(8,128)(2,1)S(1)}, bf16[48,144]{1,0:T(8,128)(2,1)S(1)}) fusion(bf16[4,48,144]{2,1,0:T(8,128)(2,1)} %constant.116.clone, s32[]{:T(128)S(6)} %select_n.110, bf16[4,48,144]{2,1,0:T(8,128)(2,1)} %constant.115.clone), kind=kLoop, calls=%fused_computation.6 | loop fusion | bytes 55300 | tf_op jit(solution)/shard_map/jit(dynamic_index_in_dim)/squeeze | solution.py:76
  6.0 2.9 %collective-permute-done.1.refs_0_ = f32[24,1152]{1,0:T(8,128)S(1)} collective-permute-done((f32[24,1152]{1,0:T(8,128)S(1)}, f32[24,1152]{1,0:T(8,128)S(1)}, u32[]{:S(2)}, u32[]{:S(2)}) %collective-permute-start.1) | collective-permute-done | bytes 110624 | tf_op jit(solution)/shard_map/ppermute | solution.py:356
  8.9 1.8 %collective-permute-done.2.refs_1_ = f32[24,1152]{1,0:T(8,128)S(1)} collective-permute-done((f32[24,1152]{1,0:T(8,128)S(1)}, f32[24,1152]{1,0:T(8,128)S(1)}, u32[]{:S(2)}, u32[]{:S(2)}) %collective-permute-start.2) | collective-permute-done | bytes 110624 | tf_op jit(solution)/shard_map/ppermute | solution.py:356
  10.8 1.5 %collective-permute-start.6 = (f32[24,2304]{1,0:T(8,128)S(1)}, f32[24,2304]{1,0:T(8,128)S(1)}, u32[]{:S(2)}, u32[]{:S(2)}) collective-permute-start(f32[24,2304]{1,0:T(8,128)S(1)} %assemble.3.refs_1_), channel_id=1, source_target_pairs={{0,4},{8,0},{16,8},{24,16},{28,24},{20,28},{12,20},{4,12},{1,5},{9... | collective-permute-start | bytes 663560 | tf_op jit(solution)/shard_map/ppermute | solution.py:375
  12.3 0.6 collective-permute-start.4
  12.9 1.5 %collective-permute-start.5 = (f32[24,2304]{1,0:T(8,128)S(1)}, f32[24,2304]{1,0:T(8,128)S(1)}, u32[]{:S(2)}, u32[]{:S(2)}) collective-permute-start(f32[24,2304]{1,0:T(8,128)S(1)} %assemble.2.refs_0_), channel_id=1, source_target_pairs={{0,4},{8,0},{16,8},{24,16},{28,24},{20,28},{12,20},{4,12},{1,5},{9... | collective-permute-start | bytes 663560 | tf_op jit(solution)/shard_map/ppermute | solution.py:375
  14.4 0.6 collective-permute-start.3
  15.2 0.6 copy-done.8
  16.3 4.3 %collective-permute-done.4.refs_1_ = f32[24,2304]{1,0:T(8,128)S(1)} collective-permute-done((f32[24,2304]{1,0:T(8,128)S(1)}, f32[24,2304]{1,0:T(8,128)S(1)}, u32[]{:S(2)}, u32[]{:S(2)}) %collective-permute-start.4) | collective-permute-done | bytes 221216 | tf_op jit(solution)/shard_map/ppermute | solution.py:375
  20.6 3.9 %collective-permute-done.3.refs_0_ = f32[24,2304]{1,0:T(8,128)S(1)} collective-permute-done((f32[24,2304]{1,0:T(8,128)S(1)}, f32[24,2304]{1,0:T(8,128)S(1)}, u32[]{:S(2)}, u32[]{:S(2)}) %collective-permute-start.3) | collective-permute-done | bytes 221216 | tf_op jit(solution)/shard_map/ppermute | solution.py:375
  24.5 0.5 collective-permute-start.7
  25.0 1.6 %collective-permute-start.8 = (f32[48,2304]{1,0:T(8,128)S(1)}, f32[48,2304]{1,0:T(8,128)S(1)}, u32[]{:S(2)}, u32[]{:S(2)}) collective-permute-start(f32[48,2304]{1,0:T(8,128)S(1)} %join.6.refs_2_.other_ref), channel_id=1, source_target_pairs={{0,4},{8,0},{16,8},{24,16},{28,24},{20,28},{12,20},{4,12},{1,5},{9... | collective-permute-start | bytes 1327112 | tf_op jit(solution)/shard_map/ppermute | solution.py:375
  26.9 3.5 %pair_step.8 = (f32[1,128]{1,0:T(1,128)S(1)}, f32[48,2304]{1,0:T(8,128)S(1)}) custom-call(f32[14,128]{1,0:T(8,128)S(1)} %broadcast_in_dim.81.weights, f32[48,2304]{1,0:T(8,128)S(1)} %join.4.refs_0_.own_ref, f32[48,2304]{1,0:T(8,128)S(1)} %join.6.refs_2_.other_ref, bf16[48,144]{1,0:T(8,128)(2,1)S(1)} %get-tuple-element.57.x_fwd, ...), custom_call_target="tpu_custom_call", output_to_operand_aliasing={{1}: (10, {})} | custom-call | flops 3221225472 | bytes 3145728 | tf_op jit(solution)/shard_map/pair_step/pallas_call | solution.py:170
  30.4 5.5 %collective-permute-done.7.refs_3_.other_ref = f32[48,2304]{1,0:T(8,128)S(1)} collective-permute-done((f32[48,2304]{1,0:T(8,128)S(1)}, f32[48,2304]{1,0:T(8,128)S(1)}, u32[]{:S(2)}, u32[]{:S(2)}) %collective-permute-start.7) | collective-permute-done | bytes 442400 | tf_op jit(solution)/shard_map/ppermute | solution.py:375
  36.2 1.7 %collective-permute-start.10 = (f32[48,2304]{1,0:T(8,128)S(1)}, f32[48,2304]{1,0:T(8,128)S(1)}, u32[]{:S(2)}, u32[]{:S(2)}) collective-permute-start(f32[48,2304]{1,0:T(8,128)S(1)} %collective-permute-done.8.refs_4_.other_ref), channel_id=1, source_target_pairs={{0,4},{8,0},{16,8},{24,16},{28,24},{20,28},{12,20},{4,12},{1,5},{9... | collective-permute-start | bytes 1327112 | tf_op jit(solution)/shard_map/ppermute | solution.py:375
  38.0 3.7 %pair_step.10 = (f32[1,128]{1,0:T(1,128)S(1)}, f32[48,2304]{1,0:T(8,128)S(1)}) custom-call(f32[14,128]{1,0:T(8,128)S(1)} %broadcast_in_dim.81.weights, f32[48,2304]{1,0:T(8,128)S(1)} %join.4.refs_0_.own_ref, f32[48,2304]{1,0:T(8,128)S(1)} %collective-permute-done.8.refs_4_.other_ref, ...), custom_call_target="tpu_custom_call", output_to_operand_aliasing={{1}: (10, {})} | custom-call | flops 3221225472 | bytes 3145728 | tf_op jit(solution)/shard_map/pair_step/pallas_call | solution.py:170
  41.7 4.6 %collective-permute-done.9.refs_5_.other_ref = f32[48,2304]{1,0:T(8,128)S(1)} collective-permute-done((f32[48,2304]{1,0:T(8,128)S(1)}, f32[48,2304]{1,0:T(8,128)S(1)}, u32[]{:S(2)}, u32[]{:S(2)}) %collective-permute-start.9) | collective-permute-done | bytes 442400 | tf_op jit(solution)/shard_map/ppermute | solution.py:375
  46.3 0.3 collective-permute-start.11
  46.7 1.8 %collective-permute-start.12 = (f32[24,2304]{1,0:T(8,128)S(1)}, f32[24,2304]{1,0:T(8,128)S(1)}, u32[]{:S(2)}, u32[]{:S(2)}) collective-permute-start(f32[24,2304]{1,0:T(8,128)S(1)} %slice.21), channel_id=1, source_target_pairs={{0,4},{8,0},{16,8},{24,16},{28,24},{20,28},{12,20},{4,12},{1,5},{9... | collective-permute-start | bytes 663560 | tf_op jit(solution)/shard_map/ppermute | solution.py:375
  48.8 3.6 %collective-permute-done.11.refs_0_ = f32[24,2304]{1,0:T(8,128)S(1)} collective-permute-done((f32[24,2304]{1,0:T(8,128)S(1)}, f32[24,2304]{1,0:T(8,128)S(1)}, u32[]{:S(2)}, u32[]{:S(2)}) %collective-permute-start.11) | collective-permute-done | bytes 221216 | tf_op jit(solution)/shard_map/ppermute | solution.py:375
  52.3 0.4 collective-permute-done.12.refs_1_
  53.3 1.3 %collective-permute-done.13.theirs = f32[2,24,1152]{2,1,0:T(8,128)S(1)} collective-permute-done((f32[2,24,1152]{2,1,0:T(8,128)S(1)}, f32[2,24,1152]{2,1,0:T(8,128)S(1)}, u32[]{:S(2)}, u32[]{:S(2)}) %collective-permute-start.13) | collective-permute-done | bytes 221216 | tf_op jit(solution)/shard_map/ppermute | solution.py:356
  54.6 1.8 %collective-permute-start.14 = (f32[48,1152]{1,0:T(8,128)S(1)}, f32[48,1152]{1,0:T(8,128)S(1)}, u32[]{:S(2)}, u32[]{:S(2)}) collective-permute-start(f32[48,1152]{1,0:T(8,128)S(1)} %pack.1), channel_id=1, source_target_pairs={{0,2},{1,3},{2,0},{3,1},{4,6},{5,7},{6,4},{7,5},{8,10},{9,11},{10,... | collective-permute-start | bytes 663560 | tf_op jit(solution)/shard_map/ppermute | solution.py:356
  56.5 0.6 broadcast_in_dim.84
  57.1 6.0 %all-to-all-start = ((f32[32,1,128]{2,1,0:T(1,128)}), f32[32,1,128]{2,1,0:T(1,128)S(1)}, u32[]{:S(2)}, u32[]{:S(2)}) async-start(f32[32,1,128]{2,1,0:T(1,128)} %broadcast_in_dim.84), calls=%async_computation | async-start | bytes 32768 | tf_op jit(solution)/shard_map/all_to_all | solution.py:361
  63.4 1.6 %collective-permute-start.16 = (f32[24,1152]{1,0:T(8,128)S(1)}, f32[24,1152]{1,0:T(8,128)S(1)}, u32[]{:S(2)}, u32[]{:S(2)}) collective-permute-start(f32[24,1152]{1,0:T(8,128)S(1)} %get-tuple-element.52), channel_id=1, source_target_pairs={{0,3},{1,2},{2,1},{3,0},{4,7},{5,6},{6,5},{7,4},{8,11},{9,10},{10,... | collective-permute-start | bytes 331784 | tf_op jit(solution)/shard_map/ppermute | solution.py:356
  65.1 5.2 %all-to-all-done = f32[32,1,128]{2,1,0:T(1,128)S(1)} async-done(((f32[32,1,128]{2,1,0:T(1,128)}), f32[32,1,128]{2,1,0:T(1,128)S(1)}, u32[]{:S(2)}, u32[]{:S(2)}) %all-to-all-start) | async-done | bytes 16416 | tf_op jit(solution)/shard_map/all_to_all | solution.py:361
  70.2 0.6 reduce_sum.65
  71.6 1.1 %finish.1 = f32[12,4,2304]{2,1,0:T(4,128)} custom-call(s32[1]{0:T(128)} %bitcast.place, f32[12,4,2304]{2,1,0:T(4,128)S(1)} %bitcast.25, f32[24,1152]{1,0:T(8,128)S(1)} %fusion.2.local_pot, f32[24,1152]{1,0:T(8,128)S(1)} %get-tuple-element.50.refs_0_, f32[24,1152]{1,0:T(8,128)S(1)} %collective-permute-done.15.refs_1_, ...), custom_call_target="tpu_custom_call" | custom-call | tf_op jit(solution)/shard_map/finish/pallas_call | solution.py:344
  (58 shorter events, 3.2 us)
Async XLA Ops:
  0.6 1.0 %copy-start = (f32[4,12,2304]{2,0,1:T(4,128)S(1)}, f32[4,12,2304]{2,0,1:T(4,128)}, u32[]{:S(2)}) copy-start(f32[4,12,2304]{2,0,1:T(4,128)} %param.10) | copy-start | bytes 1327108
  1.9 11.0 %collective-permute-start = (f32[24,1152]{1,0:T(8,128)S(1)}, f32[24,1152]{1,0:T(8,128)S(1)}, u32[]{:S(2)}, u32[]{:S(2)}) collective-permute-start(f32[24,1152]{1,0:T(8,128)S(1)} %get-tuple-element.29), channel_id=1, source_target_pairs={{0,1},{1,0},{2,3},{3,2},{4,5},{5,4},{6,7},{7,6},{8,9},{9,8},{10,11... | collective-permute-start | bytes 331784 | tf_op jit(solution)/shard_map/ppermute | solution.py:356
  2.4 6.5 %collective-permute-start.1 = (f32[24,1152]{1,0:T(8,128)S(1)}, f32[24,1152]{1,0:T(8,128)S(1)}, u32[]{:S(2)}, u32[]{:S(2)}) collective-permute-start(f32[24,1152]{1,0:T(8,128)S(1)} %get-tuple-element.30), channel_id=1, source_target_pairs={{0,2},{1,3},{2,0},{3,1},{4,6},{5,7},{6,4},{7,5},{8,10},{9,11},{10,... | collective-permute-start | bytes 331784 | tf_op jit(solution)/shard_map/ppermute | solution.py:356
  5.0 5.8 %collective-permute-start.2 = (f32[24,1152]{1,0:T(8,128)S(1)}, f32[24,1152]{1,0:T(8,128)S(1)}, u32[]{:S(2)}, u32[]{:S(2)}) collective-permute-start(f32[24,1152]{1,0:T(8,128)S(1)} %get-tuple-element.31), channel_id=1, source_target_pairs={{0,3},{1,2},{2,1},{3,0},{4,7},{5,6},{6,5},{7,4},{8,11},{9,10},{10,... | collective-permute-start | bytes 331784 | tf_op jit(solution)/shard_map/ppermute | solution.py:356
  10.8 14.2 %collective-permute-start.6 = (f32[24,2304]{1,0:T(8,128)S(1)}, f32[24,2304]{1,0:T(8,128)S(1)}, u32[]{:S(2)}, u32[]{:S(2)}) collective-permute-start(f32[24,2304]{1,0:T(8,128)S(1)} %assemble.3.refs_1_), channel_id=1, source_target_pairs={{0,4},{8,0},{16,8},{24,16},{28,24},{20,28},{12,20},{4,12},{1,5},{9... | collective-permute-start | bytes 663560 | tf_op jit(solution)/shard_map/ppermute | solution.py:375
  12.3 8.3 %collective-permute-start.4 = (f32[24,2304]{1,0:T(8,128)S(1)}, f32[24,2304]{1,0:T(8,128)S(1)}, u32[]{:S(2)}, u32[]{:S(2)}) collective-permute-start(f32[24,2304]{1,0:T(8,128)S(1)} %assemble.3.refs_1_), channel_id=1, source_target_pairs={{0,8},{8,16},{16,24},{24,28},{28,20},{20,12},{12,4},{4,0},{1,9},{9... | collective-permute-start | bytes 663560 | tf_op jit(solution)/shard_map/ppermute | solution.py:375
  12.9 2.1 %copy-start.7 = (s32[8,2]{0,1:T(2,128)S(1)}, s32[8,2]{0,1:T(2,128)}, u32[]{:S(2)}) copy-start(s32[8,2]{0,1:T(2,128)} %param.11) | copy-start | bytes 196
  12.9 12.1 %collective-permute-start.5 = (f32[24,2304]{1,0:T(8,128)S(1)}, f32[24,2304]{1,0:T(8,128)S(1)}, u32[]{:S(2)}, u32[]{:S(2)}) collective-permute-start(f32[24,2304]{1,0:T(8,128)S(1)} %assemble.2.refs_0_), channel_id=1, source_target_pairs={{0,4},{8,0},{16,8},{24,16},{28,24},{20,28},{12,20},{4,12},{1,5},{9... | collective-permute-start | bytes 663560 | tf_op jit(solution)/shard_map/ppermute | solution.py:375
  14.4 10.0 %collective-permute-start.3 = (f32[24,2304]{1,0:T(8,128)S(1)}, f32[24,2304]{1,0:T(8,128)S(1)}, u32[]{:S(2)}, u32[]{:S(2)}) collective-permute-start(f32[24,2304]{1,0:T(8,128)S(1)} %assemble.2.refs_0_), channel_id=1, source_target_pairs={{0,8},{8,16},{16,24},{24,28},{28,20},{20,12},{12,4},{4,0},{1,9},{9... | collective-permute-start | bytes 663560 | tf_op jit(solution)/shard_map/ppermute | solution.py:375
  15.0 0.7 copy-start.8
  16.3 10.5 %copy-start.2 = (f32[96,2304]{1,0:T(8,128)S(1)}, f32[96,2304]{1,0:T(8,128)}, u32[]{:S(2)}) copy-start(f32[96,2304]{1,0:T(8,128)} %constant.119.clone.table) | copy-start | bytes 2654212
  24.5 2.3 %copy-start.3 = (bf16[192,48]{1,0:T(8,128)(2,1)S(1)}, bf16[192,48]{1,0:T(8,128)(2,1)}, u32[]{:S(2)}) copy-start(bf16[192,48]{1,0:T(8,128)(2,1)} %constant.118.clone.z_fwd) | copy-start | bytes 55300
  24.5 2.3 %copy-start.4 = (bf16[48,288]{1,0:T(8,128)(2,1)S(1)}, bf16[48,288]{1,0:T(8,128)(2,1)}, u32[]{:S(2)}) copy-start(bf16[48,288]{1,0:T(8,128)(2,1)} %constant.120.clone.z_inv) | copy-start | bytes 82948
  24.5 2.3 %copy-start.5 = (bf16[96,48]{1,0:T(8,128)(2,1)S(1)}, bf16[96,48]{1,0:T(8,128)(2,1)}, u32[]{:S(2)}) copy-start(bf16[96,48]{1,0:T(8,128)(2,1)} %constant.121.clone.y_inv) | copy-start | bytes 27652
  24.5 2.3 %copy-start.6 = (bf16[48,144]{1,0:T(8,128)(2,1)S(1)}, bf16[48,144]{1,0:T(8,128)(2,1)}, u32[]{:S(2)}) copy-start(bf16[48,144]{1,0:T(8,128)(2,1)} %constant.117.clone.y_fwd) | copy-start | bytes 41476
  24.5 11.4 %collective-permute-start.7 = (f32[48,2304]{1,0:T(8,128)S(1)}, f32[48,2304]{1,0:T(8,128)S(1)}, u32[]{:S(2)}, u32[]{:S(2)}) collective-permute-start(f32[48,2304]{1,0:T(8,128)S(1)} %join.5.refs_1_.other_ref), channel_id=1, source_target_pairs={{0,8},{8,16},{16,24},{24,28},{28,20},{20,12},{12,4},{4,0},{1,9},{9... | collective-permute-start | bytes 1327112 | tf_op jit(solution)/shard_map/ppermute | solution.py:375
  25.0 11.1 %collective-permute-start.8 = (f32[48,2304]{1,0:T(8,128)S(1)}, f32[48,2304]{1,0:T(8,128)S(1)}, u32[]{:S(2)}, u32[]{:S(2)}) collective-permute-start(f32[48,2304]{1,0:T(8,128)S(1)} %join.6.refs_2_.other_ref), channel_id=1, source_target_pairs={{0,4},{8,0},{16,8},{24,16},{28,24},{20,28},{12,20},{4,12},{1,5},{9... | collective-permute-start | bytes 1327112 | tf_op jit(solution)/shard_map/ppermute | solution.py:375
  35.9 10.4 %collective-permute-start.9 = (f32[48,2304]{1,0:T(8,128)S(1)}, f32[48,2304]{1,0:T(8,128)S(1)}, u32[]{:S(2)}, u32[]{:S(2)}) collective-permute-start(f32[48,2304]{1,0:T(8,128)S(1)} %collective-permute-done.7.refs_3_.other_ref), channel_id=1, source_target_pairs={{0,8},{8,16},{16,24},{24,28},{28,20},{20,12},{12,4},{4,0},{1,9},{9... | collective-permute-start | bytes 1327112 | tf_op jit(solution)/shard_map/ppermute | solution.py:375
  36.2 10.5 %collective-permute-start.10 = (f32[48,2304]{1,0:T(8,128)S(1)}, f32[48,2304]{1,0:T(8,128)S(1)}, u32[]{:S(2)}, u32[]{:S(2)}) collective-permute-start(f32[48,2304]{1,0:T(8,128)S(1)} %collective-permute-done.8.refs_4_.other_ref), channel_id=1, source_target_pairs={{0,4},{8,0},{16,8},{24,16},{28,24},{20,28},{12,20},{4,12},{1,5},{9... | collective-permute-start | bytes 1327112 | tf_op jit(solution)/shard_map/ppermute | solution.py:375
  46.3 6.0 %collective-permute-start.11 = (f32[24,2304]{1,0:T(8,128)S(1)}, f32[24,2304]{1,0:T(8,128)S(1)}, u32[]{:S(2)}, u32[]{:S(2)}) collective-permute-start(f32[24,2304]{1,0:T(8,128)S(1)} %slice.20), channel_id=1, source_target_pairs={{0,8},{8,16},{16,24},{24,28},{28,20},{20,12},{12,4},{4,0},{1,9},{9... | collective-permute-start | bytes 663560 | tf_op jit(solution)/shard_map/ppermute | solution.py:375
  46.7 6.0 %collective-permute-start.12 = (f32[24,2304]{1,0:T(8,128)S(1)}, f32[24,2304]{1,0:T(8,128)S(1)}, u32[]{:S(2)}, u32[]{:S(2)}) collective-permute-start(f32[24,2304]{1,0:T(8,128)S(1)} %slice.21), channel_id=1, source_target_pairs={{0,4},{8,0},{16,8},{24,16},{28,24},{20,28},{12,20},{4,12},{1,5},{9... | collective-permute-start | bytes 663560 | tf_op jit(solution)/shard_map/ppermute | solution.py:375
  53.0 1.5 %collective-permute-start.13 = (f32[2,24,1152]{2,1,0:T(8,128)S(1)}, f32[2,24,1152]{2,1,0:T(8,128)S(1)}, u32[]{:S(2)}, u32[]{:S(2)}) collective-permute-start(f32[2,24,1152]{2,1,0:T(8,128)S(1)} %get-tuple-element.34), channel_id=1, source_target_pairs={{0,1},{1,0},{2,3},{3,2},{4,5},{5,4},{6,7},{7,6},{8,9},{9,8},{10,11... | collective-permute-start | bytes 663560 | tf_op jit(solution)/shard_map/ppermute | solution.py:356
  54.6 17.0 %copy-start.1 = (f32[4,12,2304]{2,0,1:T(4,128)S(1)}, f32[4,12,2304]{2,0,1:T(4,128)}, u32[]{:S(2)}) copy-start(f32[4,12,2304]{2,0,1:T(4,128)} %param.10) | copy-start | bytes 1327108
  54.6 16.8 %collective-permute-start.14 = (f32[48,1152]{1,0:T(8,128)S(1)}, f32[48,1152]{1,0:T(8,128)S(1)}, u32[]{:S(2)}, u32[]{:S(2)}) collective-permute-start(f32[48,1152]{1,0:T(8,128)S(1)} %pack.1), channel_id=1, source_target_pairs={{0,2},{1,3},{2,0},{3,1},{4,6},{5,7},{6,4},{7,5},{8,10},{9,11},{10,... | collective-permute-start | bytes 663560 | tf_op jit(solution)/shard_map/ppermute | solution.py:356
  57.1 13.1 %all-to-all-start = ((f32[32,1,128]{2,1,0:T(1,128)}), f32[32,1,128]{2,1,0:T(1,128)S(1)}, u32[]{:S(2)}, u32[]{:S(2)}) async-start(f32[32,1,128]{2,1,0:T(1,128)} %broadcast_in_dim.84), calls=%async_computation | async-start | bytes 32768 | tf_op jit(solution)/shard_map/all_to_all | solution.py:361
  63.1 8.5 %collective-permute-start.15 = (f32[24,1152]{1,0:T(8,128)S(1)}, f32[24,1152]{1,0:T(8,128)S(1)}, u32[]{:S(2)}, u32[]{:S(2)}) collective-permute-start(f32[24,1152]{1,0:T(8,128)S(1)} %get-tuple-element.51), channel_id=1, source_target_pairs={{0,1},{1,0},{2,3},{3,2},{4,5},{5,4},{6,7},{7,6},{8,9},{9,8},{10,11... | collective-permute-start | bytes 331784 | tf_op jit(solution)/shard_map/ppermute | solution.py:356
  63.4 8.2 %collective-permute-start.16 = (f32[24,1152]{1,0:T(8,128)S(1)}, f32[24,1152]{1,0:T(8,128)S(1)}, u32[]{:S(2)}, u32[]{:S(2)}) collective-permute-start(f32[24,1152]{1,0:T(8,128)S(1)} %get-tuple-element.52), channel_id=1, source_target_pairs={{0,3},{1,2},{2,1},{3,0},{4,7},{5,6},{6,5},{7,4},{8,11},{9,10},{10,... | collective-permute-start | bytes 331784 | tf_op jit(solution)/shard_map/ppermute | solution.py:356

commit v7 on v6

--- a/solution.py
+++ b/solution.py
@@ -118,7 +118,7 @@
 
     @pl.when(total_weight == 0.0)
     def _():
-        energy_out[...] = energy_in[...]
+        energy_out[...] = jnp.broadcast_to(energy_in[...], energy_out.shape)
         if len(force_refs) > 1:
             store_force(force_refs, force_in[...])
 
@@ -140,7 +140,9 @@
         folded = products[:, :128]
         for start in range(128, NX * NY, 128):
             folded = folded + products[:, start : start + 128]
-        energy_out[...] = energy_in[...] + request_weight * folded
+        energy_out[...] = jnp.broadcast_to(
+            energy_in[...] + request_weight * folded, energy_out.shape
+        )
         spectrum = apply_left(z_inv[...], weighted)
         for q in range(NX):
             high, low = split(spectrum[:, q * NY : (q + 1) * NY])
@@ -163,9 +165,10 @@
     return (planes * fold, NY * NZ // fold)
 
 
-def pair_step(slot, weights, own, other, tables, force, energy, pieces=1):
+def pair_step(slot, weights, own, other, tables, force, energy, pieces=1, copies=None):
     piece = force.shape if pieces == 1 else piece_shape(NX // pieces)
-    outs = [jax.ShapeDtypeStruct(energy.shape, jnp.float32)]
+    energy_shape = energy.shape if copies is None else (copies,) + energy.shape
+    outs = [jax.ShapeDtypeStruct(energy_shape, jnp.float32)]
     outs += [jax.ShapeDtypeStruct(piece, jnp.float32)] * pieces
     return pl.pallas_call(
         functools.partial(pair_kernel, slot),
@@ -356,9 +359,20 @@
     return lax.ppermute(value, "slab", [(i, i ^ reach) for i in range(size)])
 
 
-def share(value, devices):
-    sent = jnp.broadcast_to(value[None], (devices,) + value.shape)
-    return lax.all_to_all(sent, ("band", "slab"), 0, 0)
+def total_kernel(scale, shared, out_ref):
+    summed = jnp.sum(shared[...], axis=0)
+    out_ref[...] = scale * jnp.sum(summed, axis=1, keepdims=True)
+
+
+def total_of(shared, scale):
+    return pl.pallas_call(
+        functools.partial(total_kernel, scale),
+        out_shape=jax.ShapeDtypeStruct((1, 1), jnp.float32),
+        in_specs=in_vmem(1),
+        out_specs=in_vmem(1)[0],
+        compiler_params=pltpu.CompilerParams(vmem_limit_bytes=8 << 20),
+        name="total",
+    )(shared)
 
 
 def gather_ring(halves, band_index, bands):
@@ -434,22 +448,21 @@
         if slot < len(others) - 1:
             energy, force = pair_step(slot, weights, own, other, tables, force, energy)
         else:
-            energy, *outgoing = pair_step(slot, weights, own, other, tables, force, energy, slabs)
+            energy, *outgoing = pair_step(
+                slot, weights, own, other, tables, force, energy, slabs, bands * slabs
+            )
 
     for r in range(2, slabs, 2):
         outgoing[r] = pack(r // 2, outgoing[r], even, from_core)
     arrived = [outgoing[0]] + [slab_swap(outgoing[r], r) for r in range(1, slabs)]
-    shared = share(energy, bands * slabs)
+    shared = lax.all_to_all(energy, ("band", "slab"), 0, 0)
     rows = arrived[0].shape[0]
     squares = even[0] + from_core[0] + sum(arrived[r][rows:] for r in range(2, slabs, 2))
     density = 2.0 / total_orbs * squares
     local_pot = slater_coeff * jnp.cbrt(density)
     forces = finish(place, by_plane, local_pot, arrived)
-    energy_total = jnp.sum(shared)
-    return (
-        jnp.transpose(forces, (1, 0, 2)),
-        -energy_total / (2.0 * total_orbs * NX * NY * NZ),
-    )
+    total = total_of(shared, -1.0 / (2.0 * total_orbs * NX * NY * NZ))
+    return jnp.transpose(forces, (1, 0, 2)), total.reshape(())
 
 
 def solution(mesh):

time: 74.1 us -> 72.2 us (0.974)
  between operations: 2.74 us -> 0.95 us
  Pallas kernels: 9.67 us -> 10.8 us
  transfers between devices with their start and end apart: 18 -> 18, of which waited for: 10 -> 10; matrix products, arithmetic and copies ran while one was open for 4% -> 2% of each run, Pallas kernels for 11% -> 13%
where the time goes in v7:
time: 72.2 us; the launch traced here: 72 us
  waiting for transfers between devices  32.8 us (45%)
  starting transfers between devices  24.1 us (33%)
  Pallas kernels  10.8 us (15%)
  local copies, waits for them, and re-layouts  2.74 us (4%)
  between operations  0.95 us (1%)
    ppermute x10, waiting for transfers between devices, shift(): return lax.ppermute(value, 'band', moves)  22.2 us
    ppermute x10, starting transfers between devices, shift(): return lax.ppermute(value, 'band', moves)  10.4 us
    pallas_call x7, Pallas kernels, pair_step(): pl.pallas_call(functools.partial(pair_kernel, slot), out_shape=outs, in_s...  8.39 us
    ppermute x7, starting transfers between devices, slab_swap(): return lax.ppermute(value, 'slab', [(i, i ^ reach) for i in range(size)])  7.03 us
    all_to_all x1, starting transfers between devices, body(): shared = lax.all_to_all(energy, ('band', 'slab'), 0, 0)  6.6 us
    ppermute x7, waiting for transfers between devices, slab_swap(): return lax.ppermute(value, 'slab', [(i, i ^ reach) for i in range(size)])  5.45 us
    all_to_all x1, waiting for transfers between devices, body(): shared = lax.all_to_all(energy, ('band', 'slab'), 0, 0)  5.15 us
    unnamed x18, local copies, waits for them, and re-layouts  1.61 us
  transfers between devices with their start and end apart: 18, of which 10 were waited for; matrix products, arithmetic and copies ran while one was open for 2% of the time, Pallas kernels for 13%

profile of v7, /device:TPU:0, one launch (start us, length us, event | category | flops | bytes accessed | tf_op | source)
XLA Modules:
  0.0 72.0 jit_solution(14248830984980333009)
XLA Ops:
  0.6 1.0 %copy-done = f32[4,12,2304]{2,0,1:T(4,128)S(1)} copy-done((f32[4,12,2304]{2,0,1:T(4,128)S(1)}, f32[4,12,2304]{2,0,1:T(4,128)}, u32[]{:S(2)}) %copy-start) | copy-done | bytes 442392
  1.9 0.6 collective-permute-start
  2.4 2.6 %collective-permute-start.1 = (f32[24,1152]{1,0:T(8,128)S(1)}, f32[24,1152]{1,0:T(8,128)S(1)}, u32[]{:S(2)}, u32[]{:S(2)}) collective-permute-start(f32[24,1152]{1,0:T(8,128)S(1)} %get-tuple-element.30), channel_id=1, source_target_pairs={{0,2},{1,3},{2,0},{3,1},{4,6},{5,7},{6,4},{7,5},{8,10},{9,11},{10,... | collective-permute-start | bytes 331784 | tf_op jit(solution)/shard_map/ppermute | solution.py:359
  5.1 0.8 %dynamic-slice_bitcast_fusion = (bf16[48,144]{1,0:T(8,128)(2,1)S(1)}, bf16[48,144]{1,0:T(8,128)(2,1)S(1)}) fusion(bf16[4,48,144]{2,1,0:T(8,128)(2,1)} %constant.113.clone, s32[]{:T(128)S(6)} %select_n.110, bf16[4,48,144]{2,1,0:T(8,128)(2,1)} %constant.112.clone), kind=kLoop, calls=%fused_computation.6 | loop fusion | bytes 55300 | tf_op jit(solution)/shard_map/jit(dynamic_index_in_dim)/squeeze | solution.py:76
  6.0 2.9 %collective-permute-done.1.refs_0_ = f32[24,1152]{1,0:T(8,128)S(1)} collective-permute-done((f32[24,1152]{1,0:T(8,128)S(1)}, f32[24,1152]{1,0:T(8,128)S(1)}, u32[]{:S(2)}, u32[]{:S(2)}) %collective-permute-start.1) | collective-permute-done | bytes 110624 | tf_op jit(solution)/shard_map/ppermute | solution.py:359
  8.9 1.8 %collective-permute-done.2.refs_1_ = f32[24,1152]{1,0:T(8,128)S(1)} collective-permute-done((f32[24,1152]{1,0:T(8,128)S(1)}, f32[24,1152]{1,0:T(8,128)S(1)}, u32[]{:S(2)}, u32[]{:S(2)}) %collective-permute-start.2) | collective-permute-done | bytes 110624 | tf_op jit(solution)/shard_map/ppermute | solution.py:359
  10.8 1.5 %collective-permute-start.6 = (f32[24,2304]{1,0:T(8,128)S(1)}, f32[24,2304]{1,0:T(8,128)S(1)}, u32[]{:S(2)}, u32[]{:S(2)}) collective-permute-start(f32[24,2304]{1,0:T(8,128)S(1)} %assemble.3.refs_1_), channel_id=1, source_target_pairs={{0,4},{8,0},{16,8},{24,16},{28,24},{20,28},{12,20},{4,12},{1,5},{9... | collective-permute-start | bytes 663560 | tf_op jit(solution)/shard_map/ppermute | solution.py:389
  12.3 0.6 collective-permute-start.4
  12.9 1.5 %collective-permute-start.5 = (f32[24,2304]{1,0:T(8,128)S(1)}, f32[24,2304]{1,0:T(8,128)S(1)}, u32[]{:S(2)}, u32[]{:S(2)}) collective-permute-start(f32[24,2304]{1,0:T(8,128)S(1)} %assemble.2.refs_0_), channel_id=1, source_target_pairs={{0,4},{8,0},{16,8},{24,16},{28,24},{20,28},{12,20},{4,12},{1,5},{9... | collective-permute-start | bytes 663560 | tf_op jit(solution)/shard_map/ppermute | solution.py:389
  14.4 0.6 collective-permute-start.3
  15.2 0.6 copy-done.8
  16.3 4.3 %collective-permute-done.4.refs_1_ = f32[24,2304]{1,0:T(8,128)S(1)} collective-permute-done((f32[24,2304]{1,0:T(8,128)S(1)}, f32[24,2304]{1,0:T(8,128)S(1)}, u32[]{:S(2)}, u32[]{:S(2)}) %collective-permute-start.4) | collective-permute-done | bytes 221216 | tf_op jit(solution)/shard_map/ppermute | solution.py:389
  20.6 3.9 %collective-permute-done.3.refs_0_ = f32[24,2304]{1,0:T(8,128)S(1)} collective-permute-done((f32[24,2304]{1,0:T(8,128)S(1)}, f32[24,2304]{1,0:T(8,128)S(1)}, u32[]{:S(2)}, u32[]{:S(2)}) %collective-permute-start.3) | collective-permute-done | bytes 221216 | tf_op jit(solution)/shard_map/ppermute | solution.py:389
  24.5 0.5 collective-permute-start.7
  25.0 1.6 %collective-permute-start.8 = (f32[48,2304]{1,0:T(8,128)S(1)}, f32[48,2304]{1,0:T(8,128)S(1)}, u32[]{:S(2)}, u32[]{:S(2)}) collective-permute-start(f32[48,2304]{1,0:T(8,128)S(1)} %join.6.refs_2_.other_ref), channel_id=1, source_target_pairs={{0,4},{8,0},{16,8},{24,16},{28,24},{20,28},{12,20},{4,12},{1,5},{9... | collective-permute-start | bytes 1327112 | tf_op jit(solution)/shard_map/ppermute | solution.py:389
  26.9 3.5 %pair_step.8 = (f32[1,128]{1,0:T(1,128)S(1)}, f32[48,2304]{1,0:T(8,128)S(1)}) custom-call(f32[14,128]{1,0:T(8,128)S(1)} %broadcast_in_dim.73.weights, f32[48,2304]{1,0:T(8,128)S(1)} %join.4.refs_0_.own_ref, f32[48,2304]{1,0:T(8,128)S(1)} %join.6.refs_2_.other_ref, bf16[48,144]{1,0:T(8,128)(2,1)S(1)} %get-tuple-element.57.x_fwd, ...), custom_call_target="tpu_custom_call", output_to_operand_aliasing={{1}: (10, {})} | custom-call | flops 3221225472 | bytes 3145728 | tf_op jit(solution)/shard_map/pair_step/pallas_call | solution.py:173
  30.4 5.5 %collective-permute-done.7.refs_3_.other_ref = f32[48,2304]{1,0:T(8,128)S(1)} collective-permute-done((f32[48,2304]{1,0:T(8,128)S(1)}, f32[48,2304]{1,0:T(8,128)S(1)}, u32[]{:S(2)}, u32[]{:S(2)}) %collective-permute-start.7) | collective-permute-done | bytes 442400 | tf_op jit(solution)/shard_map/ppermute | solution.py:389
  36.2 1.7 %collective-permute-start.10 = (f32[48,2304]{1,0:T(8,128)S(1)}, f32[48,2304]{1,0:T(8,128)S(1)}, u32[]{:S(2)}, u32[]{:S(2)}) collective-permute-start(f32[48,2304]{1,0:T(8,128)S(1)} %collective-permute-done.8.refs_4_.other_ref), channel_id=1, source_target_pairs={{0,4},{8,0},{16,8},{24,16},{28,24},{20,28},{12,20},{4,12},{1,5},{9... | collective-permute-start | bytes 1327112 | tf_op jit(solution)/shard_map/ppermute | solution.py:389
  38.0 3.6 %pair_step.10 = (f32[1,128]{1,0:T(1,128)S(1)}, f32[48,2304]{1,0:T(8,128)S(1)}) custom-call(f32[14,128]{1,0:T(8,128)S(1)} %broadcast_in_dim.73.weights, f32[48,2304]{1,0:T(8,128)S(1)} %join.4.refs_0_.own_ref, f32[48,2304]{1,0:T(8,128)S(1)} %collective-permute-done.8.refs_4_.other_ref, ...), custom_call_target="tpu_custom_call", output_to_operand_aliasing={{1}: (10, {})} | custom-call | flops 3221225472 | bytes 3145728 | tf_op jit(solution)/shard_map/pair_step/pallas_call | solution.py:173
  41.7 4.6 %collective-permute-done.9.refs_5_.other_ref = f32[48,2304]{1,0:T(8,128)S(1)} collective-permute-done((f32[48,2304]{1,0:T(8,128)S(1)}, f32[48,2304]{1,0:T(8,128)S(1)}, u32[]{:S(2)}, u32[]{:S(2)}) %collective-permute-start.9) | collective-permute-done | bytes 442400 | tf_op jit(solution)/shard_map/ppermute | solution.py:389
  46.3 0.3 collective-permute-start.11
  46.7 1.8 %collective-permute-start.12 = (f32[24,2304]{1,0:T(8,128)S(1)}, f32[24,2304]{1,0:T(8,128)S(1)}, u32[]{:S(2)}, u32[]{:S(2)}) collective-permute-start(f32[24,2304]{1,0:T(8,128)S(1)} %slice.21), channel_id=1, source_target_pairs={{0,4},{8,0},{16,8},{24,16},{28,24},{20,28},{12,20},{4,12},{1,5},{9... | collective-permute-start | bytes 663560 | tf_op jit(solution)/shard_map/ppermute | solution.py:389
  48.8 3.6 %collective-permute-done.11.refs_0_ = f32[24,2304]{1,0:T(8,128)S(1)} collective-permute-done((f32[24,2304]{1,0:T(8,128)S(1)}, f32[24,2304]{1,0:T(8,128)S(1)}, u32[]{:S(2)}, u32[]{:S(2)}) %collective-permute-start.11) | collective-permute-done | bytes 221216 | tf_op jit(solution)/shard_map/ppermute | solution.py:389
  52.3 0.4 collective-permute-done.12.refs_1_
  53.0 0.8 %pair_step.13 = (f32[32,1,128]{2,1,0:T(1,128)}, f32[24,1152]{1,0:T(8,128)S(1)}, f32[24,1152]{1,0:T(8,128)S(1)}, f32[24,1152]{1,0:T(8,128)S(1)}, f32[24,1152]{1,0:T(8,128)S(1)}) custom-call(f32[14,128]{1,0:T(8,128)S(1)} %broadcast_in_dim.73.weights, f32[48,2304]{1,0:T(8,128)S(1)} %join.4.refs_0_.own_ref, f32[48,2304]{1,0:T(8,128)S(1)} %join.7.refs_7_.other_ref, ...), custom_call_target="tpu_custom_call" | custom-call | flops 3221225472 | bytes 3145728 | tf_op jit(solution)/shard_map/pair_step/pallas_call | solution.py:173
  53.8 0.7 collective-permute-done.13.theirs
  54.5 1.8 %collective-permute-start.14 = (f32[48,1152]{1,0:T(8,128)S(1)}, f32[48,1152]{1,0:T(8,128)S(1)}, u32[]{:S(2)}, u32[]{:S(2)}) collective-permute-start(f32[48,1152]{1,0:T(8,128)S(1)} %pack.1), channel_id=1, source_target_pairs={{0,2},{1,3},{2,0},{3,1},{4,6},{5,7},{6,4},{7,5},{8,10},{9,11},{10,... | collective-permute-start | bytes 663560 | tf_op jit(solution)/shard_map/ppermute | solution.py:359
  56.4 6.6 %all-to-all-start = ((f32[32,1,128]{2,1,0:T(1,128)}), f32[32,1,128]{2,1,0:T(1,128)S(1)}, u32[]{:S(2)}, u32[]{:S(2)}) async-start(f32[32,1,128]{2,1,0:T(1,128)} %get-tuple-element.53), calls=%async_computation | async-start | bytes 32768 | tf_op jit(solution)/shard_map/all_to_all | solution.py:458
  63.3 1.6 %collective-permute-start.16 = (f32[24,1152]{1,0:T(8,128)S(1)}, f32[24,1152]{1,0:T(8,128)S(1)}, u32[]{:S(2)}, u32[]{:S(2)}) collective-permute-start(f32[24,1152]{1,0:T(8,128)S(1)} %get-tuple-element.52), channel_id=1, source_target_pairs={{0,3},{1,2},{2,1},{3,0},{4,7},{5,6},{6,5},{7,4},{8,11},{9,10},{10,... | collective-permute-start | bytes 331784 | tf_op jit(solution)/shard_map/ppermute | solution.py:359
  64.9 5.2 %all-to-all-done.shared = f32[32,1,128]{2,1,0:T(1,128)S(1)} async-done(((f32[32,1,128]{2,1,0:T(1,128)}), f32[32,1,128]{2,1,0:T(1,128)S(1)}, u32[]{:S(2)}, u32[]{:S(2)}) %all-to-all-start) | async-done | bytes 16416 | tf_op jit(solution)/shard_map/all_to_all | solution.py:458
  70.1 0.6 total.1
  70.9 1.1 %finish.1 = f32[12,4,2304]{2,1,0:T(4,128)} custom-call(s32[1]{0:T(128)} %bitcast.place, f32[12,4,2304]{2,1,0:T(4,128)S(1)} %bitcast.24, f32[24,1152]{1,0:T(8,128)S(1)} %fusion.2.local_pot, f32[24,1152]{1,0:T(8,128)S(1)} %get-tuple-element.50.refs_0_, f32[24,1152]{1,0:T(8,128)S(1)} %collective-permute-done.15.refs_1_, ...), custom_call_target="tpu_custom_call" | custom-call | tf_op jit(solution)/shard_map/finish/pallas_call | solution.py:347
  (57 shorter events, 3.0 us)
Async XLA Ops:
  0.6 1.0 %copy-start = (f32[4,12,2304]{2,0,1:T(4,128)S(1)}, f32[4,12,2304]{2,0,1:T(4,128)}, u32[]{:S(2)}) copy-start(f32[4,12,2304]{2,0,1:T(4,128)} %param.10) | copy-start | bytes 1327108
  1.9 11.0 %collective-permute-start = (f32[24,1152]{1,0:T(8,128)S(1)}, f32[24,1152]{1,0:T(8,128)S(1)}, u32[]{:S(2)}, u32[]{:S(2)}) collective-permute-start(f32[24,1152]{1,0:T(8,128)S(1)} %get-tuple-element.29), channel_id=1, source_target_pairs={{0,1},{1,0},{2,3},{3,2},{4,5},{5,4},{6,7},{7,6},{8,9},{9,8},{10,11... | collective-permute-start | bytes 331784 | tf_op jit(solution)/shard_map/ppermute | solution.py:359
  2.4 6.5 %collective-permute-start.1 = (f32[24,1152]{1,0:T(8,128)S(1)}, f32[24,1152]{1,0:T(8,128)S(1)}, u32[]{:S(2)}, u32[]{:S(2)}) collective-permute-start(f32[24,1152]{1,0:T(8,128)S(1)} %get-tuple-element.30), channel_id=1, source_target_pairs={{0,2},{1,3},{2,0},{3,1},{4,6},{5,7},{6,4},{7,5},{8,10},{9,11},{10,... | collective-permute-start | bytes 331784 | tf_op jit(solution)/shard_map/ppermute | solution.py:359
  5.0 5.8 %collective-permute-start.2 = (f32[24,1152]{1,0:T(8,128)S(1)}, f32[24,1152]{1,0:T(8,128)S(1)}, u32[]{:S(2)}, u32[]{:S(2)}) collective-permute-start(f32[24,1152]{1,0:T(8,128)S(1)} %get-tuple-element.31), channel_id=1, source_target_pairs={{0,3},{1,2},{2,1},{3,0},{4,7},{5,6},{6,5},{7,4},{8,11},{9,10},{10,... | collective-permute-start | bytes 331784 | tf_op jit(solution)/shard_map/ppermute | solution.py:359
  10.8 14.2 %collective-permute-start.6 = (f32[24,2304]{1,0:T(8,128)S(1)}, f32[24,2304]{1,0:T(8,128)S(1)}, u32[]{:S(2)}, u32[]{:S(2)}) collective-permute-start(f32[24,2304]{1,0:T(8,128)S(1)} %assemble.3.refs_1_), channel_id=1, source_target_pairs={{0,4},{8,0},{16,8},{24,16},{28,24},{20,28},{12,20},{4,12},{1,5},{9... | collective-permute-start | bytes 663560 | tf_op jit(solution)/shard_map/ppermute | solution.py:389
  12.3 8.3 %collective-permute-start.4 = (f32[24,2304]{1,0:T(8,128)S(1)}, f32[24,2304]{1,0:T(8,128)S(1)}, u32[]{:S(2)}, u32[]{:S(2)}) collective-permute-start(f32[24,2304]{1,0:T(8,128)S(1)} %assemble.3.refs_1_), channel_id=1, source_target_pairs={{0,8},{8,16},{16,24},{24,28},{28,20},{20,12},{12,4},{4,0},{1,9},{9... | collective-permute-start | bytes 663560 | tf_op jit(solution)/shard_map/ppermute | solution.py:389
  12.9 2.1 %copy-start.7 = (s32[8,2]{0,1:T(2,128)S(1)}, s32[8,2]{0,1:T(2,128)}, u32[]{:S(2)}) copy-start(s32[8,2]{0,1:T(2,128)} %param.11) | copy-start | bytes 196
  12.9 12.1 %collective-permute-start.5 = (f32[24,2304]{1,0:T(8,128)S(1)}, f32[24,2304]{1,0:T(8,128)S(1)}, u32[]{:S(2)}, u32[]{:S(2)}) collective-permute-start(f32[24,2304]{1,0:T(8,128)S(1)} %assemble.2.refs_0_), channel_id=1, source_target_pairs={{0,4},{8,0},{16,8},{24,16},{28,24},{20,28},{12,20},{4,12},{1,5},{9... | collective-permute-start | bytes 663560 | tf_op jit(solution)/shard_map/ppermute | solution.py:389
  14.4 10.0 %collective-permute-start.3 = (f32[24,2304]{1,0:T(8,128)S(1)}, f32[24,2304]{1,0:T(8,128)S(1)}, u32[]{:S(2)}, u32[]{:S(2)}) collective-permute-start(f32[24,2304]{1,0:T(8,128)S(1)} %assemble.2.refs_0_), channel_id=1, source_target_pairs={{0,8},{8,16},{16,24},{24,28},{28,20},{20,12},{12,4},{4,0},{1,9},{9... | collective-permute-start | bytes 663560 | tf_op jit(solution)/shard_map/ppermute | solution.py:389
  15.0 0.7 copy-start.8
  16.3 10.5 %copy-start.2 = (f32[96,2304]{1,0:T(8,128)S(1)}, f32[96,2304]{1,0:T(8,128)}, u32[]{:S(2)}) copy-start(f32[96,2304]{1,0:T(8,128)} %constant.116.clone.table) | copy-start | bytes 2654212
  24.5 2.3 %copy-start.3 = (bf16[192,48]{1,0:T(8,128)(2,1)S(1)}, bf16[192,48]{1,0:T(8,128)(2,1)}, u32[]{:S(2)}) copy-start(bf16[192,48]{1,0:T(8,128)(2,1)} %constant.115.clone.z_fwd) | copy-start | bytes 55300
  24.5 2.3 %copy-start.4 = (bf16[48,288]{1,0:T(8,128)(2,1)S(1)}, bf16[48,288]{1,0:T(8,128)(2,1)}, u32[]{:S(2)}) copy-start(bf16[48,288]{1,0:T(8,128)(2,1)} %constant.117.clone.z_inv) | copy-start | bytes 82948
  24.5 2.3 %copy-start.5 = (bf16[96,48]{1,0:T(8,128)(2,1)S(1)}, bf16[96,48]{1,0:T(8,128)(2,1)}, u32[]{:S(2)}) copy-start(bf16[96,48]{1,0:T(8,128)(2,1)} %constant.118.clone.y_inv) | copy-start | bytes 27652
  24.5 2.3 %copy-start.6 = (bf16[48,144]{1,0:T(8,128)(2,1)S(1)}, bf16[48,144]{1,0:T(8,128)(2,1)}, u32[]{:S(2)}) copy-start(bf16[48,144]{1,0:T(8,128)(2,1)} %constant.114.clone.y_fwd) | copy-start | bytes 41476
  24.5 11.4 %collective-permute-start.7 = (f32[48,2304]{1,0:T(8,128)S(1)}, f32[48,2304]{1,0:T(8,128)S(1)}, u32[]{:S(2)}, u32[]{:S(2)}) collective-permute-start(f32[48,2304]{1,0:T(8,128)S(1)} %join.5.refs_1_.other_ref), channel_id=1, source_target_pairs={{0,8},{8,16},{16,24},{24,28},{28,20},{20,12},{12,4},{4,0},{1,9},{9... | collective-permute-start | bytes 1327112 | tf_op jit(solution)/shard_map/ppermute | solution.py:389
  25.0 11.1 %collective-permute-start.8 = (f32[48,2304]{1,0:T(8,128)S(1)}, f32[48,2304]{1,0:T(8,128)S(1)}, u32[]{:S(2)}, u32[]{:S(2)}) collective-permute-start(f32[48,2304]{1,0:T(8,128)S(1)} %join.6.refs_2_.other_ref), channel_id=1, source_target_pairs={{0,4},{8,0},{16,8},{24,16},{28,24},{20,28},{12,20},{4,12},{1,5},{9... | collective-permute-start | bytes 1327112 | tf_op jit(solution)/shard_map/ppermute | solution.py:389
  35.9 10.4 %collective-permute-start.9 = (f32[48,2304]{1,0:T(8,128)S(1)}, f32[48,2304]{1,0:T(8,128)S(1)}, u32[]{:S(2)}, u32[]{:S(2)}) collective-permute-start(f32[48,2304]{1,0:T(8,128)S(1)} %collective-permute-done.7.refs_3_.other_ref), channel_id=1, source_target_pairs={{0,8},{8,16},{16,24},{24,28},{28,20},{20,12},{12,4},{4,0},{1,9},{9... | collective-permute-start | bytes 1327112 | tf_op jit(solution)/shard_map/ppermute | solution.py:389
  36.2 10.5 %collective-permute-start.10 = (f32[48,2304]{1,0:T(8,128)S(1)}, f32[48,2304]{1,0:T(8,128)S(1)}, u32[]{:S(2)}, u32[]{:S(2)}) collective-permute-start(f32[48,2304]{1,0:T(8,128)S(1)} %collective-permute-done.8.refs_4_.other_ref), channel_id=1, source_target_pairs={{0,4},{8,0},{16,8},{24,16},{28,24},{20,28},{12,20},{4,12},{1,5},{9... | collective-permute-start | bytes 1327112 | tf_op jit(solution)/shard_map/ppermute | solution.py:389
  46.3 6.0 %collective-permute-start.11 = (f32[24,2304]{1,0:T(8,128)S(1)}, f32[24,2304]{1,0:T(8,128)S(1)}, u32[]{:S(2)}, u32[]{:S(2)}) collective-permute-start(f32[24,2304]{1,0:T(8,128)S(1)} %slice.20), channel_id=1, source_target_pairs={{0,8},{8,16},{16,24},{24,28},{28,20},{20,12},{12,4},{4,0},{1,9},{9... | collective-permute-start | bytes 663560 | tf_op jit(solution)/shard_map/ppermute | solution.py:389
  46.7 6.0 %collective-permute-start.12 = (f32[24,2304]{1,0:T(8,128)S(1)}, f32[24,2304]{1,0:T(8,128)S(1)}, u32[]{:S(2)}, u32[]{:S(2)}) collective-permute-start(f32[24,2304]{1,0:T(8,128)S(1)} %slice.21), channel_id=1, source_target_pairs={{0,4},{8,0},{16,8},{24,16},{28,24},{20,28},{12,20},{4,12},{1,5},{9... | collective-permute-start | bytes 663560 | tf_op jit(solution)/shard_map/ppermute | solution.py:389
  53.0 1.5 %collective-permute-start.13 = (f32[2,24,1152]{2,1,0:T(8,128)S(1)}, f32[2,24,1152]{2,1,0:T(8,128)S(1)}, u32[]{:S(2)}, u32[]{:S(2)}) collective-permute-start(f32[2,24,1152]{2,1,0:T(8,128)S(1)} %get-tuple-element.34), channel_id=1, source_target_pairs={{0,1},{1,0},{2,3},{3,2},{4,5},{5,4},{6,7},{7,6},{8,9},{9,8},{10,11... | collective-permute-start | bytes 663560 | tf_op jit(solution)/shard_map/ppermute | solution.py:359
  54.5 16.3 %copy-start.1 = (f32[4,12,2304]{2,0,1:T(4,128)S(1)}, f32[4,12,2304]{2,0,1:T(4,128)}, u32[]{:S(2)}) copy-start(f32[4,12,2304]{2,0,1:T(4,128)} %param.10) | copy-start | bytes 1327108
  54.5 16.2 %collective-permute-start.14 = (f32[48,1152]{1,0:T(8,128)S(1)}, f32[48,1152]{1,0:T(8,128)S(1)}, u32[]{:S(2)}, u32[]{:S(2)}) collective-permute-start(f32[48,1152]{1,0:T(8,128)S(1)} %pack.1), channel_id=1, source_target_pairs={{0,2},{1,3},{2,0},{3,1},{4,6},{5,7},{6,4},{7,5},{8,10},{9,11},{10,... | collective-permute-start | bytes 663560 | tf_op jit(solution)/shard_map/ppermute | solution.py:359
  56.4 13.7 %all-to-all-start = ((f32[32,1,128]{2,1,0:T(1,128)}), f32[32,1,128]{2,1,0:T(1,128)S(1)}, u32[]{:S(2)}, u32[]{:S(2)}) async-start(f32[32,1,128]{2,1,0:T(1,128)} %get-tuple-element.53), calls=%async_computation | async-start | bytes 32768 | tf_op jit(solution)/shard_map/all_to_all | solution.py:458
  63.0 7.8 %collective-permute-start.15 = (f32[24,1152]{1,0:T(8,128)S(1)}, f32[24,1152]{1,0:T(8,128)S(1)}, u32[]{:S(2)}, u32[]{:S(2)}) collective-permute-start(f32[24,1152]{1,0:T(8,128)S(1)} %get-tuple-element.51), channel_id=1, source_target_pairs={{0,1},{1,0},{2,3},{3,2},{4,5},{5,4},{6,7},{7,6},{8,9},{9,8},{10,11... | collective-permute-start | bytes 331784 | tf_op jit(solution)/shard_map/ppermute | solution.py:359
  63.3 7.5 %collective-permute-start.16 = (f32[24,1152]{1,0:T(8,128)S(1)}, f32[24,1152]{1,0:T(8,128)S(1)}, u32[]{:S(2)}, u32[]{:S(2)}) collective-permute-start(f32[24,1152]{1,0:T(8,128)S(1)} %get-tuple-element.52), channel_id=1, source_target_pairs={{0,3},{1,2},{2,1},{3,0},{4,7},{5,6},{6,5},{7,4},{8,11},{9,10},{10,... | collective-permute-start | bytes 331784 | tf_op jit(solution)/shard_map/ppermute | solution.py:359

commit v8 on v7

--- a/solution.py
+++ b/solution.py
@@ -15,6 +15,8 @@
 NY = 48
 NZ = 48
 NZP = 96
+SIDE_X = NX // 2
+GAP = 64
 
 
 slater_coeff = -((3.0 / math.pi) ** (1.0 / 3.0))
@@ -45,8 +47,11 @@
 
 
 def tall(matrix):
-    high, low = split_table(matrix)
-    return np.concatenate([high, low], axis=0)
+    rows, cols = matrix.shape
+    placed = np.zeros((2 * rows, 2 * GAP))
+    placed[:rows, :cols] = matrix
+    placed[rows:, GAP : GAP + cols] = matrix
+    return np.concatenate(split_table(placed), axis=0)
 
 
 def wavenumber_sq(length):
@@ -65,12 +70,15 @@
     kernel_table = 4.0 * math.pi / (NX * NY * NZP) / (total + screening * screening)
     y_matrix = cas(y_cells, y_cells, NY)
     forward = jnp.asarray(np.stack([wide(cas(x_waves, held, NX)) for held in held_x]))
-    backward = jnp.asarray(np.stack([wide(cas(held, x_waves, NX)) for held in held_x]))
+    quads = 4 * (x_waves[:SIDE_X] // 2) + x_waves[:SIDE_X] % 2
+    kept = np.concatenate([quads, quads + 2])
+    backward = jnp.asarray(np.stack([wide(cas(held, kept, NX)) for held in held_x]))
+    kernel_table = np.pad(kernel_table, ((0, 0), (0, 0), (0, GAP - NY)))
     return (
         lax.dynamic_index_in_dim(forward, slab_index, 0, keepdims=False),
         jnp.asarray(wide(y_matrix)),
         jnp.asarray(tall(cas(z_waves, z_cells, NZP))),
-        jnp.asarray(kernel_table.reshape(NZP, NX * NY).astype(np.float32)),
+        jnp.asarray(kernel_table.reshape(NZP, NX * GAP).astype(np.float32)),
         jnp.asarray(wide(cas(z_cells, z_waves, NZP))),
         jnp.asarray(tall(y_matrix)),
         lax.dynamic_index_in_dim(backward, slab_index, 0, keepdims=False),
@@ -127,36 +135,56 @@
         other = other_ref[...]
         density = own_ref[...] * other
         spectrum = apply_left(x_fwd[...], density)
+        lines[...] = jnp.zeros_like(lines)
         for y in range(NY):
-            lines[y * NX : (y + 1) * NX, :] = spectrum[:, y * NZ : (y + 1) * NZ]
-        for q in range(NX):
-            plane = apply_left(y_fwd[...], lines[pl.ds(q, NY, stride=NX), :])
+            rows = slice(y * SIDE_X, (y + 1) * SIDE_X)
+            cols = slice(y * NZ, (y + 1) * NZ)
+            lines[rows, :NZ] = spectrum[:SIDE_X, cols]
+            lines[rows, GAP : GAP + NZ] = spectrum[SIDE_X:, cols]
+        for q in range(SIDE_X):
+            plane = apply_left(y_fwd[...], lines[pl.ds(q, NY, stride=SIDE_X), :])
             high, low = split(plane)
-            high_rows[q * NY : (q + 1) * NY, :] = high
-            low_rows[q * NY : (q + 1) * NY, :] = low
-        spectrum = apply_rows(z_fwd[...], high_rows[...], low_rows[...])
-        weighted = spectrum * table[...]
-        products = jnp.sum(spectrum * weighted, axis=0, keepdims=True)
-        folded = products[:, :128]
-        for start in range(128, NX * NY, 128):
-            folded = folded + products[:, start : start + 128]
+            rows = slice(q * GAP, q * GAP + NY)
+            pad = slice(q * GAP + NY, (q + 1) * GAP)
+            high_rows[rows, :] = high
+            low_rows[rows, :] = low
+            high_rows[pad, :] = jnp.zeros((GAP - NY, 2 * GAP), jnp.bfloat16)
+            low_rows[pad, :] = jnp.zeros((GAP - NY, 2 * GAP), jnp.bfloat16)
+        both = apply_rows(z_fwd[...], high_rows[...], low_rows[...])
+        width = SIDE_X * GAP
+        inner = []
+        folded = jnp.zeros((1, 128), jnp.float32)
+        for side in range(2):
+            spectrum = both[side * NZP : (side + 1) * NZP]
+            weighted = spectrum * table[:, side * width : (side + 1) * width]
+            products = jnp.sum(spectrum * weighted, axis=0, keepdims=True)
+            for start in range(0, width, 128):
+                folded = folded + products[:, start : start + 128]
+            inner.append(apply_left(z_inv[...], weighted))
         energy_out[...] = jnp.broadcast_to(
             energy_in[...] + request_weight * folded, energy_out.shape
         )
-        spectrum = apply_left(z_inv[...], weighted)
-        for q in range(NX):
-            high, low = split(spectrum[:, q * NY : (q + 1) * NY])
-            high_rows[q * NZ : (q + 1) * NZ, :] = high
-            low_rows[q * NZ : (q + 1) * NZ, :] = low
-        spectrum = apply_rows(y_inv[...], high_rows[...], low_rows[...])
-        for q in range(NX):
-            lines[q * NY : (q + 1) * NY, :] = spectrum[:, q * NZ : (q + 1) * NZ]
+        for side in range(2):
+            for pair in range(SIDE_X // 2):
+                high, low = split(inner[side][:, pair * 2 * GAP : (pair + 1) * 2 * GAP])
+                first = (side * (SIDE_X // 2) + pair) * GAP
+                high_rows[first : first + NZ, :] = high
+                low_rows[first : first + NZ, :] = low
+        both = apply_rows(y_inv[...], high_rows[...], low_rows[...])
+        for odd in range(2):
+            for pair in range(SIDE_X // 2):
+                first = (2 * pair + odd) * NY
+                lines[first : first + NY, :] = both[
+                    odd * NY : (odd + 1) * NY, pair * 2 * GAP : (pair + 1) * 2 * GAP
+                ]
         for y in range(NY):
-            field[:, y * NZ : (y + 1) * NZ] = apply_left(
-                x_inv[...], lines[pl.ds(y, NX, stride=NY), :]
-            )
+            plane = lines[pl.ds(y, SIDE_X, stride=NY), :]
+            cols = slice(y * NZ, (y + 1) * NZ)
+            field[:SIDE_X, cols] = plane[:, :NZ]
+            field[SIDE_X:, cols] = plane[:, GAP : GAP + NZ]
+        potential = apply_left(x_inv[...], field[...])
         store_force(
-            force_refs, force_in[...] - (exchange_mix * total_weight) * (field[...] * other)
+            force_refs, force_in[...] - (exchange_mix * total_weight) * (potential * other)
         )
 
 
@@ -176,9 +204,9 @@
         in_specs=in_vmem(5 + len(tables)),
         out_specs=in_vmem(1 + pieces),
         scratch_shapes=[
-            pltpu.VMEM((NX * NY, NZ), jnp.float32),
-            pltpu.VMEM((NX * NY, NZ), jnp.bfloat16),
-            pltpu.VMEM((NX * NY, NZ), jnp.bfloat16),
+            pltpu.VMEM((SIDE_X * NY, 2 * GAP), jnp.float32),
+            pltpu.VMEM((SIDE_X * GAP, 2 * GAP), jnp.bfloat16),
+            pltpu.VMEM((SIDE_X * GAP, 2 * GAP), jnp.bfloat16),
             pltpu.VMEM((NX, NY * NZ), jnp.float32),
         ],
         input_output_aliases={3 + len(tables): 1} if pieces == 1 else {},

time: 72.2 us -> 71.4 us (0.989)
  waiting for transfers between devices: 32.8 us -> 34.8 us
  Pallas kernels: 10.8 us -> 9.28 us
  starting transfers between devices: 24.1 us -> 23.2 us
    ppermute x10, waiting for transfers between devices: 22.2 us -> 24.2 us  [shift(): return lax.ppermute(value, 'band', moves)]
    pallas_call x7, Pallas kernels: 8.39 us -> 6.84 us  [pair_step(): pl.pallas_call(functools.partial(pair_kernel, slot), out_shape=outs, in_s...]
    all_to_all x1, starting transfers between devices: 6.6 us -> 5.77 us  [body(): shared = lax.all_to_all(energy, ('band', 'slab'), 0, 0)]
  transfers between devices with their start and end apart: 18 -> 18, of which waited for: 10 -> 10; matrix products, arithmetic and copies ran while one was open for 2% -> 2% of each run, Pallas kernels for 13% -> 11%
where the time goes in v8:
time: 71.4 us; the launch traced here: 71.1 us
  waiting for transfers between devices  34.8 us (49%)
  starting transfers between devices  23.2 us (32%)
  Pallas kernels  9.28 us (13%)
  local copies, waits for them, and re-layouts  2.18 us (3%)
  between operations  0.93 us (1%)
    ppermute x10, waiting for transfers between devices, shift(): return lax.ppermute(value, 'band', moves)  24.2 us
    ppermute x10, starting transfers between devices, shift(): return lax.ppermute(value, 'band', moves)  10.4 us
    ppermute x7, starting transfers between devices, slab_swap(): return lax.ppermute(value, 'slab', [(i, i ^ reach) for i in range(size)])  7.03 us
    pallas_call x7, Pallas kernels, pair_step(): pl.pallas_call(functools.partial(pair_kernel, slot), out_shape=outs, in_s...  6.84 us
    all_to_all x1, starting transfers between devices, body(): shared = lax.all_to_all(energy, ('band', 'slab'), 0, 0)  5.77 us
    ppermute x7, waiting for transfers between devices, slab_swap(): return lax.ppermute(value, 'slab', [(i, i ^ reach) for i in range(size)])  5.44 us
    all_to_all x1, waiting for transfers between devices, body(): shared = lax.all_to_all(energy, ('band', 'slab'), 0, 0)  5.15 us
  transfers between devices with their start and end apart: 18, of which 10 were waited for; matrix products, arithmetic and copies ran while one was open for 2% of the time, Pallas kernels for 11%

profile of v8, /device:TPU:0, one launch (start us, length us, event | category | flops | bytes accessed | tf_op | source)
XLA Modules:
  0.0 71.1 jit_solution(12057239597977417475)
XLA Ops:
  0.6 1.0 %copy-done = f32[4,12,2304]{2,0,1:T(4,128)S(1)} copy-done((f32[4,12,2304]{2,0,1:T(4,128)S(1)}, f32[4,12,2304]{2,0,1:T(4,128)}, u32[]{:S(2)}) %copy-start) | copy-done | bytes 442392
  1.9 0.6 collective-permute-start
  2.4 2.6 %collective-permute-start.1 = (f32[24,1152]{1,0:T(8,128)S(1)}, f32[24,1152]{1,0:T(8,128)S(1)}, u32[]{:S(2)}, u32[]{:S(2)}) collective-permute-start(f32[24,1152]{1,0:T(8,128)S(1)} %get-tuple-element.30), channel_id=1, source_target_pairs={{0,2},{1,3},{2,0},{3,1},{4,6},{5,7},{6,4},{7,5},{8,10},{9,11},{10,... | collective-permute-start | bytes 331784 | tf_op jit(solution)/shard_map/ppermute | solution.py:387
  5.2 0.8 %dynamic-slice_bitcast_fusion = (bf16[48,144]{1,0:T(8,128)(2,1)S(1)}, bf16[48,144]{1,0:T(8,128)(2,1)S(1)}) fusion(bf16[4,48,144]{2,1,0:T(8,128)(2,1)} %constant.113.clone, s32[]{:T(128)S(6)} %select_n.110, bf16[4,48,144]{2,1,0:T(8,128)(2,1)} %constant.112.clone), kind=kLoop, calls=%fused_computation.6 | loop fusion | bytes 55300 | tf_op jit(solution)/shard_map/jit(dynamic_index_in_dim)/squeeze | solution.py:84
  6.0 2.9 %collective-permute-done.1.refs_0_ = f32[24,1152]{1,0:T(8,128)S(1)} collective-permute-done((f32[24,1152]{1,0:T(8,128)S(1)}, f32[24,1152]{1,0:T(8,128)S(1)}, u32[]{:S(2)}, u32[]{:S(2)}) %collective-permute-start.1) | collective-permute-done | bytes 110624 | tf_op jit(solution)/shard_map/ppermute | solution.py:387
  8.9 1.8 %collective-permute-done.2.refs_1_ = f32[24,1152]{1,0:T(8,128)S(1)} collective-permute-done((f32[24,1152]{1,0:T(8,128)S(1)}, f32[24,1152]{1,0:T(8,128)S(1)}, u32[]{:S(2)}, u32[]{:S(2)}) %collective-permute-start.2) | collective-permute-done | bytes 110624 | tf_op jit(solution)/shard_map/ppermute | solution.py:387
  10.8 1.5 %collective-permute-start.6 = (f32[24,2304]{1,0:T(8,128)S(1)}, f32[24,2304]{1,0:T(8,128)S(1)}, u32[]{:S(2)}, u32[]{:S(2)}) collective-permute-start(f32[24,2304]{1,0:T(8,128)S(1)} %assemble.3.refs_1_), channel_id=1, source_target_pairs={{0,4},{8,0},{16,8},{24,16},{28,24},{20,28},{12,20},{4,12},{1,5},{9... | collective-permute-start | bytes 663560 | tf_op jit(solution)/shard_map/ppermute | solution.py:417
  12.3 0.6 collective-permute-start.4
  12.9 1.5 %collective-permute-start.5 = (f32[24,2304]{1,0:T(8,128)S(1)}, f32[24,2304]{1,0:T(8,128)S(1)}, u32[]{:S(2)}, u32[]{:S(2)}) collective-permute-start(f32[24,2304]{1,0:T(8,128)S(1)} %assemble.2.refs_0_), channel_id=1, source_target_pairs={{0,4},{8,0},{16,8},{24,16},{28,24},{20,28},{12,20},{4,12},{1,5},{9... | collective-permute-start | bytes 663560 | tf_op jit(solution)/shard_map/ppermute | solution.py:417
  14.4 0.6 collective-permute-start.3
  15.8 4.8 %collective-permute-done.4.refs_1_ = f32[24,2304]{1,0:T(8,128)S(1)} collective-permute-done((f32[24,2304]{1,0:T(8,128)S(1)}, f32[24,2304]{1,0:T(8,128)S(1)}, u32[]{:S(2)}, u32[]{:S(2)}) %collective-permute-start.4) | collective-permute-done | bytes 221216 | tf_op jit(solution)/shard_map/ppermute | solution.py:417
  20.6 3.9 %collective-permute-done.3.refs_0_ = f32[24,2304]{1,0:T(8,128)S(1)} collective-permute-done((f32[24,2304]{1,0:T(8,128)S(1)}, f32[24,2304]{1,0:T(8,128)S(1)}, u32[]{:S(2)}, u32[]{:S(2)}) %collective-permute-start.3) | collective-permute-done | bytes 221216 | tf_op jit(solution)/shard_map/ppermute | solution.py:417
  24.5 0.5 collective-permute-start.7
  25.0 1.6 %collective-permute-start.8 = (f32[48,2304]{1,0:T(8,128)S(1)}, f32[48,2304]{1,0:T(8,128)S(1)}, u32[]{:S(2)}, u32[]{:S(2)}) collective-permute-start(f32[48,2304]{1,0:T(8,128)S(1)} %join.6.refs_2_.other_ref), channel_id=1, source_target_pairs={{0,4},{8,0},{16,8},{24,16},{28,24},{20,28},{12,20},{4,12},{1,5},{9... | collective-permute-start | bytes 1327112 | tf_op jit(solution)/shard_map/ppermute | solution.py:417
  26.9 2.7 %pair_step.8 = (f32[1,128]{1,0:T(1,128)S(1)}, f32[48,2304]{1,0:T(8,128)S(1)}) custom-call(f32[14,128]{1,0:T(8,128)S(1)} %broadcast_in_dim.73.weights, f32[48,2304]{1,0:T(8,128)S(1)} %join.4.refs_0_.own_ref, f32[48,2304]{1,0:T(8,128)S(1)} %join.6.refs_2_.other_ref, bf16[48,144]{1,0:T(8,128)(2,1)S(1)} %get-tuple-element.57.x_fwd, ...), custom_call_target="tpu_custom_call", output_to_operand_aliasing={{1}: (10, {})} | custom-call | flops 3221225472 | bytes 3145728 | tf_op jit(solution)/shard_map/pair_step/pallas_call | solution.py:201
  29.6 6.2 %collective-permute-done.7.refs_3_.other_ref = f32[48,2304]{1,0:T(8,128)S(1)} collective-permute-done((f32[48,2304]{1,0:T(8,128)S(1)}, f32[48,2304]{1,0:T(8,128)S(1)}, u32[]{:S(2)}, u32[]{:S(2)}) %collective-permute-start.7) | collective-permute-done | bytes 442400 | tf_op jit(solution)/shard_map/ppermute | solution.py:417
  36.1 1.7 %collective-permute-start.10 = (f32[48,2304]{1,0:T(8,128)S(1)}, f32[48,2304]{1,0:T(8,128)S(1)}, u32[]{:S(2)}, u32[]{:S(2)}) collective-permute-start(f32[48,2304]{1,0:T(8,128)S(1)} %collective-permute-done.8.refs_4_.other_ref), channel_id=1, source_target_pairs={{0,4},{8,0},{16,8},{24,16},{28,24},{20,28},{12,20},{4,12},{1,5},{9... | collective-permute-start | bytes 1327112 | tf_op jit(solution)/shard_map/ppermute | solution.py:417
  38.0 2.7 %pair_step.10 = (f32[1,128]{1,0:T(1,128)S(1)}, f32[48,2304]{1,0:T(8,128)S(1)}) custom-call(f32[14,128]{1,0:T(8,128)S(1)} %broadcast_in_dim.73.weights, f32[48,2304]{1,0:T(8,128)S(1)} %join.4.refs_0_.own_ref, f32[48,2304]{1,0:T(8,128)S(1)} %collective-permute-done.8.refs_4_.other_ref, ...), custom_call_target="tpu_custom_call", output_to_operand_aliasing={{1}: (10, {})} | custom-call | flops 3221225472 | bytes 3145728 | tf_op jit(solution)/shard_map/pair_step/pallas_call | solution.py:201
  40.7 5.6 %collective-permute-done.9.refs_5_.other_ref = f32[48,2304]{1,0:T(8,128)S(1)} collective-permute-done((f32[48,2304]{1,0:T(8,128)S(1)}, f32[48,2304]{1,0:T(8,128)S(1)}, u32[]{:S(2)}, u32[]{:S(2)}) %collective-permute-start.9) | collective-permute-done | bytes 442400 | tf_op jit(solution)/shard_map/ppermute | solution.py:417
  46.3 0.3 collective-permute-start.11
  46.6 1.8 %collective-permute-start.12 = (f32[24,2304]{1,0:T(8,128)S(1)}, f32[24,2304]{1,0:T(8,128)S(1)}, u32[]{:S(2)}, u32[]{:S(2)}) collective-permute-start(f32[24,2304]{1,0:T(8,128)S(1)} %slice.21), channel_id=1, source_target_pairs={{0,4},{8,0},{16,8},{24,16},{28,24},{20,28},{12,20},{4,12},{1,5},{9... | collective-permute-start | bytes 663560 | tf_op jit(solution)/shard_map/ppermute | solution.py:417
  48.9 3.4 %collective-permute-done.11.refs_0_ = f32[24,2304]{1,0:T(8,128)S(1)} collective-permute-done((f32[24,2304]{1,0:T(8,128)S(1)}, f32[24,2304]{1,0:T(8,128)S(1)}, u32[]{:S(2)}, u32[]{:S(2)}) %collective-permute-start.11) | collective-permute-done | bytes 221216 | tf_op jit(solution)/shard_map/ppermute | solution.py:417
  52.3 0.4 collective-permute-done.12.refs_1_
  53.0 0.8 %pair_step.13 = (f32[32,1,128]{2,1,0:T(1,128)}, f32[24,1152]{1,0:T(8,128)S(1)}, f32[24,1152]{1,0:T(8,128)S(1)}, f32[24,1152]{1,0:T(8,128)S(1)}, f32[24,1152]{1,0:T(8,128)S(1)}) custom-call(f32[14,128]{1,0:T(8,128)S(1)} %broadcast_in_dim.73.weights, f32[48,2304]{1,0:T(8,128)S(1)} %join.4.refs_0_.own_ref, f32[48,2304]{1,0:T(8,128)S(1)} %join.7.refs_7_.other_ref, ...), custom_call_target="tpu_custom_call" | custom-call | flops 3221225472 | bytes 3145728 | tf_op jit(solution)/shard_map/pair_step/pallas_call | solution.py:201
  53.8 0.7 collective-permute-done.13.theirs
  54.5 1.8 %collective-permute-start.14 = (f32[48,1152]{1,0:T(8,128)S(1)}, f32[48,1152]{1,0:T(8,128)S(1)}, u32[]{:S(2)}, u32[]{:S(2)}) collective-permute-start(f32[48,1152]{1,0:T(8,128)S(1)} %pack.1), channel_id=1, source_target_pairs={{0,2},{1,3},{2,0},{3,1},{4,6},{5,7},{6,4},{7,5},{8,10},{9,11},{10,... | collective-permute-start | bytes 663560 | tf_op jit(solution)/shard_map/ppermute | solution.py:387
  56.4 5.8 %all-to-all-start = ((f32[32,1,128]{2,1,0:T(1,128)}), f32[32,1,128]{2,1,0:T(1,128)S(1)}, u32[]{:S(2)}, u32[]{:S(2)}) async-start(f32[32,1,128]{2,1,0:T(1,128)} %get-tuple-element.53), calls=%async_computation | async-start | bytes 32768 | tf_op jit(solution)/shard_map/all_to_all | solution.py:486
  62.1 0.3 collective-permute-start.15
  62.5 1.6 %collective-permute-start.16 = (f32[24,1152]{1,0:T(8,128)S(1)}, f32[24,1152]{1,0:T(8,128)S(1)}, u32[]{:S(2)}, u32[]{:S(2)}) collective-permute-start(f32[24,1152]{1,0:T(8,128)S(1)} %get-tuple-element.52), channel_id=1, source_target_pairs={{0,3},{1,2},{2,1},{3,0},{4,7},{5,6},{6,5},{7,4},{8,11},{9,10},{10,... | collective-permute-start | bytes 331784 | tf_op jit(solution)/shard_map/ppermute | solution.py:387
  64.1 5.2 %all-to-all-done.shared = f32[32,1,128]{2,1,0:T(1,128)S(1)} async-done(((f32[32,1,128]{2,1,0:T(1,128)}), f32[32,1,128]{2,1,0:T(1,128)S(1)}, u32[]{:S(2)}, u32[]{:S(2)}) %all-to-all-start) | async-done | bytes 16416 | tf_op jit(solution)/shard_map/all_to_all | solution.py:486
  69.3 0.6 total.1
  70.0 1.1 %finish.1 = f32[12,4,2304]{2,1,0:T(4,128)} custom-call(s32[1]{0:T(128)} %bitcast.place, f32[12,4,2304]{2,1,0:T(4,128)S(1)} %bitcast.24, f32[24,1152]{1,0:T(8,128)S(1)} %fusion.2.local_pot, f32[24,1152]{1,0:T(8,128)S(1)} %get-tuple-element.50.refs_0_, f32[24,1152]{1,0:T(8,128)S(1)} %collective-permute-done.15.refs_1_, ...), custom_call_target="tpu_custom_call" | custom-call | tf_op jit(solution)/shard_map/finish/pallas_call | solution.py:375
  (57 shorter events, 2.9 us)
Async XLA Ops:
  0.6 1.0 %copy-start = (f32[4,12,2304]{2,0,1:T(4,128)S(1)}, f32[4,12,2304]{2,0,1:T(4,128)}, u32[]{:S(2)}) copy-start(f32[4,12,2304]{2,0,1:T(4,128)} %param.10) | copy-start | bytes 1327108
  1.9 11.0 %collective-permute-start = (f32[24,1152]{1,0:T(8,128)S(1)}, f32[24,1152]{1,0:T(8,128)S(1)}, u32[]{:S(2)}, u32[]{:S(2)}) collective-permute-start(f32[24,1152]{1,0:T(8,128)S(1)} %get-tuple-element.29), channel_id=1, source_target_pairs={{0,1},{1,0},{2,3},{3,2},{4,5},{5,4},{6,7},{7,6},{8,9},{9,8},{10,11... | collective-permute-start | bytes 331784 | tf_op jit(solution)/shard_map/ppermute | solution.py:387
  2.4 6.5 %collective-permute-start.1 = (f32[24,1152]{1,0:T(8,128)S(1)}, f32[24,1152]{1,0:T(8,128)S(1)}, u32[]{:S(2)}, u32[]{:S(2)}) collective-permute-start(f32[24,1152]{1,0:T(8,128)S(1)} %get-tuple-element.30), channel_id=1, source_target_pairs={{0,2},{1,3},{2,0},{3,1},{4,6},{5,7},{6,4},{7,5},{8,10},{9,11},{10,... | collective-permute-start | bytes 331784 | tf_op jit(solution)/shard_map/ppermute | solution.py:387
  5.0 5.8 %collective-permute-start.2 = (f32[24,1152]{1,0:T(8,128)S(1)}, f32[24,1152]{1,0:T(8,128)S(1)}, u32[]{:S(2)}, u32[]{:S(2)}) collective-permute-start(f32[24,1152]{1,0:T(8,128)S(1)} %get-tuple-element.31), channel_id=1, source_target_pairs={{0,3},{1,2},{2,1},{3,0},{4,7},{5,6},{6,5},{7,4},{8,11},{9,10},{10,... | collective-permute-start | bytes 331784 | tf_op jit(solution)/shard_map/ppermute | solution.py:387
  5.0 10.0 %copy-start.7 = (s32[8,2]{0,1:T(2,128)S(1)}, s32[8,2]{0,1:T(2,128)}, u32[]{:S(2)}) copy-start(s32[8,2]{0,1:T(2,128)} %param.11) | copy-start | bytes 196
  5.0 10.1 %copy-start.8 = (s32[8,2]{0,1:T(2,128)S(1)}, s32[8,2]{0,1:T(2,128)}, u32[]{:S(2)}) copy-start(s32[8,2]{0,1:T(2,128)} %param.12) | copy-start | bytes 196
  10.8 14.2 %collective-permute-start.6 = (f32[24,2304]{1,0:T(8,128)S(1)}, f32[24,2304]{1,0:T(8,128)S(1)}, u32[]{:S(2)}, u32[]{:S(2)}) collective-permute-start(f32[24,2304]{1,0:T(8,128)S(1)} %assemble.3.refs_1_), channel_id=1, source_target_pairs={{0,4},{8,0},{16,8},{24,16},{28,24},{20,28},{12,20},{4,12},{1,5},{9... | collective-permute-start | bytes 663560 | tf_op jit(solution)/shard_map/ppermute | solution.py:417
  12.3 8.3 %collective-permute-start.4 = (f32[24,2304]{1,0:T(8,128)S(1)}, f32[24,2304]{1,0:T(8,128)S(1)}, u32[]{:S(2)}, u32[]{:S(2)}) collective-permute-start(f32[24,2304]{1,0:T(8,128)S(1)} %assemble.3.refs_1_), channel_id=1, source_target_pairs={{0,8},{8,16},{16,24},{24,28},{28,20},{20,12},{12,4},{4,0},{1,9},{9... | collective-permute-start | bytes 663560 | tf_op jit(solution)/shard_map/ppermute | solution.py:417
  12.9 13.8 %copy-start.2 = (f32[96,3072]{1,0:T(8,128)S(1)}, f32[96,3072]{1,0:T(8,128)}, u32[]{:S(2)}) copy-start(f32[96,3072]{1,0:T(8,128)} %constant.116.clone.table) | copy-start | bytes 3538948
  12.9 13.8 %copy-start.3 = (bf16[384,128]{1,0:T(8,128)(2,1)S(1)}, bf16[384,128]{1,0:T(8,128)(2,1)}, u32[]{:S(2)}) copy-start(bf16[384,128]{1,0:T(8,128)(2,1)} %constant.115.clone.z_fwd) | copy-start | bytes 294916
  12.9 12.0 %collective-permute-start.5 = (f32[24,2304]{1,0:T(8,128)S(1)}, f32[24,2304]{1,0:T(8,128)S(1)}, u32[]{:S(2)}, u32[]{:S(2)}) collective-permute-start(f32[24,2304]{1,0:T(8,128)S(1)} %assemble.2.refs_0_), channel_id=1, source_target_pairs={{0,4},{8,0},{16,8},{24,16},{28,24},{20,28},{12,20},{4,12},{1,5},{9... | collective-permute-start | bytes 663560 | tf_op jit(solution)/shard_map/ppermute | solution.py:417
  14.4 10.0 %collective-permute-start.3 = (f32[24,2304]{1,0:T(8,128)S(1)}, f32[24,2304]{1,0:T(8,128)S(1)}, u32[]{:S(2)}, u32[]{:S(2)}) collective-permute-start(f32[24,2304]{1,0:T(8,128)S(1)} %assemble.2.refs_0_), channel_id=1, source_target_pairs={{0,8},{8,16},{16,24},{24,28},{28,20},{20,12},{12,4},{4,0},{1,9},{9... | collective-permute-start | bytes 663560 | tf_op jit(solution)/shard_map/ppermute | solution.py:417
  15.8 11.0 %copy-start.4 = (bf16[192,128]{1,0:T(8,128)(2,1)S(1)}, bf16[192,128]{1,0:T(8,128)(2,1)}, u32[]{:S(2)}) copy-start(bf16[192,128]{1,0:T(8,128)(2,1)} %constant.118.clone.y_inv) | copy-start | bytes 147460
  15.8 11.0 %copy-start.5 = (bf16[48,288]{1,0:T(8,128)(2,1)S(1)}, bf16[48,288]{1,0:T(8,128)(2,1)}, u32[]{:S(2)}) copy-start(bf16[48,288]{1,0:T(8,128)(2,1)} %constant.117.clone.z_inv) | copy-start | bytes 82948
  15.8 11.0 %copy-start.6 = (bf16[48,144]{1,0:T(8,128)(2,1)S(1)}, bf16[48,144]{1,0:T(8,128)(2,1)}, u32[]{:S(2)}) copy-start(bf16[48,144]{1,0:T(8,128)(2,1)} %constant.114.clone.y_fwd) | copy-start | bytes 41476
  24.5 11.4 %collective-permute-start.7 = (f32[48,2304]{1,0:T(8,128)S(1)}, f32[48,2304]{1,0:T(8,128)S(1)}, u32[]{:S(2)}, u32[]{:S(2)}) collective-permute-start(f32[48,2304]{1,0:T(8,128)S(1)} %join.5.refs_1_.other_ref), channel_id=1, source_target_pairs={{0,8},{8,16},{16,24},{24,28},{28,20},{20,12},{12,4},{4,0},{1,9},{9... | collective-permute-start | bytes 1327112 | tf_op jit(solution)/shard_map/ppermute | solution.py:417
  25.0 11.1 %collective-permute-start.8 = (f32[48,2304]{1,0:T(8,128)S(1)}, f32[48,2304]{1,0:T(8,128)S(1)}, u32[]{:S(2)}, u32[]{:S(2)}) collective-permute-start(f32[48,2304]{1,0:T(8,128)S(1)} %join.6.refs_2_.other_ref), channel_id=1, source_target_pairs={{0,4},{8,0},{16,8},{24,16},{28,24},{20,28},{12,20},{4,12},{1,5},{9... | collective-permute-start | bytes 1327112 | tf_op jit(solution)/shard_map/ppermute | solution.py:417
  35.8 10.4 %collective-permute-start.9 = (f32[48,2304]{1,0:T(8,128)S(1)}, f32[48,2304]{1,0:T(8,128)S(1)}, u32[]{:S(2)}, u32[]{:S(2)}) collective-permute-start(f32[48,2304]{1,0:T(8,128)S(1)} %collective-permute-done.7.refs_3_.other_ref), channel_id=1, source_target_pairs={{0,8},{8,16},{16,24},{24,28},{28,20},{20,12},{12,4},{4,0},{1,9},{9... | collective-permute-start | bytes 1327112 | tf_op jit(solution)/shard_map/ppermute | solution.py:417
  36.1 10.5 %collective-permute-start.10 = (f32[48,2304]{1,0:T(8,128)S(1)}, f32[48,2304]{1,0:T(8,128)S(1)}, u32[]{:S(2)}, u32[]{:S(2)}) collective-permute-start(f32[48,2304]{1,0:T(8,128)S(1)} %collective-permute-done.8.refs_4_.other_ref), channel_id=1, source_target_pairs={{0,4},{8,0},{16,8},{24,16},{28,24},{20,28},{12,20},{4,12},{1,5},{9... | collective-permute-start | bytes 1327112 | tf_op jit(solution)/shard_map/ppermute | solution.py:417
  46.3 6.0 %collective-permute-start.11 = (f32[24,2304]{1,0:T(8,128)S(1)}, f32[24,2304]{1,0:T(8,128)S(1)}, u32[]{:S(2)}, u32[]{:S(2)}) collective-permute-start(f32[24,2304]{1,0:T(8,128)S(1)} %slice.20), channel_id=1, source_target_pairs={{0,8},{8,16},{16,24},{24,28},{28,20},{20,12},{12,4},{4,0},{1,9},{9... | collective-permute-start | bytes 663560 | tf_op jit(solution)/shard_map/ppermute | solution.py:417
  46.6 6.0 %collective-permute-start.12 = (f32[24,2304]{1,0:T(8,128)S(1)}, f32[24,2304]{1,0:T(8,128)S(1)}, u32[]{:S(2)}, u32[]{:S(2)}) collective-permute-start(f32[24,2304]{1,0:T(8,128)S(1)} %slice.21), channel_id=1, source_target_pairs={{0,4},{8,0},{16,8},{24,16},{28,24},{20,28},{12,20},{4,12},{1,5},{9... | collective-permute-start | bytes 663560 | tf_op jit(solution)/shard_map/ppermute | solution.py:417
  53.0 1.5 %collective-permute-start.13 = (f32[2,24,1152]{2,1,0:T(8,128)S(1)}, f32[2,24,1152]{2,1,0:T(8,128)S(1)}, u32[]{:S(2)}, u32[]{:S(2)}) collective-permute-start(f32[2,24,1152]{2,1,0:T(8,128)S(1)} %get-tuple-element.34), channel_id=1, source_target_pairs={{0,1},{1,0},{2,3},{3,2},{4,5},{5,4},{6,7},{7,6},{8,9},{9,8},{10,11... | collective-permute-start | bytes 663560 | tf_op jit(solution)/shard_map/ppermute | solution.py:387
  53.8 16.2 %copy-start.1 = (f32[4,12,2304]{2,0,1:T(4,128)S(1)}, f32[4,12,2304]{2,0,1:T(4,128)}, u32[]{:S(2)}) copy-start(f32[4,12,2304]{2,0,1:T(4,128)} %param.10) | copy-start | bytes 1327108
  54.5 15.3 %collective-permute-start.14 = (f32[48,1152]{1,0:T(8,128)S(1)}, f32[48,1152]{1,0:T(8,128)S(1)}, u32[]{:S(2)}, u32[]{:S(2)}) collective-permute-start(f32[48,1152]{1,0:T(8,128)S(1)} %pack.1), channel_id=1, source_target_pairs={{0,2},{1,3},{2,0},{3,1},{4,6},{5,7},{6,4},{7,5},{8,10},{9,11},{10,... | collective-permute-start | bytes 663560 | tf_op jit(solution)/shard_map/ppermute | solution.py:387
  56.4 12.9 %all-to-all-start = ((f32[32,1,128]{2,1,0:T(1,128)}), f32[32,1,128]{2,1,0:T(1,128)S(1)}, u32[]{:S(2)}, u32[]{:S(2)}) async-start(f32[32,1,128]{2,1,0:T(1,128)} %get-tuple-element.53), calls=%async_computation | async-start | bytes 32768 | tf_op jit(solution)/shard_map/all_to_all | solution.py:486
  62.1 7.8 %collective-permute-start.15 = (f32[24,1152]{1,0:T(8,128)S(1)}, f32[24,1152]{1,0:T(8,128)S(1)}, u32[]{:S(2)}, u32[]{:S(2)}) collective-permute-start(f32[24,1152]{1,0:T(8,128)S(1)} %get-tuple-element.51), channel_id=1, source_target_pairs={{0,1},{1,0},{2,3},{3,2},{4,5},{5,4},{6,7},{7,6},{8,9},{9,8},{10,11... | collective-permute-start | bytes 331784 | tf_op jit(solution)/shard_map/ppermute | solution.py:387
  62.5 7.5 %collective-permute-start.16 = (f32[24,1152]{1,0:T(8,128)S(1)}, f32[24,1152]{1,0:T(8,128)S(1)}, u32[]{:S(2)}, u32[]{:S(2)}) collective-permute-start(f32[24,1152]{1,0:T(8,128)S(1)} %get-tuple-element.52), channel_id=1, source_target_pairs={{0,3},{1,2},{2,1},{3,0},{4,7},{5,6},{6,5},{7,4},{8,11},{9,10},{10,... | collective-permute-start | bytes 331784 | tf_op jit(solution)/shard_map/ppermute | solution.py:387

commit v9 on v8

--- a/solution.py
+++ b/solution.py
@@ -416,20 +416,19 @@
         moves = [(groups[p], groups[(p + by) % bands]) for p in range(bands)]
         return lax.ppermute(value, "band", moves)
 
-    came = [(shift(half, 1), shift(half, -1)) for half in halves]
+    def pass_on(halves, by):
+        return [shift(half, by) for half in halves]
+
+    ahead = behind = halves
     blocks = []
     steps = bands // 2 - 1
     for step in range(steps):
-        if step == 0:
-            ahead, behind = (join(*pair) for pair in zip(*came))
-        else:
-            ahead = shift(ahead, 1)
-            behind = shift(behind, -1)
-        blocks.append((ahead, group_at(position - step - 1)))
-        blocks.append((behind, group_at(position + step + 1)))
-    half = ahead.shape[0] // 2
-    head = shift(ahead[:half], 1)
-    tail = shift(behind[half:], -1)
+        ahead = pass_on(ahead, 1)
+        behind = pass_on(behind, -1)
+        blocks.append((join(*ahead), group_at(position - step - 1)))
+        blocks.append((join(*behind), group_at(position + step + 1)))
+    head = shift(ahead[0], 1)
+    tail = shift(behind[1], -1)
     blocks.append((join(head, tail), group_at(position + steps + 1)))
     return blocks
 

time: 71.4 us -> 73.4 us (1.028)
  waiting for transfers between devices: 34.8 us -> 29.5 us
  starting transfers between devices: 23.2 us -> 28 us
  local copies, waits for them, and re-layouts: 2.18 us -> 4.44 us
    ppermute x10 -> x14, starting transfers between devices: 10.4 us -> 18.4 us  [shift(): return lax.ppermute(value, 'band', moves)]
    ppermute x10 -> x14, waiting for transfers between devices: 24.2 us -> 18.9 us  [shift(): return lax.ppermute(value, 'band', moves)]
    all_to_all x1, starting transfers between devices: 5.77 us -> 3.17 us  [body(): shared = lax.all_to_all(energy, ('band', 'slab'), 0, 0)]
    unnamed x18 -> x20, local copies, waits for them, and re-layouts: 1.05 us -> 3.34 us
  transfers between devices with their start and end apart: 18 -> 22, of which waited for: 10 -> 10; matrix products, arithmetic and copies ran while one was open for 2% -> 2% of each run, Pallas kernels for 11% -> 11%
where the time goes in v9:
time: 73.4 us; the launch traced here: 73 us
  waiting for transfers between devices  29.5 us (40%)
  starting transfers between devices  28 us (38%)
  Pallas kernels  9.38 us (13%)
  local copies, waits for them, and re-layouts  4.44 us (6%)
  between operations  0.98 us (1%)
    ppermute x14, waiting for transfers between devices, shift(): return lax.ppermute(value, 'band', moves)  18.9 us
    ppermute x14, starting transfers between devices, shift(): return lax.ppermute(value, 'band', moves)  18.4 us
    pallas_call x7, Pallas kernels, pair_step(): pl.pallas_call(functools.partial(pair_kernel, slot), out_shape=outs, in_s...  6.84 us
    ppermute x7, starting transfers between devices, slab_swap(): return lax.ppermute(value, 'slab', [(i, i ^ reach) for i in range(size)])  6.47 us
    ppermute x7, waiting for transfers between devices, slab_swap(): return lax.ppermute(value, 'slab', [(i, i ^ reach) for i in range(size)])  5.44 us
    all_to_all x1, waiting for transfers between devices, body(): shared = lax.all_to_all(energy, ('band', 'slab'), 0, 0)  5.15 us
    unnamed x20, local copies, waits for them, and re-layouts  3.34 us
    all_to_all x1, starting transfers between devices, body(): shared = lax.all_to_all(energy, ('band', 'slab'), 0, 0)  3.17 us
  transfers between devices with their start and end apart: 22, of which 10 were waited for; matrix products, arithmetic and copies ran while one was open for 2% of the time, Pallas kernels for 11%

profile of v9, /device:TPU:0, one launch (start us, length us, event | category | flops | bytes accessed | tf_op | source)
XLA Modules:
  0.0 73.0 jit_solution(4785065960332048755)
XLA Ops:
  0.6 1.0 %copy-done = f32[4,12,2304]{2,0,1:T(4,128)S(1)} copy-done((f32[4,12,2304]{2,0,1:T(4,128)S(1)}, f32[4,12,2304]{2,0,1:T(4,128)}, u32[]{:S(2)}) %copy-start) | copy-done | bytes 442392
  2.4 2.6 %collective-permute-start.1 = (f32[24,1152]{1,0:T(8,128)S(1)}, f32[24,1152]{1,0:T(8,128)S(1)}, u32[]{:S(2)}, u32[]{:S(2)}) collective-permute-start(f32[24,1152]{1,0:T(8,128)S(1)} %get-tuple-element.30), channel_id=1, source_target_pairs={{0,2},{1,3},{2,0},{3,1},{4,6},{5,7},{6,4},{7,5},{8,10},{9,11},{10,... | collective-permute-start | bytes 331784 | tf_op jit(solution)/shard_map/ppermute | solution.py:387
  5.2 0.8 %dynamic-slice_bitcast_fusion = (bf16[48,144]{1,0:T(8,128)(2,1)S(1)}, bf16[48,144]{1,0:T(8,128)(2,1)S(1)}) fusion(bf16[4,48,144]{2,1,0:T(8,128)(2,1)} %constant.113.clone, s32[]{:T(128)S(6)} %select_n.110, bf16[4,48,144]{2,1,0:T(8,128)(2,1)} %constant.112.clone), kind=kLoop, calls=%fused_computation.6 | loop fusion | bytes 55300 | tf_op jit(solution)/shard_map/jit(dynamic_index_in_dim)/squeeze | solution.py:84
  6.0 2.9 %collective-permute-done.1.refs_0_ = f32[24,1152]{1,0:T(8,128)S(1)} collective-permute-done((f32[24,1152]{1,0:T(8,128)S(1)}, f32[24,1152]{1,0:T(8,128)S(1)}, u32[]{:S(2)}, u32[]{:S(2)}) %collective-permute-start.1) | collective-permute-done | bytes 110624 | tf_op jit(solution)/shard_map/ppermute | solution.py:387
  8.9 1.8 %collective-permute-done.2.refs_1_ = f32[24,1152]{1,0:T(8,128)S(1)} collective-permute-done((f32[24,1152]{1,0:T(8,128)S(1)}, f32[24,1152]{1,0:T(8,128)S(1)}, u32[]{:S(2)}, u32[]{:S(2)}) %collective-permute-start.2) | collective-permute-done | bytes 110624 | tf_op jit(solution)/shard_map/ppermute | solution.py:387
  10.8 1.5 %collective-permute-start.6 = (f32[24,2304]{1,0:T(8,128)S(1)}, f32[24,2304]{1,0:T(8,128)S(1)}, u32[]{:S(2)}, u32[]{:S(2)}) collective-permute-start(f32[24,2304]{1,0:T(8,128)S(1)} %assemble.3.refs_1_), channel_id=1, source_target_pairs={{0,4},{8,0},{16,8},{24,16},{28,24},{20,28},{12,20},{4,12},{1,5},{9... | collective-permute-start | bytes 663560 | tf_op jit(solution)/shard_map/ppermute | solution.py:417
  12.9 1.5 %collective-permute-start.5 = (f32[24,2304]{1,0:T(8,128)S(1)}, f32[24,2304]{1,0:T(8,128)S(1)}, u32[]{:S(2)}, u32[]{:S(2)}) collective-permute-start(f32[24,2304]{1,0:T(8,128)S(1)} %assemble.2.refs_0_), channel_id=1, source_target_pairs={{0,4},{8,0},{16,8},{24,16},{28,24},{20,28},{12,20},{4,12},{1,5},{9... | collective-permute-start | bytes 663560 | tf_op jit(solution)/shard_map/ppermute | solution.py:417
  14.4 0.6 collective-permute-start.3
  15.8 3.4 %collective-permute-done.6.refs_1_ = f32[24,2304]{1,0:T(8,128)S(1)} collective-permute-done((f32[24,2304]{1,0:T(8,128)S(1)}, f32[24,2304]{1,0:T(8,128)S(1)}, u32[]{:S(2)}, u32[]{:S(2)}) %collective-permute-start.6) | collective-permute-done | bytes 221216 | tf_op jit(solution)/shard_map/ppermute | solution.py:417
  19.2 1.4 %collective-permute-start.10 = (f32[24,2304]{1,0:T(8,128)S(1)}, f32[24,2304]{1,0:T(8,128)S(1)}, u32[]{:S(2)}, u32[]{:S(2)}) collective-permute-start(f32[24,2304]{1,0:T(8,128)S(1)} %collective-permute-done.6.refs_1_), channel_id=1, source_target_pairs={{0,4},{8,0},{16,8},{24,16},{28,24},{20,28},{12,20},{4,12},{1,5},{9... | collective-permute-start | bytes 663560 | tf_op jit(solution)/shard_map/ppermute | solution.py:417
  21.2 4.1 %collective-permute-done.3.refs_0_ = f32[24,2304]{1,0:T(8,128)S(1)} collective-permute-done((f32[24,2304]{1,0:T(8,128)S(1)}, f32[24,2304]{1,0:T(8,128)S(1)}, u32[]{:S(2)}, u32[]{:S(2)}) %collective-permute-start.3) | collective-permute-done | bytes 221216 | tf_op jit(solution)/shard_map/ppermute | solution.py:417
  25.5 0.8 %copy-done.4 = bf16[192,128]{1,0:T(8,128)(2,1)S(1)} copy-done((bf16[192,128]{1,0:T(8,128)(2,1)S(1)}, bf16[192,128]{1,0:T(8,128)(2,1)}, u32[]{:S(2)}) %copy-start.4) | copy-done | bytes 49176
  26.3 0.8 %copy-done.5 = bf16[48,288]{1,0:T(8,128)(2,1)S(1)} copy-done((bf16[48,288]{1,0:T(8,128)(2,1)S(1)}, bf16[48,288]{1,0:T(8,128)(2,1)}, u32[]{:S(2)}) %copy-start.5) | copy-done | bytes 27672
  27.0 0.7 %copy-done.7 = bf16[48,144]{1,0:T(8,128)(2,1)S(1)} copy-done((bf16[48,144]{1,0:T(8,128)(2,1)S(1)}, bf16[48,144]{1,0:T(8,128)(2,1)}, u32[]{:S(2)}) %copy-start.7) | copy-done | bytes 13848
  27.9 1.6 %collective-permute-start.9 = (f32[24,2304]{1,0:T(8,128)S(1)}, f32[24,2304]{1,0:T(8,128)S(1)}, u32[]{:S(2)}, u32[]{:S(2)}) collective-permute-start(f32[24,2304]{1,0:T(8,128)S(1)} %collective-permute-done.5.refs_0_), channel_id=1, source_target_pairs={{0,4},{8,0},{16,8},{24,16},{28,24},{20,28},{12,20},{4,12},{1,5},{9... | collective-permute-start | bytes 663560 | tf_op jit(solution)/shard_map/ppermute | solution.py:417
  29.6 1.6 %collective-permute-start.7 = (f32[24,2304]{1,0:T(8,128)S(1)}, f32[24,2304]{1,0:T(8,128)S(1)}, u32[]{:S(2)}, u32[]{:S(2)}) collective-permute-start(f32[24,2304]{1,0:T(8,128)S(1)} %collective-permute-done.3.refs_0_), channel_id=1, source_target_pairs={{0,8},{8,16},{16,24},{24,28},{28,20},{20,12},{12,4},{4,0},{1,9},{9... | collective-permute-start | bytes 663560 | tf_op jit(solution)/shard_map/ppermute | solution.py:417
  31.2 2.7 %pair_step.8 = (f32[1,128]{1,0:T(1,128)S(1)}, f32[48,2304]{1,0:T(8,128)S(1)}) custom-call(f32[14,128]{1,0:T(8,128)S(1)} %broadcast_in_dim.73.weights, f32[48,2304]{1,0:T(8,128)S(1)} %join.8.refs_0_.own_ref, f32[48,2304]{1,0:T(8,128)S(1)} %join.10.refs_2_.other_ref, bf16[48,144]{1,0:T(8,128)(2,1)S(1)} %get-tuple-element.57.x_fwd, ...), custom_call_target="tpu_custom_call", output_to_operand_aliasing={{1}: (10, {})} | custom-call | flops 3221225472 | bytes 3145728 | tf_op jit(solution)/shard_map/pair_step/pallas_call | solution.py:201
  34.0 2.0 %collective-permute-start.12 = (f32[24,2304]{1,0:T(8,128)S(1)}, f32[24,2304]{1,0:T(8,128)S(1)}, u32[]{:S(2)}, u32[]{:S(2)}) collective-permute-start(f32[24,2304]{1,0:T(8,128)S(1)} %collective-permute-done.8.refs_1_), channel_id=1, source_target_pairs={{0,8},{8,16},{16,24},{24,28},{28,20},{20,12},{12,4},{4,0},{1,9},{9... | collective-permute-start | bytes 663560 | tf_op jit(solution)/shard_map/ppermute | solution.py:417
  36.0 3.1 %collective-permute-done.7.refs_0_ = f32[24,2304]{1,0:T(8,128)S(1)} collective-permute-done((f32[24,2304]{1,0:T(8,128)S(1)}, f32[24,2304]{1,0:T(8,128)S(1)}, u32[]{:S(2)}, u32[]{:S(2)}) %collective-permute-start.7) | collective-permute-done | bytes 221216 | tf_op jit(solution)/shard_map/ppermute | solution.py:417
  39.3 4.8 %collective-permute-start.13 = (f32[24,2304]{1,0:T(8,128)S(1)}, f32[24,2304]{1,0:T(8,128)S(1)}, u32[]{:S(2)}, u32[]{:S(2)}) collective-permute-start(f32[24,2304]{1,0:T(8,128)S(1)} %collective-permute-done.9.refs_0_), channel_id=1, source_target_pairs={{0,4},{8,0},{16,8},{24,16},{28,24},{20,28},{12,20},{4,12},{1,5},{9... | collective-permute-start | bytes 663560 | tf_op jit(solution)/shard_map/ppermute | solution.py:417
  44.1 2.7 %pair_step.10 = (f32[1,128]{1,0:T(1,128)S(1)}, f32[48,2304]{1,0:T(8,128)S(1)}) custom-call(f32[14,128]{1,0:T(8,128)S(1)} %broadcast_in_dim.73.weights, f32[48,2304]{1,0:T(8,128)S(1)} %join.8.refs_0_.own_ref, f32[48,2304]{1,0:T(8,128)S(1)} %join.12.refs_4_.other_ref, bf16[48,144]{1,0:T(8,128)(2,1)S(1)} %get-tuple-element.57.x_fwd, ...), custom_call_target="tpu_custom_call", output_to_operand_aliasing={{1}: (10, {})} | custom-call | flops 3221225472 | bytes 3145728 | tf_op jit(solution)/shard_map/pair_step/pallas_call | solution.py:201
  46.9 2.1 %collective-permute-start.16 = (f32[24,2304]{1,0:T(8,128)S(1)}, f32[24,2304]{1,0:T(8,128)S(1)}, u32[]{:S(2)}, u32[]{:S(2)}) collective-permute-start(f32[24,2304]{1,0:T(8,128)S(1)} %collective-permute-done.14.refs_1_), channel_id=1, source_target_pairs={{0,4},{8,0},{16,8},{24,16},{28,24},{20,28},{12,20},{4,12},{1,5},{9... | collective-permute-start | bytes 663560 | tf_op jit(solution)/shard_map/ppermute | solution.py:417
  48.9 2.8 %collective-permute-done.11.refs_0_ = f32[24,2304]{1,0:T(8,128)S(1)} collective-permute-done((f32[24,2304]{1,0:T(8,128)S(1)}, f32[24,2304]{1,0:T(8,128)S(1)}, u32[]{:S(2)}, u32[]{:S(2)}) %collective-permute-start.11) | collective-permute-done | bytes 221216 | tf_op jit(solution)/shard_map/ppermute | solution.py:417
  52.8 4.9 %collective-permute-done.15.refs_0_ = f32[24,2304]{1,0:T(8,128)S(1)} collective-permute-done((f32[24,2304]{1,0:T(8,128)S(1)}, f32[24,2304]{1,0:T(8,128)S(1)}, u32[]{:S(2)}, u32[]{:S(2)}) %collective-permute-start.15) | collective-permute-done | bytes 221216 | tf_op jit(solution)/shard_map/ppermute | solution.py:417
  58.1 0.8 %pair_step.13 = (f32[32,1,128]{2,1,0:T(1,128)}, f32[24,1152]{1,0:T(8,128)S(1)}, f32[24,1152]{1,0:T(8,128)S(1)}, f32[24,1152]{1,0:T(8,128)S(1)}, f32[24,1152]{1,0:T(8,128)S(1)}) custom-call(f32[14,128]{1,0:T(8,128)S(1)} %broadcast_in_dim.73.weights, f32[48,2304]{1,0:T(8,128)S(1)} %join.8.refs_0_.own_ref, f32[48,2304]{1,0:T(8,128)S(1)} %join.15.refs_7_.other_ref, ...), custom_call_target="tpu_custom_call" | custom-call | flops 3221225472 | bytes 3145728 | tf_op jit(solution)/shard_map/pair_step/pallas_call | solution.py:201
  58.9 0.7 collective-permute-done.17.theirs
  59.6 1.3 %collective-permute-start.18 = (f32[48,1152]{1,0:T(8,128)S(1)}, f32[48,1152]{1,0:T(8,128)S(1)}, u32[]{:S(2)}, u32[]{:S(2)}) collective-permute-start(f32[48,1152]{1,0:T(8,128)S(1)} %pack.1), channel_id=1, source_target_pairs={{0,2},{1,3},{2,0},{3,1},{4,6},{5,7},{6,4},{7,5},{8,10},{9,11},{10,... | collective-permute-start | bytes 663560 | tf_op jit(solution)/shard_map/ppermute | solution.py:387
  60.9 3.2 %all-to-all-start = ((f32[32,1,128]{2,1,0:T(1,128)}), f32[32,1,128]{2,1,0:T(1,128)S(1)}, u32[]{:S(2)}, u32[]{:S(2)}) async-start(f32[32,1,128]{2,1,0:T(1,128)} %get-tuple-element.53), calls=%async_computation | async-start | bytes 32768 | tf_op jit(solution)/shard_map/all_to_all | solution.py:485
  64.4 1.6 %collective-permute-start.20 = (f32[24,1152]{1,0:T(8,128)S(1)}, f32[24,1152]{1,0:T(8,128)S(1)}, u32[]{:S(2)}, u32[]{:S(2)}) collective-permute-start(f32[24,1152]{1,0:T(8,128)S(1)} %get-tuple-element.52), channel_id=1, source_target_pairs={{0,3},{1,2},{2,1},{3,0},{4,7},{5,6},{6,5},{7,4},{8,11},{9,10},{10,... | collective-permute-start | bytes 331784 | tf_op jit(solution)/shard_map/ppermute | solution.py:387
  66.0 5.2 %all-to-all-done.shared = f32[32,1,128]{2,1,0:T(1,128)S(1)} async-done(((f32[32,1,128]{2,1,0:T(1,128)}), f32[32,1,128]{2,1,0:T(1,128)S(1)}, u32[]{:S(2)}, u32[]{:S(2)}) %all-to-all-start) | async-done | bytes 16416 | tf_op jit(solution)/shard_map/all_to_all | solution.py:485
  71.1 0.6 total.1
  71.9 1.1 %finish.1 = f32[12,4,2304]{2,1,0:T(4,128)} custom-call(s32[1]{0:T(128)} %bitcast.place, f32[12,4,2304]{2,1,0:T(4,128)S(1)} %bitcast.24, f32[24,1152]{1,0:T(8,128)S(1)} %fusion.2.local_pot, f32[24,1152]{1,0:T(8,128)S(1)} %get-tuple-element.50.refs_0_, f32[24,1152]{1,0:T(8,128)S(1)} %collective-permute-done.19.refs_1_, ...), custom_call_target="tpu_custom_call" | custom-call | tf_op jit(solution)/shard_map/finish/pallas_call | solution.py:375
  (69 shorter events, 5.3 us)
Async XLA Ops:
  0.6 1.0 %copy-start = (f32[4,12,2304]{2,0,1:T(4,128)S(1)}, f32[4,12,2304]{2,0,1:T(4,128)}, u32[]{:S(2)}) copy-start(f32[4,12,2304]{2,0,1:T(4,128)} %param.10) | copy-start | bytes 1327108
  1.9 11.0 %collective-permute-start = (f32[24,1152]{1,0:T(8,128)S(1)}, f32[24,1152]{1,0:T(8,128)S(1)}, u32[]{:S(2)}, u32[]{:S(2)}) collective-permute-start(f32[24,1152]{1,0:T(8,128)S(1)} %get-tuple-element.29), channel_id=1, source_target_pairs={{0,1},{1,0},{2,3},{3,2},{4,5},{5,4},{6,7},{7,6},{8,9},{9,8},{10,11... | collective-permute-start | bytes 331784 | tf_op jit(solution)/shard_map/ppermute | solution.py:387
  2.4 6.5 %collective-permute-start.1 = (f32[24,1152]{1,0:T(8,128)S(1)}, f32[24,1152]{1,0:T(8,128)S(1)}, u32[]{:S(2)}, u32[]{:S(2)}) collective-permute-start(f32[24,1152]{1,0:T(8,128)S(1)} %get-tuple-element.30), channel_id=1, source_target_pairs={{0,2},{1,3},{2,0},{3,1},{4,6},{5,7},{6,4},{7,5},{8,10},{9,11},{10,... | collective-permute-start | bytes 331784 | tf_op jit(solution)/shard_map/ppermute | solution.py:387
  5.0 5.8 %collective-permute-start.2 = (f32[24,1152]{1,0:T(8,128)S(1)}, f32[24,1152]{1,0:T(8,128)S(1)}, u32[]{:S(2)}, u32[]{:S(2)}) collective-permute-start(f32[24,1152]{1,0:T(8,128)S(1)} %get-tuple-element.31), channel_id=1, source_target_pairs={{0,3},{1,2},{2,1},{3,0},{4,7},{5,6},{6,5},{7,4},{8,11},{9,10},{10,... | collective-permute-start | bytes 331784 | tf_op jit(solution)/shard_map/ppermute | solution.py:387
  5.0 10.0 %copy-start.8 = (s32[8,2]{0,1:T(2,128)S(1)}, s32[8,2]{0,1:T(2,128)}, u32[]{:S(2)}) copy-start(s32[8,2]{0,1:T(2,128)} %param.11) | copy-start | bytes 196
  5.0 10.1 %copy-start.9 = (s32[8,2]{0,1:T(2,128)S(1)}, s32[8,2]{0,1:T(2,128)}, u32[]{:S(2)}) copy-start(s32[8,2]{0,1:T(2,128)} %param.12) | copy-start | bytes 196
  10.8 14.7 %copy-start.2 = (f32[96,3072]{1,0:T(8,128)S(1)}, f32[96,3072]{1,0:T(8,128)}, u32[]{:S(2)}) copy-start(f32[96,3072]{1,0:T(8,128)} %constant.116.clone.table) | copy-start | bytes 3538948
  10.8 14.7 %copy-start.3 = (bf16[384,128]{1,0:T(8,128)(2,1)S(1)}, bf16[384,128]{1,0:T(8,128)(2,1)}, u32[]{:S(2)}) copy-start(bf16[384,128]{1,0:T(8,128)(2,1)} %constant.115.clone.z_fwd) | copy-start | bytes 294916
  10.8 8.4 %collective-permute-start.6 = (f32[24,2304]{1,0:T(8,128)S(1)}, f32[24,2304]{1,0:T(8,128)S(1)}, u32[]{:S(2)}, u32[]{:S(2)}) collective-permute-start(f32[24,2304]{1,0:T(8,128)S(1)} %assemble.3.refs_1_), channel_id=1, source_target_pairs={{0,4},{8,0},{16,8},{24,16},{28,24},{20,28},{12,20},{4,12},{1,5},{9... | collective-permute-start | bytes 663560 | tf_op jit(solution)/shard_map/ppermute | solution.py:417
  12.3 8.3 %collective-permute-start.4 = (f32[24,2304]{1,0:T(8,128)S(1)}, f32[24,2304]{1,0:T(8,128)S(1)}, u32[]{:S(2)}, u32[]{:S(2)}) collective-permute-start(f32[24,2304]{1,0:T(8,128)S(1)} %assemble.3.refs_1_), channel_id=1, source_target_pairs={{0,8},{8,16},{16,24},{24,28},{28,20},{20,12},{12,4},{4,0},{1,9},{9... | collective-permute-start | bytes 663560 | tf_op jit(solution)/shard_map/ppermute | solution.py:417
  12.9 15.0 %collective-permute-start.5 = (f32[24,2304]{1,0:T(8,128)S(1)}, f32[24,2304]{1,0:T(8,128)S(1)}, u32[]{:S(2)}, u32[]{:S(2)}) collective-permute-start(f32[24,2304]{1,0:T(8,128)S(1)} %assemble.2.refs_0_), channel_id=1, source_target_pairs={{0,4},{8,0},{16,8},{24,16},{28,24},{20,28},{12,20},{4,12},{1,5},{9... | collective-permute-start | bytes 663560 | tf_op jit(solution)/shard_map/ppermute | solution.py:417
  14.4 10.9 %collective-permute-start.3 = (f32[24,2304]{1,0:T(8,128)S(1)}, f32[24,2304]{1,0:T(8,128)S(1)}, u32[]{:S(2)}, u32[]{:S(2)}) collective-permute-start(f32[24,2304]{1,0:T(8,128)S(1)} %assemble.2.refs_0_), channel_id=1, source_target_pairs={{0,8},{8,16},{16,24},{24,28},{28,20},{20,12},{12,4},{4,0},{1,9},{9... | collective-permute-start | bytes 663560 | tf_op jit(solution)/shard_map/ppermute | solution.py:417
  19.2 14.7 %collective-permute-start.10 = (f32[24,2304]{1,0:T(8,128)S(1)}, f32[24,2304]{1,0:T(8,128)S(1)}, u32[]{:S(2)}, u32[]{:S(2)}) collective-permute-start(f32[24,2304]{1,0:T(8,128)S(1)} %collective-permute-done.6.refs_1_), channel_id=1, source_target_pairs={{0,4},{8,0},{16,8},{24,16},{28,24},{20,28},{12,20},{4,12},{1,5},{9... | collective-permute-start | bytes 663560 | tf_op jit(solution)/shard_map/ppermute | solution.py:417
  20.6 13.4 %collective-permute-start.8 = (f32[24,2304]{1,0:T(8,128)S(1)}, f32[24,2304]{1,0:T(8,128)S(1)}, u32[]{:S(2)}, u32[]{:S(2)}) collective-permute-start(f32[24,2304]{1,0:T(8,128)S(1)} %collective-permute-done.4.refs_1_), channel_id=1, source_target_pairs={{0,8},{8,16},{16,24},{24,28},{28,20},{20,12},{12,4},{4,0},{1,9},{9... | collective-permute-start | bytes 663560 | tf_op jit(solution)/shard_map/ppermute | solution.py:417
  25.5 0.8 %copy-start.4 = (bf16[192,128]{1,0:T(8,128)(2,1)S(1)}, bf16[192,128]{1,0:T(8,128)(2,1)}, u32[]{:S(2)}) copy-start(bf16[192,128]{1,0:T(8,128)(2,1)} %constant.118.clone.y_inv) | copy-start | bytes 147460
  26.3 0.8 %copy-start.5 = (bf16[48,288]{1,0:T(8,128)(2,1)S(1)}, bf16[48,288]{1,0:T(8,128)(2,1)}, u32[]{:S(2)}) copy-start(bf16[48,288]{1,0:T(8,128)(2,1)} %constant.117.clone.z_inv) | copy-start | bytes 82948
  27.0 0.7 %copy-start.7 = (bf16[48,144]{1,0:T(8,128)(2,1)S(1)}, bf16[48,144]{1,0:T(8,128)(2,1)}, u32[]{:S(2)}) copy-start(bf16[48,144]{1,0:T(8,128)(2,1)} %constant.114.clone.y_fwd) | copy-start | bytes 41476
  27.8 3.5 %copy-start.6 = (bf16[48,288]{1,0:T(8,128)(2,1)S(1)}, bf16[48,288]{1,0:T(8,128)(2,1)}, u32[]{:S(2)}) copy-start(bf16[48,288]{1,0:T(8,128)(2,1)} %constant.117.clone.z_inv) | copy-start | bytes 82948
  27.9 11.4 %collective-permute-start.9 = (f32[24,2304]{1,0:T(8,128)S(1)}, f32[24,2304]{1,0:T(8,128)S(1)}, u32[]{:S(2)}, u32[]{:S(2)}) collective-permute-start(f32[24,2304]{1,0:T(8,128)S(1)} %collective-permute-done.5.refs_0_), channel_id=1, source_target_pairs={{0,4},{8,0},{16,8},{24,16},{28,24},{20,28},{12,20},{4,12},{1,5},{9... | collective-permute-start | bytes 663560 | tf_op jit(solution)/shard_map/ppermute | solution.py:417
  29.6 9.6 %collective-permute-start.7 = (f32[24,2304]{1,0:T(8,128)S(1)}, f32[24,2304]{1,0:T(8,128)S(1)}, u32[]{:S(2)}, u32[]{:S(2)}) collective-permute-start(f32[24,2304]{1,0:T(8,128)S(1)} %collective-permute-done.3.refs_0_), channel_id=1, source_target_pairs={{0,8},{8,16},{16,24},{24,28},{28,20},{20,12},{12,4},{4,0},{1,9},{9... | collective-permute-start | bytes 663560 | tf_op jit(solution)/shard_map/ppermute | solution.py:417
  33.9 12.9 %collective-permute-start.14 = (f32[24,2304]{1,0:T(8,128)S(1)}, f32[24,2304]{1,0:T(8,128)S(1)}, u32[]{:S(2)}, u32[]{:S(2)}) collective-permute-start(f32[24,2304]{1,0:T(8,128)S(1)} %collective-permute-done.10.refs_1_), channel_id=1, source_target_pairs={{0,4},{8,0},{16,8},{24,16},{28,24},{20,28},{12,20},{4,12},{1,5},{9... | collective-permute-start | bytes 663560 | tf_op jit(solution)/shard_map/ppermute | solution.py:417
  34.0 17.8 %collective-permute-start.12 = (f32[24,2304]{1,0:T(8,128)S(1)}, f32[24,2304]{1,0:T(8,128)S(1)}, u32[]{:S(2)}, u32[]{:S(2)}) collective-permute-start(f32[24,2304]{1,0:T(8,128)S(1)} %collective-permute-done.8.refs_1_), channel_id=1, source_target_pairs={{0,8},{8,16},{16,24},{24,28},{28,20},{20,12},{12,4},{4,0},{1,9},{9... | collective-permute-start | bytes 663560 | tf_op jit(solution)/shard_map/ppermute | solution.py:417
  39.3 12.8 %collective-permute-start.13 = (f32[24,2304]{1,0:T(8,128)S(1)}, f32[24,2304]{1,0:T(8,128)S(1)}, u32[]{:S(2)}, u32[]{:S(2)}) collective-permute-start(f32[24,2304]{1,0:T(8,128)S(1)} %collective-permute-done.9.refs_0_), channel_id=1, source_target_pairs={{0,4},{8,0},{16,8},{24,16},{28,24},{20,28},{12,20},{4,12},{1,5},{9... | collective-permute-start | bytes 663560 | tf_op jit(solution)/shard_map/ppermute | solution.py:417
  44.1 7.6 %collective-permute-start.11 = (f32[24,2304]{1,0:T(8,128)S(1)}, f32[24,2304]{1,0:T(8,128)S(1)}, u32[]{:S(2)}, u32[]{:S(2)}) collective-permute-start(f32[24,2304]{1,0:T(8,128)S(1)} %collective-permute-done.7.refs_0_), channel_id=1, source_target_pairs={{0,8},{8,16},{16,24},{24,28},{28,20},{20,12},{12,4},{4,0},{1,9},{9... | collective-permute-start | bytes 663560 | tf_op jit(solution)/shard_map/ppermute | solution.py:417
  46.9 6.0 %collective-permute-start.16 = (f32[24,2304]{1,0:T(8,128)S(1)}, f32[24,2304]{1,0:T(8,128)S(1)}, u32[]{:S(2)}, u32[]{:S(2)}) collective-permute-start(f32[24,2304]{1,0:T(8,128)S(1)} %collective-permute-done.14.refs_1_), channel_id=1, source_target_pairs={{0,4},{8,0},{16,8},{24,16},{28,24},{20,28},{12,20},{4,12},{1,5},{9... | collective-permute-start | bytes 663560 | tf_op jit(solution)/shard_map/ppermute | solution.py:417
  51.8 5.9 %collective-permute-start.15 = (f32[24,2304]{1,0:T(8,128)S(1)}, f32[24,2304]{1,0:T(8,128)S(1)}, u32[]{:S(2)}, u32[]{:S(2)}) collective-permute-start(f32[24,2304]{1,0:T(8,128)S(1)} %collective-permute-done.11.refs_0_), channel_id=1, source_target_pairs={{0,8},{8,16},{16,24},{24,28},{28,20},{20,12},{12,4},{4,0},{1,9},{9... | collective-permute-start | bytes 663560 | tf_op jit(solution)/shard_map/ppermute | solution.py:417
  58.0 1.5 %collective-permute-start.17 = (f32[2,24,1152]{2,1,0:T(8,128)S(1)}, f32[2,24,1152]{2,1,0:T(8,128)S(1)}, u32[]{:S(2)}, u32[]{:S(2)}) collective-permute-start(f32[2,24,1152]{2,1,0:T(8,128)S(1)} %get-tuple-element.34), channel_id=1, source_target_pairs={{0,1},{1,0},{2,3},{3,2},{4,5},{5,4},{6,7},{7,6},{8,9},{9,8},{10,11... | collective-permute-start | bytes 663560 | tf_op jit(solution)/shard_map/ppermute | solution.py:387
  58.9 13.0 %copy-start.1 = (f32[4,12,2304]{2,0,1:T(4,128)S(1)}, f32[4,12,2304]{2,0,1:T(4,128)}, u32[]{:S(2)}) copy-start(f32[4,12,2304]{2,0,1:T(4,128)} %param.10) | copy-start | bytes 1327108
  59.6 12.2 %collective-permute-start.18 = (f32[48,1152]{1,0:T(8,128)S(1)}, f32[48,1152]{1,0:T(8,128)S(1)}, u32[]{:S(2)}, u32[]{:S(2)}) collective-permute-start(f32[48,1152]{1,0:T(8,128)S(1)} %pack.1), channel_id=1, source_target_pairs={{0,2},{1,3},{2,0},{3,1},{4,6},{5,7},{6,4},{7,5},{8,10},{9,11},{10,... | collective-permute-start | bytes 663560 | tf_op jit(solution)/shard_map/ppermute | solution.py:387
  60.9 10.3 %all-to-all-start = ((f32[32,1,128]{2,1,0:T(1,128)}), f32[32,1,128]{2,1,0:T(1,128)S(1)}, u32[]{:S(2)}, u32[]{:S(2)}) async-start(f32[32,1,128]{2,1,0:T(1,128)} %get-tuple-element.53), calls=%async_computation | async-start | bytes 32768 | tf_op jit(solution)/shard_map/all_to_all | solution.py:485
  64.0 7.8 %collective-permute-start.19 = (f32[24,1152]{1,0:T(8,128)S(1)}, f32[24,1152]{1,0:T(8,128)S(1)}, u32[]{:S(2)}, u32[]{:S(2)}) collective-permute-start(f32[24,1152]{1,0:T(8,128)S(1)} %get-tuple-element.51), channel_id=1, source_target_pairs={{0,1},{1,0},{2,3},{3,2},{4,5},{5,4},{6,7},{7,6},{8,9},{9,8},{10,11... | collective-permute-start | bytes 331784 | tf_op jit(solution)/shard_map/ppermute | solution.py:387
  64.4 7.5 %collective-permute-start.20 = (f32[24,1152]{1,0:T(8,128)S(1)}, f32[24,1152]{1,0:T(8,128)S(1)}, u32[]{:S(2)}, u32[]{:S(2)}) collective-permute-start(f32[24,1152]{1,0:T(8,128)S(1)} %get-tuple-element.52), channel_id=1, source_target_pairs={{0,3},{1,2},{2,1},{3,0},{4,7},{5,6},{6,5},{7,4},{8,11},{9,10},{10,... | collective-permute-start | bytes 331784 | tf_op jit(solution)/shard_map/ppermute | solution.py:387

commit v10 on v9

--- a/solution.py
+++ b/solution.py
@@ -337,6 +337,23 @@
     )(piece, mine, theirs)
 
 
+def stage_kernel(*refs):
+    count = len(refs) // 2
+    for source, target in zip(refs[:count], refs[count:]):
+        target[...] = source[...]
+
+
+def stage(tables):
+    return pl.pallas_call(
+        stage_kernel,
+        out_shape=[jax.ShapeDtypeStruct(table.shape, table.dtype) for table in tables],
+        in_specs=in_vmem(len(tables)),
+        out_specs=in_vmem(len(tables)),
+        compiler_params=pltpu.CompilerParams(vmem_limit_bytes=8 << 20),
+        name="stage",
+    )(*tables)
+
+
 def join_kernel(*refs):
     out_ref = refs[-1]
     first = 0
@@ -452,7 +469,8 @@
     force = clear((NX, NY * NZ))
 
     own, partners, counts = lax.optimization_barrier((own, partners, counts))
-    tables = transform_tables(slab_index, slabs)
+    x_fwd, *tables, x_inv = transform_tables(slab_index, slabs)
+    tables = [x_fwd, *stage(tables), x_inv]
 
     groups = jnp.stack([group for _, group in others]).astype(jnp.int32)
     active = (slab_index < counts).astype(jnp.float32)

time: 73.4 us -> 70 us (0.954)
  waiting for transfers between devices: 29.5 us -> 16.3 us
  local copies, waits for them, and re-layouts: 4.44 us -> 9.51 us
  starting transfers between devices: 28 us -> 30.8 us
  other arithmetic: 0.64 us -> 1.89 us
    ppermute x14, waiting for transfers between devices: 18.9 us -> 10.4 us  [shift(): return lax.ppermute(value, 'band', moves)]
    ppermute x7, waiting for transfers between devices: 5.44 us -> 0.7 us  [slab_swap(): return lax.ppermute(value, 'slab', [(i, i ^ reach) for i in range(size)])]
    all_to_all x1, starting transfers between devices: 3.17 us -> 5.98 us  [body(): shared = lax.all_to_all(energy, ('band', 'slab'), 0, 0)]
    unnamed x20 -> x32, local copies, waits for them, and re-layouts: 3.34 us -> 6.07 us
    broadcast_in_dim x2, local copies, waits for them, and re-layouts: 0.15 us -> 1.32 us  [body(): weights = jnp.broadcast_to(weights[:, None], weights.shape + (128,))]
  transfers between devices with their start and end apart: 22 -> 22, of which waited for: 10 -> 8; matrix products, arithmetic and copies ran while one was open for 2% -> 8% of each run, Pallas kernels for 11% -> 11%
where the time goes in v10:
time: 70 us; the launch traced here: 69.5 us
  starting transfers between devices  30.8 us (44%)
  waiting for transfers between devices  16.3 us (23%)
  Pallas kernels  10 us (14%)
  local copies, waits for them, and re-layouts  9.51 us (14%)
  other arithmetic  1.89 us (3%)
  between operations  1.02 us (1%)
    ppermute x14, starting transfers between devices, shift(): return lax.ppermute(value, 'band', moves)  18.2 us
    ppermute x14, waiting for transfers between devices, shift(): return lax.ppermute(value, 'band', moves)  10.4 us
    pallas_call x7, Pallas kernels, pair_step(): pl.pallas_call(functools.partial(pair_kernel, slot), out_shape=outs, in_s...  6.88 us
    ppermute x7, starting transfers between devices, slab_swap(): return lax.ppermute(value, 'slab', [(i, i ^ reach) for i in range(size)])  6.58 us
    unnamed x32, local copies, waits for them, and re-layouts  6.07 us
    all_to_all x1, starting transfers between devices, body(): shared = lax.all_to_all(energy, ('band', 'slab'), 0, 0)  5.98 us
    all_to_all x1, waiting for transfers between devices, body(): shared = lax.all_to_all(energy, ('band', 'slab'), 0, 0)  5.15 us
  transfers between devices with their start and end apart: 22, of which 8 were waited for; matrix products, arithmetic and copies ran while one was open for 8% of the time, Pallas kernels for 11%

profile of v10, /device:TPU:0, one launch (start us, length us, event | category | flops | bytes accessed | tf_op | source)
XLA Modules:
  0.0 69.5 jit_solution(7974808798422449800)
XLA Ops:
  0.6 1.0 %copy-done = f32[4,12,2304]{2,0,1:T(4,128)S(1)} copy-done((f32[4,12,2304]{2,0,1:T(4,128)S(1)}, f32[4,12,2304]{2,0,1:T(4,128)}, u32[]{:S(2)}) %copy-start) | copy-done | bytes 442392
  1.7 0.8 %prepare.1 = (f32[24,1152]{1,0:T(8,128)S(1)}, f32[24,1152]{1,0:T(8,128)}, f32[24,1152]{1,0:T(8,128)}, f32[24,1152]{1,0:T(8,128)S(1)}) custom-call(s32[1]{0:T(128)} %bitcast.place, f32[12,4,2304]{2,1,0:T(4,128)S(1)} %bitcast.23), custom_call_target="tpu_custom_call" | custom-call | tf_op jit(solution)/shard_map/prepare/pallas_call | solution.py:252
  2.9 2.5 %collective-permute-start.1 = (f32[24,1152]{1,0:T(8,128)}, f32[24,1152]{1,0:T(8,128)S(1)}, u32[]{:S(2)}, u32[]{:S(2)}) collective-permute-start(f32[24,1152]{1,0:T(8,128)} %get-tuple-element.35), channel_id=1, source_target_pairs={{0,2},{1,3},{2,0},{3,1},{4,6},{5,7},{6,4},{7,5},{8,10},{9,11},{10,... | collective-permute-start | bytes 331784 | tf_op jit(solution)/shard_map/ppermute | solution.py:404
  5.6 0.8 %dynamic-slice_bitcast_fusion = (bf16[48,144]{1,0:T(8,128)(2,1)S(1)}, bf16[48,144]{1,0:T(8,128)(2,1)S(1)}) fusion(bf16[4,48,144]{2,1,0:T(8,128)(2,1)} %constant.113.clone, s32[]{:T(128)S(6)} %select_n.110, bf16[4,48,144]{2,1,0:T(8,128)(2,1)} %constant.112.clone), kind=kLoop, calls=%fused_computation.6 | loop fusion | bytes 55300 | tf_op jit(solution)/shard_map/jit(dynamic_index_in_dim)/squeeze | solution.py:84
  6.4 0.8 %copy-done.4 = bf16[192,128]{1,0:T(8,128)(2,1)S(1)} copy-done((bf16[192,128]{1,0:T(8,128)(2,1)S(1)}, bf16[192,128]{1,0:T(8,128)(2,1)}, u32[]{:S(2)}) %copy-start.4) | copy-done | bytes 49176
  7.2 0.8 %copy-done.5 = bf16[48,288]{1,0:T(8,128)(2,1)S(1)} copy-done((bf16[48,288]{1,0:T(8,128)(2,1)S(1)}, bf16[48,288]{1,0:T(8,128)(2,1)}, u32[]{:S(2)}) %copy-start.5) | copy-done | bytes 27672
  8.0 0.7 %copy-done.6 = bf16[48,144]{1,0:T(8,128)(2,1)S(1)} copy-done((bf16[48,144]{1,0:T(8,128)(2,1)S(1)}, bf16[48,144]{1,0:T(8,128)(2,1)}, u32[]{:S(2)}) %copy-start.6) | copy-done | bytes 13848
  11.3 1.9 %collective-permute-start.3 = (f32[24,2304]{1,0:T(8,128)S(1)}, f32[24,2304]{1,0:T(8,128)S(1)}, u32[]{:S(2)}, u32[]{:S(2)}) collective-permute-start(f32[24,2304]{1,0:T(8,128)S(1)} %assemble.2.refs_0_), channel_id=1, source_target_pairs={{0,8},{8,16},{16,24},{24,28},{28,20},{20,12},{12,4},{4,0},{1,9},{9... | collective-permute-start | bytes 663560 | tf_op jit(solution)/shard_map/ppermute | solution.py:434
  13.6 1.7 %collective-permute-start.5 = (f32[24,2304]{1,0:T(8,128)S(1)}, f32[24,2304]{1,0:T(8,128)S(1)}, u32[]{:S(2)}, u32[]{:S(2)}) collective-permute-start(f32[24,2304]{1,0:T(8,128)S(1)} %assemble.2.refs_0_), channel_id=1, source_target_pairs={{0,4},{8,0},{16,8},{24,16},{28,24},{20,28},{12,20},{4,12},{1,5},{9... | collective-permute-start | bytes 663560 | tf_op jit(solution)/shard_map/ppermute | solution.py:434
  15.7 0.8 %fusion.5 = (f32[8]{0:T(128)S(1)}, f32[2]{0:T(128)S(1)}) fusion(s32[8,2]{0,1:T(2,128)S(1)} %copy-done.14, s32[8,2]{0,1:T(2,128)} %param.12, s32[]{:T(128)S(6)} %axis_index.25, s32[]{:T(128)} %axis_index.22, pred[8]{0:T(512)(128)(4,1)S(1)} %iota_compare_fusion.1), kind=kLoop, calls=%fused_computation.14 | loop fusion | flops 102 | bytes 184 | tf_op jit(solution)/shard_map/reduce_sum | solution.py:483
  17.4 0.8 %copy.20 = f32[7,2]{1,0:T(8,128)S(1)} copy(f32[7,2]{0,1:T(2,128)} %pad_maximum_fusion) | data formatting | bytes 112 | tf_op jit(solution)/shard_map/stack | solution.py:486
  18.7 1.0 %collective-permute-done.3.refs_0_ = f32[24,2304]{1,0:T(8,128)S(1)} collective-permute-done((f32[24,2304]{1,0:T(8,128)S(1)}, f32[24,2304]{1,0:T(8,128)S(1)}, u32[]{:S(2)}, u32[]{:S(2)}) %collective-permute-start.3) | collective-permute-done | bytes 221216 | tf_op jit(solution)/shard_map/ppermute | solution.py:434
  19.7 1.8 %collective-permute-start.7 = (f32[24,2304]{1,0:T(8,128)S(1)}, f32[24,2304]{1,0:T(8,128)S(1)}, u32[]{:S(2)}, u32[]{:S(2)}) collective-permute-start(f32[24,2304]{1,0:T(8,128)S(1)} %collective-permute-done.3.refs_0_), channel_id=1, source_target_pairs={{0,8},{8,16},{16,24},{24,28},{28,20},{20,12},{12,4},{4,0},{1,9},{9... | collective-permute-start | bytes 663560 | tf_op jit(solution)/shard_map/ppermute | solution.py:434
  21.5 2.9 %collective-permute-done.4.refs_1_ = f32[24,2304]{1,0:T(8,128)S(1)} collective-permute-done((f32[24,2304]{1,0:T(8,128)S(1)}, f32[24,2304]{1,0:T(8,128)S(1)}, u32[]{:S(2)}, u32[]{:S(2)}) %collective-permute-start.4) | collective-permute-done | bytes 221216 | tf_op jit(solution)/shard_map/ppermute | solution.py:434
  24.4 1.8 %collective-permute-start.8 = (f32[24,2304]{1,0:T(8,128)S(1)}, f32[24,2304]{1,0:T(8,128)S(1)}, u32[]{:S(2)}, u32[]{:S(2)}) collective-permute-start(f32[24,2304]{1,0:T(8,128)S(1)} %collective-permute-done.4.refs_1_), channel_id=1, source_target_pairs={{0,8},{8,16},{16,24},{24,28},{28,20},{20,12},{12,4},{4,0},{1,9},{9... | collective-permute-start | bytes 663560 | tf_op jit(solution)/shard_map/ppermute | solution.py:434
  26.6 0.7 %broadcast_in_dim.73.weights = f32[14,128]{1,0:T(8,128)S(1)} broadcast(f32[14]{0:T(128)} %broadcast_in_dim.72), dimensions={0} | broadcast | bytes 7224 | tf_op jit(solution)/shard_map/broadcast_in_dim | solution.py:487
  27.3 0.9 %copy-done.8 = bf16[384,128]{1,0:T(8,128)(2,1)S(1)} copy-done((bf16[384,128]{1,0:T(8,128)(2,1)S(1)}, bf16[384,128]{1,0:T(8,128)(2,1)}, u32[]{:S(2)}) %copy-start.8) | copy-done | bytes 98328
  28.3 1.8 %collective-permute-start.9 = (f32[24,2304]{1,0:T(8,128)S(1)}, f32[24,2304]{1,0:T(8,128)S(1)}, u32[]{:S(2)}, u32[]{:S(2)}) collective-permute-start(f32[24,2304]{1,0:T(8,128)S(1)} %collective-permute-done.5.refs_0_), channel_id=1, source_target_pairs={{0,4},{8,0},{16,8},{24,16},{28,24},{20,28},{12,20},{4,12},{1,5},{9... | collective-permute-start | bytes 663560 | tf_op jit(solution)/shard_map/ppermute | solution.py:434
  30.1 2.7 %pair_step.8 = (f32[1,128]{1,0:T(1,128)S(1)}, f32[48,2304]{1,0:T(8,128)S(1)}) custom-call(f32[14,128]{1,0:T(8,128)S(1)} %broadcast_in_dim.73.weights, f32[48,2304]{1,0:T(8,128)S(1)} %join.8.refs_0_.own_ref, f32[48,2304]{1,0:T(8,128)S(1)} %join.10.refs_2_.other_ref, bf16[48,144]{1,0:T(8,128)(2,1)S(1)} %get-tuple-element.67.x_fwd, ...), custom_call_target="tpu_custom_call", output_to_operand_aliasing={{1}: (10, {})} | custom-call | flops 3221225472 | bytes 3145728 | tf_op jit(solution)/shard_map/pair_step/pallas_call | solution.py:201
  33.2 4.4 %collective-permute-start.12 = (f32[24,2304]{1,0:T(8,128)S(1)}, f32[24,2304]{1,0:T(8,128)S(1)}, u32[]{:S(2)}, u32[]{:S(2)}) collective-permute-start(f32[24,2304]{1,0:T(8,128)S(1)} %collective-permute-done.8.refs_1_), channel_id=1, source_target_pairs={{0,8},{8,16},{16,24},{24,28},{28,20},{20,12},{12,4},{4,0},{1,9},{9... | collective-permute-start | bytes 663560 | tf_op jit(solution)/shard_map/ppermute | solution.py:434
  37.9 2.1 %collective-permute-start.13 = (f32[24,2304]{1,0:T(8,128)S(1)}, f32[24,2304]{1,0:T(8,128)S(1)}, u32[]{:S(2)}, u32[]{:S(2)}) collective-permute-start(f32[24,2304]{1,0:T(8,128)S(1)} %collective-permute-done.9.refs_0_), channel_id=1, source_target_pairs={{0,4},{8,0},{16,8},{24,16},{28,24},{20,28},{12,20},{4,12},{1,5},{9... | collective-permute-start | bytes 663560 | tf_op jit(solution)/shard_map/ppermute | solution.py:434
  40.0 2.7 %pair_step.10 = (f32[1,128]{1,0:T(1,128)S(1)}, f32[48,2304]{1,0:T(8,128)S(1)}) custom-call(f32[14,128]{1,0:T(8,128)S(1)} %broadcast_in_dim.73.weights, f32[48,2304]{1,0:T(8,128)S(1)} %join.8.refs_0_.own_ref, f32[48,2304]{1,0:T(8,128)S(1)} %join.12.refs_4_.other_ref, bf16[48,144]{1,0:T(8,128)(2,1)S(1)} %get-tuple-element.67.x_fwd, ...), custom_call_target="tpu_custom_call", output_to_operand_aliasing={{1}: (10, {})} | custom-call | flops 3221225472 | bytes 3145728 | tf_op jit(solution)/shard_map/pair_step/pallas_call | solution.py:201
  42.8 1.5 %collective-permute-done.14.refs_1_ = f32[24,2304]{1,0:T(8,128)S(1)} collective-permute-done((f32[24,2304]{1,0:T(8,128)S(1)}, f32[24,2304]{1,0:T(8,128)S(1)}, u32[]{:S(2)}, u32[]{:S(2)}) %collective-permute-start.14) | collective-permute-done | bytes 221216 | tf_op jit(solution)/shard_map/ppermute | solution.py:434
  44.3 1.7 %collective-permute-start.16 = (f32[24,2304]{1,0:T(8,128)S(1)}, f32[24,2304]{1,0:T(8,128)S(1)}, u32[]{:S(2)}, u32[]{:S(2)}) collective-permute-start(f32[24,2304]{1,0:T(8,128)S(1)} %collective-permute-done.14.refs_1_), channel_id=1, source_target_pairs={{0,4},{8,0},{16,8},{24,16},{28,24},{20,28},{12,20},{4,12},{1,5},{9... | collective-permute-start | bytes 663560 | tf_op jit(solution)/shard_map/ppermute | solution.py:434
  46.3 2.5 %collective-permute-done.13.refs_0_ = f32[24,2304]{1,0:T(8,128)S(1)} collective-permute-done((f32[24,2304]{1,0:T(8,128)S(1)}, f32[24,2304]{1,0:T(8,128)S(1)}, u32[]{:S(2)}, u32[]{:S(2)}) %collective-permute-start.13) | collective-permute-done | bytes 221216 | tf_op jit(solution)/shard_map/ppermute | solution.py:434
  49.0 2.2 %collective-permute-done.16.refs_1_ = f32[24,2304]{1,0:T(8,128)S(1)} collective-permute-done((f32[24,2304]{1,0:T(8,128)S(1)}, f32[24,2304]{1,0:T(8,128)S(1)}, u32[]{:S(2)}, u32[]{:S(2)}) %collective-permute-start.16) | collective-permute-done | bytes 221216 | tf_op jit(solution)/shard_map/ppermute | solution.py:434
  51.6 0.8 %pair_step.13 = (f32[32,1,128]{2,1,0:T(1,128)}, f32[24,1152]{1,0:T(8,128)S(1)}, f32[24,1152]{1,0:T(8,128)S(1)}, f32[24,1152]{1,0:T(8,128)S(1)}, f32[24,1152]{1,0:T(8,128)S(1)}) custom-call(f32[14,128]{1,0:T(8,128)S(1)} %broadcast_in_dim.73.weights, f32[48,2304]{1,0:T(8,128)S(1)} %join.8.refs_0_.own_ref, f32[48,2304]{1,0:T(8,128)S(1)} %join.15.refs_7_.other_ref, ...), custom_call_target="tpu_custom_call" | custom-call | flops 3221225472 | bytes 3145728 | tf_op jit(solution)/shard_map/pair_step/pallas_call | solution.py:201
  53.1 1.4 %collective-permute-start.18 = (f32[48,1152]{1,0:T(8,128)S(1)}, f32[48,1152]{1,0:T(8,128)S(1)}, u32[]{:S(2)}, u32[]{:S(2)}) collective-permute-start(f32[48,1152]{1,0:T(8,128)S(1)} %pack.1), channel_id=1, source_target_pairs={{0,2},{1,3},{2,0},{3,1},{4,6},{5,7},{6,4},{7,5},{8,10},{9,11},{10,... | collective-permute-start | bytes 663560 | tf_op jit(solution)/shard_map/ppermute | solution.py:404
  54.5 6.0 %all-to-all-start = ((f32[32,1,128]{2,1,0:T(1,128)}), f32[32,1,128]{2,1,0:T(1,128)S(1)}, u32[]{:S(2)}, u32[]{:S(2)}) async-start(f32[32,1,128]{2,1,0:T(1,128)} %get-tuple-element.63), calls=%async_computation | async-start | bytes 32768 | tf_op jit(solution)/shard_map/all_to_all | solution.py:503
  60.8 1.6 %collective-permute-start.20 = (f32[24,1152]{1,0:T(8,128)S(1)}, f32[24,1152]{1,0:T(8,128)S(1)}, u32[]{:S(2)}, u32[]{:S(2)}) collective-permute-start(f32[24,1152]{1,0:T(8,128)S(1)} %get-tuple-element.62), channel_id=1, source_target_pairs={{0,3},{1,2},{2,1},{3,0},{4,7},{5,6},{6,5},{7,4},{8,11},{9,10},{10,... | collective-permute-start | bytes 331784 | tf_op jit(solution)/shard_map/ppermute | solution.py:404
  62.5 5.2 %all-to-all-done.shared = f32[32,1,128]{2,1,0:T(1,128)S(1)} async-done(((f32[32,1,128]{2,1,0:T(1,128)}), f32[32,1,128]{2,1,0:T(1,128)S(1)}, u32[]{:S(2)}, u32[]{:S(2)}) %all-to-all-start) | async-done | bytes 16416 | tf_op jit(solution)/shard_map/all_to_all | solution.py:503
  68.4 1.1 %finish.1 = f32[12,4,2304]{2,1,0:T(4,128)} custom-call(s32[1]{0:T(128)} %bitcast.place, f32[12,4,2304]{2,1,0:T(4,128)S(1)} %bitcast.24, f32[24,1152]{1,0:T(8,128)S(1)} %fusion.2.local_pot, f32[24,1152]{1,0:T(8,128)S(1)} %get-tuple-element.60.refs_0_, f32[24,1152]{1,0:T(8,128)S(1)} %collective-permute-done.19.refs_1_, ...), custom_call_target="tpu_custom_call" | custom-call | tf_op jit(solution)/shard_map/finish/pallas_call | solution.py:392
  (82 shorter events, 9.2 us)
Async XLA Ops:
  0.6 1.0 %copy-start = (f32[4,12,2304]{2,0,1:T(4,128)S(1)}, f32[4,12,2304]{2,0,1:T(4,128)}, u32[]{:S(2)}) copy-start(f32[4,12,2304]{2,0,1:T(4,128)} %param.10) | copy-start | bytes 1327108
  1.7 4.8 %copy-start.2 = (f32[96,3072]{1,0:T(8,128)S(1)}, f32[96,3072]{1,0:T(8,128)}, u32[]{:S(2)}) copy-start(f32[96,3072]{1,0:T(8,128)} %constant.116.clone.refs_2_) | copy-start | bytes 3538948
  1.7 4.8 %copy-start.3 = (bf16[384,128]{1,0:T(8,128)(2,1)S(1)}, bf16[384,128]{1,0:T(8,128)(2,1)}, u32[]{:S(2)}) copy-start(bf16[384,128]{1,0:T(8,128)(2,1)} %constant.115.clone.refs_1_) | copy-start | bytes 294916
  2.4 8.9 %collective-permute-start = (f32[24,1152]{1,0:T(8,128)}, f32[24,1152]{1,0:T(8,128)S(1)}, u32[]{:S(2)}, u32[]{:S(2)}) collective-permute-start(f32[24,1152]{1,0:T(8,128)} %get-tuple-element.34), channel_id=1, source_target_pairs={{0,1},{1,0},{2,3},{3,2},{4,5},{5,4},{6,7},{7,6},{8,9},{9,8},{10,11... | collective-permute-start | bytes 331784 | tf_op jit(solution)/shard_map/ppermute | solution.py:404
  2.9 10.3 %collective-permute-start.1 = (f32[24,1152]{1,0:T(8,128)}, f32[24,1152]{1,0:T(8,128)S(1)}, u32[]{:S(2)}, u32[]{:S(2)}) collective-permute-start(f32[24,1152]{1,0:T(8,128)} %get-tuple-element.35), channel_id=1, source_target_pairs={{0,2},{1,3},{2,0},{3,1},{4,6},{5,7},{6,4},{7,5},{8,10},{9,11},{10,... | collective-permute-start | bytes 331784 | tf_op jit(solution)/shard_map/ppermute | solution.py:404
  5.4 7.8 %collective-permute-start.2 = (f32[24,1152]{1,0:T(8,128)S(1)}, f32[24,1152]{1,0:T(8,128)S(1)}, u32[]{:S(2)}, u32[]{:S(2)}) collective-permute-start(f32[24,1152]{1,0:T(8,128)S(1)} %get-tuple-element.36), channel_id=1, source_target_pairs={{0,3},{1,2},{2,1},{3,0},{4,7},{5,6},{6,5},{7,4},{8,11},{9,10},{10,... | collective-permute-start | bytes 331784 | tf_op jit(solution)/shard_map/ppermute | solution.py:404
  10.7 4.9 %copy-start.14 = (s32[8,2]{0,1:T(2,128)S(1)}, s32[8,2]{0,1:T(2,128)}, u32[]{:S(2)}) copy-start(s32[8,2]{0,1:T(2,128)} %param.11) | copy-start | bytes 196
  11.3 5.2 %copy-start.15 = (s32[7]{0:T(128)S(1)}, s32[7]{0:T(128)}, u32[]{:S(2)}) copy-start(s32[7]{0:T(128)} %stack.36) | copy-start | bytes 88
  11.3 16.0 %copy-start.11 = (bf16[192,128]{1,0:T(8,128)(2,1)S(1)}, bf16[192,128]{1,0:T(8,128)(2,1)}, u32[]{:S(2)}) copy-start(bf16[192,128]{1,0:T(8,128)(2,1)} %copy-done.10) | copy-start | bytes 147460
  11.3 16.0 %copy-start.13 = (bf16[48,144]{1,0:T(8,128)(2,1)S(1)}, bf16[48,144]{1,0:T(8,128)(2,1)}, u32[]{:S(2)}) copy-start(bf16[48,144]{1,0:T(8,128)(2,1)} %copy-done.12) | copy-start | bytes 41476
  11.3 8.4 %collective-permute-start.3 = (f32[24,2304]{1,0:T(8,128)S(1)}, f32[24,2304]{1,0:T(8,128)S(1)}, u32[]{:S(2)}, u32[]{:S(2)}) collective-permute-start(f32[24,2304]{1,0:T(8,128)S(1)} %assemble.2.refs_0_), channel_id=1, source_target_pairs={{0,8},{8,16},{16,24},{24,28},{28,20},{20,12},{12,4},{4,0},{1,9},{9... | collective-permute-start | bytes 663560 | tf_op jit(solution)/shard_map/ppermute | solution.py:434
  13.3 13.0 %collective-permute-start.6 = (f32[24,2304]{1,0:T(8,128)S(1)}, f32[24,2304]{1,0:T(8,128)S(1)}, u32[]{:S(2)}, u32[]{:S(2)}) collective-permute-start(f32[24,2304]{1,0:T(8,128)S(1)} %assemble.3.refs_1_), channel_id=1, source_target_pairs={{0,4},{8,0},{16,8},{24,16},{28,24},{20,28},{12,20},{4,12},{1,5},{9... | collective-permute-start | bytes 663560 | tf_op jit(solution)/shard_map/ppermute | solution.py:434
  13.6 14.8 %collective-permute-start.5 = (f32[24,2304]{1,0:T(8,128)S(1)}, f32[24,2304]{1,0:T(8,128)S(1)}, u32[]{:S(2)}, u32[]{:S(2)}) collective-permute-start(f32[24,2304]{1,0:T(8,128)S(1)} %assemble.2.refs_0_), channel_id=1, source_target_pairs={{0,4},{8,0},{16,8},{24,16},{28,24},{20,28},{12,20},{4,12},{1,5},{9... | collective-permute-start | bytes 663560 | tf_op jit(solution)/shard_map/ppermute | solution.py:434
  15.3 9.2 %collective-permute-start.4 = (f32[24,2304]{1,0:T(8,128)S(1)}, f32[24,2304]{1,0:T(8,128)S(1)}, u32[]{:S(2)}, u32[]{:S(2)}) collective-permute-start(f32[24,2304]{1,0:T(8,128)S(1)} %assemble.3.refs_1_), channel_id=1, source_target_pairs={{0,8},{8,16},{16,24},{24,28},{28,20},{20,12},{12,4},{4,0},{1,9},{9... | collective-permute-start | bytes 663560 | tf_op jit(solution)/shard_map/ppermute | solution.py:434
  19.7 13.2 %collective-permute-start.7 = (f32[24,2304]{1,0:T(8,128)S(1)}, f32[24,2304]{1,0:T(8,128)S(1)}, u32[]{:S(2)}, u32[]{:S(2)}) collective-permute-start(f32[24,2304]{1,0:T(8,128)S(1)} %collective-permute-done.3.refs_0_), channel_id=1, source_target_pairs={{0,8},{8,16},{16,24},{24,28},{28,20},{20,12},{12,4},{4,0},{1,9},{9... | collective-permute-start | bytes 663560 | tf_op jit(solution)/shard_map/ppermute | solution.py:434
  24.4 8.8 %collective-permute-start.8 = (f32[24,2304]{1,0:T(8,128)S(1)}, f32[24,2304]{1,0:T(8,128)S(1)}, u32[]{:S(2)}, u32[]{:S(2)}) collective-permute-start(f32[24,2304]{1,0:T(8,128)S(1)} %collective-permute-done.4.refs_1_), channel_id=1, source_target_pairs={{0,8},{8,16},{16,24},{24,28},{28,20},{20,12},{12,4},{4,0},{1,9},{9... | collective-permute-start | bytes 663560 | tf_op jit(solution)/shard_map/ppermute | solution.py:434
  26.3 11.4 %collective-permute-start.10 = (f32[24,2304]{1,0:T(8,128)S(1)}, f32[24,2304]{1,0:T(8,128)S(1)}, u32[]{:S(2)}, u32[]{:S(2)}) collective-permute-start(f32[24,2304]{1,0:T(8,128)S(1)} %collective-permute-done.6.refs_1_), channel_id=1, source_target_pairs={{0,4},{8,0},{16,8},{24,16},{28,24},{20,28},{12,20},{4,12},{1,5},{9... | collective-permute-start | bytes 663560 | tf_op jit(solution)/shard_map/ppermute | solution.py:434
  27.3 0.9 %copy-start.8 = (bf16[384,128]{1,0:T(8,128)(2,1)S(1)}, bf16[384,128]{1,0:T(8,128)(2,1)}, u32[]{:S(2)}) copy-start(bf16[384,128]{1,0:T(8,128)(2,1)} %copy-done.7) | copy-start | bytes 294916
  28.2 1.9 %copy-start.9 = (bf16[384,128]{1,0:T(8,128)(2,1)S(1)}, bf16[384,128]{1,0:T(8,128)(2,1)}, u32[]{:S(2)}) copy-start(bf16[384,128]{1,0:T(8,128)(2,1)} %copy-done.7) | copy-start | bytes 294916
  28.3 9.5 %collective-permute-start.9 = (f32[24,2304]{1,0:T(8,128)S(1)}, f32[24,2304]{1,0:T(8,128)S(1)}, u32[]{:S(2)}, u32[]{:S(2)}) collective-permute-start(f32[24,2304]{1,0:T(8,128)S(1)} %collective-permute-done.5.refs_0_), channel_id=1, source_target_pairs={{0,4},{8,0},{16,8},{24,16},{28,24},{20,28},{12,20},{4,12},{1,5},{9... | collective-permute-start | bytes 663560 | tf_op jit(solution)/shard_map/ppermute | solution.py:434
  32.9 9.9 %collective-permute-start.11 = (f32[24,2304]{1,0:T(8,128)S(1)}, f32[24,2304]{1,0:T(8,128)S(1)}, u32[]{:S(2)}, u32[]{:S(2)}) collective-permute-start(f32[24,2304]{1,0:T(8,128)S(1)} %collective-permute-done.7.refs_0_), channel_id=1, source_target_pairs={{0,8},{8,16},{16,24},{24,28},{28,20},{20,12},{12,4},{4,0},{1,9},{9... | collective-permute-start | bytes 663560 | tf_op jit(solution)/shard_map/ppermute | solution.py:434
  33.2 12.7 %collective-permute-start.12 = (f32[24,2304]{1,0:T(8,128)S(1)}, f32[24,2304]{1,0:T(8,128)S(1)}, u32[]{:S(2)}, u32[]{:S(2)}) collective-permute-start(f32[24,2304]{1,0:T(8,128)S(1)} %collective-permute-done.8.refs_1_), channel_id=1, source_target_pairs={{0,8},{8,16},{16,24},{24,28},{28,20},{20,12},{12,4},{4,0},{1,9},{9... | collective-permute-start | bytes 663560 | tf_op jit(solution)/shard_map/ppermute | solution.py:434
  37.6 6.7 %collective-permute-start.14 = (f32[24,2304]{1,0:T(8,128)S(1)}, f32[24,2304]{1,0:T(8,128)S(1)}, u32[]{:S(2)}, u32[]{:S(2)}) collective-permute-start(f32[24,2304]{1,0:T(8,128)S(1)} %collective-permute-done.10.refs_1_), channel_id=1, source_target_pairs={{0,4},{8,0},{16,8},{24,16},{28,24},{20,28},{12,20},{4,12},{1,5},{9... | collective-permute-start | bytes 663560 | tf_op jit(solution)/shard_map/ppermute | solution.py:434
  37.9 11.0 %collective-permute-start.13 = (f32[24,2304]{1,0:T(8,128)S(1)}, f32[24,2304]{1,0:T(8,128)S(1)}, u32[]{:S(2)}, u32[]{:S(2)}) collective-permute-start(f32[24,2304]{1,0:T(8,128)S(1)} %collective-permute-done.9.refs_0_), channel_id=1, source_target_pairs={{0,4},{8,0},{16,8},{24,16},{28,24},{20,28},{12,20},{4,12},{1,5},{9... | collective-permute-start | bytes 663560 | tf_op jit(solution)/shard_map/ppermute | solution.py:434
  42.7 6.3 %collective-permute-start.15 = (f32[24,2304]{1,0:T(8,128)S(1)}, f32[24,2304]{1,0:T(8,128)S(1)}, u32[]{:S(2)}, u32[]{:S(2)}) collective-permute-start(f32[24,2304]{1,0:T(8,128)S(1)} %collective-permute-done.11.refs_0_), channel_id=1, source_target_pairs={{0,8},{8,16},{16,24},{24,28},{28,20},{20,12},{12,4},{4,0},{1,9},{9... | collective-permute-start | bytes 663560 | tf_op jit(solution)/shard_map/ppermute | solution.py:434
  44.3 6.9 %collective-permute-start.16 = (f32[24,2304]{1,0:T(8,128)S(1)}, f32[24,2304]{1,0:T(8,128)S(1)}, u32[]{:S(2)}, u32[]{:S(2)}) collective-permute-start(f32[24,2304]{1,0:T(8,128)S(1)} %collective-permute-done.14.refs_1_), channel_id=1, source_target_pairs={{0,4},{8,0},{16,8},{24,16},{28,24},{20,28},{12,20},{4,12},{1,5},{9... | collective-permute-start | bytes 663560 | tf_op jit(solution)/shard_map/ppermute | solution.py:434
  51.5 1.5 %collective-permute-start.17 = (f32[2,24,1152]{2,1,0:T(8,128)S(1)}, f32[2,24,1152]{2,1,0:T(8,128)S(1)}, u32[]{:S(2)}, u32[]{:S(2)}) collective-permute-start(f32[2,24,1152]{2,1,0:T(8,128)S(1)} %get-tuple-element.39), channel_id=1, source_target_pairs={{0,1},{1,0},{2,3},{3,2},{4,5},{5,4},{6,7},{7,6},{8,9},{9,8},{10,11... | collective-permute-start | bytes 663560 | tf_op jit(solution)/shard_map/ppermute | solution.py:404
  52.4 16.0 %copy-start.1 = (f32[4,12,2304]{2,0,1:T(4,128)S(1)}, f32[4,12,2304]{2,0,1:T(4,128)}, u32[]{:S(2)}) copy-start(f32[4,12,2304]{2,0,1:T(4,128)} %param.10) | copy-start | bytes 1327108
  53.1 15.2 %collective-permute-start.18 = (f32[48,1152]{1,0:T(8,128)S(1)}, f32[48,1152]{1,0:T(8,128)S(1)}, u32[]{:S(2)}, u32[]{:S(2)}) collective-permute-start(f32[48,1152]{1,0:T(8,128)S(1)} %pack.1), channel_id=1, source_target_pairs={{0,2},{1,3},{2,0},{3,1},{4,6},{5,7},{6,4},{7,5},{8,10},{9,11},{10,... | collective-permute-start | bytes 663560 | tf_op jit(solution)/shard_map/ppermute | solution.py:404
  54.5 13.1 %all-to-all-start = ((f32[32,1,128]{2,1,0:T(1,128)}), f32[32,1,128]{2,1,0:T(1,128)S(1)}, u32[]{:S(2)}, u32[]{:S(2)}) async-start(f32[32,1,128]{2,1,0:T(1,128)} %get-tuple-element.63), calls=%async_computation | async-start | bytes 32768 | tf_op jit(solution)/shard_map/all_to_all | solution.py:503
  60.5 7.8 %collective-permute-start.19 = (f32[24,1152]{1,0:T(8,128)S(1)}, f32[24,1152]{1,0:T(8,128)S(1)}, u32[]{:S(2)}, u32[]{:S(2)}) collective-permute-start(f32[24,1152]{1,0:T(8,128)S(1)} %get-tuple-element.61), channel_id=1, source_target_pairs={{0,1},{1,0},{2,3},{3,2},{4,5},{5,4},{6,7},{7,6},{8,9},{9,8},{10,11... | collective-permute-start | bytes 331784 | tf_op jit(solution)/shard_map/ppermute | solution.py:404
  60.8 7.5 %collective-permute-start.20 = (f32[24,1152]{1,0:T(8,128)S(1)}, f32[24,1152]{1,0:T(8,128)S(1)}, u32[]{:S(2)}, u32[]{:S(2)}) collective-permute-start(f32[24,1152]{1,0:T(8,128)S(1)} %get-tuple-element.62), channel_id=1, source_target_pairs={{0,3},{1,2},{2,1},{3,0},{4,7},{5,6},{6,5},{7,4},{8,11},{9,10},{10,... | collective-permute-start | bytes 331784 | tf_op jit(solution)/shard_map/ppermute | solution.py:404
  (6 other events, 4.2 us)

commit v11 on v9

--- a/solution.py
+++ b/solution.py
@@ -58,7 +58,7 @@
     return (2.0 * np.pi * np.fft.fftfreq(length)) ** 2
 
 
-def transform_tables(slab_index, slabs):
+def transform_tables(slabs):
     x_waves, y_cells, z_cells, z_waves = (np.arange(count) for count in (NX, NY, NZ, NZP))
     planes = NX // slabs
     held_x = [(slab ^ (x_waves // planes)) * planes + x_waves % planes for slab in range(slabs)]
@@ -69,20 +69,17 @@
     )
     kernel_table = 4.0 * math.pi / (NX * NY * NZP) / (total + screening * screening)
     y_matrix = cas(y_cells, y_cells, NY)
-    forward = jnp.asarray(np.stack([wide(cas(x_waves, held, NX)) for held in held_x]))
+    forward = [wide(cas(x_waves, held, NX)) for held in held_x]
     quads = 4 * (x_waves[:SIDE_X] // 2) + x_waves[:SIDE_X] % 2
     kept = np.concatenate([quads, quads + 2])
-    backward = jnp.asarray(np.stack([wide(cas(held, kept, NX)) for held in held_x]))
+    backward = [wide(cas(held, kept, NX)) for held in held_x]
     kernel_table = np.pad(kernel_table, ((0, 0), (0, 0), (0, GAP - NY)))
-    return (
-        lax.dynamic_index_in_dim(forward, slab_index, 0, keepdims=False),
-        jnp.asarray(wide(y_matrix)),
-        jnp.asarray(tall(cas(z_waves, z_cells, NZP))),
-        jnp.asarray(kernel_table.reshape(NZP, NX * GAP).astype(np.float32)),
-        jnp.asarray(wide(cas(z_cells, z_waves, NZP))),
-        jnp.asarray(tall(y_matrix)),
-        lax.dynamic_index_in_dim(backward, slab_index, 0, keepdims=False),
-    )
+    lanes = 3 * NZP
+    wides = [wide(y_matrix), wide(cas(z_cells, z_waves, NZP)), *forward, *backward]
+    wides = [np.pad(matrix, ((0, 0), (0, lanes - matrix.shape[1]))) for matrix in wides]
+    talls = [tall(cas(z_waves, z_cells, NZP)), tall(y_matrix)]
+    flat = kernel_table.reshape(NZP, NX * GAP).astype(np.float32)
+    return tuple(jnp.asarray(table) for table in (np.stack(wides), np.concatenate(talls), flat))
 
 
 def apply_left(matrix, value):
@@ -337,6 +334,36 @@
     )(piece, mine, theirs)
 
 
+def stage_kernel(
+    slabs, place, wides, talls, flat, x_fwd, y_fwd, z_fwd, table, z_inv, y_inv, x_inv
+):
+    y_fwd[...] = wides[0, :, : 3 * NY]
+    z_inv[...] = wides[1]
+    x_fwd[...] = pick(place[0], [wides[2 + slab, :, : 3 * NX] for slab in range(slabs)])
+    x_inv[...] = pick(place[0], [wides[2 + slabs + slab, :, : 3 * NX] for slab in range(slabs)])
+    z_fwd[...] = talls[: 4 * NZP]
+    y_inv[...] = talls[4 * NZP :]
+    table[...] = flat[...]
+
+
+def stage(place, slabs):
+    tables = transform_tables(slabs)
+    halves = jnp.bfloat16
+    shapes = [
+        ((NX, 3 * NX), halves), ((NY, 3 * NY), halves), ((4 * NZP, 2 * GAP), halves),
+        ((NZP, NX * GAP), jnp.float32), ((NZ, 3 * NZP), halves), ((4 * NY, 2 * GAP), halves),
+        ((NX, 3 * NX), halves),
+    ]
+    return pl.pallas_call(
+        functools.partial(stage_kernel, slabs),
+        out_shape=[jax.ShapeDtypeStruct(shape, kind) for shape, kind in shapes],
+        in_specs=with_scalar(len(tables)),
+        out_specs=in_vmem(len(shapes)),
+        compiler_params=pltpu.CompilerParams(vmem_limit_bytes=8 << 20),
+        name="stage",
+    )(place, *tables)
+
+
 def join_kernel(*refs):
     out_ref = refs[-1]
     first = 0
@@ -452,7 +479,7 @@
     force = clear((NX, NY * NZ))
 
     own, partners, counts = lax.optimization_barrier((own, partners, counts))
-    tables = transform_tables(slab_index, slabs)
+    tables = stage(place, slabs)
 
     groups = jnp.stack([group for _, group in others]).astype(jnp.int32)
     active = (slab_index < counts).astype(jnp.float32)

time: 73.4 us -> 68.8 us (0.937)
  waiting for transfers between devices: 29.5 us -> 18 us
  starting transfers between devices: 28 us -> 31.5 us
  local copies, waits for them, and re-layouts: 4.44 us -> 7.31 us
    ppermute x14, waiting for transfers between devices: 18.9 us -> 12.1 us  [shift(): return lax.ppermute(value, 'band', moves)]
    ppermute x7, waiting for transfers between devices: 5.44 us -> 0.7 us  [slab_swap(): return lax.ppermute(value, 'slab', [(i, i ^ reach) for i in range(size)])]
    unnamed x20 -> x34, local copies, waits for them, and re-layouts: 3.34 us -> 6.98 us
    all_to_all x1, starting transfers between devices: 3.17 us -> 6.07 us  [body(): shared = lax.all_to_all(energy, ('band', 'slab'), 0, 0)]
    squeeze x1 -> x0, local copies, waits for them, and re-layouts: 0.77 us -> none  [transform_tables(): lax.dynamic_index_in_dim(backward, slab_index, 0, keepdims=False)]
  transfers between devices with their start and end apart: 22 -> 22, of which waited for: 10 -> 8; matrix products, arithmetic and copies ran while one was open for 2% -> 1% of each run, Pallas kernels for 11% -> 12%
where the time goes in v11:
time: 68.8 us; the launch traced here: 68.5 us
  starting transfers between devices  31.5 us (46%)
  waiting for transfers between devices  18 us (26%)
  Pallas kernels  10 us (15%)
  local copies, waits for them, and re-layouts  7.31 us (11%)
  between operations  1.03 us (1%)
    ppermute x14, starting transfers between devices, shift(): return lax.ppermute(value, 'band', moves)  18.8 us
    ppermute x14, waiting for transfers between devices, shift(): return lax.ppermute(value, 'band', moves)  12.1 us
    unnamed x34, local copies, waits for them, and re-layouts  6.98 us
    pallas_call x7, Pallas kernels, pair_step(): pl.pallas_call(functools.partial(pair_kernel, slot), out_shape=outs, in_s...  6.88 us
    ppermute x7, starting transfers between devices, slab_swap(): return lax.ppermute(value, 'slab', [(i, i ^ reach) for i in range(size)])  6.58 us
    all_to_all x1, starting transfers between devices, body(): shared = lax.all_to_all(energy, ('band', 'slab'), 0, 0)  6.07 us
    all_to_all x1, waiting for transfers between devices, body(): shared = lax.all_to_all(energy, ('band', 'slab'), 0, 0)  5.15 us
  transfers between devices with their start and end apart: 22, of which 8 were waited for; matrix products, arithmetic and copies ran while one was open for 1% of the time, Pallas kernels for 12%

profile of v11, /device:TPU:0, one launch (start us, length us, event | category | flops | bytes accessed | tf_op | source)
XLA Modules:
  0.0 68.5 jit_solution(17009778463744842045)
XLA Ops:
  0.6 1.0 %copy-done = f32[4,12,2304]{2,0,1:T(4,128)S(1)} copy-done((f32[4,12,2304]{2,0,1:T(4,128)S(1)}, f32[4,12,2304]{2,0,1:T(4,128)}, u32[]{:S(2)}) %copy-start) | copy-done | bytes 442392
  1.7 0.8 %prepare.1 = (f32[24,1152]{1,0:T(8,128)S(1)}, f32[24,1152]{1,0:T(8,128)}, f32[24,1152]{1,0:T(8,128)S(1)}, f32[24,1152]{1,0:T(8,128)S(1)}) custom-call(s32[1]{0:T(128)} %bitcast.place, f32[12,4,2304]{2,1,0:T(4,128)S(1)} %bitcast.19), custom_call_target="tpu_custom_call" | custom-call | tf_op jit(solution)/shard_map/prepare/pallas_call | solution.py:249
  2.9 2.5 %collective-permute-start.1 = (f32[24,1152]{1,0:T(8,128)S(1)}, f32[24,1152]{1,0:T(8,128)S(1)}, u32[]{:S(2)}, u32[]{:S(2)}) collective-permute-start(f32[24,1152]{1,0:T(8,128)S(1)} %get-tuple-element.37), channel_id=1, source_target_pairs={{0,2},{1,3},{2,0},{3,1},{4,6},{5,7},{6,4},{7,5},{8,10},{9,11},{10,... | collective-permute-start | bytes 331784 | tf_op jit(solution)/shard_map/ppermute | solution.py:414
  5.7 1.0 %copy-done.3 = bf16[10,48,288]{2,1,0:T(8,128)(2,1)S(1)} copy-done((bf16[10,48,288]{2,1,0:T(8,128)(2,1)S(1)}, bf16[10,48,288]{2,1,0:T(8,128)(2,1)}, u32[]{:S(2)}) %copy-start.3) | copy-done | bytes 276504
  6.6 0.9 %copy-done.4 = bf16[576,128]{1,0:T(8,128)(2,1)S(1)} copy-done((bf16[576,128]{1,0:T(8,128)(2,1)S(1)}, bf16[576,128]{1,0:T(8,128)(2,1)}, u32[]{:S(2)}) %copy-start.4) | copy-done | bytes 147480
  7.7 0.6 copy-done.5
  10.2 1.9 %collective-permute-start.3 = (f32[24,2304]{1,0:T(8,128)S(1)}, f32[24,2304]{1,0:T(8,128)S(1)}, u32[]{:S(2)}, u32[]{:S(2)}) collective-permute-start(f32[24,2304]{1,0:T(8,128)S(1)} %assemble.2.refs_0_), channel_id=1, source_target_pairs={{0,8},{8,16},{16,24},{24,28},{28,20},{20,12},{12,4},{4,0},{1,9},{9... | collective-permute-start | bytes 663560 | tf_op jit(solution)/shard_map/ppermute | solution.py:444
  12.2 0.7 %collective-permute-start.6 = (f32[24,2304]{1,0:T(8,128)S(1)}, f32[24,2304]{1,0:T(8,128)S(1)}, u32[]{:S(2)}, u32[]{:S(2)}) collective-permute-start(f32[24,2304]{1,0:T(8,128)S(1)} %assemble.3.refs_1_), channel_id=1, source_target_pairs={{0,4},{8,0},{16,8},{24,16},{28,24},{20,28},{12,20},{4,12},{1,5},{9... | collective-permute-start | bytes 663560 | tf_op jit(solution)/shard_map/ppermute | solution.py:444
  12.9 1.6 %collective-permute-start.5 = (f32[24,2304]{1,0:T(8,128)S(1)}, f32[24,2304]{1,0:T(8,128)S(1)}, u32[]{:S(2)}, u32[]{:S(2)}) collective-permute-start(f32[24,2304]{1,0:T(8,128)S(1)} %assemble.2.refs_0_), channel_id=1, source_target_pairs={{0,4},{8,0},{16,8},{24,16},{28,24},{20,28},{12,20},{4,12},{1,5},{9... | collective-permute-start | bytes 663560 | tf_op jit(solution)/shard_map/ppermute | solution.py:444
  15.6 3.0 %collective-permute-done.3.refs_0_ = f32[24,2304]{1,0:T(8,128)S(1)} collective-permute-done((f32[24,2304]{1,0:T(8,128)S(1)}, f32[24,2304]{1,0:T(8,128)S(1)}, u32[]{:S(2)}, u32[]{:S(2)}) %collective-permute-start.3) | collective-permute-done | bytes 221216 | tf_op jit(solution)/shard_map/ppermute | solution.py:444
  18.6 1.8 %collective-permute-start.7 = (f32[24,2304]{1,0:T(8,128)S(1)}, f32[24,2304]{1,0:T(8,128)S(1)}, u32[]{:S(2)}, u32[]{:S(2)}) collective-permute-start(f32[24,2304]{1,0:T(8,128)S(1)} %collective-permute-done.3.refs_0_), channel_id=1, source_target_pairs={{0,8},{8,16},{16,24},{24,28},{28,20},{20,12},{12,4},{4,0},{1,9},{9... | collective-permute-start | bytes 663560 | tf_op jit(solution)/shard_map/ppermute | solution.py:444
  20.4 2.9 %collective-permute-done.4.refs_1_ = f32[24,2304]{1,0:T(8,128)S(1)} collective-permute-done((f32[24,2304]{1,0:T(8,128)S(1)}, f32[24,2304]{1,0:T(8,128)S(1)}, u32[]{:S(2)}, u32[]{:S(2)}) %collective-permute-start.4) | collective-permute-done | bytes 221216 | tf_op jit(solution)/shard_map/ppermute | solution.py:444
  23.3 1.8 %collective-permute-start.8 = (f32[24,2304]{1,0:T(8,128)S(1)}, f32[24,2304]{1,0:T(8,128)S(1)}, u32[]{:S(2)}, u32[]{:S(2)}) collective-permute-start(f32[24,2304]{1,0:T(8,128)S(1)} %collective-permute-done.4.refs_1_), channel_id=1, source_target_pairs={{0,8},{8,16},{16,24},{24,28},{28,20},{20,12},{12,4},{4,0},{1,9},{9... | collective-permute-start | bytes 663560 | tf_op jit(solution)/shard_map/ppermute | solution.py:444
  25.5 0.9 %copy-done.6 = bf16[384,128]{1,0:T(8,128)(2,1)S(1)} copy-done((bf16[384,128]{1,0:T(8,128)(2,1)S(1)}, bf16[384,128]{1,0:T(8,128)(2,1)}, u32[]{:S(2)}) %copy-start.6) | copy-done | bytes 98328
  26.4 0.7 %copy-done.13 = bf16[48,144]{1,0:T(8,128)(2,1)S(1)} copy-done((bf16[48,144]{1,0:T(8,128)(2,1)S(1)}, bf16[48,144]{1,0:T(8,128)(2,1)}, u32[]{:S(2)}) %copy-start.13) | copy-done | bytes 13848
  27.3 1.8 %collective-permute-start.9 = (f32[24,2304]{1,0:T(8,128)S(1)}, f32[24,2304]{1,0:T(8,128)S(1)}, u32[]{:S(2)}, u32[]{:S(2)}) collective-permute-start(f32[24,2304]{1,0:T(8,128)S(1)} %collective-permute-done.5.refs_0_), channel_id=1, source_target_pairs={{0,4},{8,0},{16,8},{24,16},{28,24},{20,28},{12,20},{4,12},{1,5},{9... | collective-permute-start | bytes 663560 | tf_op jit(solution)/shard_map/ppermute | solution.py:444
  29.1 2.7 %pair_step.8 = (f32[1,128]{1,0:T(1,128)S(1)}, f32[48,2304]{1,0:T(8,128)S(1)}) custom-call(f32[14,128]{1,0:T(8,128)S(1)} %broadcast_in_dim.73.weights, f32[48,2304]{1,0:T(8,128)S(1)} %join.8.refs_0_.own_ref, f32[48,2304]{1,0:T(8,128)S(1)} %join.10.refs_2_.other_ref, bf16[48,144]{1,0:T(8,128)(2,1)S(1)} %copy-done.9, ...), custom_call_target="tpu_custom_call", output_to_operand_aliasing={{1}: (10, {})} | custom-call | flops 3221225472 | bytes 3145728 | tf_op jit(solution)/shard_map/pair_step/pallas_call | solution.py:198
  32.1 4.5 %collective-permute-start.12 = (f32[24,2304]{1,0:T(8,128)S(1)}, f32[24,2304]{1,0:T(8,128)S(1)}, u32[]{:S(2)}, u32[]{:S(2)}) collective-permute-start(f32[24,2304]{1,0:T(8,128)S(1)} %collective-permute-done.8.refs_1_), channel_id=1, source_target_pairs={{0,8},{8,16},{16,24},{24,28},{28,20},{20,12},{12,4},{4,0},{1,9},{9... | collective-permute-start | bytes 663560 | tf_op jit(solution)/shard_map/ppermute | solution.py:444
  36.9 2.0 %collective-permute-start.13 = (f32[24,2304]{1,0:T(8,128)S(1)}, f32[24,2304]{1,0:T(8,128)S(1)}, u32[]{:S(2)}, u32[]{:S(2)}) collective-permute-start(f32[24,2304]{1,0:T(8,128)S(1)} %collective-permute-done.9.refs_0_), channel_id=1, source_target_pairs={{0,4},{8,0},{16,8},{24,16},{28,24},{20,28},{12,20},{4,12},{1,5},{9... | collective-permute-start | bytes 663560 | tf_op jit(solution)/shard_map/ppermute | solution.py:444
  38.9 2.7 %pair_step.10 = (f32[1,128]{1,0:T(1,128)S(1)}, f32[48,2304]{1,0:T(8,128)S(1)}) custom-call(f32[14,128]{1,0:T(8,128)S(1)} %broadcast_in_dim.73.weights, f32[48,2304]{1,0:T(8,128)S(1)} %join.8.refs_0_.own_ref, f32[48,2304]{1,0:T(8,128)S(1)} %join.12.refs_4_.other_ref, bf16[48,144]{1,0:T(8,128)(2,1)S(1)} %copy-done.9, ...), custom_call_target="tpu_custom_call", output_to_operand_aliasing={{1}: (10, {})} | custom-call | flops 3221225472 | bytes 3145728 | tf_op jit(solution)/shard_map/pair_step/pallas_call | solution.py:198
  41.7 1.5 %collective-permute-done.14.refs_1_ = f32[24,2304]{1,0:T(8,128)S(1)} collective-permute-done((f32[24,2304]{1,0:T(8,128)S(1)}, f32[24,2304]{1,0:T(8,128)S(1)}, u32[]{:S(2)}, u32[]{:S(2)}) %collective-permute-start.14) | collective-permute-done | bytes 221216 | tf_op jit(solution)/shard_map/ppermute | solution.py:444
  43.2 1.8 %collective-permute-start.16 = (f32[24,2304]{1,0:T(8,128)S(1)}, f32[24,2304]{1,0:T(8,128)S(1)}, u32[]{:S(2)}, u32[]{:S(2)}) collective-permute-start(f32[24,2304]{1,0:T(8,128)S(1)} %collective-permute-done.14.refs_1_), channel_id=1, source_target_pairs={{0,4},{8,0},{16,8},{24,16},{28,24},{20,28},{12,20},{4,12},{1,5},{9... | collective-permute-start | bytes 663560 | tf_op jit(solution)/shard_map/ppermute | solution.py:444
  45.4 2.4 %collective-permute-done.13.refs_0_ = f32[24,2304]{1,0:T(8,128)S(1)} collective-permute-done((f32[24,2304]{1,0:T(8,128)S(1)}, f32[24,2304]{1,0:T(8,128)S(1)}, u32[]{:S(2)}, u32[]{:S(2)}) %collective-permute-start.13) | collective-permute-done | bytes 221216 | tf_op jit(solution)/shard_map/ppermute | solution.py:444
  47.9 2.2 %collective-permute-done.16.refs_1_ = f32[24,2304]{1,0:T(8,128)S(1)} collective-permute-done((f32[24,2304]{1,0:T(8,128)S(1)}, f32[24,2304]{1,0:T(8,128)S(1)}, u32[]{:S(2)}, u32[]{:S(2)}) %collective-permute-start.16) | collective-permute-done | bytes 221216 | tf_op jit(solution)/shard_map/ppermute | solution.py:444
  50.5 0.8 %pair_step.13 = (f32[32,1,128]{2,1,0:T(1,128)}, f32[24,1152]{1,0:T(8,128)S(1)}, f32[24,1152]{1,0:T(8,128)S(1)}, f32[24,1152]{1,0:T(8,128)S(1)}, f32[24,1152]{1,0:T(8,128)S(1)}) custom-call(f32[14,128]{1,0:T(8,128)S(1)} %broadcast_in_dim.73.weights, f32[48,2304]{1,0:T(8,128)S(1)} %join.8.refs_0_.own_ref, f32[48,2304]{1,0:T(8,128)S(1)} %join.15.refs_7_.other_ref, ...), custom_call_target="tpu_custom_call" | custom-call | flops 3221225472 | bytes 3145728 | tf_op jit(solution)/shard_map/pair_step/pallas_call | solution.py:198
  51.3 0.7 collective-permute-done.17.theirs
  52.0 1.4 %collective-permute-start.18 = (f32[48,1152]{1,0:T(8,128)S(1)}, f32[48,1152]{1,0:T(8,128)S(1)}, u32[]{:S(2)}, u32[]{:S(2)}) collective-permute-start(f32[48,1152]{1,0:T(8,128)S(1)} %pack.1), channel_id=1, source_target_pairs={{0,2},{1,3},{2,0},{3,1},{4,6},{5,7},{6,4},{7,5},{8,10},{9,11},{10,... | collective-permute-start | bytes 663560 | tf_op jit(solution)/shard_map/ppermute | solution.py:414
  53.4 6.1 %all-to-all-start = ((f32[32,1,128]{2,1,0:T(1,128)}), f32[32,1,128]{2,1,0:T(1,128)S(1)}, u32[]{:S(2)}, u32[]{:S(2)}) async-start(f32[32,1,128]{2,1,0:T(1,128)} %get-tuple-element.67), calls=%async_computation | async-start | bytes 32768 | tf_op jit(solution)/shard_map/all_to_all | solution.py:512
  59.8 1.6 %collective-permute-start.20 = (f32[24,1152]{1,0:T(8,128)S(1)}, f32[24,1152]{1,0:T(8,128)S(1)}, u32[]{:S(2)}, u32[]{:S(2)}) collective-permute-start(f32[24,1152]{1,0:T(8,128)S(1)} %get-tuple-element.66), channel_id=1, source_target_pairs={{0,3},{1,2},{2,1},{3,0},{4,7},{5,6},{6,5},{7,4},{8,11},{9,10},{10,... | collective-permute-start | bytes 331784 | tf_op jit(solution)/shard_map/ppermute | solution.py:414
  61.4 5.2 %all-to-all-done.shared = f32[32,1,128]{2,1,0:T(1,128)S(1)} async-done(((f32[32,1,128]{2,1,0:T(1,128)}), f32[32,1,128]{2,1,0:T(1,128)S(1)}, u32[]{:S(2)}, u32[]{:S(2)}) %all-to-all-start) | async-done | bytes 16416 | tf_op jit(solution)/shard_map/all_to_all | solution.py:512
  66.6 0.6 total.1
  67.4 1.1 %finish.1 = f32[12,4,2304]{2,1,0:T(4,128)} custom-call(s32[1]{0:T(128)} %bitcast.place, f32[12,4,2304]{2,1,0:T(4,128)S(1)} %bitcast.20, f32[24,1152]{1,0:T(8,128)S(1)} %fusion.2.local_pot, f32[24,1152]{1,0:T(8,128)S(1)} %get-tuple-element.64.refs_0_, f32[24,1152]{1,0:T(8,128)S(1)} %collective-permute-done.19.refs_1_, ...), custom_call_target="tpu_custom_call" | custom-call | tf_op jit(solution)/shard_map/finish/pallas_call | solution.py:402
  (83 shorter events, 6.4 us)
Async XLA Ops:
  0.6 1.0 %copy-start = (f32[4,12,2304]{2,0,1:T(4,128)S(1)}, f32[4,12,2304]{2,0,1:T(4,128)}, u32[]{:S(2)}) copy-start(f32[4,12,2304]{2,0,1:T(4,128)} %param.6) | copy-start | bytes 1327108
  1.7 4.0 %copy-start.2 = (f32[96,3072]{1,0:T(8,128)S(1)}, f32[96,3072]{1,0:T(8,128)}, u32[]{:S(2)}) copy-start(f32[96,3072]{1,0:T(8,128)} %constant.100.clone.flat) | copy-start | bytes 3538948
  2.4 7.8 %collective-permute-start = (f32[24,1152]{1,0:T(8,128)}, f32[24,1152]{1,0:T(8,128)S(1)}, u32[]{:S(2)}, u32[]{:S(2)}) collective-permute-start(f32[24,1152]{1,0:T(8,128)} %get-tuple-element.36), channel_id=1, source_target_pairs={{0,1},{1,0},{2,3},{3,2},{4,5},{5,4},{6,7},{7,6},{8,9},{9,8},{10,11... | collective-permute-start | bytes 331784 | tf_op jit(solution)/shard_map/ppermute | solution.py:414
  2.9 9.2 %collective-permute-start.1 = (f32[24,1152]{1,0:T(8,128)S(1)}, f32[24,1152]{1,0:T(8,128)S(1)}, u32[]{:S(2)}, u32[]{:S(2)}) collective-permute-start(f32[24,1152]{1,0:T(8,128)S(1)} %get-tuple-element.37), channel_id=1, source_target_pairs={{0,2},{1,3},{2,0},{3,1},{4,6},{5,7},{6,4},{7,5},{8,10},{9,11},{10,... | collective-permute-start | bytes 331784 | tf_op jit(solution)/shard_map/ppermute | solution.py:414
  5.4 6.7 %collective-permute-start.2 = (f32[24,1152]{1,0:T(8,128)S(1)}, f32[24,1152]{1,0:T(8,128)S(1)}, u32[]{:S(2)}, u32[]{:S(2)}) collective-permute-start(f32[24,1152]{1,0:T(8,128)S(1)} %get-tuple-element.38), channel_id=1, source_target_pairs={{0,3},{1,2},{2,1},{3,0},{4,7},{5,6},{6,5},{7,4},{8,11},{9,10},{10,... | collective-permute-start | bytes 331784 | tf_op jit(solution)/shard_map/ppermute | solution.py:414
  5.6 1.0 %copy-start.3 = (bf16[10,48,288]{2,1,0:T(8,128)(2,1)S(1)}, bf16[10,48,288]{2,1,0:T(8,128)(2,1)}, u32[]{:S(2)}) copy-start(bf16[10,48,288]{2,1,0:T(8,128)(2,1)} %constant.98.clone.wides) | copy-start | bytes 829444
  10.1 4.8 %copy-start.15 = (s32[8,2]{0,1:T(2,128)S(1)}, s32[8,2]{0,1:T(2,128)}, u32[]{:S(2)}) copy-start(s32[8,2]{0,1:T(2,128)} %param.7) | copy-start | bytes 196
  10.1 4.9 %copy-start.16 = (s32[8,2]{0,1:T(2,128)S(1)}, s32[8,2]{0,1:T(2,128)}, u32[]{:S(2)}) copy-start(s32[8,2]{0,1:T(2,128)} %param.8) | copy-start | bytes 196
  10.2 15.3 %copy-start.9 = (bf16[48,144]{1,0:T(8,128)(2,1)S(1)}, bf16[48,144]{1,0:T(8,128)(2,1)}, u32[]{:S(2)}) copy-start(bf16[48,144]{1,0:T(8,128)(2,1)} %copy-done.8) | copy-start | bytes 41476
  10.2 15.3 %copy-start.11 = (bf16[48,144]{1,0:T(8,128)(2,1)S(1)}, bf16[48,144]{1,0:T(8,128)(2,1)}, u32[]{:S(2)}) copy-start(bf16[48,144]{1,0:T(8,128)(2,1)} %copy-done.10) | copy-start | bytes 41476
  10.2 8.4 %collective-permute-start.3 = (f32[24,2304]{1,0:T(8,128)S(1)}, f32[24,2304]{1,0:T(8,128)S(1)}, u32[]{:S(2)}, u32[]{:S(2)}) collective-permute-start(f32[24,2304]{1,0:T(8,128)S(1)} %assemble.2.refs_0_), channel_id=1, source_target_pairs={{0,8},{8,16},{16,24},{24,28},{28,20},{20,12},{12,4},{4,0},{1,9},{9... | collective-permute-start | bytes 663560 | tf_op jit(solution)/shard_map/ppermute | solution.py:444
  12.2 13.0 %collective-permute-start.6 = (f32[24,2304]{1,0:T(8,128)S(1)}, f32[24,2304]{1,0:T(8,128)S(1)}, u32[]{:S(2)}, u32[]{:S(2)}) collective-permute-start(f32[24,2304]{1,0:T(8,128)S(1)} %assemble.3.refs_1_), channel_id=1, source_target_pairs={{0,4},{8,0},{16,8},{24,16},{28,24},{20,28},{12,20},{4,12},{1,5},{9... | collective-permute-start | bytes 663560 | tf_op jit(solution)/shard_map/ppermute | solution.py:444
  12.9 14.4 %collective-permute-start.5 = (f32[24,2304]{1,0:T(8,128)S(1)}, f32[24,2304]{1,0:T(8,128)S(1)}, u32[]{:S(2)}, u32[]{:S(2)}) collective-permute-start(f32[24,2304]{1,0:T(8,128)S(1)} %assemble.2.refs_0_), channel_id=1, source_target_pairs={{0,4},{8,0},{16,8},{24,16},{28,24},{20,28},{12,20},{4,12},{1,5},{9... | collective-permute-start | bytes 663560 | tf_op jit(solution)/shard_map/ppermute | solution.py:444
  14.5 8.9 %collective-permute-start.4 = (f32[24,2304]{1,0:T(8,128)S(1)}, f32[24,2304]{1,0:T(8,128)S(1)}, u32[]{:S(2)}, u32[]{:S(2)}) collective-permute-start(f32[24,2304]{1,0:T(8,128)S(1)} %assemble.3.refs_1_), channel_id=1, source_target_pairs={{0,8},{8,16},{16,24},{24,28},{28,20},{20,12},{12,4},{4,0},{1,9},{9... | collective-permute-start | bytes 663560 | tf_op jit(solution)/shard_map/ppermute | solution.py:444
  18.6 13.3 %collective-permute-start.7 = (f32[24,2304]{1,0:T(8,128)S(1)}, f32[24,2304]{1,0:T(8,128)S(1)}, u32[]{:S(2)}, u32[]{:S(2)}) collective-permute-start(f32[24,2304]{1,0:T(8,128)S(1)} %collective-permute-done.3.refs_0_), channel_id=1, source_target_pairs={{0,8},{8,16},{16,24},{24,28},{28,20},{20,12},{12,4},{4,0},{1,9},{9... | collective-permute-start | bytes 663560 | tf_op jit(solution)/shard_map/ppermute | solution.py:444
  23.3 8.8 %collective-permute-start.8 = (f32[24,2304]{1,0:T(8,128)S(1)}, f32[24,2304]{1,0:T(8,128)S(1)}, u32[]{:S(2)}, u32[]{:S(2)}) collective-permute-start(f32[24,2304]{1,0:T(8,128)S(1)} %collective-permute-done.4.refs_1_), channel_id=1, source_target_pairs={{0,8},{8,16},{16,24},{24,28},{28,20},{20,12},{12,4},{4,0},{1,9},{9... | collective-permute-start | bytes 663560 | tf_op jit(solution)/shard_map/ppermute | solution.py:444
  25.2 11.5 %collective-permute-start.10 = (f32[24,2304]{1,0:T(8,128)S(1)}, f32[24,2304]{1,0:T(8,128)S(1)}, u32[]{:S(2)}, u32[]{:S(2)}) collective-permute-start(f32[24,2304]{1,0:T(8,128)S(1)} %collective-permute-done.6.refs_1_), channel_id=1, source_target_pairs={{0,4},{8,0},{16,8},{24,16},{28,24},{20,28},{12,20},{4,12},{1,5},{9... | collective-permute-start | bytes 663560 | tf_op jit(solution)/shard_map/ppermute | solution.py:444
  27.2 2.0 %copy-start.7 = (bf16[384,128]{1,0:T(8,128)(2,1)S(1)}, bf16[384,128]{1,0:T(8,128)(2,1)}, u32[]{:S(2)}) copy-start(bf16[384,128]{1,0:T(8,128)(2,1)} %copy-done.5) | copy-start | bytes 294916
  27.2 2.0 %copy-start.14 = (bf16[48,144]{1,0:T(8,128)(2,1)S(1)}, bf16[48,144]{1,0:T(8,128)(2,1)}, u32[]{:S(2)}) copy-start(bf16[48,144]{1,0:T(8,128)(2,1)} %copy-done.12) | copy-start | bytes 41476
  27.3 9.5 %collective-permute-start.9 = (f32[24,2304]{1,0:T(8,128)S(1)}, f32[24,2304]{1,0:T(8,128)S(1)}, u32[]{:S(2)}, u32[]{:S(2)}) collective-permute-start(f32[24,2304]{1,0:T(8,128)S(1)} %collective-permute-done.5.refs_0_), channel_id=1, source_target_pairs={{0,4},{8,0},{16,8},{24,16},{28,24},{20,28},{12,20},{4,12},{1,5},{9... | collective-permute-start | bytes 663560 | tf_op jit(solution)/shard_map/ppermute | solution.py:444
  31.9 9.7 %collective-permute-start.11 = (f32[24,2304]{1,0:T(8,128)S(1)}, f32[24,2304]{1,0:T(8,128)S(1)}, u32[]{:S(2)}, u32[]{:S(2)}) collective-permute-start(f32[24,2304]{1,0:T(8,128)S(1)} %collective-permute-done.7.refs_0_), channel_id=1, source_target_pairs={{0,8},{8,16},{16,24},{24,28},{28,20},{20,12},{12,4},{4,0},{1,9},{9... | collective-permute-start | bytes 663560 | tf_op jit(solution)/shard_map/ppermute | solution.py:444
  32.1 12.9 %collective-permute-start.12 = (f32[24,2304]{1,0:T(8,128)S(1)}, f32[24,2304]{1,0:T(8,128)S(1)}, u32[]{:S(2)}, u32[]{:S(2)}) collective-permute-start(f32[24,2304]{1,0:T(8,128)S(1)} %collective-permute-done.8.refs_1_), channel_id=1, source_target_pairs={{0,8},{8,16},{16,24},{24,28},{28,20},{20,12},{12,4},{4,0},{1,9},{9... | collective-permute-start | bytes 663560 | tf_op jit(solution)/shard_map/ppermute | solution.py:444
  36.6 6.6 %collective-permute-start.14 = (f32[24,2304]{1,0:T(8,128)S(1)}, f32[24,2304]{1,0:T(8,128)S(1)}, u32[]{:S(2)}, u32[]{:S(2)}) collective-permute-start(f32[24,2304]{1,0:T(8,128)S(1)} %collective-permute-done.10.refs_1_), channel_id=1, source_target_pairs={{0,4},{8,0},{16,8},{24,16},{28,24},{20,28},{12,20},{4,12},{1,5},{9... | collective-permute-start | bytes 663560 | tf_op jit(solution)/shard_map/ppermute | solution.py:444
  36.9 10.9 %collective-permute-start.13 = (f32[24,2304]{1,0:T(8,128)S(1)}, f32[24,2304]{1,0:T(8,128)S(1)}, u32[]{:S(2)}, u32[]{:S(2)}) collective-permute-start(f32[24,2304]{1,0:T(8,128)S(1)} %collective-permute-done.9.refs_0_), channel_id=1, source_target_pairs={{0,4},{8,0},{16,8},{24,16},{28,24},{20,28},{12,20},{4,12},{1,5},{9... | collective-permute-start | bytes 663560 | tf_op jit(solution)/shard_map/ppermute | solution.py:444
  41.6 6.3 %collective-permute-start.15 = (f32[24,2304]{1,0:T(8,128)S(1)}, f32[24,2304]{1,0:T(8,128)S(1)}, u32[]{:S(2)}, u32[]{:S(2)}) collective-permute-start(f32[24,2304]{1,0:T(8,128)S(1)} %collective-permute-done.11.refs_0_), channel_id=1, source_target_pairs={{0,8},{8,16},{16,24},{24,28},{28,20},{20,12},{12,4},{4,0},{1,9},{9... | collective-permute-start | bytes 663560 | tf_op jit(solution)/shard_map/ppermute | solution.py:444
  43.2 6.9 %collective-permute-start.16 = (f32[24,2304]{1,0:T(8,128)S(1)}, f32[24,2304]{1,0:T(8,128)S(1)}, u32[]{:S(2)}, u32[]{:S(2)}) collective-permute-start(f32[24,2304]{1,0:T(8,128)S(1)} %collective-permute-done.14.refs_1_), channel_id=1, source_target_pairs={{0,4},{8,0},{16,8},{24,16},{28,24},{20,28},{12,20},{4,12},{1,5},{9... | collective-permute-start | bytes 663560 | tf_op jit(solution)/shard_map/ppermute | solution.py:444
  50.4 1.5 %collective-permute-start.17 = (f32[2,24,1152]{2,1,0:T(8,128)S(1)}, f32[2,24,1152]{2,1,0:T(8,128)S(1)}, u32[]{:S(2)}, u32[]{:S(2)}) collective-permute-start(f32[2,24,1152]{2,1,0:T(8,128)S(1)} %get-tuple-element.41), channel_id=1, source_target_pairs={{0,1},{1,0},{2,3},{3,2},{4,5},{5,4},{6,7},{7,6},{8,9},{9,8},{10,11... | collective-permute-start | bytes 663560 | tf_op jit(solution)/shard_map/ppermute | solution.py:414
  51.3 16.1 %copy-start.1 = (f32[4,12,2304]{2,0,1:T(4,128)S(1)}, f32[4,12,2304]{2,0,1:T(4,128)}, u32[]{:S(2)}) copy-start(f32[4,12,2304]{2,0,1:T(4,128)} %param.6) | copy-start | bytes 1327108
  52.0 15.2 %collective-permute-start.18 = (f32[48,1152]{1,0:T(8,128)S(1)}, f32[48,1152]{1,0:T(8,128)S(1)}, u32[]{:S(2)}, u32[]{:S(2)}) collective-permute-start(f32[48,1152]{1,0:T(8,128)S(1)} %pack.1), channel_id=1, source_target_pairs={{0,2},{1,3},{2,0},{3,1},{4,6},{5,7},{6,4},{7,5},{8,10},{9,11},{10,... | collective-permute-start | bytes 663560 | tf_op jit(solution)/shard_map/ppermute | solution.py:414
  53.4 13.2 %all-to-all-start = ((f32[32,1,128]{2,1,0:T(1,128)}), f32[32,1,128]{2,1,0:T(1,128)S(1)}, u32[]{:S(2)}, u32[]{:S(2)}) async-start(f32[32,1,128]{2,1,0:T(1,128)} %get-tuple-element.67), calls=%async_computation | async-start | bytes 32768 | tf_op jit(solution)/shard_map/all_to_all | solution.py:512
  59.5 7.8 %collective-permute-start.19 = (f32[24,1152]{1,0:T(8,128)S(1)}, f32[24,1152]{1,0:T(8,128)S(1)}, u32[]{:S(2)}, u32[]{:S(2)}) collective-permute-start(f32[24,1152]{1,0:T(8,128)S(1)} %get-tuple-element.65), channel_id=1, source_target_pairs={{0,1},{1,0},{2,3},{3,2},{4,5},{5,4},{6,7},{7,6},{8,9},{9,8},{10,11... | collective-permute-start | bytes 331784 | tf_op jit(solution)/shard_map/ppermute | solution.py:414
  59.8 7.5 %collective-permute-start.20 = (f32[24,1152]{1,0:T(8,128)S(1)}, f32[24,1152]{1,0:T(8,128)S(1)}, u32[]{:S(2)}, u32[]{:S(2)}) collective-permute-start(f32[24,1152]{1,0:T(8,128)S(1)} %get-tuple-element.66), channel_id=1, source_target_pairs={{0,3},{1,2},{2,1},{3,0},{4,7},{5,6},{6,5},{7,4},{8,11},{9,10},{10,... | collective-permute-start | bytes 331784 | tf_op jit(solution)/shard_map/ppermute | solution.py:414
  (7 other events, 5.0 us)

commit v12 on v11

--- a/solution.py
+++ b/solution.py
@@ -207,7 +207,7 @@
             pltpu.VMEM((NX, NY * NZ), jnp.float32),
         ],
         input_output_aliases={3 + len(tables): 1} if pieces == 1 else {},
-        compiler_params=pltpu.CompilerParams(vmem_limit_bytes=32 << 20),
+        compiler_params=pltpu.CompilerParams(vmem_limit_bytes=16 << 20),
         cost_estimate=pl.CostEstimate(flops=3 << 30, transcendentals=0, bytes_accessed=3 << 20),
         name="pair_step",
     )(weights, own, other, *tables, force, energy)
@@ -452,8 +452,9 @@
     for step in range(steps):
         ahead = pass_on(ahead, 1)
         behind = pass_on(behind, -1)
-        blocks.append((join(*ahead), group_at(position - step - 1)))
-        blocks.append((join(*behind), group_at(position + step + 1)))
+        joined = join(*ahead), join(*behind)
+        blocks.append((joined[0], group_at(position - step - 1)))
+        blocks.append((joined[1], group_at(position + step + 1)))
     head = shift(ahead[0], 1)
     tail = shift(behind[1], -1)
     blocks.append((join(head, tail), group_at(position + steps + 1)))

time: 68.8 us -> 68.8 us (level)
  no operation moved by 1% of the time
where the time goes in v12:
time: 68.8 us; the launch traced here: 68.5 us
  starting transfers between devices  31.5 us (46%)
  waiting for transfers between devices  18 us (26%)
  Pallas kernels  10 us (15%)
  local copies, waits for them, and re-layouts  7.31 us (11%)
  between operations  1.03 us (1%)
    ppermute x14, starting transfers between devices, shift(): return lax.ppermute(value, 'band', moves)  18.8 us
    ppermute x14, waiting for transfers between devices, shift(): return lax.ppermute(value, 'band', moves)  12.1 us
    unnamed x34, local copies, waits for them, and re-layouts  6.98 us
    pallas_call x7, Pallas kernels, pair_step(): pl.pallas_call(functools.partial(pair_kernel, slot), out_shape=outs, in_s...  6.88 us
    ppermute x7, starting transfers between devices, slab_swap(): return lax.ppermute(value, 'slab', [(i, i ^ reach) for i in range(size)])  6.58 us
    all_to_all x1, starting transfers between devices, body(): shared = lax.all_to_all(energy, ('band', 'slab'), 0, 0)  6.07 us
    all_to_all x1, waiting for transfers between devices, body(): shared = lax.all_to_all(energy, ('band', 'slab'), 0, 0)  5.15 us
  transfers between devices with their start and end apart: 22, of which 8 were waited for; matrix products, arithmetic and copies ran while one was open for 1% of the time, Pallas kernels for 12%

profile of v12, /device:TPU:0, one launch (start us, length us, event | category | flops | bytes accessed | tf_op | source)
XLA Modules:
  0.0 68.5 jit_solution(3694432001863166179)
XLA Ops:
  0.6 1.0 %copy-done = f32[4,12,2304]{2,0,1:T(4,128)S(1)} copy-done((f32[4,12,2304]{2,0,1:T(4,128)S(1)}, f32[4,12,2304]{2,0,1:T(4,128)}, u32[]{:S(2)}) %copy-start) | copy-done | bytes 442392
  1.7 0.8 %prepare.1 = (f32[24,1152]{1,0:T(8,128)S(1)}, f32[24,1152]{1,0:T(8,128)}, f32[24,1152]{1,0:T(8,128)S(1)}, f32[24,1152]{1,0:T(8,128)S(1)}) custom-call(s32[1]{0:T(128)} %bitcast.place, f32[12,4,2304]{2,1,0:T(4,128)S(1)} %bitcast.19), custom_call_target="tpu_custom_call" | custom-call | tf_op jit(solution)/shard_map/prepare/pallas_call | solution.py:249
  2.9 2.5 %collective-permute-start.1 = (f32[24,1152]{1,0:T(8,128)S(1)}, f32[24,1152]{1,0:T(8,128)S(1)}, u32[]{:S(2)}, u32[]{:S(2)}) collective-permute-start(f32[24,1152]{1,0:T(8,128)S(1)} %get-tuple-element.37), channel_id=1, source_target_pairs={{0,2},{1,3},{2,0},{3,1},{4,6},{5,7},{6,4},{7,5},{8,10},{9,11},{10,... | collective-permute-start | bytes 331784 | tf_op jit(solution)/shard_map/ppermute | solution.py:414
  5.7 1.0 %copy-done.3 = bf16[10,48,288]{2,1,0:T(8,128)(2,1)S(1)} copy-done((bf16[10,48,288]{2,1,0:T(8,128)(2,1)S(1)}, bf16[10,48,288]{2,1,0:T(8,128)(2,1)}, u32[]{:S(2)}) %copy-start.3) | copy-done | bytes 276504
  6.6 0.9 %copy-done.4 = bf16[576,128]{1,0:T(8,128)(2,1)S(1)} copy-done((bf16[576,128]{1,0:T(8,128)(2,1)S(1)}, bf16[576,128]{1,0:T(8,128)(2,1)}, u32[]{:S(2)}) %copy-start.4) | copy-done | bytes 147480
  7.7 0.6 copy-done.5
  10.2 1.9 %collective-permute-start.3 = (f32[24,2304]{1,0:T(8,128)S(1)}, f32[24,2304]{1,0:T(8,128)S(1)}, u32[]{:S(2)}, u32[]{:S(2)}) collective-permute-start(f32[24,2304]{1,0:T(8,128)S(1)} %assemble.2.refs_0_), channel_id=1, source_target_pairs={{0,8},{8,16},{16,24},{24,28},{28,20},{20,12},{12,4},{4,0},{1,9},{9... | collective-permute-start | bytes 663560 | tf_op jit(solution)/shard_map/ppermute | solution.py:444
  12.2 0.7 %collective-permute-start.6 = (f32[24,2304]{1,0:T(8,128)S(1)}, f32[24,2304]{1,0:T(8,128)S(1)}, u32[]{:S(2)}, u32[]{:S(2)}) collective-permute-start(f32[24,2304]{1,0:T(8,128)S(1)} %assemble.3.refs_1_), channel_id=1, source_target_pairs={{0,4},{8,0},{16,8},{24,16},{28,24},{20,28},{12,20},{4,12},{1,5},{9... | collective-permute-start | bytes 663560 | tf_op jit(solution)/shard_map/ppermute | solution.py:444
  12.9 1.6 %collective-permute-start.5 = (f32[24,2304]{1,0:T(8,128)S(1)}, f32[24,2304]{1,0:T(8,128)S(1)}, u32[]{:S(2)}, u32[]{:S(2)}) collective-permute-start(f32[24,2304]{1,0:T(8,128)S(1)} %assemble.2.refs_0_), channel_id=1, source_target_pairs={{0,4},{8,0},{16,8},{24,16},{28,24},{20,28},{12,20},{4,12},{1,5},{9... | collective-permute-start | bytes 663560 | tf_op jit(solution)/shard_map/ppermute | solution.py:444
  15.6 3.0 %collective-permute-done.3.refs_0_ = f32[24,2304]{1,0:T(8,128)S(1)} collective-permute-done((f32[24,2304]{1,0:T(8,128)S(1)}, f32[24,2304]{1,0:T(8,128)S(1)}, u32[]{:S(2)}, u32[]{:S(2)}) %collective-permute-start.3) | collective-permute-done | bytes 221216 | tf_op jit(solution)/shard_map/ppermute | solution.py:444
  18.6 1.8 %collective-permute-start.7 = (f32[24,2304]{1,0:T(8,128)S(1)}, f32[24,2304]{1,0:T(8,128)S(1)}, u32[]{:S(2)}, u32[]{:S(2)}) collective-permute-start(f32[24,2304]{1,0:T(8,128)S(1)} %collective-permute-done.3.refs_0_), channel_id=1, source_target_pairs={{0,8},{8,16},{16,24},{24,28},{28,20},{20,12},{12,4},{4,0},{1,9},{9... | collective-permute-start | bytes 663560 | tf_op jit(solution)/shard_map/ppermute | solution.py:444
  20.4 2.9 %collective-permute-done.4.refs_1_ = f32[24,2304]{1,0:T(8,128)S(1)} collective-permute-done((f32[24,2304]{1,0:T(8,128)S(1)}, f32[24,2304]{1,0:T(8,128)S(1)}, u32[]{:S(2)}, u32[]{:S(2)}) %collective-permute-start.4) | collective-permute-done | bytes 221216 | tf_op jit(solution)/shard_map/ppermute | solution.py:444
  23.3 1.8 %collective-permute-start.8 = (f32[24,2304]{1,0:T(8,128)S(1)}, f32[24,2304]{1,0:T(8,128)S(1)}, u32[]{:S(2)}, u32[]{:S(2)}) collective-permute-start(f32[24,2304]{1,0:T(8,128)S(1)} %collective-permute-done.4.refs_1_), channel_id=1, source_target_pairs={{0,8},{8,16},{16,24},{24,28},{28,20},{20,12},{12,4},{4,0},{1,9},{9... | collective-permute-start | bytes 663560 | tf_op jit(solution)/shard_map/ppermute | solution.py:444
  25.5 0.9 %copy-done.6 = bf16[384,128]{1,0:T(8,128)(2,1)S(1)} copy-done((bf16[384,128]{1,0:T(8,128)(2,1)S(1)}, bf16[384,128]{1,0:T(8,128)(2,1)}, u32[]{:S(2)}) %copy-start.6) | copy-done | bytes 98328
  26.4 0.7 %copy-done.13 = bf16[48,144]{1,0:T(8,128)(2,1)S(1)} copy-done((bf16[48,144]{1,0:T(8,128)(2,1)S(1)}, bf16[48,144]{1,0:T(8,128)(2,1)}, u32[]{:S(2)}) %copy-start.13) | copy-done | bytes 13848
  27.3 1.8 %collective-permute-start.9 = (f32[24,2304]{1,0:T(8,128)S(1)}, f32[24,2304]{1,0:T(8,128)S(1)}, u32[]{:S(2)}, u32[]{:S(2)}) collective-permute-start(f32[24,2304]{1,0:T(8,128)S(1)} %collective-permute-done.5.refs_0_), channel_id=1, source_target_pairs={{0,4},{8,0},{16,8},{24,16},{28,24},{20,28},{12,20},{4,12},{1,5},{9... | collective-permute-start | bytes 663560 | tf_op jit(solution)/shard_map/ppermute | solution.py:444
  29.1 2.7 %pair_step.8 = (f32[1,128]{1,0:T(1,128)S(1)}, f32[48,2304]{1,0:T(8,128)S(1)}) custom-call(f32[14,128]{1,0:T(8,128)S(1)} %broadcast_in_dim.73.weights, f32[48,2304]{1,0:T(8,128)S(1)} %join.8.refs_0_.own_ref, f32[48,2304]{1,0:T(8,128)S(1)} %join.10.refs_2_.other_ref, bf16[48,144]{1,0:T(8,128)(2,1)S(1)} %copy-done.9, ...), custom_call_target="tpu_custom_call", output_to_operand_aliasing={{1}: (10, {})} | custom-call | flops 3221225472 | bytes 3145728 | tf_op jit(solution)/shard_map/pair_step/pallas_call | solution.py:198
  32.1 4.5 %collective-permute-start.12 = (f32[24,2304]{1,0:T(8,128)S(1)}, f32[24,2304]{1,0:T(8,128)S(1)}, u32[]{:S(2)}, u32[]{:S(2)}) collective-permute-start(f32[24,2304]{1,0:T(8,128)S(1)} %collective-permute-done.8.refs_1_), channel_id=1, source_target_pairs={{0,8},{8,16},{16,24},{24,28},{28,20},{20,12},{12,4},{4,0},{1,9},{9... | collective-permute-start | bytes 663560 | tf_op jit(solution)/shard_map/ppermute | solution.py:444
  36.9 2.0 %collective-permute-start.13 = (f32[24,2304]{1,0:T(8,128)S(1)}, f32[24,2304]{1,0:T(8,128)S(1)}, u32[]{:S(2)}, u32[]{:S(2)}) collective-permute-start(f32[24,2304]{1,0:T(8,128)S(1)} %collective-permute-done.9.refs_0_), channel_id=1, source_target_pairs={{0,4},{8,0},{16,8},{24,16},{28,24},{20,28},{12,20},{4,12},{1,5},{9... | collective-permute-start | bytes 663560 | tf_op jit(solution)/shard_map/ppermute | solution.py:444
  38.9 2.7 %pair_step.10 = (f32[1,128]{1,0:T(1,128)S(1)}, f32[48,2304]{1,0:T(8,128)S(1)}) custom-call(f32[14,128]{1,0:T(8,128)S(1)} %broadcast_in_dim.73.weights, f32[48,2304]{1,0:T(8,128)S(1)} %join.8.refs_0_.own_ref, f32[48,2304]{1,0:T(8,128)S(1)} %join.12.refs_4_.other_ref, bf16[48,144]{1,0:T(8,128)(2,1)S(1)} %copy-done.9, ...), custom_call_target="tpu_custom_call", output_to_operand_aliasing={{1}: (10, {})} | custom-call | flops 3221225472 | bytes 3145728 | tf_op jit(solution)/shard_map/pair_step/pallas_call | solution.py:198
  41.7 1.5 %collective-permute-done.14.refs_1_ = f32[24,2304]{1,0:T(8,128)S(1)} collective-permute-done((f32[24,2304]{1,0:T(8,128)S(1)}, f32[24,2304]{1,0:T(8,128)S(1)}, u32[]{:S(2)}, u32[]{:S(2)}) %collective-permute-start.14) | collective-permute-done | bytes 221216 | tf_op jit(solution)/shard_map/ppermute | solution.py:444
  43.2 1.8 %collective-permute-start.16 = (f32[24,2304]{1,0:T(8,128)S(1)}, f32[24,2304]{1,0:T(8,128)S(1)}, u32[]{:S(2)}, u32[]{:S(2)}) collective-permute-start(f32[24,2304]{1,0:T(8,128)S(1)} %collective-permute-done.14.refs_1_), channel_id=1, source_target_pairs={{0,4},{8,0},{16,8},{24,16},{28,24},{20,28},{12,20},{4,12},{1,5},{9... | collective-permute-start | bytes 663560 | tf_op jit(solution)/shard_map/ppermute | solution.py:444
  45.4 2.4 %collective-permute-done.13.refs_0_ = f32[24,2304]{1,0:T(8,128)S(1)} collective-permute-done((f32[24,2304]{1,0:T(8,128)S(1)}, f32[24,2304]{1,0:T(8,128)S(1)}, u32[]{:S(2)}, u32[]{:S(2)}) %collective-permute-start.13) | collective-permute-done | bytes 221216 | tf_op jit(solution)/shard_map/ppermute | solution.py:444
  47.9 2.2 %collective-permute-done.16.refs_1_ = f32[24,2304]{1,0:T(8,128)S(1)} collective-permute-done((f32[24,2304]{1,0:T(8,128)S(1)}, f32[24,2304]{1,0:T(8,128)S(1)}, u32[]{:S(2)}, u32[]{:S(2)}) %collective-permute-start.16) | collective-permute-done | bytes 221216 | tf_op jit(solution)/shard_map/ppermute | solution.py:444
  50.5 0.8 %pair_step.13 = (f32[32,1,128]{2,1,0:T(1,128)}, f32[24,1152]{1,0:T(8,128)S(1)}, f32[24,1152]{1,0:T(8,128)S(1)}, f32[24,1152]{1,0:T(8,128)S(1)}, f32[24,1152]{1,0:T(8,128)S(1)}) custom-call(f32[14,128]{1,0:T(8,128)S(1)} %broadcast_in_dim.73.weights, f32[48,2304]{1,0:T(8,128)S(1)} %join.8.refs_0_.own_ref, f32[48,2304]{1,0:T(8,128)S(1)} %join.15.refs_7_.other_ref, ...), custom_call_target="tpu_custom_call" | custom-call | flops 3221225472 | bytes 3145728 | tf_op jit(solution)/shard_map/pair_step/pallas_call | solution.py:198
  51.3 0.7 collective-permute-done.17.theirs
  52.0 1.4 %collective-permute-start.18 = (f32[48,1152]{1,0:T(8,128)S(1)}, f32[48,1152]{1,0:T(8,128)S(1)}, u32[]{:S(2)}, u32[]{:S(2)}) collective-permute-start(f32[48,1152]{1,0:T(8,128)S(1)} %pack.1), channel_id=1, source_target_pairs={{0,2},{1,3},{2,0},{3,1},{4,6},{5,7},{6,4},{7,5},{8,10},{9,11},{10,... | collective-permute-start | bytes 663560 | tf_op jit(solution)/shard_map/ppermute | solution.py:414
  53.4 6.1 %all-to-all-start = ((f32[32,1,128]{2,1,0:T(1,128)}), f32[32,1,128]{2,1,0:T(1,128)S(1)}, u32[]{:S(2)}, u32[]{:S(2)}) async-start(f32[32,1,128]{2,1,0:T(1,128)} %get-tuple-element.67), calls=%async_computation | async-start | bytes 32768 | tf_op jit(solution)/shard_map/all_to_all | solution.py:513
  59.8 1.6 %collective-permute-start.20 = (f32[24,1152]{1,0:T(8,128)S(1)}, f32[24,1152]{1,0:T(8,128)S(1)}, u32[]{:S(2)}, u32[]{:S(2)}) collective-permute-start(f32[24,1152]{1,0:T(8,128)S(1)} %get-tuple-element.66), channel_id=1, source_target_pairs={{0,3},{1,2},{2,1},{3,0},{4,7},{5,6},{6,5},{7,4},{8,11},{9,10},{10,... | collective-permute-start | bytes 331784 | tf_op jit(solution)/shard_map/ppermute | solution.py:414
  61.4 5.2 %all-to-all-done.shared = f32[32,1,128]{2,1,0:T(1,128)S(1)} async-done(((f32[32,1,128]{2,1,0:T(1,128)}), f32[32,1,128]{2,1,0:T(1,128)S(1)}, u32[]{:S(2)}, u32[]{:S(2)}) %all-to-all-start) | async-done | bytes 16416 | tf_op jit(solution)/shard_map/all_to_all | solution.py:513
  66.6 0.6 total.1
  67.4 1.1 %finish.1 = f32[12,4,2304]{2,1,0:T(4,128)} custom-call(s32[1]{0:T(128)} %bitcast.place, f32[12,4,2304]{2,1,0:T(4,128)S(1)} %bitcast.20, f32[24,1152]{1,0:T(8,128)S(1)} %fusion.2.local_pot, f32[24,1152]{1,0:T(8,128)S(1)} %get-tuple-element.64.refs_0_, f32[24,1152]{1,0:T(8,128)S(1)} %collective-permute-done.19.refs_1_, ...), custom_call_target="tpu_custom_call" | custom-call | tf_op jit(solution)/shard_map/finish/pallas_call | solution.py:402
  (83 shorter events, 6.4 us)
Async XLA Ops:
  0.6 1.0 %copy-start = (f32[4,12,2304]{2,0,1:T(4,128)S(1)}, f32[4,12,2304]{2,0,1:T(4,128)}, u32[]{:S(2)}) copy-start(f32[4,12,2304]{2,0,1:T(4,128)} %param.6) | copy-start | bytes 1327108
  1.7 4.0 %copy-start.2 = (f32[96,3072]{1,0:T(8,128)S(1)}, f32[96,3072]{1,0:T(8,128)}, u32[]{:S(2)}) copy-start(f32[96,3072]{1,0:T(8,128)} %constant.100.clone.flat) | copy-start | bytes 3538948
  2.4 7.8 %collective-permute-start = (f32[24,1152]{1,0:T(8,128)}, f32[24,1152]{1,0:T(8,128)S(1)}, u32[]{:S(2)}, u32[]{:S(2)}) collective-permute-start(f32[24,1152]{1,0:T(8,128)} %get-tuple-element.36), channel_id=1, source_target_pairs={{0,1},{1,0},{2,3},{3,2},{4,5},{5,4},{6,7},{7,6},{8,9},{9,8},{10,11... | collective-permute-start | bytes 331784 | tf_op jit(solution)/shard_map/ppermute | solution.py:414
  2.9 9.2 %collective-permute-start.1 = (f32[24,1152]{1,0:T(8,128)S(1)}, f32[24,1152]{1,0:T(8,128)S(1)}, u32[]{:S(2)}, u32[]{:S(2)}) collective-permute-start(f32[24,1152]{1,0:T(8,128)S(1)} %get-tuple-element.37), channel_id=1, source_target_pairs={{0,2},{1,3},{2,0},{3,1},{4,6},{5,7},{6,4},{7,5},{8,10},{9,11},{10,... | collective-permute-start | bytes 331784 | tf_op jit(solution)/shard_map/ppermute | solution.py:414
  5.4 6.7 %collective-permute-start.2 = (f32[24,1152]{1,0:T(8,128)S(1)}, f32[24,1152]{1,0:T(8,128)S(1)}, u32[]{:S(2)}, u32[]{:S(2)}) collective-permute-start(f32[24,1152]{1,0:T(8,128)S(1)} %get-tuple-element.38), channel_id=1, source_target_pairs={{0,3},{1,2},{2,1},{3,0},{4,7},{5,6},{6,5},{7,4},{8,11},{9,10},{10,... | collective-permute-start | bytes 331784 | tf_op jit(solution)/shard_map/ppermute | solution.py:414
  5.6 1.0 %copy-start.3 = (bf16[10,48,288]{2,1,0:T(8,128)(2,1)S(1)}, bf16[10,48,288]{2,1,0:T(8,128)(2,1)}, u32[]{:S(2)}) copy-start(bf16[10,48,288]{2,1,0:T(8,128)(2,1)} %constant.98.clone.wides) | copy-start | bytes 829444
  10.1 4.8 %copy-start.15 = (s32[8,2]{0,1:T(2,128)S(1)}, s32[8,2]{0,1:T(2,128)}, u32[]{:S(2)}) copy-start(s32[8,2]{0,1:T(2,128)} %param.7) | copy-start | bytes 196
  10.1 4.9 %copy-start.16 = (s32[8,2]{0,1:T(2,128)S(1)}, s32[8,2]{0,1:T(2,128)}, u32[]{:S(2)}) copy-start(s32[8,2]{0,1:T(2,128)} %param.8) | copy-start | bytes 196
  10.2 15.3 %copy-start.9 = (bf16[48,144]{1,0:T(8,128)(2,1)S(1)}, bf16[48,144]{1,0:T(8,128)(2,1)}, u32[]{:S(2)}) copy-start(bf16[48,144]{1,0:T(8,128)(2,1)} %copy-done.8) | copy-start | bytes 41476
  10.2 15.3 %copy-start.11 = (bf16[48,144]{1,0:T(8,128)(2,1)S(1)}, bf16[48,144]{1,0:T(8,128)(2,1)}, u32[]{:S(2)}) copy-start(bf16[48,144]{1,0:T(8,128)(2,1)} %copy-done.10) | copy-start | bytes 41476
  10.2 8.4 %collective-permute-start.3 = (f32[24,2304]{1,0:T(8,128)S(1)}, f32[24,2304]{1,0:T(8,128)S(1)}, u32[]{:S(2)}, u32[]{:S(2)}) collective-permute-start(f32[24,2304]{1,0:T(8,128)S(1)} %assemble.2.refs_0_), channel_id=1, source_target_pairs={{0,8},{8,16},{16,24},{24,28},{28,20},{20,12},{12,4},{4,0},{1,9},{9... | collective-permute-start | bytes 663560 | tf_op jit(solution)/shard_map/ppermute | solution.py:444
  12.2 13.0 %collective-permute-start.6 = (f32[24,2304]{1,0:T(8,128)S(1)}, f32[24,2304]{1,0:T(8,128)S(1)}, u32[]{:S(2)}, u32[]{:S(2)}) collective-permute-start(f32[24,2304]{1,0:T(8,128)S(1)} %assemble.3.refs_1_), channel_id=1, source_target_pairs={{0,4},{8,0},{16,8},{24,16},{28,24},{20,28},{12,20},{4,12},{1,5},{9... | collective-permute-start | bytes 663560 | tf_op jit(solution)/shard_map/ppermute | solution.py:444
  12.9 14.4 %collective-permute-start.5 = (f32[24,2304]{1,0:T(8,128)S(1)}, f32[24,2304]{1,0:T(8,128)S(1)}, u32[]{:S(2)}, u32[]{:S(2)}) collective-permute-start(f32[24,2304]{1,0:T(8,128)S(1)} %assemble.2.refs_0_), channel_id=1, source_target_pairs={{0,4},{8,0},{16,8},{24,16},{28,24},{20,28},{12,20},{4,12},{1,5},{9... | collective-permute-start | bytes 663560 | tf_op jit(solution)/shard_map/ppermute | solution.py:444
  14.5 8.9 %collective-permute-start.4 = (f32[24,2304]{1,0:T(8,128)S(1)}, f32[24,2304]{1,0:T(8,128)S(1)}, u32[]{:S(2)}, u32[]{:S(2)}) collective-permute-start(f32[24,2304]{1,0:T(8,128)S(1)} %assemble.3.refs_1_), channel_id=1, source_target_pairs={{0,8},{8,16},{16,24},{24,28},{28,20},{20,12},{12,4},{4,0},{1,9},{9... | collective-permute-start | bytes 663560 | tf_op jit(solution)/shard_map/ppermute | solution.py:444
  18.6 13.3 %collective-permute-start.7 = (f32[24,2304]{1,0:T(8,128)S(1)}, f32[24,2304]{1,0:T(8,128)S(1)}, u32[]{:S(2)}, u32[]{:S(2)}) collective-permute-start(f32[24,2304]{1,0:T(8,128)S(1)} %collective-permute-done.3.refs_0_), channel_id=1, source_target_pairs={{0,8},{8,16},{16,24},{24,28},{28,20},{20,12},{12,4},{4,0},{1,9},{9... | collective-permute-start | bytes 663560 | tf_op jit(solution)/shard_map/ppermute | solution.py:444
  23.3 8.8 %collective-permute-start.8 = (f32[24,2304]{1,0:T(8,128)S(1)}, f32[24,2304]{1,0:T(8,128)S(1)}, u32[]{:S(2)}, u32[]{:S(2)}) collective-permute-start(f32[24,2304]{1,0:T(8,128)S(1)} %collective-permute-done.4.refs_1_), channel_id=1, source_target_pairs={{0,8},{8,16},{16,24},{24,28},{28,20},{20,12},{12,4},{4,0},{1,9},{9... | collective-permute-start | bytes 663560 | tf_op jit(solution)/shard_map/ppermute | solution.py:444
  25.2 11.5 %collective-permute-start.10 = (f32[24,2304]{1,0:T(8,128)S(1)}, f32[24,2304]{1,0:T(8,128)S(1)}, u32[]{:S(2)}, u32[]{:S(2)}) collective-permute-start(f32[24,2304]{1,0:T(8,128)S(1)} %collective-permute-done.6.refs_1_), channel_id=1, source_target_pairs={{0,4},{8,0},{16,8},{24,16},{28,24},{20,28},{12,20},{4,12},{1,5},{9... | collective-permute-start | bytes 663560 | tf_op jit(solution)/shard_map/ppermute | solution.py:444
  27.2 2.0 %copy-start.7 = (bf16[384,128]{1,0:T(8,128)(2,1)S(1)}, bf16[384,128]{1,0:T(8,128)(2,1)}, u32[]{:S(2)}) copy-start(bf16[384,128]{1,0:T(8,128)(2,1)} %copy-done.5) | copy-start | bytes 294916
  27.2 2.0 %copy-start.14 = (bf16[48,144]{1,0:T(8,128)(2,1)S(1)}, bf16[48,144]{1,0:T(8,128)(2,1)}, u32[]{:S(2)}) copy-start(bf16[48,144]{1,0:T(8,128)(2,1)} %copy-done.12) | copy-start | bytes 41476
  27.3 9.5 %collective-permute-start.9 = (f32[24,2304]{1,0:T(8,128)S(1)}, f32[24,2304]{1,0:T(8,128)S(1)}, u32[]{:S(2)}, u32[]{:S(2)}) collective-permute-start(f32[24,2304]{1,0:T(8,128)S(1)} %collective-permute-done.5.refs_0_), channel_id=1, source_target_pairs={{0,4},{8,0},{16,8},{24,16},{28,24},{20,28},{12,20},{4,12},{1,5},{9... | collective-permute-start | bytes 663560 | tf_op jit(solution)/shard_map/ppermute | solution.py:444
  31.9 9.7 %collective-permute-start.11 = (f32[24,2304]{1,0:T(8,128)S(1)}, f32[24,2304]{1,0:T(8,128)S(1)}, u32[]{:S(2)}, u32[]{:S(2)}) collective-permute-start(f32[24,2304]{1,0:T(8,128)S(1)} %collective-permute-done.7.refs_0_), channel_id=1, source_target_pairs={{0,8},{8,16},{16,24},{24,28},{28,20},{20,12},{12,4},{4,0},{1,9},{9... | collective-permute-start | bytes 663560 | tf_op jit(solution)/shard_map/ppermute | solution.py:444
  32.1 12.9 %collective-permute-start.12 = (f32[24,2304]{1,0:T(8,128)S(1)}, f32[24,2304]{1,0:T(8,128)S(1)}, u32[]{:S(2)}, u32[]{:S(2)}) collective-permute-start(f32[24,2304]{1,0:T(8,128)S(1)} %collective-permute-done.8.refs_1_), channel_id=1, source_target_pairs={{0,8},{8,16},{16,24},{24,28},{28,20},{20,12},{12,4},{4,0},{1,9},{9... | collective-permute-start | bytes 663560 | tf_op jit(solution)/shard_map/ppermute | solution.py:444
  36.6 6.6 %collective-permute-start.14 = (f32[24,2304]{1,0:T(8,128)S(1)}, f32[24,2304]{1,0:T(8,128)S(1)}, u32[]{:S(2)}, u32[]{:S(2)}) collective-permute-start(f32[24,2304]{1,0:T(8,128)S(1)} %collective-permute-done.10.refs_1_), channel_id=1, source_target_pairs={{0,4},{8,0},{16,8},{24,16},{28,24},{20,28},{12,20},{4,12},{1,5},{9... | collective-permute-start | bytes 663560 | tf_op jit(solution)/shard_map/ppermute | solution.py:444
  36.9 10.9 %collective-permute-start.13 = (f32[24,2304]{1,0:T(8,128)S(1)}, f32[24,2304]{1,0:T(8,128)S(1)}, u32[]{:S(2)}, u32[]{:S(2)}) collective-permute-start(f32[24,2304]{1,0:T(8,128)S(1)} %collective-permute-done.9.refs_0_), channel_id=1, source_target_pairs={{0,4},{8,0},{16,8},{24,16},{28,24},{20,28},{12,20},{4,12},{1,5},{9... | collective-permute-start | bytes 663560 | tf_op jit(solution)/shard_map/ppermute | solution.py:444
  41.6 6.3 %collective-permute-start.15 = (f32[24,2304]{1,0:T(8,128)S(1)}, f32[24,2304]{1,0:T(8,128)S(1)}, u32[]{:S(2)}, u32[]{:S(2)}) collective-permute-start(f32[24,2304]{1,0:T(8,128)S(1)} %collective-permute-done.11.refs_0_), channel_id=1, source_target_pairs={{0,8},{8,16},{16,24},{24,28},{28,20},{20,12},{12,4},{4,0},{1,9},{9... | collective-permute-start | bytes 663560 | tf_op jit(solution)/shard_map/ppermute | solution.py:444
  43.2 6.9 %collective-permute-start.16 = (f32[24,2304]{1,0:T(8,128)S(1)}, f32[24,2304]{1,0:T(8,128)S(1)}, u32[]{:S(2)}, u32[]{:S(2)}) collective-permute-start(f32[24,2304]{1,0:T(8,128)S(1)} %collective-permute-done.14.refs_1_), channel_id=1, source_target_pairs={{0,4},{8,0},{16,8},{24,16},{28,24},{20,28},{12,20},{4,12},{1,5},{9... | collective-permute-start | bytes 663560 | tf_op jit(solution)/shard_map/ppermute | solution.py:444
  50.4 1.5 %collective-permute-start.17 = (f32[2,24,1152]{2,1,0:T(8,128)S(1)}, f32[2,24,1152]{2,1,0:T(8,128)S(1)}, u32[]{:S(2)}, u32[]{:S(2)}) collective-permute-start(f32[2,24,1152]{2,1,0:T(8,128)S(1)} %get-tuple-element.41), channel_id=1, source_target_pairs={{0,1},{1,0},{2,3},{3,2},{4,5},{5,4},{6,7},{7,6},{8,9},{9,8},{10,11... | collective-permute-start | bytes 663560 | tf_op jit(solution)/shard_map/ppermute | solution.py:414
  51.3 16.1 %copy-start.1 = (f32[4,12,2304]{2,0,1:T(4,128)S(1)}, f32[4,12,2304]{2,0,1:T(4,128)}, u32[]{:S(2)}) copy-start(f32[4,12,2304]{2,0,1:T(4,128)} %param.6) | copy-start | bytes 1327108
  52.0 15.2 %collective-permute-start.18 = (f32[48,1152]{1,0:T(8,128)S(1)}, f32[48,1152]{1,0:T(8,128)S(1)}, u32[]{:S(2)}, u32[]{:S(2)}) collective-permute-start(f32[48,1152]{1,0:T(8,128)S(1)} %pack.1), channel_id=1, source_target_pairs={{0,2},{1,3},{2,0},{3,1},{4,6},{5,7},{6,4},{7,5},{8,10},{9,11},{10,... | collective-permute-start | bytes 663560 | tf_op jit(solution)/shard_map/ppermute | solution.py:414
  53.4 13.2 %all-to-all-start = ((f32[32,1,128]{2,1,0:T(1,128)}), f32[32,1,128]{2,1,0:T(1,128)S(1)}, u32[]{:S(2)}, u32[]{:S(2)}) async-start(f32[32,1,128]{2,1,0:T(1,128)} %get-tuple-element.67), calls=%async_computation | async-start | bytes 32768 | tf_op jit(solution)/shard_map/all_to_all | solution.py:513
  59.5 7.8 %collective-permute-start.19 = (f32[24,1152]{1,0:T(8,128)S(1)}, f32[24,1152]{1,0:T(8,128)S(1)}, u32[]{:S(2)}, u32[]{:S(2)}) collective-permute-start(f32[24,1152]{1,0:T(8,128)S(1)} %get-tuple-element.65), channel_id=1, source_target_pairs={{0,1},{1,0},{2,3},{3,2},{4,5},{5,4},{6,7},{7,6},{8,9},{9,8},{10,11... | collective-permute-start | bytes 331784 | tf_op jit(solution)/shard_map/ppermute | solution.py:414
  59.8 7.5 %collective-permute-start.20 = (f32[24,1152]{1,0:T(8,128)S(1)}, f32[24,1152]{1,0:T(8,128)S(1)}, u32[]{:S(2)}, u32[]{:S(2)}) collective-permute-start(f32[24,1152]{1,0:T(8,128)S(1)} %get-tuple-element.66), channel_id=1, source_target_pairs={{0,3},{1,2},{2,1},{3,0},{4,7},{5,6},{6,5},{7,4},{8,11},{9,10},{10,... | collective-permute-start | bytes 331784 | tf_op jit(solution)/shard_map/ppermute | solution.py:414
  (7 other events, 5.0 us)
